TPU v7x, 32 devices: a whole 2x2x4 slice. The times are simulated.
32 devices in a mesh: row: 8 (over z, core), vec: 4 (over y, x).
Axes of the slice: x: 2, y: 2, z: 4, core: 2. Of those that a mesh axis runs over, the one named last changes fastest.
Arguments:
- vectors: float32 [8192, 512], P('row', 'vec'), may hold values from -6 to 6
- reflectors: float32 [3, 8192, 512], P(None, ('row', 'vec')), may hold values from -0.0625 to 0.0625
- triangles: float32 [3, 512, 512], P(None, None, 'vec'), may hold values from -0.04 to 2, as said below
Outputs:
- transformed: float32 [8192, 512], P('row', 'vec')
Inputs may be any that keep to these rules, and one draw needn't show every extreme that they name: Each triangles[k] is upper triangular with a diagonal between 0.5 and 2.
All inputs are finite; a program needn't handle non-finite values.
Results may differ from a plain program's by a relative error of at most 0.0001.
Values sent between devices are 32-bit elements; how exact they have to be, the bound alone decides.
No kernel may reach another device: no remote copies, remote signals or barrier semaphores. Data moves between devices by JAX's collectives and lax.ppermute only.
A program may use at most 64 MiB of HBM per device.

v0:
```python
import jax
import jax.numpy as jnp
from jax import lax
from jax.sharding import PartitionSpec as P


def per_device(vectors, reflectors, triangles):
    highest = lax.Precision.HIGHEST
    panels = reflectors.shape[0]
    current = vectors
    for step in range(panels):
        panel = panels - 1 - step
        section = lax.all_gather(reflectors[panel], "vec", axis=0, tiled=True)
        factor = lax.all_gather(triangles[panel], "vec", axis=1, tiled=True)
        partial_value = lax.dot_general(
            section,
            current,
            (((0,), (0,)), ((), ())),
            precision=highest,
            preferred_element_type=jnp.float32,
        )
        share = lax.psum_scatter(partial_value, "row", scatter_dimension=1, tiled=True)
        owned = jnp.dot(factor, share, precision=highest, preferred_element_type=jnp.float32)
        coefficients = lax.all_gather(owned, "row", axis=1, tiled=True)
        current = current - jnp.dot(
            section, coefficients, precision=highest, preferred_element_type=jnp.float32
        )
    return current


def solution(mesh):
    return jax.shard_map(
        per_device,
        mesh=mesh,
        in_specs=(P("row", "vec"), P(None, ("row", "vec"), None), P(None, None, "vec")),
        out_specs=P("row", "vec"),
        check_vma=False,
    )
```

profile of v0, /device:TPU:0, one launch (start us, length us, event | category | flops | bytes accessed | tf_op | source)
XLA Modules:
  0.0 327.5 jit_solution(10815522950681176785)
XLA Ops:
  6.5 2.6 fusion.43
  9.3 0.9 fusion.44
  10.3 37.0 %all-gather.13.cloned.1.call-done = f32[1,1024,512]{2,1,0:T(8,128)} async-done(((f32[1,256,512]{2,1,0:T(8,128)}), f32[1,1024,512]{2,1,0:T(8,128)}) %all-gather.13.cloned.1.call-update) | async-done | bytes 2097168 | tf_op jit(solution)/shard_map/all_gather | solution.py:13
  47.3 3.7 %fusion.30 = f32[128,512]{1,0:T(8,128)} fusion(f32[1024,128]{1,0:T(8,128)S(1)} %copy-done.3, f32[1,1024,512]{2,1,0:T(8,128)} %all-gather.13.cloned.1.call-done), kind=kOutput, calls=%fused_computation.18 | convolution fusion | flops 805306368 | bytes 2883584
  52.4 23.1 %all-gather.15.cloned.1.call-done = f32[1,512,512]{2,1,0:T(8,128)} async-done(((f32[1,512,128]{2,1,0:T(8,128)}), f32[1,512,512]{2,1,0:T(8,128)}) %all-gather.15.cloned.1.call-update) | async-done | bytes 1048592 | tf_op jit(solution)/shard_map/all_gather | solution.py:14
  75.5 33.1 %reduce-scatter.10.cloned.1.call-done = f32[16,512]{1,0:T(8,128)} async-done(((f32[128,512]{1,0:T(8,128)}), f32[16,512]{1,0:T(8,128)}) %reduce-scatter.10.cloned.1.call-update) | async-done | bytes 32784
  108.6 2.2 convolution_bitcast_fusion.2
  110.8 14.2 %all_gather.29 = f32[512,128]{0,1:T(8,128)S(1)} all-gather(f32[512,16]{0,1:T(8,128)S(1)} %convolution_bitcast_fusion.2), channel_id=1, replica_groups=mesh['row'=8,'vec'=4] {'row'}, dimensions={1}, use_global_device_ids=true | all-gather | bytes 294912 | tf_op jit(solution)/shard_map/all_gather | solution.py:24
  125.0 2.3 fusion.27
  127.3 16.3 %all-gather.17.cloned.1.call-done = f32[1,1024,512]{2,1,0:T(8,128)} async-done(((f32[1,256,512]{2,1,0:T(8,128)}), f32[1,1024,512]{2,1,0:T(8,128)}) %all-gather.17.cloned.1.call-update) | async-done | bytes 2097168 | tf_op jit(solution)/shard_map/all_gather | solution.py:13
  143.6 3.7 %fusion.33 = f32[512,128]{0,1:T(8,128)} fusion(f32[1024,128]{0,1:T(8,128)S(1)} %fusion.27, f32[1,1024,512]{2,1,0:T(8,128)} %all-gather.17.cloned.1.call-done), kind=kOutput, calls=%fused_computation.19 | convolution fusion | flops 805306368 | bytes 2883584 | tf_op jit(solution)/shard_map/dot_general | solution.py:15
  148.9 22.8 %all-gather.19.cloned.1.call-done = f32[1,512,512]{2,1,0:T(8,128)} async-done(((f32[1,512,128]{2,1,0:T(8,128)}), f32[1,512,512]{2,1,0:T(8,128)}) %all-gather.19.cloned.1.call-update) | async-done | bytes 1048592 | tf_op jit(solution)/shard_map/all_gather | solution.py:14
  171.7 32.9 %reduce-scatter.6.cloned.1.call-done = f32[512,16]{0,1:T(8,128)} async-done(((f32[512,128]{0,1:T(8,128)}), f32[512,16]{0,1:T(8,128)}) %reduce-scatter.6.cloned.1.call-update) | async-done | bytes 32784 | tf_op jit(solution)/shard_map/reduce_scatter | solution.py:22
  204.6 2.2 convolution_bitcast_fusion.1
  206.8 14.2 %all_gather.32 = f32[512,128]{0,1:T(8,128)S(1)} all-gather(f32[512,16]{0,1:T(8,128)S(1)} %convolution_bitcast_fusion.1), channel_id=1, replica_groups=mesh['row'=8,'vec'=4] {'row'}, dimensions={1}, use_global_device_ids=true | all-gather | bytes 294912 | tf_op jit(solution)/shard_map/all_gather | solution.py:24
  221.0 2.3 fusion.24
  223.3 16.6 %all-gather.21.cloned.1.call-done = f32[1,1024,512]{2,1,0:T(8,128)} async-done(((f32[1,256,512]{2,1,0:T(8,128)}), f32[1,1024,512]{2,1,0:T(8,128)}) %all-gather.21.cloned.1.call-update) | async-done | bytes 2097168 | tf_op jit(solution)/shard_map/all_gather | solution.py:13
  239.8 3.7 %fusion.36 = f32[512,128]{0,1:T(8,128)} fusion(f32[1024,128]{0,1:T(8,128)S(1)} %fusion.24, f32[1,1024,512]{2,1,0:T(8,128)} %all-gather.21.cloned.1.call-done), kind=kOutput, calls=%fused_computation.20 | convolution fusion | flops 805306368 | bytes 2883584 | tf_op jit(solution)/shard_map/dot_general | solution.py:15
  243.6 24.5 %all-gather.23.cloned.1.call-done = f32[1,512,512]{2,1,0:T(8,128)} async-done(((f32[1,512,128]{2,1,0:T(8,128)}), f32[1,512,512]{2,1,0:T(8,128)}) %all-gather.23.cloned.1.call-update) | async-done | bytes 1048592 | tf_op jit(solution)/shard_map/all_gather | solution.py:14
  268.1 33.1 %reduce-scatter.8.cloned.1.call-done = f32[512,16]{0,1:T(8,128)} async-done(((f32[512,128]{0,1:T(8,128)}), f32[512,16]{0,1:T(8,128)}) %reduce-scatter.8.cloned.1.call-update) | async-done | bytes 32784 | tf_op jit(solution)/shard_map/reduce_scatter | solution.py:22
  301.2 2.2 convolution_bitcast_fusion
  303.4 14.4 %all_gather.35 = f32[512,128]{0,1:T(8,128)S(1)} all-gather(f32[512,16]{0,1:T(8,128)S(1)} %convolution_bitcast_fusion), channel_id=1, replica_groups=mesh['row'=8,'vec'=4] {'row'}, dimensions={1}, use_global_device_ids=true | all-gather | bytes 294912 | tf_op jit(solution)/shard_map/all_gather | solution.py:24
  317.7 2.3 fusion.21
  320.0 1.0 copy.7
  (29 shorter events, 3.1 us)
Async XLA Ops:
  6.5 2.7 copy-start.4
  6.5 40.7 %copy-start.3 = (f32[1024,128]{1,0:T(8,128)S(1)}, f32[1024,128]{1,0:T(8,128)}, u32[]{:S(2)}) copy-start(f32[1024,128]{1,0:T(8,128)} %param.3) | copy-start | bytes 1572868
  6.5 40.7 %all-gather.13.cloned.1.call-start = ((), (), s32[]{:S(2)}) async-start(), calls=%async_computation.5 | async-start | bytes 2621440 | tf_op jit(solution)/shard_map/all_gather | solution.py:13
  9.2 66.3 %all-gather.15.cloned.1.call-start = ((), (), s32[]{:S(2)}) async-start(), calls=%async_computation.6 | async-start | bytes 1310720 | tf_op jit(solution)/shard_map/all_gather | solution.py:14
  10.2 98.4 %reduce-scatter.10.cloned.1.call-start = ((), (), s32[]{:S(2)}) async-start(), calls=%async_computation.11 | async-start | bytes 294912
  51.0 74.0 %copy-start.1 = (f32[1,1024,512]{2,1,0:T(8,128)S(1)}, f32[1,1024,512]{2,1,0:T(8,128)}, u32[]{:S(2)}) copy-start(f32[1,1024,512]{2,1,0:T(8,128)} %all-gather.13.cloned.1.call-done) | copy-start | bytes 6291460
  51.0 92.6 %all-gather.17.cloned.1.call-start = ((), (), s32[]{:S(2)}) async-start(), calls=%async_computation.7 | async-start | bytes 2621440 | tf_op jit(solution)/shard_map/all_gather | solution.py:13
  51.6 120.1 %all-gather.19.cloned.1.call-start = ((), (), s32[]{:S(2)}) async-start(), calls=%async_computation.8 | async-start | bytes 1310720 | tf_op jit(solution)/shard_map/all_gather | solution.py:14
  52.2 152.4 %reduce-scatter.6.cloned.1.call-start = ((), (), s32[]{:S(2)}) async-start(), calls=%async_computation.3 | async-start | bytes 294912 | tf_op jit(solution)/shard_map/reduce_scatter | solution.py:22
  143.6 77.4 %copy-start = (f32[1,1024,512]{2,1,0:T(8,128)S(1)}, f32[1,1024,512]{2,1,0:T(8,128)}, u32[]{:S(2)}) copy-start(f32[1,1024,512]{2,1,0:T(8,128)} %all-gather.17.cloned.1.call-done) | copy-start | bytes 6291460
  147.4 92.5 %all-gather.21.cloned.1.call-start = ((), (), s32[]{:S(2)}) async-start(), calls=%async_computation.9 | async-start | bytes 2621440 | tf_op jit(solution)/shard_map/all_gather | solution.py:13
  148.1 119.9 %all-gather.23.cloned.1.call-start = ((), (), s32[]{:S(2)}) async-start(), calls=%async_computation.10 | async-start | bytes 1310720 | tf_op jit(solution)/shard_map/all_gather | solution.py:14
  148.9 152.3 %reduce-scatter.8.cloned.1.call-start = ((), (), s32[]{:S(2)}) async-start(), calls=%async_computation.4 | async-start | bytes 294912 | tf_op jit(solution)/shard_map/reduce_scatter | solution.py:22
  239.8 77.9 %copy-start.2 = (f32[1,1024,512]{2,1,0:T(8,128)S(1)}, f32[1,1024,512]{2,1,0:T(8,128)}, u32[]{:S(2)}) copy-start(f32[1,1024,512]{2,1,0:T(8,128)} %all-gather.21.cloned.1.call-done) | copy-start | bytes 6291460
Sparse Core Ops, SparseCore 0:
  9.3 37.8 all-gather.12
  49.1 26.3 all-gather.14
  77.7 30.8 reduce-scatter.9
  110.3 33.2 all-gather.16
  145.3 26.3 all-gather.18
  173.8 30.7 reduce-scatter.5
  206.4 33.3 all-gather.20
  241.7 26.3 all-gather.22
  270.3 30.8 reduce-scatter.7
where the time goes:
time: 328 us
  waiting for transfers between devices  242 us (74%)
  blocking collectives  42.7 us (13%)
  matrix products  24.6 us (8%)
  between operations  13.2 us (4%)
  local copies, waits for them, and re-layouts  4.77 us (1%)
    all_gather x3, waiting for transfers between devices, per_device(): factor = lax.all_gather(triangles[panel], 'vec', axis=1, tiled=True)  70.3 us
    all_gather x3, waiting for transfers between devices, per_device(): section = lax.all_gather(reflectors[panel], 'vec', axis=0, tiled=True)  69.9 us
    reduce_scatter x2, waiting for transfers between devices, per_device(): lax.psum_scatter(partial_value, 'row', scatter_dimension=1, tiled=True)  66 us
    all_gather x3, blocking collectives, per_device(): coefficients = lax.all_gather(owned, 'row', axis=1, tiled=True)  42.7 us
    unnamed x10, waiting for transfers between devices  35.6 us
    dot_general x2, matrix products, per_device(): lax.dot_general(section, current, (((0,), (0,)), ((), ())), precision=hig...  7.48 us
    dot_general x3, matrix products, per_device(): jnp.dot(section, coefficients, precision=highest, preferred_element_type=...  6.85 us
    dot_general x3, matrix products, per_device(): jnp.dot(factor, share, precision=highest, preferred_element_type=jnp.floa...  6.58 us
  transfers between devices with their start and end apart: 9, of which 9 were waited for; matrix products, arithmetic and copies ran while one was open for 6% of the time, Pallas kernels for 0%

commit v1 on v0

v1 whole, which is shorter than its diff:
```python
import functools

import jax
import jax.numpy as jnp
from jax import lax
from jax.experimental import pallas as pl
from jax.experimental.pallas import tpu as pltpu
from jax.sharding import Mesh, PartitionSpec as P

F32, BF16 = jnp.float32, jnp.bfloat16
NN = (((1,), (0,)), ((), ()))
NT = (((1,), (1,)), ((), ()))


def split(a):
    head = a.astype(BF16)
    return head, (a - head.astype(F32)).astype(BF16)


def dot3(a, b, dims):
    (ah, al), (bh, bl) = split(a), split(b)
    one = functools.partial(lax.dot_general, dimension_numbers=dims, preferred_element_type=F32)
    return one(ah, bh) + (one(ah, bl) + one(al, bh))


def place():
    return lax.axis_index("y") * 2 + lax.axis_index("x"), lax.axis_index("core")


def blocks_of(refs, width):
    own, along_x, along_y, low, high = refs
    rows = own.shape[-2]
    half = rows // 2
    return [
        (0, 0, rows, own),
        (1, 0, rows, along_x),
        (2, 0, rows, along_y),
        (3, 0, half, low),
        (3, half, half, high),
    ]


def window(place_v, block, first, size, rows):
    return pl.ds(pl.multiple_of((place_v ^ block) * rows + first, 8), size)


def project(total, current, refs, v, width):
    rows = refs[0].shape[-2]
    for block, first, size, ref in blocks_of(refs, width):
        x = current[window(v, block, first, size, rows), :]
        part = dot3(x.T, ref[:, :width], NN)
        total = part if total is None else total + part
    return total


def give_out(total, core, keep, send):
    half = keep.shape[0]
    mine = core == 0
    keep[...] = jnp.where(mine, total[:half], total[half:])
    send[...] = jnp.where(mine, total[half:], total[:half])


def first_kernel(width, x, *refs):
    v, core = place()
    refs, (keep, send) = refs[:5], refs[5:]
    give_out(project(None, x, refs, v, width), core, keep, send)


def both_halves(mine, other, core):
    a, b = mine[...], other[...]
    first = core == 0
    return jnp.concatenate([jnp.where(first, a, b), jnp.where(first, b, a)], axis=0)


def update(current, out, refs, coefficients, v, width):
    rows = refs[0].shape[-2]
    for block, first, size, ref in blocks_of(refs, width):
        at = window(v, block, first, size, rows)
        out[at, :] = current[at, :] - dot3(ref[:, :width], coefficients, NT)


def middle_kernel(width, x, mine, other, *refs):
    v, core = place()
    old, new, (out, keep, send) = refs[:5], refs[5:10], refs[10:]
    update(x, out, old, both_halves(mine, other, core), v, width)
    give_out(project(None, out, new, v, width), core, keep, send)


def last_kernel(width, x, mine, other, *refs):
    v, core = place()
    update(x, refs[5], refs[:5], both_halves(mine, other, core), v, width)


def solve_kernel(panel, column, s, r1, r2, r3, factor, exchanged, along_x, along_y, low, high, out):
    v, core = place()
    total = (s[...] + r1[...]) + (r2[...] + r3[...])
    share = factor.shape[-1]
    half = factor.shape[-2] // 2
    at = pl.ds(column, share)
    ex = exchanged.shape[-1] // 3
    mine = [
        factor[panel, pl.ds(pl.multiple_of(core * half, 8), half), :],
        along_x[:, at],
        along_y[:, at],
        jnp.concatenate([low[:, at], high[:, at]], axis=0),
    ]
    other = [factor[panel, pl.ds(pl.multiple_of((1 - core) * half, 8), half), :]]
    other += [exchanged[:, i * ex : i * ex + share] for i in range(3)]
    sums = [None, None]
    parts = split_columns(total, v, share)
    for block in range(4):
        for i, t in enumerate((mine[block], other[block])):
            part = dot3(parts[block], t, NT)
            sums[i] = part if sums[i] is None else sums[i] + part
    out[...] = jnp.where(core == 0, jnp.concatenate(sums, axis=1), jnp.concatenate(sums[::-1], axis=1))


def split_columns(total, v, share):
    b = [total[:, i * share : (i + 1) * share] for i in range(4)]
    odd, up = (v & 1) == 1, (v & 2) == 2
    p, q = jnp.where(odd, b[1], b[0]), jnp.where(odd, b[0], b[1])
    r, s = jnp.where(odd, b[3], b[2]), jnp.where(odd, b[2], b[3])
    return [jnp.where(up, r, p), jnp.where(up, s, q), jnp.where(up, p, r), jnp.where(up, q, s)]


def vmem(n):
    return [pl.BlockSpec(memory_space=pltpu.VMEM)] * n


def call(kernel, outs, args, flops, name):
    nbytes = sum(4 * a.size for a in args) + sum(4 * o.size for o in outs)
    return pl.pallas_call(
        kernel,
        out_shape=outs,
        in_specs=vmem(len(args)),
        out_specs=vmem(len(outs)),
        name=name,
        cost_estimate=pl.CostEstimate(flops=flops, bytes_accessed=nbytes, transcendentals=0),
    )(*args)


def swap(a, axis, by=1):
    n = lax.axis_size(axis)
    return lax.ppermute(a, axis, [(i, i ^ by) for i in range(n)])


def gather(pack):
    half = pack.shape[0] // 2
    along_x, along_y = swap(pack, "x"), swap(pack, "y")
    return pack, along_x, along_y, swap(along_y[:half], "x"), swap(along_x[half:], "y")


def fast(vectors, reflectors, triangles):
    rows, share = vectors.shape
    panels, own_rows, width = reflectors.shape
    core = lax.axis_index("core")
    half = width // 2
    part = jax.ShapeDtypeStruct((share // 2, width), F32)
    whole = jax.ShapeDtypeStruct((rows, share), F32)
    work = 2 * rows * width * share

    def factor_half(panel):
        return lax.dynamic_slice(triangles[panel], (core * half, 0), (half, share))

    riders = {panels - 1: []}
    for panel in range(panels - 1):
        riders[panel] = [panel + 1]
    riders[0] = riders[0] + [0]
    sections, factors = {}, {}
    for panel in reversed(range(panels)):
        pack = jnp.concatenate([reflectors[panel]] + [factor_half(r) for r in riders[panel]], axis=1)
        sections[panel] = gather(pack)
        received = sections[panel][1:]
        for i, r in enumerate(riders[panel]):
            at = width + i * share
            cut = [a[:, at : at + share] for a in received]
            mine = jnp.concatenate([cut[0], cut[1], jnp.concatenate(cut[2:], axis=0)], axis=1)
            factors[r] = (at, swap(mine, "core"), received)

    def reduced(keep, send, panel):
        s = keep + swap(send, "core")
        r = [swap(s, "z", by) for by in (1, 2, 3)]
        at, exchanged, received = factors[panel]
        mine = call(
            functools.partial(solve_kernel, panel, at),
            [part],
            [s, *r, triangles, exchanged, *received],
            2 * width * width * share // 2,
            "solve",
        )[0]
        return mine, swap(mine, "core")

    top = panels - 1
    keep, send = call(functools.partial(first_kernel, width), [part, part], [vectors, *sections[top]], work, "first")
    current = vectors
    for panel in reversed(range(1, panels)):
        c = reduced(keep, send, panel)
        current, keep, send = call(
            functools.partial(middle_kernel, width),
            [whole, part, part],
            [current, *c, *sections[panel], *sections[panel - 1]],
            2 * work,
            "middle",
        )
    c = reduced(keep, send, 0)
    return call(functools.partial(last_kernel, width), [whole], [current, *c, *sections[0]], work, "last")[0]


def general(vectors, reflectors, triangles):
    highest = lax.Precision.HIGHEST
    row, vec = ("z", "core"), ("y", "x")
    current = vectors
    for panel in reversed(range(reflectors.shape[0])):
        section = lax.all_gather(reflectors[panel], vec, axis=0, tiled=True)
        factor = lax.all_gather(triangles[panel], vec, axis=1, tiled=True)
        partial_value = lax.dot_general(
            section, current, (((0,), (0,)), ((), ())), precision=highest, preferred_element_type=F32
        )
        share = lax.psum_scatter(partial_value, row, scatter_dimension=1, tiled=True)
        owned = jnp.dot(factor, share, precision=highest, preferred_element_type=F32)
        coefficients = lax.all_gather(owned, row, axis=1, tiled=True)
        current = current - jnp.dot(section, coefficients, precision=highest, preferred_element_type=F32)
    return current


def solution(mesh):
    rows, vecs = mesh.shape["row"], mesh.shape["vec"]
    side = next(s for s in range(int(vecs**0.5), 0, -1) if vecs % s == 0)
    cores = 2 if rows % 2 == 0 else 1
    fine = Mesh(mesh.devices.reshape(rows // cores, cores, side, vecs // side), ("z", "core", "y", "x"))
    small = fine.devices.shape == (4, 2, 2, 2)
    row, vec = ("z", "core"), ("y", "x")
    return jax.shard_map(
        fast if small else general,
        mesh=fine,
        in_specs=(P(row, vec), P(None, row + vec, None), P(None, None, vec)),
        out_specs=P(row, vec),
        check_vma=False,
    )
```

time: 328 us -> 148 us (0.45)
  waiting for transfers between devices: 242 us -> 71 us
  blocking collectives: 42.7 us -> 0 us
  starting transfers between devices: 0.32 us -> 31.8 us
  Pallas kernels: 0 us -> 27.9 us
  matrix products: 24.6 us -> 0 us
  between operations: 13.2 us -> 0.37 us
  local copies, waits for them, and re-layouts: 4.77 us -> 14 us
    all_gather x6 -> x0, waiting for transfers between devices: 140 us -> none  [the longest x3 70.3 us: per_device(): factor = lax.all_gather(triangles[panel], 'vec', axis=1, tiled=True)]
    ppermute x0 -> x30, waiting for transfers between devices: none -> 71 us  [swap(): return lax.ppermute(a, axis, [(i, i ^ by) for i in range(n)])]
    reduce_scatter x2 -> x0, waiting for transfers between devices: 66 us -> none  [per_device(): lax.psum_scatter(partial_value, 'row', scatter_dimension=1, tiled=True)]
    all_gather x3 -> x0, blocking collectives: 42.7 us -> none  [per_device(): coefficients = lax.all_gather(owned, 'row', axis=1, tiled=True)]
    unnamed x10 -> x0, waiting for transfers between devices: 35.6 us -> none
    ppermute x0 -> x30, starting transfers between devices: none -> 31.8 us  [swap(): return lax.ppermute(a, axis, [(i, i ^ by) for i in range(n)])]
    pallas_call x0 -> x7, Pallas kernels: none -> 27.9 us  [call(): pl.pallas_call(kernel, out_shape=outs, in_specs=vmem(len(args)), out_spec...]
    dot_general x8 -> x0, matrix products: 20.9 us -> none  [the longest x2 7.48 us: per_device(): lax.dot_general(section, current, (((0,), (0,)), ((), ())), precision=hig...]
  transfers between devices with their start and end apart: 9 -> 30, of which waited for: 9 -> 16; matrix products, arithmetic and copies ran while one was open for 6% -> 5% of each run, Pallas kernels for 0% -> 9%
where the time goes in v1:
time: 148 us
  waiting for transfers between devices  71 us (48%)
  starting transfers between devices  31.8 us (21%)
  Pallas kernels  27.9 us (19%)
  local copies, waits for them, and re-layouts  14 us (9%)
  other arithmetic  3.02 us (2%)
    ppermute x30, waiting for transfers between devices, swap(): return lax.ppermute(a, axis, [(i, i ^ by) for i in range(n)])  71 us
    ppermute x30, starting transfers between devices, swap(): return lax.ppermute(a, axis, [(i, i ^ by) for i in range(n)])  31.8 us
    pallas_call x7, Pallas kernels, call(): pl.pallas_call(kernel, out_shape=outs, in_specs=vmem(len(args)), out_spec...  27.9 us
    unnamed x62, local copies, waits for them, and re-layouts  6.64 us
  transfers between devices with their start and end apart: 30, of which 16 were waited for; matrix products, arithmetic and copies ran while one was open for 5% of the time, Pallas kernels for 9%

profile of v1, /device:TPU:0, one launch (start us, length us, event | category | flops | bytes accessed | tf_op | source)
XLA Modules:
  0.0 148.1 jit_solution(15324131593987699517)
XLA Ops:
  0.0 2.4 %slice_bitcast_fusion = (f32[256,512]{1,0:T(8,128)S(1)}, f32[256,512]{1,0:T(8,128)}, f32[256,512]{1,0:T(8,128)S(1)}) fusion(f32[3,256,512]{2,1,0:T(8,128)} %param.4), kind=kLoop, calls=%fused_computation.2 | loop fusion | bytes 3145728 | tf_op jit(solution)/shard_map/squeeze | solution.py:171
  2.4 3.0 %collective-permute-start.1 = (f32[256,512]{1,0:T(8,128)}, f32[256,512]{1,0:T(8,128)}, u32[]{:S(2)}, u32[]{:S(2)}) collective-permute-start(f32[256,512]{1,0:T(8,128)} %get-tuple-element.22.refs_0_), channel_id=1, source_target_pairs={{0,2},{2,0},{1,3},{3,1},{4,6},{6,4},{5,7},{7,5},{8,10},{10,8},{9,1... | collective-permute-start | bytes 1572872 | tf_op jit(solution)/shard_map/ppermute | solution.py:144
  10.7 7.8 %collective-permute-done.1.refs_2_ = f32[256,512]{1,0:T(8,128)} collective-permute-done((f32[256,512]{1,0:T(8,128)}, f32[256,512]{1,0:T(8,128)}, u32[]{:S(2)}, u32[]{:S(2)}) %collective-permute-start.1) | collective-permute-done | bytes 524320 | tf_op jit(solution)/shard_map/ppermute | solution.py:144
  23.0 9.4 %collective-permute-done.9.along_y.refs_7_.refs_2_ = f32[256,640]{1,0:T(8,128)S(1)} collective-permute-done((f32[256,640]{1,0:T(8,128)S(1)}, f32[256,640]{1,0:T(8,128)S(1)}, u32[]{:S(2)}, u32[]{:S(2)}) %collective-permute-start.9) | collective-permute-done | bytes 655392 | tf_op jit(solution)/shard_map/ppermute | solution.py:144
  32.4 2.0 %collective-permute-start.3 = (f32[128,512]{1,0:T(8,128)S(1)}, f32[128,512]{1,0:T(8,128)}, u32[]{:S(2)}, u32[]{:S(2)}) collective-permute-start(f32[128,512]{1,0:T(8,128)S(1)} %slice.97), channel_id=1, source_target_pairs={{0,2},{2,0},{1,3},{3,1},{4,6},{6,4},{5,7},{7,5},{8,10},{10,8},{9,1... | collective-permute-start | bytes 786440 | tf_op jit(solution)/shard_map/ppermute | solution.py:144
  35.2 16.1 %collective-permute-done.8.along_x.refs_6_.refs_1_ = f32[256,640]{1,0:T(8,128)S(1)} collective-permute-done((f32[256,640]{1,0:T(8,128)S(1)}, f32[256,640]{1,0:T(8,128)S(1)}, u32[]{:S(2)}, u32[]{:S(2)}) %collective-permute-start.8) | collective-permute-done | bytes 655392 | tf_op jit(solution)/shard_map/ppermute | solution.py:144
  53.5 3.5 %collective-permute-done.2.refs_3_ = f32[128,512]{1,0:T(8,128)} collective-permute-done((f32[128,512]{1,0:T(8,128)S(1)}, f32[128,512]{1,0:T(8,128)}, u32[]{:S(2)}, u32[]{:S(2)}) %collective-permute-start.2) | collective-permute-done | bytes 262176 | tf_op jit(solution)/shard_map/ppermute | solution.py:144
  57.0 3.2 %first.1 = (f32[64,512]{1,0:T(8,128)}, f32[64,512]{1,0:T(8,128)}) custom-call(f32[1024,128]{1,0:T(8,128)} %x.3, f32[256,512]{1,0:T(8,128)} %get-tuple-element.22.refs_0_, f32[256,512]{1,0:T(8,128)} %collective-permute-done.refs_1_, f32[256,512]{1,0:T(8,128)} %collective-permute-done.1.refs_2_, f32[128,512]{1,0:T(8,128)} %collective-permute-done.2.refs_3_, ...), custom_call_target="tpu_custom_call" | custom-call | flops 134217728 | bytes 2883584 | tf_op jit(solution)/shard_map/first/pallas_call | solution.py:132
  60.3 2.1 %collective-permute-start.20 = (f32[128,768]{1,0:T(8,128)S(1)}, f32[128,768]{1,0:T(8,128)S(1)}, u32[]{:S(2)}, u32[]{:S(2)}) collective-permute-start(f32[128,768]{1,0:T(8,128)S(1)} %slice.106), channel_id=1, source_target_pairs={{0,1},{1,0},{2,3},{3,2},{4,5},{5,4},{6,7},{7,6},{8,9},{9,8},{10,11... | collective-permute-start | bytes 1179656 | tf_op jit(solution)/shard_map/ppermute | solution.py:144
  65.4 3.7 %collective-permute-start.7 = (f32[64,512]{1,0:T(8,128)S(1)}, f32[64,512]{1,0:T(8,128)S(1)}, u32[]{:S(2)}, u32[]{:S(2)}) collective-permute-start(f32[64,512]{1,0:T(8,128)S(1)} %add.14.s), channel_id=1, source_target_pairs={{0,24},{8,16},{16,8},{24,0},{1,25},{9,17},{17,9},{25,1},{2,26},{10... | collective-permute-start | bytes 393224 | tf_op jit(solution)/shard_map/ppermute | solution.py:144
  70.0 2.1 %collective-permute-done.20.low.refs_8_.refs_3_ = f32[128,768]{1,0:T(8,128)S(1)} collective-permute-done((f32[128,768]{1,0:T(8,128)S(1)}, f32[128,768]{1,0:T(8,128)S(1)}, u32[]{:S(2)}, u32[]{:S(2)}) %collective-permute-start.20) | collective-permute-done | bytes 393248 | tf_op jit(solution)/shard_map/ppermute | solution.py:144
  73.8 6.4 %collective-permute-done.6.r2 = f32[64,512]{1,0:T(8,128)S(1)} collective-permute-done((f32[64,512]{1,0:T(8,128)S(1)}, f32[64,512]{1,0:T(8,128)S(1)}, u32[]{:S(2)}, u32[]{:S(2)}) %collective-permute-start.6) | collective-permute-done | bytes 131104 | tf_op jit(solution)/shard_map/ppermute | solution.py:144
  82.3 3.4 %solve.3.mine = f32[64,512]{1,0:T(8,128)} custom-call(f32[64,512]{1,0:T(8,128)} %copy-done.14, f32[64,512]{1,0:T(8,128)} %copy-done.30, f32[64,512]{1,0:T(8,128)} %copy-done.29, f32[64,512]{1,0:T(8,128)} %copy-done.28, f32[3,512,128]{2,1,0:T(8,128)} %factor.5, f32[256,384]{1,0:T(8,128)} %copy-done.17, f32[256,640]{1,0:T(8,128)} %copy-done.4, ...), custom_call_target="tpu_custom_call" | custom-call | flops 33554432 | bytes 3801088 | tf_op jit(solution)/shard_map/solve/pallas_call | solution.py:132
  87.9 5.1 %middle.2 = (f32[1024,128]{1,0:T(8,128)}, f32[64,512]{1,0:T(8,128)}, f32[64,512]{1,0:T(8,128)}) custom-call(f32[1024,128]{1,0:T(8,128)} %x.3, f32[64,512]{1,0:T(8,128)} %solve.3.mine, f32[64,512]{1,0:T(8,128)} %copy-done.22, f32[256,512]{1,0:T(8,128)} %get-tuple-element.22.refs_0_, f32[256,512]{1,0:T(8,128)} %collective-permute-done.refs_1_, ...), custom_call_target="tpu_custom_call" | custom-call | flops 268435456 | bytes 6291456 | tf_op jit(solution)/shard_map/middle/pallas_call | solution.py:132
  95.5 2.5 %collective-permute-start.17 = (f32[64,512]{1,0:T(8,128)S(1)}, f32[64,512]{1,0:T(8,128)S(1)}, u32[]{:S(2)}, u32[]{:S(2)}) collective-permute-start(f32[64,512]{1,0:T(8,128)S(1)} %add.16.s), channel_id=1, source_target_pairs={{0,24},{8,16},{16,8},{24,0},{1,25},{9,17},{17,9},{25,1},{2,26},{10... | collective-permute-start | bytes 393224 | tf_op jit(solution)/shard_map/ppermute | solution.py:144
  100.0 3.9 %collective-permute-done.17.r3 = f32[64,512]{1,0:T(8,128)S(1)} collective-permute-done((f32[64,512]{1,0:T(8,128)S(1)}, f32[64,512]{1,0:T(8,128)S(1)}, u32[]{:S(2)}, u32[]{:S(2)}) %collective-permute-start.17) | collective-permute-done | bytes 131104 | tf_op jit(solution)/shard_map/ppermute | solution.py:144
  103.9 4.8 %collective-permute-done.16.r2 = f32[64,512]{1,0:T(8,128)S(1)} collective-permute-done((f32[64,512]{1,0:T(8,128)S(1)}, f32[64,512]{1,0:T(8,128)S(1)}, u32[]{:S(2)}, u32[]{:S(2)}) %collective-permute-start.16) | collective-permute-done | bytes 131104 | tf_op jit(solution)/shard_map/ppermute | solution.py:144
  110.0 3.5 %solve.4.mine = f32[64,512]{1,0:T(8,128)} custom-call(f32[64,512]{1,0:T(8,128)} %copy-done.10, f32[64,512]{1,0:T(8,128)} %copy-done.25, f32[64,512]{1,0:T(8,128)} %copy-done.23, f32[64,512]{1,0:T(8,128)} %copy-done.20, f32[3,512,128]{2,1,0:T(8,128)} %factor.5, f32[256,384]{1,0:T(8,128)} %copy-done.16, f32[256,768]{1,0:T(8,128)} %copy-done.1, ...), custom_call_target="tpu_custom_call" | custom-call | flops 33554432 | bytes 4194304 | tf_op jit(solution)/shard_map/solve/pallas_call | solution.py:132
  115.7 5.4 %middle.3 = (f32[1024,128]{1,0:T(8,128)}, f32[64,512]{1,0:T(8,128)}, f32[64,512]{1,0:T(8,128)}) custom-call(f32[1024,128]{1,0:T(8,128)} %get-tuple-element.15.x, f32[64,512]{1,0:T(8,128)} %solve.4.mine, f32[64,512]{1,0:T(8,128)} %copy-done.19, f32[256,640]{1,0:T(8,128)} %copy-done.7, f32[256,640]{1,0:T(8,128)} %copy-done.4, f32[256,640]{1,0:T(8,128)} %copy-done.3, ...), custom_call_target="tpu_custom_call" | custom-call | flops 268435456 | bytes 7340032 | tf_op jit(solution)/shard_map/middle/pallas_call | solution.py:132
  123.6 2.4 %collective-permute-start.27 = (f32[64,512]{1,0:T(8,128)S(1)}, f32[64,512]{1,0:T(8,128)S(1)}, u32[]{:S(2)}, u32[]{:S(2)}) collective-permute-start(f32[64,512]{1,0:T(8,128)S(1)} %add.17.s), channel_id=1, source_target_pairs={{0,24},{8,16},{16,8},{24,0},{1,25},{9,17},{17,9},{25,1},{2,26},{10... | collective-permute-start | bytes 393224 | tf_op jit(solution)/shard_map/ppermute | solution.py:144
  128.1 3.9 %collective-permute-done.27.r3 = f32[64,512]{1,0:T(8,128)S(1)} collective-permute-done((f32[64,512]{1,0:T(8,128)S(1)}, f32[64,512]{1,0:T(8,128)S(1)}, u32[]{:S(2)}, u32[]{:S(2)}) %collective-permute-start.27) | collective-permute-done | bytes 131104 | tf_op jit(solution)/shard_map/ppermute | solution.py:144
  132.0 5.1 %collective-permute-done.26.r2 = f32[64,512]{1,0:T(8,128)S(1)} collective-permute-done((f32[64,512]{1,0:T(8,128)S(1)}, f32[64,512]{1,0:T(8,128)S(1)}, u32[]{:S(2)}, u32[]{:S(2)}) %collective-permute-start.26) | collective-permute-done | bytes 131104 | tf_op jit(solution)/shard_map/ppermute | solution.py:144
  138.4 3.5 %solve.5.mine = f32[64,512]{1,0:T(8,128)} custom-call(f32[64,512]{1,0:T(8,128)} %copy-done.11, f32[64,512]{1,0:T(8,128)} %copy-done.26, f32[64,512]{1,0:T(8,128)} %copy-done.24, f32[64,512]{1,0:T(8,128)} %copy-done.21, f32[3,512,128]{2,1,0:T(8,128)} %factor.5, f32[256,384]{1,0:T(8,128)} %copy-done.15, f32[256,768]{1,0:T(8,128)} %copy-done.1, ...), custom_call_target="tpu_custom_call" | custom-call | flops 33554432 | bytes 4194304 | tf_op jit(solution)/shard_map/solve/pallas_call | solution.py:132
  144.2 3.9 %last.1 = f32[1024,128]{1,0:T(8,128)} custom-call(f32[1024,128]{1,0:T(8,128)} %get-tuple-element.18.x, f32[64,512]{1,0:T(8,128)} %solve.5.mine, f32[64,512]{1,0:T(8,128)} %copy-done.27, f32[256,768]{1,0:T(8,128)} %pad_maximum_fusion.refs_5_.refs_0_, f32[256,768]{1,0:T(8,128)} %copy-done.1, f32[256,768]{1,0:T(8,128)} %copy-done, f32[128,768]{1,0:T(8,128)} %copy-done.5, ...), custom_call_target="tpu_custom_call" | custom-call | flops 134217728 | bytes 4456448 | tf_op jit(solution)/shard_map/last/pallas_call | solution.py:132
  (133 shorter events, 38.5 us)
Async XLA Ops:
  2.4 16.1 %collective-permute-start.1 = (f32[256,512]{1,0:T(8,128)}, f32[256,512]{1,0:T(8,128)}, u32[]{:S(2)}, u32[]{:S(2)}) collective-permute-start(f32[256,512]{1,0:T(8,128)} %get-tuple-element.22.refs_0_), channel_id=1, source_target_pairs={{0,2},{2,0},{1,3},{3,1},{4,6},{6,4},{5,7},{7,5},{8,10},{10,8},{9,1... | collective-permute-start | bytes 1572872 | tf_op jit(solution)/shard_map/ppermute | solution.py:144
  5.4 16.1 %collective-permute-start = (f32[256,512]{1,0:T(8,128)}, f32[256,512]{1,0:T(8,128)}, u32[]{:S(2)}, u32[]{:S(2)}) collective-permute-start(f32[256,512]{1,0:T(8,128)} %get-tuple-element.22.refs_0_), channel_id=1, source_target_pairs={{0,1},{1,0},{2,3},{3,2},{4,5},{5,4},{6,7},{7,6},{8,9},{9,8},{10,11... | collective-permute-start | bytes 1572872 | tf_op jit(solution)/shard_map/ppermute | solution.py:144
  7.0 25.4 %collective-permute-start.9 = (f32[256,640]{1,0:T(8,128)S(1)}, f32[256,640]{1,0:T(8,128)S(1)}, u32[]{:S(2)}, u32[]{:S(2)}) collective-permute-start(f32[256,640]{1,0:T(8,128)S(1)} %pad_maximum_fusion.1.refs_5_.refs_0_), channel_id=1, source_target_pairs={{0,2},{2,0},{1,3},{3,1},{4,6},{6,4},{5,7},{7,5},{8,10},{10,8},{9,1... | collective-permute-start | bytes 1966088 | tf_op jit(solution)/shard_map/ppermute | solution.py:144
  8.6 51.7 %collective-permute-start.19 = (f32[256,768]{1,0:T(8,128)}, f32[256,768]{1,0:T(8,128)S(1)}, u32[]{:S(2)}, u32[]{:S(2)}) collective-permute-start(f32[256,768]{1,0:T(8,128)} %pad_maximum_fusion.refs_5_.refs_0_), channel_id=1, source_target_pairs={{0,2},{2,0},{1,3},{3,1},{4,6},{6,4},{5,7},{7,5},{8,10},{10,8},{9,1... | collective-permute-start | bytes 2359304 | tf_op jit(solution)/shard_map/ppermute | solution.py:144
  10.1 52.3 %collective-permute-start.18 = (f32[256,768]{1,0:T(8,128)}, f32[256,768]{1,0:T(8,128)S(1)}, u32[]{:S(2)}, u32[]{:S(2)}) collective-permute-start(f32[256,768]{1,0:T(8,128)} %pad_maximum_fusion.refs_5_.refs_0_), channel_id=1, source_target_pairs={{0,1},{1,0},{2,3},{3,2},{4,5},{5,4},{6,7},{7,6},{8,9},{9,8},{10,11... | collective-permute-start | bytes 2359304 | tf_op jit(solution)/shard_map/ppermute | solution.py:144
  18.5 32.8 %collective-permute-start.8 = (f32[256,640]{1,0:T(8,128)S(1)}, f32[256,640]{1,0:T(8,128)S(1)}, u32[]{:S(2)}, u32[]{:S(2)}) collective-permute-start(f32[256,640]{1,0:T(8,128)S(1)} %pad_maximum_fusion.1.refs_5_.refs_0_), channel_id=1, source_target_pairs={{0,1},{1,0},{2,3},{3,2},{4,5},{5,4},{6,7},{7,6},{8,9},{9,8},{10,11... | collective-permute-start | bytes 1966088 | tf_op jit(solution)/shard_map/ppermute | solution.py:144
  21.4 35.6 %collective-permute-start.2 = (f32[128,512]{1,0:T(8,128)S(1)}, f32[128,512]{1,0:T(8,128)}, u32[]{:S(2)}, u32[]{:S(2)}) collective-permute-start(f32[128,512]{1,0:T(8,128)S(1)} %slice.96), channel_id=1, source_target_pairs={{0,1},{1,0},{2,3},{3,2},{4,5},{5,4},{6,7},{7,6},{8,9},{9,8},{10,11... | collective-permute-start | bytes 786440 | tf_op jit(solution)/shard_map/ppermute | solution.py:144
  32.4 24.6 %collective-permute-start.3 = (f32[128,512]{1,0:T(8,128)S(1)}, f32[128,512]{1,0:T(8,128)}, u32[]{:S(2)}, u32[]{:S(2)}) collective-permute-start(f32[128,512]{1,0:T(8,128)S(1)} %slice.97), channel_id=1, source_target_pairs={{0,2},{2,0},{1,3},{3,1},{4,6},{6,4},{5,7},{7,5},{8,10},{10,8},{9,1... | collective-permute-start | bytes 786440 | tf_op jit(solution)/shard_map/ppermute | solution.py:144
  51.3 17.8 %collective-permute-start.10 = (f32[128,640]{1,0:T(8,128)}, f32[128,640]{1,0:T(8,128)S(1)}, u32[]{:S(2)}, u32[]{:S(2)}) collective-permute-start(f32[128,640]{1,0:T(8,128)} %slice.100), channel_id=1, source_target_pairs={{0,1},{1,0},{2,3},{3,2},{4,5},{5,4},{6,7},{7,6},{8,9},{9,8},{10,11... | collective-permute-start | bytes 983048 | tf_op jit(solution)/shard_map/ppermute | solution.py:144
  57.0 12.1 %collective-permute-start.11 = (f32[128,640]{1,0:T(8,128)}, f32[128,640]{1,0:T(8,128)S(1)}, u32[]{:S(2)}, u32[]{:S(2)}) collective-permute-start(f32[128,640]{1,0:T(8,128)} %slice.102), channel_id=1, source_target_pairs={{0,2},{2,0},{1,3},{3,1},{4,6},{6,4},{5,7},{7,5},{8,10},{10,8},{9,1... | collective-permute-start | bytes 983048 | tf_op jit(solution)/shard_map/ppermute | solution.py:144
  60.3 11.8 %collective-permute-start.20 = (f32[128,768]{1,0:T(8,128)S(1)}, f32[128,768]{1,0:T(8,128)S(1)}, u32[]{:S(2)}, u32[]{:S(2)}) collective-permute-start(f32[128,768]{1,0:T(8,128)S(1)} %slice.106), channel_id=1, source_target_pairs={{0,1},{1,0},{2,3},{3,2},{4,5},{5,4},{6,7},{7,6},{8,9},{9,8},{10,11... | collective-permute-start | bytes 1179656 | tf_op jit(solution)/shard_map/ppermute | solution.py:144
  62.4 11.3 %collective-permute-start.21 = (f32[128,768]{1,0:T(8,128)S(1)}, f32[128,768]{1,0:T(8,128)S(1)}, u32[]{:S(2)}, u32[]{:S(2)}) collective-permute-start(f32[128,768]{1,0:T(8,128)S(1)} %slice.108), channel_id=1, source_target_pairs={{0,2},{2,0},{1,3},{3,1},{4,6},{6,4},{5,7},{7,5},{8,10},{10,8},{9,1... | collective-permute-start | bytes 1179656 | tf_op jit(solution)/shard_map/ppermute | solution.py:144
  65.4 8.4 %collective-permute-start.7 = (f32[64,512]{1,0:T(8,128)S(1)}, f32[64,512]{1,0:T(8,128)S(1)}, u32[]{:S(2)}, u32[]{:S(2)}) collective-permute-start(f32[64,512]{1,0:T(8,128)S(1)} %add.14.s), channel_id=1, source_target_pairs={{0,24},{8,16},{16,8},{24,0},{1,25},{9,17},{17,9},{25,1},{2,26},{10... | collective-permute-start | bytes 393224 | tf_op jit(solution)/shard_map/ppermute | solution.py:144
  69.1 11.1 %collective-permute-start.6 = (f32[64,512]{1,0:T(8,128)S(1)}, f32[64,512]{1,0:T(8,128)S(1)}, u32[]{:S(2)}, u32[]{:S(2)}) collective-permute-start(f32[64,512]{1,0:T(8,128)S(1)} %add.14.s), channel_id=1, source_target_pairs={{0,16},{8,24},{16,0},{24,8},{1,17},{9,25},{17,1},{25,9},{2,18},{10... | collective-permute-start | bytes 393224 | tf_op jit(solution)/shard_map/ppermute | solution.py:144
  69.1 11.1 %collective-permute-start.5 = (f32[64,512]{1,0:T(8,128)S(1)}, f32[64,512]{1,0:T(8,128)S(1)}, u32[]{:S(2)}, u32[]{:S(2)}) collective-permute-start(f32[64,512]{1,0:T(8,128)S(1)} %add.14.s), channel_id=1, source_target_pairs={{0,8},{8,0},{16,24},{24,16},{1,9},{9,1},{17,25},{25,17},{2,10},{10... | collective-permute-start | bytes 393224 | tf_op jit(solution)/shard_map/ppermute | solution.py:144
  72.2 8.7 %collective-permute-start.12 = (f32[256,384]{1,0:T(8,128)S(1)}, f32[256,384]{1,0:T(8,128)S(1)}, u32[]{:S(2)}, u32[]{:S(2)}) collective-permute-start(f32[256,384]{1,0:T(8,128)S(1)} %maximum_maximum_fusion), channel_id=1, source_target_pairs={{0,4},{4,0},{1,5},{5,1},{2,6},{6,2},{3,7},{7,3},{8,12},{12,8},{9,1... | collective-permute-start | bytes 1179656 | tf_op jit(solution)/shard_map/ppermute | solution.py:144
  85.8 14.2 %collective-permute-start.22 = (f32[256,384]{1,0:T(8,128)S(1)}, f32[256,384]{1,0:T(8,128)S(1)}, u32[]{:S(2)}, u32[]{:S(2)}) collective-permute-start(f32[256,384]{1,0:T(8,128)S(1)} %maximum_maximum_fusion.1), channel_id=1, source_target_pairs={{0,4},{4,0},{1,5},{5,1},{2,6},{6,2},{3,7},{7,3},{8,12},{12,8},{9,1... | collective-permute-start | bytes 1179656 | tf_op jit(solution)/shard_map/ppermute | solution.py:144
  95.5 8.4 %collective-permute-start.17 = (f32[64,512]{1,0:T(8,128)S(1)}, f32[64,512]{1,0:T(8,128)S(1)}, u32[]{:S(2)}, u32[]{:S(2)}) collective-permute-start(f32[64,512]{1,0:T(8,128)S(1)} %add.16.s), channel_id=1, source_target_pairs={{0,24},{8,16},{16,8},{24,0},{1,25},{9,17},{17,9},{25,1},{2,26},{10... | collective-permute-start | bytes 393224 | tf_op jit(solution)/shard_map/ppermute | solution.py:144
  98.1 10.6 %collective-permute-start.16 = (f32[64,512]{1,0:T(8,128)S(1)}, f32[64,512]{1,0:T(8,128)S(1)}, u32[]{:S(2)}, u32[]{:S(2)}) collective-permute-start(f32[64,512]{1,0:T(8,128)S(1)} %add.16.s), channel_id=1, source_target_pairs={{0,16},{8,24},{16,0},{24,8},{1,17},{9,25},{17,1},{25,9},{2,18},{10... | collective-permute-start | bytes 393224 | tf_op jit(solution)/shard_map/ppermute | solution.py:144
  98.1 10.6 %collective-permute-start.15 = (f32[64,512]{1,0:T(8,128)S(1)}, f32[64,512]{1,0:T(8,128)S(1)}, u32[]{:S(2)}, u32[]{:S(2)}) collective-permute-start(f32[64,512]{1,0:T(8,128)S(1)} %add.16.s), channel_id=1, source_target_pairs={{0,8},{8,0},{16,24},{24,16},{1,9},{9,1},{17,25},{25,17},{2,10},{10... | collective-permute-start | bytes 393224 | tf_op jit(solution)/shard_map/ppermute | solution.py:144
  113.7 14.4 %collective-permute-start.28 = (f32[256,384]{1,0:T(8,128)S(1)}, f32[256,384]{1,0:T(8,128)S(1)}, u32[]{:S(2)}, u32[]{:S(2)}) collective-permute-start(f32[256,384]{1,0:T(8,128)S(1)} %maximum_maximum_fusion.2), channel_id=1, source_target_pairs={{0,4},{4,0},{1,5},{5,1},{2,6},{6,2},{3,7},{7,3},{8,12},{12,8},{9,1... | collective-permute-start | bytes 1179656 | tf_op jit(solution)/shard_map/ppermute | solution.py:144
  123.6 8.4 %collective-permute-start.27 = (f32[64,512]{1,0:T(8,128)S(1)}, f32[64,512]{1,0:T(8,128)S(1)}, u32[]{:S(2)}, u32[]{:S(2)}) collective-permute-start(f32[64,512]{1,0:T(8,128)S(1)} %add.17.s), channel_id=1, source_target_pairs={{0,24},{8,16},{16,8},{24,0},{1,25},{9,17},{17,9},{25,1},{2,26},{10... | collective-permute-start | bytes 393224 | tf_op jit(solution)/shard_map/ppermute | solution.py:144
  126.1 11.1 %collective-permute-start.26 = (f32[64,512]{1,0:T(8,128)S(1)}, f32[64,512]{1,0:T(8,128)S(1)}, u32[]{:S(2)}, u32[]{:S(2)}) collective-permute-start(f32[64,512]{1,0:T(8,128)S(1)} %add.17.s), channel_id=1, source_target_pairs={{0,16},{8,24},{16,0},{24,8},{1,17},{9,25},{17,1},{25,9},{2,18},{10... | collective-permute-start | bytes 393224 | tf_op jit(solution)/shard_map/ppermute | solution.py:144
  126.1 11.1 %collective-permute-start.25 = (f32[64,512]{1,0:T(8,128)S(1)}, f32[64,512]{1,0:T(8,128)S(1)}, u32[]{:S(2)}, u32[]{:S(2)}) collective-permute-start(f32[64,512]{1,0:T(8,128)S(1)} %add.17.s), channel_id=1, source_target_pairs={{0,8},{8,0},{16,24},{24,16},{1,9},{9,1},{17,25},{25,17},{2,10},{10... | collective-permute-start | bytes 393224 | tf_op jit(solution)/shard_map/ppermute | solution.py:144
  (39 other events, 262.6 us)

commit v2 on v1

--- a/solution.py
+++ b/solution.py
@@ -7,6 +7,7 @@
 from jax.experimental.pallas import tpu as pltpu
 from jax.sharding import Mesh, PartitionSpec as P
 
+
 F32, BF16 = jnp.float32, jnp.bfloat16
 NN = (((1,), (0,)), ((), ()))
 NT = (((1,), (1,)), ((), ()))
@@ -27,7 +28,7 @@
     return lax.axis_index("y") * 2 + lax.axis_index("x"), lax.axis_index("core")
 
 
-def blocks_of(refs, width):
+def blocks_of(refs):
     own, along_x, along_y, low, high = refs
     rows = own.shape[-2]
     half = rows // 2
@@ -46,7 +47,7 @@
 
 def project(total, current, refs, v, width):
     rows = refs[0].shape[-2]
-    for block, first, size, ref in blocks_of(refs, width):
+    for block, first, size, ref in blocks_of(refs):
         x = current[window(v, block, first, size, rows), :]
         part = dot3(x.T, ref[:, :width], NN)
         total = part if total is None else total + part
@@ -74,7 +75,7 @@
 
 def update(current, out, refs, coefficients, v, width):
     rows = refs[0].shape[-2]
-    for block, first, size, ref in blocks_of(refs, width):
+    for block, first, size, ref in blocks_of(refs):
         at = window(v, block, first, size, rows)
         out[at, :] = current[at, :] - dot3(ref[:, :width], coefficients, NT)
 
@@ -127,14 +128,14 @@
     return [pl.BlockSpec(memory_space=pltpu.VMEM)] * n
 
 
-def call(kernel, outs, args, flops, name):
+def call(kernel, outs, args, flops):
     nbytes = sum(4 * a.size for a in args) + sum(4 * o.size for o in outs)
     return pl.pallas_call(
         kernel,
         out_shape=outs,
         in_specs=vmem(len(args)),
         out_specs=vmem(len(outs)),
-        name=name,
+        compiler_params=pltpu.CompilerParams(vmem_limit_bytes=12 * 2**20),
         cost_estimate=pl.CostEstimate(flops=flops, bytes_accessed=nbytes, transcendentals=0),
     )(*args)
 
@@ -147,12 +148,13 @@
 def gather(pack):
     half = pack.shape[0] // 2
     along_x, along_y = swap(pack, "x"), swap(pack, "y")
-    return pack, along_x, along_y, swap(along_y[:half], "x"), swap(along_x[half:], "y")
+    low, high = swap(along_y[:half], "x"), swap(along_x[half:], "y")
+    return pack, along_x, along_y, low, high
 
 
 def fast(vectors, reflectors, triangles):
     rows, share = vectors.shape
-    panels, own_rows, width = reflectors.shape
+    panels, _, width = reflectors.shape
     core = lax.axis_index("core")
     half = width // 2
     part = jax.ShapeDtypeStruct((share // 2, width), F32)
@@ -170,6 +172,9 @@
     for panel in reversed(range(panels)):
         pack = jnp.concatenate([reflectors[panel]] + [factor_half(r) for r in riders[panel]], axis=1)
         sections[panel] = gather(pack)
+        if panel == panels - 1:
+            along_x, reflectors, triangles = lax.optimization_barrier((sections[panel][1], reflectors, triangles))
+            sections[panel] = (pack, along_x, *sections[panel][2:])
         received = sections[panel][1:]
         for i, r in enumerate(riders[panel]):
             at = width + i * share
@@ -186,12 +191,11 @@
             [part],
             [s, *r, triangles, exchanged, *received],
             2 * width * width * share // 2,
-            "solve",
         )[0]
         return mine, swap(mine, "core")
 
     top = panels - 1
-    keep, send = call(functools.partial(first_kernel, width), [part, part], [vectors, *sections[top]], work, "first")
+    keep, send = call(functools.partial(first_kernel, width), [part, part], [vectors, *sections[top]], work)
     current = vectors
     for panel in reversed(range(1, panels)):
         c = reduced(keep, send, panel)
@@ -200,10 +204,9 @@
             [whole, part, part],
             [current, *c, *sections[panel], *sections[panel - 1]],
             2 * work,
-            "middle",
         )
     c = reduced(keep, send, 0)
-    return call(functools.partial(last_kernel, width), [whole], [current, *c, *sections[0]], work, "last")[0]
+    return call(functools.partial(last_kernel, width), [whole], [current, *c, *sections[0]], work)[0]
 
 
 def general(vectors, reflectors, triangles):
@@ -230,8 +233,12 @@
     fine = Mesh(mesh.devices.reshape(rows // cores, cores, side, vecs // side), ("z", "core", "y", "x"))
     small = fine.devices.shape == (4, 2, 2, 2)
     row, vec = ("z", "core"), ("y", "x")
+
+    def body(*args):
+        return (fast if small else general)(*args)
+
     return jax.shard_map(
-        fast if small else general,
+        body,
         mesh=fine,
         in_specs=(P(row, vec), P(None, row + vec, None), P(None, None, vec)),
         out_specs=P(row, vec),

time: 148 us -> 121 us (0.82)
  Pallas kernels: 27.9 us -> 8.25 us
  local copies, waits for them, and re-layouts: 14 us -> 1.54 us
  waiting for transfers between devices: 71 us -> 81.3 us
  other arithmetic: 3.02 us -> 0.26 us
  starting transfers between devices: 31.8 us -> 29.5 us
    pallas_call x7, Pallas kernels: 27.9 us -> 8.25 us  [call(): pl.pallas_call(kernel, out_shape=outs, in_specs=vmem(len(args)), out_spec...]
    ppermute x30, waiting for transfers between devices: 71 us -> 81.3 us  [swap(): return lax.ppermute(a, axis, [(i, i ^ by) for i in range(n)])]
    unnamed x62 -> x6, local copies, waits for them, and re-layouts: 6.64 us -> 0.01 us
    slice x6, local copies, waits for them, and re-layouts: 3.5 us -> 0.13 us  [gather(): low, high = (swap(along_y[:half], 'x'), swap(along_x[half:], 'y'))]
    ppermute x30, starting transfers between devices: 31.8 us -> 29.5 us  [swap(): return lax.ppermute(a, axis, [(i, i ^ by) for i in range(n)])]
    add x3, other arithmetic: 1.87 us -> 0.06 us  [reduced(): s = keep + swap(send, 'core')]
  transfers between devices with their start and end apart: 30 -> 30, of which waited for: 16 -> 18; matrix products, arithmetic and copies ran while one was open for 5% -> 1% of each run, Pallas kernels for 9% -> 4%
where the time goes in v2:
time: 121 us
  waiting for transfers between devices  81.3 us (67%)
  starting transfers between devices  29.5 us (24%)
  Pallas kernels  8.25 us (7%)
  local copies, waits for them, and re-layouts  1.54 us (1%)
    ppermute x30, waiting for transfers between devices, swap(): return lax.ppermute(a, axis, [(i, i ^ by) for i in range(n)])  81.3 us
    ppermute x30, starting transfers between devices, swap(): return lax.ppermute(a, axis, [(i, i ^ by) for i in range(n)])  29.5 us
    pallas_call x7, Pallas kernels, call(): pl.pallas_call(kernel, out_shape=outs, in_specs=vmem(len(args)), out_spec...  8.25 us
  transfers between devices with their start and end apart: 30, of which 18 were waited for; matrix products, arithmetic and copies ran while one was open for 1% of the time, Pallas kernels for 4%

profile of v2, /device:TPU:0, one launch (start us, length us, event | category | flops | bytes accessed | tf_op | source)
XLA Modules:
  0.0 121.2 jit_solution(7151137994841373194)
XLA Ops:
  1.2 3.0 %collective-permute-start = (f32[256,512]{1,0:T(8,128)S(1)}, f32[256,512]{1,0:T(8,128)S(1)}, u32[]{:S(2)}, u32[]{:S(2)}) collective-permute-start(f32[256,512]{1,0:T(8,128)S(1)} %slice_bitcast_fusion.2.refs_0_), channel_id=1, source_target_pairs={{0,1},{1,0},{2,3},{3,2},{4,5},{5,4},{6,7},{7,6},{8,9},{9,8},{10,11... | collective-permute-start | bytes 1572872 | tf_op jit(solution)/shard_map/ppermute | solution.py:145
  4.2 1.5 %collective-permute-start.1 = (f32[256,512]{1,0:T(8,128)S(1)}, f32[256,512]{1,0:T(8,128)S(1)}, u32[]{:S(2)}, u32[]{:S(2)}) collective-permute-start(f32[256,512]{1,0:T(8,128)S(1)} %slice_bitcast_fusion.2.refs_0_), channel_id=1, source_target_pairs={{0,2},{2,0},{1,3},{3,1},{4,6},{6,4},{5,7},{7,5},{8,10},{10,8},{9,1... | collective-permute-start | bytes 1572872 | tf_op jit(solution)/shard_map/ppermute | solution.py:145
  5.7 10.4 %collective-permute-done.refs_1_ = f32[256,512]{1,0:T(8,128)S(1)} collective-permute-done((f32[256,512]{1,0:T(8,128)S(1)}, f32[256,512]{1,0:T(8,128)S(1)}, u32[]{:S(2)}, u32[]{:S(2)}) %collective-permute-start) | collective-permute-done | bytes 524320 | tf_op jit(solution)/shard_map/ppermute | solution.py:145
  16.4 1.8 %collective-permute-start.19 = (f32[256,768]{1,0:T(8,128)S(1)}, f32[256,768]{1,0:T(8,128)S(1)}, u32[]{:S(2)}, u32[]{:S(2)}) collective-permute-start(f32[256,768]{1,0:T(8,128)S(1)} %pad_maximum_fusion.refs_5_.refs_0_), channel_id=1, source_target_pairs={{0,2},{2,0},{1,3},{3,1},{4,6},{6,4},{5,7},{7,5},{8,10},{10,8},{9,1... | collective-permute-start | bytes 2359304 | tf_op jit(solution)/shard_map/ppermute | solution.py:145
  18.2 1.5 %collective-permute-start.18 = (f32[256,768]{1,0:T(8,128)S(1)}, f32[256,768]{1,0:T(8,128)S(1)}, u32[]{:S(2)}, u32[]{:S(2)}) collective-permute-start(f32[256,768]{1,0:T(8,128)S(1)} %pad_maximum_fusion.refs_5_.refs_0_), channel_id=1, source_target_pairs={{0,1},{1,0},{2,3},{3,2},{4,5},{5,4},{6,7},{7,6},{8,9},{9,8},{10,11... | collective-permute-start | bytes 2359304 | tf_op jit(solution)/shard_map/ppermute | solution.py:145
  20.7 1.7 %collective-permute-start.8 = (f32[256,640]{1,0:T(8,128)S(1)}, f32[256,640]{1,0:T(8,128)S(1)}, u32[]{:S(2)}, u32[]{:S(2)}) collective-permute-start(f32[256,640]{1,0:T(8,128)S(1)} %pad_maximum_fusion.1.refs_5_.refs_0_), channel_id=1, source_target_pairs={{0,1},{1,0},{2,3},{3,2},{4,5},{5,4},{6,7},{7,6},{8,9},{9,8},{10,11... | collective-permute-start | bytes 1966088 | tf_op jit(solution)/shard_map/ppermute | solution.py:145
  22.5 21.8 %collective-permute-done.2.refs_3_ = f32[128,512]{1,0:T(8,128)S(1)} collective-permute-done((f32[128,512]{1,0:T(8,128)S(1)}, f32[128,512]{1,0:T(8,128)S(1)}, u32[]{:S(2)}, u32[]{:S(2)}) %collective-permute-start.2) | collective-permute-done | bytes 262176 | tf_op jit(solution)/shard_map/ppermute | solution.py:145
  44.5 10.3 %collective-permute-done.3.refs_4_ = f32[128,512]{1,0:T(8,128)S(1)} collective-permute-done((f32[128,512]{1,0:T(8,128)S(1)}, f32[128,512]{1,0:T(8,128)S(1)}, u32[]{:S(2)}, u32[]{:S(2)}) %collective-permute-start.3) | collective-permute-done | bytes 262176 | tf_op jit(solution)/shard_map/ppermute | solution.py:145
  57.1 3.6 %collective-permute-start.7 = (f32[64,512]{1,0:T(8,128)S(1)}, f32[64,512]{1,0:T(8,128)S(1)}, u32[]{:S(2)}, u32[]{:S(2)}) collective-permute-start(f32[64,512]{1,0:T(8,128)S(1)} %add.14.s), channel_id=1, source_target_pairs={{0,24},{8,16},{16,8},{24,0},{1,25},{9,17},{17,9},{25,1},{2,26},{10... | collective-permute-start | bytes 393224 | tf_op jit(solution)/shard_map/ppermute | solution.py:145
  60.7 1.6 %collective-permute-start.10 = (f32[128,640]{1,0:T(8,128)S(1)}, f32[128,640]{1,0:T(8,128)S(1)}, u32[]{:S(2)}, u32[]{:S(2)}) collective-permute-start(f32[128,640]{1,0:T(8,128)S(1)} %slice.100), channel_id=1, source_target_pairs={{0,1},{1,0},{2,3},{3,2},{4,5},{5,4},{6,7},{7,6},{8,9},{9,8},{10,11... | collective-permute-start | bytes 983048 | tf_op jit(solution)/shard_map/ppermute | solution.py:145
  62.3 1.6 %collective-permute-start.11 = (f32[128,640]{1,0:T(8,128)S(1)}, f32[128,640]{1,0:T(8,128)S(1)}, u32[]{:S(2)}, u32[]{:S(2)}) collective-permute-start(f32[128,640]{1,0:T(8,128)S(1)} %slice.102), channel_id=1, source_target_pairs={{0,2},{2,0},{1,3},{3,1},{4,6},{6,4},{5,7},{7,5},{8,10},{10,8},{9,1... | collective-permute-start | bytes 983048 | tf_op jit(solution)/shard_map/ppermute | solution.py:145
  65.2 6.1 %collective-permute-done.10.low.refs_8_.refs_3_ = f32[128,640]{1,0:T(8,128)S(1)} collective-permute-done((f32[128,640]{1,0:T(8,128)S(1)}, f32[128,640]{1,0:T(8,128)S(1)}, u32[]{:S(2)}, u32[]{:S(2)}) %collective-permute-start.10) | collective-permute-done | bytes 327712 | tf_op jit(solution)/shard_map/ppermute | solution.py:145
  71.4 1.6 %collective-permute-done.11.high.refs_9_.refs_4_ = f32[128,640]{1,0:T(8,128)S(1)} collective-permute-done((f32[128,640]{1,0:T(8,128)S(1)}, f32[128,640]{1,0:T(8,128)S(1)}, u32[]{:S(2)}, u32[]{:S(2)}) %collective-permute-start.11) | collective-permute-done | bytes 327712 | tf_op jit(solution)/shard_map/ppermute | solution.py:145
  73.0 5.7 %collective-permute-done.20.low.refs_8_.refs_3_ = f32[128,768]{1,0:T(8,128)S(1)} collective-permute-done((f32[128,768]{1,0:T(8,128)S(1)}, f32[128,768]{1,0:T(8,128)S(1)}, u32[]{:S(2)}, u32[]{:S(2)}) %collective-permute-start.20) | collective-permute-done | bytes 393248 | tf_op jit(solution)/shard_map/ppermute | solution.py:145
  82.5 1.8 %shard_map.39 = (f32[1024,128]{1,0:T(8,128)S(1)}, f32[64,512]{1,0:T(8,128)S(1)}, f32[64,512]{1,0:T(8,128)S(1)}) custom-call(f32[1024,128]{1,0:T(8,128)S(1)} %copy-done.1, f32[64,512]{1,0:T(8,128)S(1)} %shard_map.38.mine, f32[64,512]{1,0:T(8,128)S(1)} %collective-permute-done.13.other, f32[256,512]{1,0:T(8,128)S(1)} %slice_bitcast_fusion.2.refs_0_, ...), custom_call_target="tpu_custom_call" | custom-call | flops 268435456 | bytes 6291456 | tf_op jit(solution)/shard_map/pallas_call | solution.py:133
  86.8 3.4 %collective-permute-start.15 = (f32[64,512]{1,0:T(8,128)S(1)}, f32[64,512]{1,0:T(8,128)S(1)}, u32[]{:S(2)}, u32[]{:S(2)}) collective-permute-start(f32[64,512]{1,0:T(8,128)S(1)} %add.16.s), channel_id=1, source_target_pairs={{0,8},{8,0},{16,24},{24,16},{1,9},{9,1},{17,25},{25,17},{2,10},{10... | collective-permute-start | bytes 393224 | tf_op jit(solution)/shard_map/ppermute | solution.py:145
  90.2 3.9 %collective-permute-done.17.r3 = f32[64,512]{1,0:T(8,128)S(1)} collective-permute-done((f32[64,512]{1,0:T(8,128)S(1)}, f32[64,512]{1,0:T(8,128)S(1)}, u32[]{:S(2)}, u32[]{:S(2)}) %collective-permute-start.17) | collective-permute-done | bytes 131104 | tf_op jit(solution)/shard_map/ppermute | solution.py:145
  94.1 4.7 %collective-permute-done.16.r2 = f32[64,512]{1,0:T(8,128)S(1)} collective-permute-done((f32[64,512]{1,0:T(8,128)S(1)}, f32[64,512]{1,0:T(8,128)S(1)}, u32[]{:S(2)}, u32[]{:S(2)}) %collective-permute-start.16) | collective-permute-done | bytes 131104 | tf_op jit(solution)/shard_map/ppermute | solution.py:145
  100.9 1.8 %shard_map.41 = (f32[1024,128]{1,0:T(8,128)S(1)}, f32[64,512]{1,0:T(8,128)S(1)}, f32[64,512]{1,0:T(8,128)S(1)}) custom-call(f32[1024,128]{1,0:T(8,128)S(1)} %get-tuple-element.21.x, f32[64,512]{1,0:T(8,128)S(1)} %shard_map.40.mine, f32[64,512]{1,0:T(8,128)S(1)} %collective-permute-done.23.other, f32[256,640]{1,0:T(8,128)S(1)} %pad_maximum_fusion.1.refs_5_.refs_0_, ...), custom_call_target="tpu_custom_call" | custom-call | flops 268435456 | bytes 7340032 | tf_op jit(solution)/shard_map/pallas_call | solution.py:133
  104.2 1.4 %collective-permute-start.27 = (f32[64,512]{1,0:T(8,128)S(1)}, f32[64,512]{1,0:T(8,128)S(1)}, u32[]{:S(2)}, u32[]{:S(2)}) collective-permute-start(f32[64,512]{1,0:T(8,128)S(1)} %add.17.s), channel_id=1, source_target_pairs={{0,24},{8,16},{16,8},{24,0},{1,25},{9,17},{17,9},{25,1},{2,26},{10... | collective-permute-start | bytes 393224 | tf_op jit(solution)/shard_map/ppermute | solution.py:145
  105.6 3.1 %collective-permute-start.25 = (f32[64,512]{1,0:T(8,128)S(1)}, f32[64,512]{1,0:T(8,128)S(1)}, u32[]{:S(2)}, u32[]{:S(2)}) collective-permute-start(f32[64,512]{1,0:T(8,128)S(1)} %add.17.s), channel_id=1, source_target_pairs={{0,8},{8,0},{16,24},{24,16},{1,9},{9,1},{17,25},{25,17},{2,10},{10... | collective-permute-start | bytes 393224 | tf_op jit(solution)/shard_map/ppermute | solution.py:145
  108.7 3.9 %collective-permute-done.27.r3 = f32[64,512]{1,0:T(8,128)S(1)} collective-permute-done((f32[64,512]{1,0:T(8,128)S(1)}, f32[64,512]{1,0:T(8,128)S(1)}, u32[]{:S(2)}, u32[]{:S(2)}) %collective-permute-start.27) | collective-permute-done | bytes 131104 | tf_op jit(solution)/shard_map/ppermute | solution.py:145
  112.6 4.7 %collective-permute-done.26.r2 = f32[64,512]{1,0:T(8,128)S(1)} collective-permute-done((f32[64,512]{1,0:T(8,128)S(1)}, f32[64,512]{1,0:T(8,128)S(1)}, u32[]{:S(2)}, u32[]{:S(2)}) %collective-permute-start.26) | collective-permute-done | bytes 131104 | tf_op jit(solution)/shard_map/ppermute | solution.py:145
  119.3 1.8 %shard_map.43 = f32[1024,128]{1,0:T(8,128)} custom-call(f32[1024,128]{1,0:T(8,128)S(1)} %get-tuple-element.24.x, f32[64,512]{1,0:T(8,128)S(1)} %shard_map.42.mine, f32[64,512]{1,0:T(8,128)S(1)} %collective-permute-done.29.other, f32[256,768]{1,0:T(8,128)S(1)} %pad_maximum_fusion.refs_5_.refs_0_, ...), custom_call_target="tpu_custom_call" | custom-call | flops 134217728 | bytes 4456448 | tf_op jit(solution)/shard_map/pallas_call | solution.py:133
  (76 shorter events, 18.1 us)
Async XLA Ops:
  1.2 15.0 %collective-permute-start = (f32[256,512]{1,0:T(8,128)S(1)}, f32[256,512]{1,0:T(8,128)S(1)}, u32[]{:S(2)}, u32[]{:S(2)}) collective-permute-start(f32[256,512]{1,0:T(8,128)S(1)} %slice_bitcast_fusion.2.refs_0_), channel_id=1, source_target_pairs={{0,1},{1,0},{2,3},{3,2},{4,5},{5,4},{6,7},{7,6},{8,9},{9,8},{10,11... | collective-permute-start | bytes 1572872 | tf_op jit(solution)/shard_map/ppermute | solution.py:145
  4.2 15.5 %collective-permute-start.1 = (f32[256,512]{1,0:T(8,128)S(1)}, f32[256,512]{1,0:T(8,128)S(1)}, u32[]{:S(2)}, u32[]{:S(2)}) collective-permute-start(f32[256,512]{1,0:T(8,128)S(1)} %slice_bitcast_fusion.2.refs_0_), channel_id=1, source_target_pairs={{0,2},{2,0},{1,3},{3,1},{4,6},{6,4},{5,7},{7,5},{8,10},{10,8},{9,1... | collective-permute-start | bytes 1572872 | tf_op jit(solution)/shard_map/ppermute | solution.py:145
  16.4 47.6 %collective-permute-start.19 = (f32[256,768]{1,0:T(8,128)S(1)}, f32[256,768]{1,0:T(8,128)S(1)}, u32[]{:S(2)}, u32[]{:S(2)}) collective-permute-start(f32[256,768]{1,0:T(8,128)S(1)} %pad_maximum_fusion.refs_5_.refs_0_), channel_id=1, source_target_pairs={{0,2},{2,0},{1,3},{3,1},{4,6},{6,4},{5,7},{7,5},{8,10},{10,8},{9,1... | collective-permute-start | bytes 2359304 | tf_op jit(solution)/shard_map/ppermute | solution.py:145
  18.2 46.4 %collective-permute-start.18 = (f32[256,768]{1,0:T(8,128)S(1)}, f32[256,768]{1,0:T(8,128)S(1)}, u32[]{:S(2)}, u32[]{:S(2)}) collective-permute-start(f32[256,768]{1,0:T(8,128)S(1)} %pad_maximum_fusion.refs_5_.refs_0_), channel_id=1, source_target_pairs={{0,1},{1,0},{2,3},{3,2},{4,5},{5,4},{6,7},{7,6},{8,9},{9,8},{10,11... | collective-permute-start | bytes 2359304 | tf_op jit(solution)/shard_map/ppermute | solution.py:145
  19.7 24.5 %collective-permute-start.2 = (f32[128,512]{1,0:T(8,128)S(1)}, f32[128,512]{1,0:T(8,128)S(1)}, u32[]{:S(2)}, u32[]{:S(2)}) collective-permute-start(f32[128,512]{1,0:T(8,128)S(1)} %slice.96), channel_id=1, source_target_pairs={{0,1},{1,0},{2,3},{3,2},{4,5},{5,4},{6,7},{7,6},{8,9},{9,8},{10,11... | collective-permute-start | bytes 786440 | tf_op jit(solution)/shard_map/ppermute | solution.py:145
  20.4 40.3 %collective-permute-start.9 = (f32[256,640]{1,0:T(8,128)S(1)}, f32[256,640]{1,0:T(8,128)S(1)}, u32[]{:S(2)}, u32[]{:S(2)}) collective-permute-start(f32[256,640]{1,0:T(8,128)S(1)} %pad_maximum_fusion.1.refs_5_.refs_0_), channel_id=1, source_target_pairs={{0,2},{2,0},{1,3},{3,1},{4,6},{6,4},{5,7},{7,5},{8,10},{10,8},{9,1... | collective-permute-start | bytes 1966088 | tf_op jit(solution)/shard_map/ppermute | solution.py:145
  20.7 41.6 %collective-permute-start.8 = (f32[256,640]{1,0:T(8,128)S(1)}, f32[256,640]{1,0:T(8,128)S(1)}, u32[]{:S(2)}, u32[]{:S(2)}) collective-permute-start(f32[256,640]{1,0:T(8,128)S(1)} %pad_maximum_fusion.1.refs_5_.refs_0_), channel_id=1, source_target_pairs={{0,1},{1,0},{2,3},{3,2},{4,5},{5,4},{6,7},{7,6},{8,9},{9,8},{10,11... | collective-permute-start | bytes 1966088 | tf_op jit(solution)/shard_map/ppermute | solution.py:145
  44.2 10.6 %collective-permute-start.3 = (f32[128,512]{1,0:T(8,128)S(1)}, f32[128,512]{1,0:T(8,128)S(1)}, u32[]{:S(2)}, u32[]{:S(2)}) collective-permute-start(f32[128,512]{1,0:T(8,128)S(1)} %slice.97), channel_id=1, source_target_pairs={{0,2},{2,0},{1,3},{3,1},{4,6},{6,4},{5,7},{7,5},{8,10},{10,8},{9,1... | collective-permute-start | bytes 786440 | tf_op jit(solution)/shard_map/ppermute | solution.py:145
  57.1 23.0 %collective-permute-start.7 = (f32[64,512]{1,0:T(8,128)S(1)}, f32[64,512]{1,0:T(8,128)S(1)}, u32[]{:S(2)}, u32[]{:S(2)}) collective-permute-start(f32[64,512]{1,0:T(8,128)S(1)} %add.14.s), channel_id=1, source_target_pairs={{0,24},{8,16},{16,8},{24,0},{1,25},{9,17},{17,9},{25,1},{2,26},{10... | collective-permute-start | bytes 393224 | tf_op jit(solution)/shard_map/ppermute | solution.py:145
  60.7 10.6 %collective-permute-start.10 = (f32[128,640]{1,0:T(8,128)S(1)}, f32[128,640]{1,0:T(8,128)S(1)}, u32[]{:S(2)}, u32[]{:S(2)}) collective-permute-start(f32[128,640]{1,0:T(8,128)S(1)} %slice.100), channel_id=1, source_target_pairs={{0,1},{1,0},{2,3},{3,2},{4,5},{5,4},{6,7},{7,6},{8,9},{9,8},{10,11... | collective-permute-start | bytes 983048 | tf_op jit(solution)/shard_map/ppermute | solution.py:145
  62.3 10.6 %collective-permute-start.11 = (f32[128,640]{1,0:T(8,128)S(1)}, f32[128,640]{1,0:T(8,128)S(1)}, u32[]{:S(2)}, u32[]{:S(2)}) collective-permute-start(f32[128,640]{1,0:T(8,128)S(1)} %slice.102), channel_id=1, source_target_pairs={{0,2},{2,0},{1,3},{3,1},{4,6},{6,4},{5,7},{7,5},{8,10},{10,8},{9,1... | collective-permute-start | bytes 983048 | tf_op jit(solution)/shard_map/ppermute | solution.py:145
  64.0 14.7 %collective-permute-start.20 = (f32[128,768]{1,0:T(8,128)S(1)}, f32[128,768]{1,0:T(8,128)S(1)}, u32[]{:S(2)}, u32[]{:S(2)}) collective-permute-start(f32[128,768]{1,0:T(8,128)S(1)} %slice.106), channel_id=1, source_target_pairs={{0,1},{1,0},{2,3},{3,2},{4,5},{5,4},{6,7},{7,6},{8,9},{9,8},{10,11... | collective-permute-start | bytes 1179656 | tf_op jit(solution)/shard_map/ppermute | solution.py:145
  64.6 15.4 %collective-permute-start.21 = (f32[128,768]{1,0:T(8,128)S(1)}, f32[128,768]{1,0:T(8,128)S(1)}, u32[]{:S(2)}, u32[]{:S(2)}) collective-permute-start(f32[128,768]{1,0:T(8,128)S(1)} %slice.108), channel_id=1, source_target_pairs={{0,2},{2,0},{1,3},{3,1},{4,6},{6,4},{5,7},{7,5},{8,10},{10,8},{9,1... | collective-permute-start | bytes 1179656 | tf_op jit(solution)/shard_map/ppermute | solution.py:145
  71.4 8.7 %collective-permute-start.6 = (f32[64,512]{1,0:T(8,128)S(1)}, f32[64,512]{1,0:T(8,128)S(1)}, u32[]{:S(2)}, u32[]{:S(2)}) collective-permute-start(f32[64,512]{1,0:T(8,128)S(1)} %add.14.s), channel_id=1, source_target_pairs={{0,16},{8,24},{16,0},{24,8},{1,17},{9,25},{17,1},{25,9},{2,18},{10... | collective-permute-start | bytes 393224 | tf_op jit(solution)/shard_map/ppermute | solution.py:145
  73.0 7.1 %collective-permute-start.5 = (f32[64,512]{1,0:T(8,128)S(1)}, f32[64,512]{1,0:T(8,128)S(1)}, u32[]{:S(2)}, u32[]{:S(2)}) collective-permute-start(f32[64,512]{1,0:T(8,128)S(1)} %add.14.s), channel_id=1, source_target_pairs={{0,8},{8,0},{16,24},{24,16},{1,9},{9,1},{17,25},{25,17},{2,10},{10... | collective-permute-start | bytes 393224 | tf_op jit(solution)/shard_map/ppermute | solution.py:145
  78.7 1.7 %collective-permute-start.12 = (f32[256,384]{1,0:T(8,128)S(1)}, f32[256,384]{1,0:T(8,128)S(1)}, u32[]{:S(2)}, u32[]{:S(2)}) collective-permute-start(f32[256,384]{1,0:T(8,128)S(1)} %maximum_maximum_fusion), channel_id=1, source_target_pairs={{0,4},{4,0},{1,5},{5,1},{2,6},{6,2},{3,7},{7,3},{8,12},{12,8},{9,1... | collective-permute-start | bytes 1179656 | tf_op jit(solution)/shard_map/ppermute | solution.py:145
  81.3 8.9 %collective-permute-start.22 = (f32[256,384]{1,0:T(8,128)S(1)}, f32[256,384]{1,0:T(8,128)S(1)}, u32[]{:S(2)}, u32[]{:S(2)}) collective-permute-start(f32[256,384]{1,0:T(8,128)S(1)} %maximum_maximum_fusion.1), channel_id=1, source_target_pairs={{0,4},{4,0},{1,5},{5,1},{2,6},{6,2},{3,7},{7,3},{8,12},{12,8},{9,1... | collective-permute-start | bytes 1179656 | tf_op jit(solution)/shard_map/ppermute | solution.py:145
  85.8 8.4 %collective-permute-start.17 = (f32[64,512]{1,0:T(8,128)S(1)}, f32[64,512]{1,0:T(8,128)S(1)}, u32[]{:S(2)}, u32[]{:S(2)}) collective-permute-start(f32[64,512]{1,0:T(8,128)S(1)} %add.16.s), channel_id=1, source_target_pairs={{0,24},{8,16},{16,8},{24,0},{1,25},{9,17},{17,9},{25,1},{2,26},{10... | collective-permute-start | bytes 393224 | tf_op jit(solution)/shard_map/ppermute | solution.py:145
  86.1 12.7 %collective-permute-start.16 = (f32[64,512]{1,0:T(8,128)S(1)}, f32[64,512]{1,0:T(8,128)S(1)}, u32[]{:S(2)}, u32[]{:S(2)}) collective-permute-start(f32[64,512]{1,0:T(8,128)S(1)} %add.16.s), channel_id=1, source_target_pairs={{0,16},{8,24},{16,0},{24,8},{1,17},{9,25},{17,1},{25,9},{2,18},{10... | collective-permute-start | bytes 393224 | tf_op jit(solution)/shard_map/ppermute | solution.py:145
  86.8 12.0 %collective-permute-start.15 = (f32[64,512]{1,0:T(8,128)S(1)}, f32[64,512]{1,0:T(8,128)S(1)}, u32[]{:S(2)}, u32[]{:S(2)}) collective-permute-start(f32[64,512]{1,0:T(8,128)S(1)} %add.16.s), channel_id=1, source_target_pairs={{0,8},{8,0},{16,24},{24,16},{1,9},{9,1},{17,25},{25,17},{2,10},{10... | collective-permute-start | bytes 393224 | tf_op jit(solution)/shard_map/ppermute | solution.py:145
  99.6 9.0 %collective-permute-start.28 = (f32[256,384]{1,0:T(8,128)S(1)}, f32[256,384]{1,0:T(8,128)S(1)}, u32[]{:S(2)}, u32[]{:S(2)}) collective-permute-start(f32[256,384]{1,0:T(8,128)S(1)} %maximum_maximum_fusion.2), channel_id=1, source_target_pairs={{0,4},{4,0},{1,5},{5,1},{2,6},{6,2},{3,7},{7,3},{8,12},{12,8},{9,1... | collective-permute-start | bytes 1179656 | tf_op jit(solution)/shard_map/ppermute | solution.py:145
  104.2 8.4 %collective-permute-start.27 = (f32[64,512]{1,0:T(8,128)S(1)}, f32[64,512]{1,0:T(8,128)S(1)}, u32[]{:S(2)}, u32[]{:S(2)}) collective-permute-start(f32[64,512]{1,0:T(8,128)S(1)} %add.17.s), channel_id=1, source_target_pairs={{0,24},{8,16},{16,8},{24,0},{1,25},{9,17},{17,9},{25,1},{2,26},{10... | collective-permute-start | bytes 393224 | tf_op jit(solution)/shard_map/ppermute | solution.py:145
  105.6 11.7 %collective-permute-start.26 = (f32[64,512]{1,0:T(8,128)S(1)}, f32[64,512]{1,0:T(8,128)S(1)}, u32[]{:S(2)}, u32[]{:S(2)}) collective-permute-start(f32[64,512]{1,0:T(8,128)S(1)} %add.17.s), channel_id=1, source_target_pairs={{0,16},{8,24},{16,0},{24,8},{1,17},{9,25},{17,1},{25,9},{2,18},{10... | collective-permute-start | bytes 393224 | tf_op jit(solution)/shard_map/ppermute | solution.py:145
  105.6 11.7 %collective-permute-start.25 = (f32[64,512]{1,0:T(8,128)S(1)}, f32[64,512]{1,0:T(8,128)S(1)}, u32[]{:S(2)}, u32[]{:S(2)}) collective-permute-start(f32[64,512]{1,0:T(8,128)S(1)} %add.17.s), channel_id=1, source_target_pairs={{0,8},{8,0},{16,24},{24,16},{1,9},{9,1},{17,25},{25,17},{2,10},{10... | collective-permute-start | bytes 393224 | tf_op jit(solution)/shard_map/ppermute | solution.py:145
  (9 other events, 73.5 us)

commit v3 on v2

v3 whole, which is shorter than its diff:
```python
import functools

import jax
import jax.numpy as jnp
from jax import lax
from jax.experimental import pallas as pl
from jax.experimental.pallas import tpu as pltpu
from jax.sharding import Mesh, PartitionSpec as P


F32, BF16 = jnp.float32, jnp.bfloat16
NN = (((1,), (0,)), ((), ()))
NT = (((1,), (1,)), ((), ()))
PIECES = 8


def split(a):
    head = a.astype(BF16)
    return head, (a - head.astype(F32)).astype(BF16)


def dot3(a, b, dims):
    (ah, al), (bh, bl) = split(a), split(b)
    one = functools.partial(lax.dot_general, dimension_numbers=dims, preferred_element_type=F32)
    return one(ah, bh) + (one(ah, bl) + one(al, bh))


def place():
    return lax.axis_index("y") * 2 + lax.axis_index("x"), lax.axis_index("core")


def blocks_of(refs):
    size = refs[0].shape[0]
    return [(i // 2, i % 2 * size, ref) for i, ref in enumerate(refs)]


def window(v, block, first, size):
    return pl.ds(pl.multiple_of((v ^ block) * 2 * size + first, 8), size)


def project(current, refs, v):
    total = None
    for block, first, ref in blocks_of(refs):
        x = current[window(v, block, first, ref.shape[0]), :]
        part = dot3(x.T, ref[...], NN)
        total = part if total is None else total + part
    return total


def give_out(total, core, keep, send):
    half = keep.shape[0]
    mine = core == 0
    keep[...] = jnp.where(mine, total[:half], total[half:])
    send[...] = jnp.where(mine, total[half:], total[:half])


def first_kernel(x, *refs):
    v, core = place()
    refs, (keep, send) = refs[:PIECES], refs[PIECES:]
    give_out(project(x, refs, v), core, keep, send)


def both_halves(mine, other, core):
    a, b = mine[...], other[...]
    first = core == 0
    return jnp.concatenate([jnp.where(first, a, b), jnp.where(first, b, a)], axis=0)


def update(current, out, refs, coefficients, v):
    for block, first, ref in blocks_of(refs):
        at = window(v, block, first, ref.shape[0])
        out[at, :] = current[at, :] - dot3(ref[...], coefficients, NT)


def middle_kernel(x, mine, other, *refs):
    v, core = place()
    old, new, (out, keep, send) = refs[:PIECES], refs[PIECES : 2 * PIECES], refs[2 * PIECES :]
    update(x, out, old, both_halves(mine, other, core), v)
    give_out(project(out, new, v), core, keep, send)


def last_kernel(x, mine, other, *refs):
    v, core = place()
    update(x, refs[PIECES], refs[:PIECES], both_halves(mine, other, core), v)


def solve_kernel(panel, n, *refs):
    v, core = place()
    total = refs[0][...]
    for i in range(1, n):
        total = total + refs[i][...]
    factor, exchanged, *mine = refs[n:-1]
    out = refs[-1]
    share = factor.shape[-1]
    half = factor.shape[-2] // 2
    mine = [factor[panel, pl.ds(pl.multiple_of(core * half, 8), half), :]] + [a[...] for a in mine]
    other = [factor[panel, pl.ds(pl.multiple_of((1 - core) * half, 8), half), :]]
    other += [exchanged[:, i * share : (i + 1) * share] for i in range(3)]
    sums = [None, None]
    parts = split_columns(total, v, share)
    for block in range(4):
        for i, t in enumerate((mine[block], other[block])):
            part = dot3(parts[block], t, NT)
            sums[i] = part if sums[i] is None else sums[i] + part
    out[...] = jnp.where(core == 0, jnp.concatenate(sums, axis=1), jnp.concatenate(sums[::-1], axis=1))


def split_columns(total, v, share):
    b = [total[:, i * share : (i + 1) * share] for i in range(4)]
    odd, up = (v & 1) == 1, (v & 2) == 2
    p, q = jnp.where(odd, b[1], b[0]), jnp.where(odd, b[0], b[1])
    r, s = jnp.where(odd, b[3], b[2]), jnp.where(odd, b[2], b[3])
    return [jnp.where(up, r, p), jnp.where(up, s, q), jnp.where(up, p, r), jnp.where(up, q, s)]


def vmem(n):
    return [pl.BlockSpec(memory_space=pltpu.VMEM)] * n


def call(kernel, outs, args, flops):
    nbytes = sum(4 * a.size for a in args) + sum(4 * o.size for o in outs)
    return pl.pallas_call(
        kernel,
        out_shape=outs,
        in_specs=vmem(len(args)),
        out_specs=vmem(len(outs)),
        compiler_params=pltpu.CompilerParams(vmem_limit_bytes=12 * 2**20),
        cost_estimate=pl.CostEstimate(flops=flops, bytes_accessed=nbytes, transcendentals=0),
    )(*args)


def swap(a, axis, by=1):
    n = lax.axis_size(axis)
    return lax.ppermute(a, axis, [(i, i ^ by) for i in range(n)])


def gather(block):
    half = block.shape[0] // 2
    a, b = block[:half], block[half:]
    ya, xb = swap(a, "y"), swap(b, "x")
    xa, yb = swap(a, "x"), swap(b, "y")
    return a, b, xa, xb, ya, yb, swap(ya, "x"), swap(xb, "y")


def cross(a):
    return lax.ppermute(a, ("y", "x"), [(i, i ^ 3) for i in range(4)])


def fast(vectors, reflectors, triangles):
    rows, share = vectors.shape
    panels, _, width = reflectors.shape
    core, sums = lax.axis_index("core"), lax.axis_size("z")
    half = width // 2
    part = jax.ShapeDtypeStruct((share // 2, width), F32)
    whole = jax.ShapeDtypeStruct((rows, share), F32)
    work = 2 * rows * width * share
    top = panels - 1

    sections, factors = {}, {}
    for k in reversed(range(panels)):
        sections[k] = gather(reflectors[k])
        own = lax.dynamic_slice(triangles[k], (core * half, 0), (half, share))
        received = swap(own, "x"), swap(own, "y"), cross(own)
        factors[k] = (swap(jnp.concatenate(received, axis=1), "core"), *received)
        if k == top:
            pieces = list(sections[k])
            pieces[4], reflectors, triangles = lax.optimization_barrier((pieces[4], reflectors, triangles))
            sections[k] = tuple(pieces)

    def reduced(keep, send, k):
        s = keep + swap(send, "core")
        r = [swap(s, "z", by) for by in range(1, sums)]
        mine = call(
            functools.partial(solve_kernel, k, sums), [part], [s, *r, triangles, *factors[k]], width * width * share
        )[0]
        return mine, swap(mine, "core")

    keep, send = call(first_kernel, [part, part], [vectors, *sections[top]], work)
    current = vectors
    for k in reversed(range(1, panels)):
        c = reduced(keep, send, k)
        current, keep, send = call(
            middle_kernel, [whole, part, part], [current, *c, *sections[k], *sections[k - 1]], 2 * work
        )
    c = reduced(keep, send, 0)
    return call(last_kernel, [whole], [current, *c, *sections[0]], work)[0]


def general(vectors, reflectors, triangles):
    highest = lax.Precision.HIGHEST
    row, vec = ("z", "core"), ("y", "x")
    current = vectors
    for panel in reversed(range(reflectors.shape[0])):
        section = lax.all_gather(reflectors[panel], vec, axis=0, tiled=True)
        factor = lax.all_gather(triangles[panel], vec, axis=1, tiled=True)
        partial_value = lax.dot_general(
            section, current, (((0,), (0,)), ((), ())), precision=highest, preferred_element_type=F32
        )
        share = lax.psum_scatter(partial_value, row, scatter_dimension=1, tiled=True)
        owned = jnp.dot(factor, share, precision=highest, preferred_element_type=F32)
        coefficients = lax.all_gather(owned, row, axis=1, tiled=True)
        current = current - jnp.dot(section, coefficients, precision=highest, preferred_element_type=F32)
    return current


def solution(mesh):
    rows, vecs = mesh.shape["row"], mesh.shape["vec"]
    side = next(s for s in range(int(vecs**0.5), 0, -1) if vecs % s == 0)
    cores = 2 if rows % 2 == 0 else 1
    fine = Mesh(mesh.devices.reshape(rows // cores, cores, side, vecs // side), ("z", "core", "y", "x"))
    halves = [fine.shape[axis] == 2 for axis in ("core", "y", "x")]
    small = all(halves) and fine.shape["z"] & (fine.shape["z"] - 1) == 0
    row, vec = ("z", "core"), ("y", "x")

    def body(*args):
        return (fast if small else general)(*args)

    return jax.shard_map(
        body,
        mesh=fine,
        in_specs=(P(row, vec), P(None, row + vec, None), P(None, None, vec)),
        out_specs=P(row, vec),
        check_vma=False,
    )
```

time: 121 us -> 119 us (0.983)
  waiting for transfers between devices: 81.3 us -> 61.5 us
  starting transfers between devices: 29.5 us -> 46.7 us
    ppermute x30 -> x42, waiting for transfers between devices: 81.3 us -> 59.8 us  [swap(): return lax.ppermute(a, axis, [(i, i ^ by) for i in range(n)])]
    ppermute x30 -> x42, starting transfers between devices: 29.5 us -> 40.3 us  [swap(): return lax.ppermute(a, axis, [(i, i ^ by) for i in range(n)])]
    ppermute x0 -> x3, starting transfers between devices: none -> 6.36 us  [cross(): return lax.ppermute(a, ('y', 'x'), [(i, i ^ 3) for i in range(4)])]
    ppermute x0 -> x3, waiting for transfers between devices: none -> 1.65 us  [cross(): return lax.ppermute(a, ('y', 'x'), [(i, i ^ 3) for i in range(4)])]
    squeeze x2 -> x0, local copies, waits for them, and re-layouts: 1.22 us -> none  [fast(): reflectors[panel]]
  transfers between devices with their start and end apart: 30 -> 45, of which waited for: 18 -> 21; matrix products, arithmetic and copies ran while one was open for 1% -> 0% of each run, Pallas kernels for 4% -> 5%
where the time goes in v3:
time: 119 us
  waiting for transfers between devices  61.5 us (52%)
  starting transfers between devices  46.7 us (39%)
  Pallas kernels  8.89 us (7%)
  local copies, waits for them, and re-layouts  1.36 us (1%)
    ppermute x42, waiting for transfers between devices, swap(): return lax.ppermute(a, axis, [(i, i ^ by) for i in range(n)])  59.8 us
    ppermute x42, starting transfers between devices, swap(): return lax.ppermute(a, axis, [(i, i ^ by) for i in range(n)])  40.3 us
    pallas_call x7, Pallas kernels, call(): pl.pallas_call(kernel, out_shape=outs, in_specs=vmem(len(args)), out_spec...  8.89 us
    ppermute x3, starting transfers between devices, cross(): return lax.ppermute(a, ('y', 'x'), [(i, i ^ 3) for i in range(4)])  6.36 us
  transfers between devices with their start and end apart: 45, of which 21 were waited for; matrix products, arithmetic and copies ran while one was open for 0% of the time, Pallas kernels for 5%

profile of v3, /device:TPU:0, one launch (start us, length us, event | category | flops | bytes accessed | tf_op | source)
XLA Modules:
  0.0 118.8 jit_solution(7075367520762905314)
XLA Ops:
  1.2 3.0 %collective-permute-start.1 = (f32[128,512]{1,0:T(8,128)S(1)}, f32[128,512]{1,0:T(8,128)S(1)}, u32[]{:S(2)}, u32[]{:S(2)}) collective-permute-start(f32[128,512]{1,0:T(8,128)S(1)} %get-tuple-element.31.refs_1_), channel_id=1, source_target_pairs={{0,1},{1,0},{2,3},{3,2},{4,5},{5,4},{6,7},{7,6},{8,9},{9,8},{10,11... | collective-permute-start | bytes 786440 | tf_op jit(solution)/shard_map/ppermute | solution.py:134
  6.4 2.9 %collective-permute-start.12 = (f32[256,128]{1,0:T(8,128)S(1)}, f32[256,128]{1,0:T(8,128)S(1)}, u32[]{:S(2)}, u32[]{:S(2)}) collective-permute-start(f32[256,128]{1,0:T(8,128)S(1)} %dynamic-slice_bitcast_fusion.2), channel_id=1, source_target_pairs={{0,3},{1,2},{2,1},{3,0},{4,7},{5,6},{6,5},{7,4},{8,11},{9,10},{10,... | collective-permute-start | bytes 393224 | tf_op jit(solution)/shard_map/ppermute | solution.py:146
  9.3 4.9 %collective-permute-done.10.refs_6_ = f32[256,128]{1,0:T(8,128)S(1)} collective-permute-done((f32[256,128]{1,0:T(8,128)S(1)}, f32[256,128]{1,0:T(8,128)S(1)}, u32[]{:S(2)}, u32[]{:S(2)}) %collective-permute-start.10) | collective-permute-done | bytes 131104 | tf_op jit(solution)/shard_map/ppermute | solution.py:134
  14.2 2.0 %collective-permute-start = (f32[128,512]{1,0:T(8,128)S(1)}, f32[128,512]{1,0:T(8,128)S(1)}, u32[]{:S(2)}, u32[]{:S(2)}) collective-permute-start(f32[128,512]{1,0:T(8,128)S(1)} %get-tuple-element.32.refs_0_), channel_id=1, source_target_pairs={{0,1},{1,0},{2,3},{3,2},{4,5},{5,4},{6,7},{7,6},{8,9},{9,8},{10,11... | collective-permute-start | bytes 786440 | tf_op jit(solution)/shard_map/ppermute | solution.py:134
  17.3 2.5 %collective-permute-start.3 = (f32[128,512]{1,0:T(8,128)S(1)}, f32[128,512]{1,0:T(8,128)S(1)}, u32[]{:S(2)}, u32[]{:S(2)}) collective-permute-start(f32[128,512]{1,0:T(8,128)S(1)} %get-tuple-element.31.refs_1_), channel_id=1, source_target_pairs={{0,2},{2,0},{1,3},{3,1},{4,6},{6,4},{5,7},{7,5},{8,10},{10,8},{9,1... | collective-permute-start | bytes 786440 | tf_op jit(solution)/shard_map/ppermute | solution.py:134
  20.1 3.3 %collective-permute-done.refs_2_ = f32[128,512]{1,0:T(8,128)S(1)} collective-permute-done((f32[128,512]{1,0:T(8,128)S(1)}, f32[128,512]{1,0:T(8,128)S(1)}, u32[]{:S(2)}, u32[]{:S(2)}) %collective-permute-start) | collective-permute-done | bytes 262176 | tf_op jit(solution)/shard_map/ppermute | solution.py:134
  23.4 2.0 %collective-permute-start.17 = (f32[128,512]{1,0:T(8,128)S(1)}, f32[128,512]{1,0:T(8,128)S(1)}, u32[]{:S(2)}, u32[]{:S(2)}) collective-permute-start(f32[128,512]{1,0:T(8,128)S(1)} %get-tuple-element.30.refs_8_.refs_0_), channel_id=1, source_target_pairs={{0,2},{2,0},{1,3},{3,1},{4,6},{6,4},{5,7},{7,5},{8,10},{10,8},{9,1... | collective-permute-start | bytes 786440 | tf_op jit(solution)/shard_map/ppermute | solution.py:134
  26.9 4.7 %collective-permute-done.5.refs_7_ = f32[128,512]{1,0:T(8,128)S(1)} collective-permute-done((f32[128,512]{1,0:T(8,128)S(1)}, f32[128,512]{1,0:T(8,128)S(1)}, u32[]{:S(2)}, u32[]{:S(2)}) %collective-permute-start.5) | collective-permute-done | bytes 262176 | tf_op jit(solution)/shard_map/ppermute | solution.py:134
  35.7 3.2 %collective-permute-done.25.refs_6_ = f32[256,128]{1,0:T(8,128)S(1)} collective-permute-done((f32[256,128]{1,0:T(8,128)S(1)}, f32[256,128]{1,0:T(8,128)S(1)}, u32[]{:S(2)}, u32[]{:S(2)}) %collective-permute-start.25) | collective-permute-done | bytes 131104 | tf_op jit(solution)/shard_map/ppermute | solution.py:134
  40.5 2.6 %collective-permute-start.8 = (f32[64,512]{1,0:T(8,128)S(1)}, f32[64,512]{1,0:T(8,128)S(1)}, u32[]{:S(2)}, u32[]{:S(2)}) collective-permute-start(f32[64,512]{1,0:T(8,128)S(1)} %add.14.refs_0_), channel_id=1, source_target_pairs={{0,16},{8,24},{16,0},{24,8},{1,17},{9,25},{17,1},{25,9},{2,18},{10... | collective-permute-start | bytes 393224 | tf_op jit(solution)/shard_map/ppermute | solution.py:134
  44.6 2.0 %collective-permute-start.27 = (f32[256,128]{1,0:T(8,128)S(1)}, f32[256,128]{1,0:T(8,128)S(1)}, u32[]{:S(2)}, u32[]{:S(2)}) collective-permute-start(f32[256,128]{1,0:T(8,128)S(1)} %dynamic-slice_bitcast_fusion.1), channel_id=1, source_target_pairs={{0,3},{1,2},{2,1},{3,0},{4,7},{5,6},{6,5},{7,4},{8,11},{9,10},{10,... | collective-permute-start | bytes 393224 | tf_op jit(solution)/shard_map/ppermute | solution.py:146
  47.2 6.0 %collective-permute-done.8.refs_2_ = f32[64,512]{1,0:T(8,128)S(1)} collective-permute-done((f32[64,512]{1,0:T(8,128)S(1)}, f32[64,512]{1,0:T(8,128)S(1)}, u32[]{:S(2)}, u32[]{:S(2)}) %collective-permute-start.8) | collective-permute-done | bytes 131104 | tf_op jit(solution)/shard_map/ppermute | solution.py:134
  57.2 2.3 %collective-permute-done.19.refs_14_.refs_6_ = f32[128,512]{1,0:T(8,128)S(1)} collective-permute-done((f32[128,512]{1,0:T(8,128)S(1)}, f32[128,512]{1,0:T(8,128)S(1)}, u32[]{:S(2)}, u32[]{:S(2)}) %collective-permute-start.19) | collective-permute-done | bytes 262176 | tf_op jit(solution)/shard_map/ppermute | solution.py:134
  59.5 1.9 %collective-permute-done.20.refs_15_.refs_7_ = f32[128,512]{1,0:T(8,128)S(1)} collective-permute-done((f32[128,512]{1,0:T(8,128)S(1)}, f32[128,512]{1,0:T(8,128)S(1)}, u32[]{:S(2)}, u32[]{:S(2)}) %collective-permute-start.20) | collective-permute-done | bytes 262176 | tf_op jit(solution)/shard_map/ppermute | solution.py:134
  61.4 2.0 %shard_map.39 = (f32[1024,128]{1,0:T(8,128)S(1)}, f32[64,512]{1,0:T(8,128)S(1)}, f32[64,512]{1,0:T(8,128)S(1)}) custom-call(f32[1024,128]{1,0:T(8,128)S(1)} %copy-done.1, f32[64,512]{1,0:T(8,128)S(1)} %shard_map.38.mine, f32[64,512]{1,0:T(8,128)S(1)} %collective-permute-done.14.other, f32[128,512]{1,0:T(8,128)S(1)} %get-tuple-element.32.refs_0_, ...), custom_call_target="tpu_custom_call" | custom-call | flops 268435456 | bytes 5767168 | tf_op jit(solution)/shard_map/pallas_call | solution.py:122
  67.8 7.6 %collective-permute-done.40.refs_6_ = f32[256,128]{1,0:T(8,128)S(1)} collective-permute-done((f32[256,128]{1,0:T(8,128)S(1)}, f32[256,128]{1,0:T(8,128)S(1)}, u32[]{:S(2)}, u32[]{:S(2)}) %collective-permute-start.40) | collective-permute-done | bytes 131104 | tf_op jit(solution)/shard_map/ppermute | solution.py:134
  76.9 2.3 %collective-permute-start.23 = (f32[64,512]{1,0:T(8,128)S(1)}, f32[64,512]{1,0:T(8,128)S(1)}, u32[]{:S(2)}, u32[]{:S(2)}) collective-permute-start(f32[64,512]{1,0:T(8,128)S(1)} %add.16.refs_0_), channel_id=1, source_target_pairs={{0,16},{8,24},{16,0},{24,8},{1,17},{9,25},{17,1},{25,9},{2,18},{10... | collective-permute-start | bytes 393224 | tf_op jit(solution)/shard_map/ppermute | solution.py:134
  83.5 6.1 %collective-permute-done.23.refs_2_ = f32[64,512]{1,0:T(8,128)S(1)} collective-permute-done((f32[64,512]{1,0:T(8,128)S(1)}, f32[64,512]{1,0:T(8,128)S(1)}, u32[]{:S(2)}, u32[]{:S(2)}) %collective-permute-start.23) | collective-permute-done | bytes 131104 | tf_op jit(solution)/shard_map/ppermute | solution.py:134
  93.2 2.7 %collective-permute-done.34.refs_14_.refs_6_ = f32[128,512]{1,0:T(8,128)S(1)} collective-permute-done((f32[128,512]{1,0:T(8,128)S(1)}, f32[128,512]{1,0:T(8,128)S(1)}, u32[]{:S(2)}, u32[]{:S(2)}) %collective-permute-start.34) | collective-permute-done | bytes 262176 | tf_op jit(solution)/shard_map/ppermute | solution.py:134
  97.2 2.0 %shard_map.41 = (f32[1024,128]{1,0:T(8,128)S(1)}, f32[64,512]{1,0:T(8,128)S(1)}, f32[64,512]{1,0:T(8,128)S(1)}) custom-call(f32[1024,128]{1,0:T(8,128)S(1)} %get-tuple-element.21.x, f32[64,512]{1,0:T(8,128)S(1)} %shard_map.40.mine, f32[64,512]{1,0:T(8,128)S(1)} %collective-permute-done.29.other, f32[128,512]{1,0:T(8,128)S(1)} %get-tuple-element.30.refs_8_.refs_0_, ...), custom_call_target="tpu_custom_call" | custom-call | flops 268435456 | bytes 5767168 | tf_op jit(solution)/shard_map/pallas_call | solution.py:122
  102.0 2.6 %collective-permute-start.38 = (f32[64,512]{1,0:T(8,128)S(1)}, f32[64,512]{1,0:T(8,128)S(1)}, u32[]{:S(2)}, u32[]{:S(2)}) collective-permute-start(f32[64,512]{1,0:T(8,128)S(1)} %add.17.refs_0_), channel_id=1, source_target_pairs={{0,16},{8,24},{16,0},{24,8},{1,17},{9,25},{17,1},{25,9},{2,18},{10... | collective-permute-start | bytes 393224 | tf_op jit(solution)/shard_map/ppermute | solution.py:134
  105.1 3.4 %collective-permute-done.37.refs_1_ = f32[64,512]{1,0:T(8,128)S(1)} collective-permute-done((f32[64,512]{1,0:T(8,128)S(1)}, f32[64,512]{1,0:T(8,128)S(1)}, u32[]{:S(2)}, u32[]{:S(2)}) %collective-permute-start.37) | collective-permute-done | bytes 131104 | tf_op jit(solution)/shard_map/ppermute | solution.py:134
  108.5 6.3 %collective-permute-done.38.refs_2_ = f32[64,512]{1,0:T(8,128)S(1)} collective-permute-done((f32[64,512]{1,0:T(8,128)S(1)}, f32[64,512]{1,0:T(8,128)S(1)}, u32[]{:S(2)}, u32[]{:S(2)}) %collective-permute-start.38) | collective-permute-done | bytes 131104 | tf_op jit(solution)/shard_map/ppermute | solution.py:134
  117.0 1.8 %shard_map.43 = f32[1024,128]{1,0:T(8,128)} custom-call(f32[1024,128]{1,0:T(8,128)S(1)} %get-tuple-element.24.x, f32[64,512]{1,0:T(8,128)S(1)} %shard_map.42.mine, f32[64,512]{1,0:T(8,128)S(1)} %collective-permute-done.44.other, f32[128,512]{1,0:T(8,128)S(1)} %get-tuple-element.28.refs_8_.refs_0_, f32[128,512]{1,0:T(8,128)S(1)} %get-tuple-element.27.refs_9_.refs_1_, ...), custom_call_target="tpu_custom_call" | custom-call | flops 134217728 | bytes 3407872 | tf_op jit(solution)/shard_map/pallas_call | solution.py:122
  (93 shorter events, 38.4 us)
Async XLA Ops:
  1.2 18.6 %collective-permute-start.1 = (f32[128,512]{1,0:T(8,128)S(1)}, f32[128,512]{1,0:T(8,128)S(1)}, u32[]{:S(2)}, u32[]{:S(2)}) collective-permute-start(f32[128,512]{1,0:T(8,128)S(1)} %get-tuple-element.31.refs_1_), channel_id=1, source_target_pairs={{0,1},{1,0},{2,3},{3,2},{4,5},{5,4},{6,7},{7,6},{8,9},{9,8},{10,11... | collective-permute-start | bytes 786440 | tf_op jit(solution)/shard_map/ppermute | solution.py:134
  4.2 15.6 %collective-permute-start.2 = (f32[128,512]{1,0:T(8,128)S(1)}, f32[128,512]{1,0:T(8,128)S(1)}, u32[]{:S(2)}, u32[]{:S(2)}) collective-permute-start(f32[128,512]{1,0:T(8,128)S(1)} %get-tuple-element.32.refs_0_), channel_id=1, source_target_pairs={{0,2},{2,0},{1,3},{3,1},{4,6},{6,4},{5,7},{7,5},{8,10},{10,8},{9,1... | collective-permute-start | bytes 786440 | tf_op jit(solution)/shard_map/ppermute | solution.py:134
  6.4 10.9 %collective-permute-start.11 = (f32[256,128]{1,0:T(8,128)S(1)}, f32[256,128]{1,0:T(8,128)S(1)}, u32[]{:S(2)}, u32[]{:S(2)}) collective-permute-start(f32[256,128]{1,0:T(8,128)S(1)} %dynamic-slice_bitcast_fusion.2), channel_id=1, source_target_pairs={{0,2},{2,0},{1,3},{3,1},{4,6},{6,4},{5,7},{7,5},{8,10},{10,8},{9,1... | collective-permute-start | bytes 393224 | tf_op jit(solution)/shard_map/ppermute | solution.py:134
  6.4 13.4 %collective-permute-start.12 = (f32[256,128]{1,0:T(8,128)S(1)}, f32[256,128]{1,0:T(8,128)S(1)}, u32[]{:S(2)}, u32[]{:S(2)}) collective-permute-start(f32[256,128]{1,0:T(8,128)S(1)} %dynamic-slice_bitcast_fusion.2), channel_id=1, source_target_pairs={{0,3},{1,2},{2,1},{3,0},{4,7},{5,6},{6,5},{7,4},{8,11},{9,10},{10,... | collective-permute-start | bytes 393224 | tf_op jit(solution)/shard_map/ppermute | solution.py:146
  19.8 11.9 %collective-permute-start.5 = (f32[128,512]{1,0:T(8,128)S(1)}, f32[128,512]{1,0:T(8,128)S(1)}, u32[]{:S(2)}, u32[]{:S(2)}) collective-permute-start(f32[128,512]{1,0:T(8,128)S(1)} %collective-permute-done.1.refs_3_), channel_id=1, source_target_pairs={{0,2},{2,0},{1,3},{3,1},{4,6},{6,4},{5,7},{7,5},{8,10},{10,8},{9,1... | collective-permute-start | bytes 786440 | tf_op jit(solution)/shard_map/ppermute | solution.py:134
  19.8 11.9 %collective-permute-start.4 = (f32[128,512]{1,0:T(8,128)S(1)}, f32[128,512]{1,0:T(8,128)S(1)}, u32[]{:S(2)}, u32[]{:S(2)}) collective-permute-start(f32[128,512]{1,0:T(8,128)S(1)} %collective-permute-done.2.refs_4_), channel_id=1, source_target_pairs={{0,1},{1,0},{2,3},{3,2},{4,5},{5,4},{6,7},{7,6},{8,9},{9,8},{10,11... | collective-permute-start | bytes 786440 | tf_op jit(solution)/shard_map/ppermute | solution.py:134
  19.9 23.1 %collective-permute-start.13 = (f32[256,384]{1,0:T(8,128)S(1)}, f32[256,384]{1,0:T(8,128)S(1)}, u32[]{:S(2)}, u32[]{:S(2)}) collective-permute-start(f32[256,384]{1,0:T(8,128)S(1)} %pad_maximum_fusion), channel_id=1, source_target_pairs={{0,4},{4,0},{1,5},{5,1},{2,6},{6,2},{3,7},{7,3},{8,12},{12,8},{9,1... | collective-permute-start | bytes 1179656 | tf_op jit(solution)/shard_map/ppermute | solution.py:134
  23.4 20.3 %collective-permute-start.17 = (f32[128,512]{1,0:T(8,128)S(1)}, f32[128,512]{1,0:T(8,128)S(1)}, u32[]{:S(2)}, u32[]{:S(2)}) collective-permute-start(f32[128,512]{1,0:T(8,128)S(1)} %get-tuple-element.30.refs_8_.refs_0_), channel_id=1, source_target_pairs={{0,2},{2,0},{1,3},{3,1},{4,6},{6,4},{5,7},{7,5},{8,10},{10,8},{9,1... | collective-permute-start | bytes 786440 | tf_op jit(solution)/shard_map/ppermute | solution.py:134
  26.9 17.6 %collective-permute-start.16 = (f32[128,512]{1,0:T(8,128)S(1)}, f32[128,512]{1,0:T(8,128)S(1)}, u32[]{:S(2)}, u32[]{:S(2)}) collective-permute-start(f32[128,512]{1,0:T(8,128)S(1)} %get-tuple-element.29.refs_9_.refs_1_), channel_id=1, source_target_pairs={{0,1},{1,0},{2,3},{3,2},{4,5},{5,4},{6,7},{7,6},{8,9},{9,8},{10,11... | collective-permute-start | bytes 786440 | tf_op jit(solution)/shard_map/ppermute | solution.py:134
  40.5 12.7 %collective-permute-start.8 = (f32[64,512]{1,0:T(8,128)S(1)}, f32[64,512]{1,0:T(8,128)S(1)}, u32[]{:S(2)}, u32[]{:S(2)}) collective-permute-start(f32[64,512]{1,0:T(8,128)S(1)} %add.14.refs_0_), channel_id=1, source_target_pairs={{0,16},{8,24},{16,0},{24,8},{1,17},{9,25},{17,1},{25,9},{2,18},{10... | collective-permute-start | bytes 393224 | tf_op jit(solution)/shard_map/ppermute | solution.py:134
  43.7 12.9 %collective-permute-start.15 = (f32[128,512]{1,0:T(8,128)S(1)}, f32[128,512]{1,0:T(8,128)S(1)}, u32[]{:S(2)}, u32[]{:S(2)}) collective-permute-start(f32[128,512]{1,0:T(8,128)S(1)} %get-tuple-element.30.refs_8_.refs_0_), channel_id=1, source_target_pairs={{0,1},{1,0},{2,3},{3,2},{4,5},{5,4},{6,7},{7,6},{8,9},{9,8},{10,11... | collective-permute-start | bytes 786440 | tf_op jit(solution)/shard_map/ppermute | solution.py:134
  44.6 12.0 %collective-permute-start.27 = (f32[256,128]{1,0:T(8,128)S(1)}, f32[256,128]{1,0:T(8,128)S(1)}, u32[]{:S(2)}, u32[]{:S(2)}) collective-permute-start(f32[256,128]{1,0:T(8,128)S(1)} %dynamic-slice_bitcast_fusion.1), channel_id=1, source_target_pairs={{0,3},{1,2},{2,1},{3,0},{4,7},{5,6},{6,5},{7,4},{8,11},{9,10},{10,... | collective-permute-start | bytes 393224 | tf_op jit(solution)/shard_map/ppermute | solution.py:146
  46.6 10.6 %collective-permute-start.18 = (f32[128,512]{1,0:T(8,128)S(1)}, f32[128,512]{1,0:T(8,128)S(1)}, u32[]{:S(2)}, u32[]{:S(2)}) collective-permute-start(f32[128,512]{1,0:T(8,128)S(1)} %get-tuple-element.29.refs_9_.refs_1_), channel_id=1, source_target_pairs={{0,2},{2,0},{1,3},{3,1},{4,6},{6,4},{5,7},{7,5},{8,10},{10,8},{9,1... | collective-permute-start | bytes 786440 | tf_op jit(solution)/shard_map/ppermute | solution.py:134
  56.6 24.6 %collective-permute-start.28 = (f32[256,384]{1,0:T(8,128)S(1)}, f32[256,384]{1,0:T(8,128)S(1)}, u32[]{:S(2)}, u32[]{:S(2)}) collective-permute-start(f32[256,384]{1,0:T(8,128)S(1)} %pad_maximum_fusion.1), channel_id=1, source_target_pairs={{0,4},{4,0},{1,5},{5,1},{2,6},{6,2},{3,7},{7,3},{8,12},{12,8},{9,1... | collective-permute-start | bytes 1179656 | tf_op jit(solution)/shard_map/ppermute | solution.py:134
  63.5 15.6 %collective-permute-start.32 = (f32[128,512]{1,0:T(8,128)S(1)}, f32[128,512]{1,0:T(8,128)S(1)}, u32[]{:S(2)}, u32[]{:S(2)}) collective-permute-start(f32[128,512]{1,0:T(8,128)S(1)} %get-tuple-element.28.refs_8_.refs_0_), channel_id=1, source_target_pairs={{0,2},{2,0},{1,3},{3,1},{4,6},{6,4},{5,7},{7,5},{8,10},{10,8},{9,1... | collective-permute-start | bytes 786440 | tf_op jit(solution)/shard_map/ppermute | solution.py:134
  64.2 15.8 %collective-permute-start.31 = (f32[128,512]{1,0:T(8,128)S(1)}, f32[128,512]{1,0:T(8,128)S(1)}, u32[]{:S(2)}, u32[]{:S(2)}) collective-permute-start(f32[128,512]{1,0:T(8,128)S(1)} %get-tuple-element.27.refs_9_.refs_1_), channel_id=1, source_target_pairs={{0,1},{1,0},{2,3},{3,2},{4,5},{5,4},{6,7},{7,6},{8,9},{9,8},{10,11... | collective-permute-start | bytes 786440 | tf_op jit(solution)/shard_map/ppermute | solution.py:134
  66.3 10.6 %collective-permute-start.41 = (f32[256,128]{1,0:T(8,128)S(1)}, f32[256,128]{1,0:T(8,128)S(1)}, u32[]{:S(2)}, u32[]{:S(2)}) collective-permute-start(f32[256,128]{1,0:T(8,128)S(1)} %dynamic-slice_bitcast_fusion), channel_id=1, source_target_pairs={{0,2},{2,0},{1,3},{3,1},{4,6},{6,4},{5,7},{7,5},{8,10},{10,8},{9,1... | collective-permute-start | bytes 393224 | tf_op jit(solution)/shard_map/ppermute | solution.py:134
  76.9 12.7 %collective-permute-start.23 = (f32[64,512]{1,0:T(8,128)S(1)}, f32[64,512]{1,0:T(8,128)S(1)}, u32[]{:S(2)}, u32[]{:S(2)}) collective-permute-start(f32[64,512]{1,0:T(8,128)S(1)} %add.16.refs_0_), channel_id=1, source_target_pairs={{0,16},{8,24},{16,0},{24,8},{1,17},{9,25},{17,1},{25,9},{2,18},{10... | collective-permute-start | bytes 393224 | tf_op jit(solution)/shard_map/ppermute | solution.py:134
  79.2 11.3 %collective-permute-start.24 = (f32[64,512]{1,0:T(8,128)S(1)}, f32[64,512]{1,0:T(8,128)S(1)}, u32[]{:S(2)}, u32[]{:S(2)}) collective-permute-start(f32[64,512]{1,0:T(8,128)S(1)} %add.16.refs_0_), channel_id=1, source_target_pairs={{0,24},{8,16},{16,8},{24,0},{1,25},{9,17},{17,9},{25,1},{2,26},{10... | collective-permute-start | bytes 393224 | tf_op jit(solution)/shard_map/ppermute | solution.py:134
  80.0 12.7 %collective-permute-start.30 = (f32[128,512]{1,0:T(8,128)S(1)}, f32[128,512]{1,0:T(8,128)S(1)}, u32[]{:S(2)}, u32[]{:S(2)}) collective-permute-start(f32[128,512]{1,0:T(8,128)S(1)} %get-tuple-element.28.refs_8_.refs_0_), channel_id=1, source_target_pairs={{0,1},{1,0},{2,3},{3,2},{4,5},{5,4},{6,7},{7,6},{8,9},{9,8},{10,11... | collective-permute-start | bytes 786440 | tf_op jit(solution)/shard_map/ppermute | solution.py:134
  81.2 11.4 %collective-permute-start.42 = (f32[256,128]{1,0:T(8,128)S(1)}, f32[256,128]{1,0:T(8,128)S(1)}, u32[]{:S(2)}, u32[]{:S(2)}) collective-permute-start(f32[256,128]{1,0:T(8,128)S(1)} %dynamic-slice_bitcast_fusion), channel_id=1, source_target_pairs={{0,3},{1,2},{2,1},{3,0},{4,7},{5,6},{6,5},{7,4},{8,11},{9,10},{10,... | collective-permute-start | bytes 393224 | tf_op jit(solution)/shard_map/ppermute | solution.py:146
  82.7 10.6 %collective-permute-start.33 = (f32[128,512]{1,0:T(8,128)S(1)}, f32[128,512]{1,0:T(8,128)S(1)}, u32[]{:S(2)}, u32[]{:S(2)}) collective-permute-start(f32[128,512]{1,0:T(8,128)S(1)} %get-tuple-element.27.refs_9_.refs_1_), channel_id=1, source_target_pairs={{0,2},{2,0},{1,3},{3,1},{4,6},{6,4},{5,7},{7,5},{8,10},{10,8},{9,1... | collective-permute-start | bytes 786440 | tf_op jit(solution)/shard_map/ppermute | solution.py:134
  92.7 12.5 %collective-permute-start.43 = (f32[256,384]{1,0:T(8,128)S(1)}, f32[256,384]{1,0:T(8,128)S(1)}, u32[]{:S(2)}, u32[]{:S(2)}) collective-permute-start(f32[256,384]{1,0:T(8,128)S(1)} %pad_maximum_fusion.2), channel_id=1, source_target_pairs={{0,4},{4,0},{1,5},{5,1},{2,6},{6,2},{3,7},{7,3},{8,12},{12,8},{9,1... | collective-permute-start | bytes 1179656 | tf_op jit(solution)/shard_map/ppermute | solution.py:134
  102.0 12.9 %collective-permute-start.38 = (f32[64,512]{1,0:T(8,128)S(1)}, f32[64,512]{1,0:T(8,128)S(1)}, u32[]{:S(2)}, u32[]{:S(2)}) collective-permute-start(f32[64,512]{1,0:T(8,128)S(1)} %add.17.refs_0_), channel_id=1, source_target_pairs={{0,16},{8,24},{16,0},{24,8},{1,17},{9,25},{17,1},{25,9},{2,18},{10... | collective-permute-start | bytes 393224 | tf_op jit(solution)/shard_map/ppermute | solution.py:134
  (25 other events, 201.6 us)

commit v4 on v3

--- a/solution.py
+++ b/solution.py
@@ -29,18 +29,18 @@
     return lax.axis_index("y") * 2 + lax.axis_index("x"), lax.axis_index("core")
 
 
-def blocks_of(refs):
+def blocks_of(refs, skip=0):
     size = refs[0].shape[0]
-    return [(i // 2, i % 2 * size, ref) for i, ref in enumerate(refs)]
+    return [(i // 2, i % 2 * size, ref) for i, ref in enumerate(refs, skip)]
 
 
 def window(v, block, first, size):
     return pl.ds(pl.multiple_of((v ^ block) * 2 * size + first, 8), size)
 
 
-def project(current, refs, v):
+def project(current, refs, v, skip=0):
     total = None
-    for block, first, ref in blocks_of(refs):
+    for block, first, ref in blocks_of(refs, skip):
         x = current[window(v, block, first, ref.shape[0]), :]
         part = dot3(x.T, ref[...], NN)
         total = part if total is None else total + part
@@ -54,10 +54,15 @@
     send[...] = jnp.where(mine, total[half:], total[:half])
 
 
-def first_kernel(x, *refs):
-    v, core = place()
-    refs, (keep, send) = refs[:PIECES], refs[PIECES:]
-    give_out(project(x, refs, v), core, keep, send)
+def early_kernel(x, *refs):
+    v, _ = place()
+    refs[-1][...] = project(x, refs[:-1], v)
+
+
+def late_kernel(x, total, *refs):
+    v, core = place()
+    refs, (keep, send) = refs[:-2], refs[-2:]
+    give_out(total[...] + project(x, refs, v, PIECES - len(refs)), core, keep, send)
 
 
 def both_halves(mine, other, core):
@@ -161,7 +166,8 @@
         sections[k] = gather(reflectors[k])
         own = lax.dynamic_slice(triangles[k], (core * half, 0), (half, share))
         received = swap(own, "x"), swap(own, "y"), cross(own)
-        factors[k] = (swap(jnp.concatenate(received, axis=1), "core"), *received)
+        joined = jnp.concatenate(received, axis=1)
+        factors[k] = (swap(joined, "core"), *received)
         if k == top:
             pieces = list(sections[k])
             pieces[4], reflectors, triangles = lax.optimization_barrier((pieces[4], reflectors, triangles))
@@ -175,7 +181,9 @@
         )[0]
         return mine, swap(mine, "core")
 
-    keep, send = call(first_kernel, [part, part], [vectors, *sections[top]], work)
+    early, late = sections[top][:-2], sections[top][-2:]
+    total = call(early_kernel, [jax.ShapeDtypeStruct((share, width), F32)], [vectors, *early], work * 3 // 4)[0]
+    keep, send = call(late_kernel, [part, part], [vectors, total, *late], work // 4)
     current = vectors
     for k in reversed(range(1, panels)):
         c = reduced(keep, send, k)

time: 119 us -> 117 us (0.983)
  waiting for transfers between devices: 61.5 us -> 58.9 us
    ppermute x42, waiting for transfers between devices: 59.8 us -> 57.9 us  [swap(): return lax.ppermute(a, axis, [(i, i ^ by) for i in range(n)])]
    pallas_call x7 -> x8, Pallas kernels: 8.89 us -> 9.08 us  [call(): pl.pallas_call(kernel, out_shape=outs, in_specs=vmem(len(args)), out_spec...]
  transfers between devices with their start and end apart: 45 -> 45, of which waited for: 21 -> 21; matrix products, arithmetic and copies ran while one was open for 0% -> 0% of each run, Pallas kernels for 5% -> 6%
where the time goes in v4:
time: 117 us
  waiting for transfers between devices  58.9 us (50%)
  starting transfers between devices  47.3 us (40%)
  Pallas kernels  9.08 us (8%)
  local copies, waits for them, and re-layouts  1.35 us (1%)
    ppermute x42, waiting for transfers between devices, swap(): return lax.ppermute(a, axis, [(i, i ^ by) for i in range(n)])  57.9 us
    ppermute x42, starting transfers between devices, swap(): return lax.ppermute(a, axis, [(i, i ^ by) for i in range(n)])  41.3 us
    pallas_call x8, Pallas kernels, call(): pl.pallas_call(kernel, out_shape=outs, in_specs=vmem(len(args)), out_spec...  9.08 us
    ppermute x3, starting transfers between devices, cross(): return lax.ppermute(a, ('y', 'x'), [(i, i ^ 3) for i in range(4)])  5.99 us
  transfers between devices with their start and end apart: 45, of which 21 were waited for; matrix products, arithmetic and copies ran while one was open for 0% of the time, Pallas kernels for 6%

profile of v4, /device:TPU:0, one launch (start us, length us, event | category | flops | bytes accessed | tf_op | source)
XLA Modules:
  0.0 117.0 jit_solution(10325332349725387102)
XLA Ops:
  1.2 3.1 %collective-permute-start.2 = (f32[128,512]{1,0:T(8,128)S(1)}, f32[128,512]{1,0:T(8,128)S(1)}, u32[]{:S(2)}, u32[]{:S(2)}) collective-permute-start(f32[128,512]{1,0:T(8,128)S(1)} %get-tuple-element.32.refs_0_), channel_id=1, source_target_pairs={{0,2},{2,0},{1,3},{3,1},{4,6},{6,4},{5,7},{7,5},{8,10},{10,8},{9,1... | collective-permute-start | bytes 786440 | tf_op jit(solution)/shard_map/ppermute | solution.py:139
  6.5 2.9 %collective-permute-start.12 = (f32[256,128]{1,0:T(8,128)S(1)}, f32[256,128]{1,0:T(8,128)S(1)}, u32[]{:S(2)}, u32[]{:S(2)}) collective-permute-start(f32[256,128]{1,0:T(8,128)S(1)} %dynamic-slice_bitcast_fusion.2), channel_id=1, source_target_pairs={{0,3},{1,2},{2,1},{3,0},{4,7},{5,6},{6,5},{7,4},{8,11},{9,10},{10,... | collective-permute-start | bytes 393224 | tf_op jit(solution)/shard_map/ppermute | solution.py:151
  9.3 6.9 %collective-permute-done.10.refs_6_ = f32[256,128]{1,0:T(8,128)S(1)} collective-permute-done((f32[256,128]{1,0:T(8,128)S(1)}, f32[256,128]{1,0:T(8,128)S(1)}, u32[]{:S(2)}, u32[]{:S(2)}) %collective-permute-start.10) | collective-permute-done | bytes 131104 | tf_op jit(solution)/shard_map/ppermute | solution.py:139
  18.7 2.0 %collective-permute-start.4 = (f32[128,512]{1,0:T(8,128)S(1)}, f32[128,512]{1,0:T(8,128)S(1)}, u32[]{:S(2)}, u32[]{:S(2)}) collective-permute-start(f32[128,512]{1,0:T(8,128)S(1)} %collective-permute-done.2.refs_4_), channel_id=1, source_target_pairs={{0,1},{1,0},{2,3},{3,2},{4,5},{5,4},{6,7},{7,6},{8,9},{9,8},{10,11... | collective-permute-start | bytes 786440 | tf_op jit(solution)/shard_map/ppermute | solution.py:139
  20.7 1.5 %collective-permute-start.5 = (f32[128,512]{1,0:T(8,128)S(1)}, f32[128,512]{1,0:T(8,128)S(1)}, u32[]{:S(2)}, u32[]{:S(2)}) collective-permute-start(f32[128,512]{1,0:T(8,128)S(1)} %collective-permute-done.1.refs_3_), channel_id=1, source_target_pairs={{0,2},{2,0},{1,3},{3,1},{4,6},{6,4},{5,7},{7,5},{8,10},{10,8},{9,1... | collective-permute-start | bytes 786440 | tf_op jit(solution)/shard_map/ppermute | solution.py:139
  22.3 2.3 %collective-permute-done.refs_2_ = f32[128,512]{1,0:T(8,128)S(1)} collective-permute-done((f32[128,512]{1,0:T(8,128)S(1)}, f32[128,512]{1,0:T(8,128)S(1)}, u32[]{:S(2)}, u32[]{:S(2)}) %collective-permute-start) | collective-permute-done | bytes 262176 | tf_op jit(solution)/shard_map/ppermute | solution.py:139
  26.7 3.7 %collective-permute-done.5.refs_1_.refs_7_ = f32[128,512]{1,0:T(8,128)S(1)} collective-permute-done((f32[128,512]{1,0:T(8,128)S(1)}, f32[128,512]{1,0:T(8,128)S(1)}, u32[]{:S(2)}, u32[]{:S(2)}) %collective-permute-start.5) | collective-permute-done | bytes 262176 | tf_op jit(solution)/shard_map/ppermute | solution.py:139
  33.3 4.1 %collective-permute-done.25.refs_6_ = f32[256,128]{1,0:T(8,128)S(1)} collective-permute-done((f32[256,128]{1,0:T(8,128)S(1)}, f32[256,128]{1,0:T(8,128)S(1)}, u32[]{:S(2)}, u32[]{:S(2)}) %collective-permute-start.25) | collective-permute-done | bytes 131104 | tf_op jit(solution)/shard_map/ppermute | solution.py:139
  37.3 1.6 %collective-permute-start.7 = (f32[64,512]{1,0:T(8,128)S(1)}, f32[64,512]{1,0:T(8,128)S(1)}, u32[]{:S(2)}, u32[]{:S(2)}) collective-permute-start(f32[64,512]{1,0:T(8,128)S(1)} %add.14.refs_0_), channel_id=1, source_target_pairs={{0,8},{8,0},{16,24},{24,16},{1,9},{9,1},{17,25},{25,17},{2,10},{10... | collective-permute-start | bytes 393224 | tf_op jit(solution)/shard_map/ppermute | solution.py:139
  38.9 2.6 %collective-permute-start.8 = (f32[64,512]{1,0:T(8,128)S(1)}, f32[64,512]{1,0:T(8,128)S(1)}, u32[]{:S(2)}, u32[]{:S(2)}) collective-permute-start(f32[64,512]{1,0:T(8,128)S(1)} %add.14.refs_0_), channel_id=1, source_target_pairs={{0,16},{8,24},{16,0},{24,8},{1,17},{9,25},{17,1},{25,9},{2,18},{10... | collective-permute-start | bytes 393224 | tf_op jit(solution)/shard_map/ppermute | solution.py:139
  45.6 6.0 %collective-permute-done.8.refs_2_ = f32[64,512]{1,0:T(8,128)S(1)} collective-permute-done((f32[64,512]{1,0:T(8,128)S(1)}, f32[64,512]{1,0:T(8,128)S(1)}, u32[]{:S(2)}, u32[]{:S(2)}) %collective-permute-start.8) | collective-permute-done | bytes 131104 | tf_op jit(solution)/shard_map/ppermute | solution.py:139
  55.0 3.0 %collective-permute-done.19.refs_14_.refs_6_ = f32[128,512]{1,0:T(8,128)S(1)} collective-permute-done((f32[128,512]{1,0:T(8,128)S(1)}, f32[128,512]{1,0:T(8,128)S(1)}, u32[]{:S(2)}, u32[]{:S(2)}) %collective-permute-start.19) | collective-permute-done | bytes 262176 | tf_op jit(solution)/shard_map/ppermute | solution.py:139
  59.4 2.0 %shard_map.40 = (f32[1024,128]{1,0:T(8,128)S(1)}, f32[64,512]{1,0:T(8,128)S(1)}, f32[64,512]{1,0:T(8,128)S(1)}) custom-call(f32[1024,128]{1,0:T(8,128)S(1)} %copy-done.1, f32[64,512]{1,0:T(8,128)S(1)} %shard_map.39.mine, f32[64,512]{1,0:T(8,128)S(1)} %collective-permute-done.14.other, f32[128,512]{1,0:T(8,128)S(1)} %get-tuple-element.32.refs_0_, ...), custom_call_target="tpu_custom_call" | custom-call | flops 268435456 | bytes 5767168 | tf_op jit(solution)/shard_map/pallas_call | solution.py:127
  65.7 8.4 %collective-permute-done.40.refs_6_ = f32[256,128]{1,0:T(8,128)S(1)} collective-permute-done((f32[256,128]{1,0:T(8,128)S(1)}, f32[256,128]{1,0:T(8,128)S(1)}, u32[]{:S(2)}, u32[]{:S(2)}) %collective-permute-start.40) | collective-permute-done | bytes 131104 | tf_op jit(solution)/shard_map/ppermute | solution.py:139
  74.8 2.9 %collective-permute-start.23 = (f32[64,512]{1,0:T(8,128)S(1)}, f32[64,512]{1,0:T(8,128)S(1)}, u32[]{:S(2)}, u32[]{:S(2)}) collective-permute-start(f32[64,512]{1,0:T(8,128)S(1)} %add.16.refs_0_), channel_id=1, source_target_pairs={{0,16},{8,24},{16,0},{24,8},{1,17},{9,25},{17,1},{25,9},{2,18},{10... | collective-permute-start | bytes 393224 | tf_op jit(solution)/shard_map/ppermute | solution.py:139
  79.1 1.9 %collective-permute-start.42 = (f32[256,128]{1,0:T(8,128)S(1)}, f32[256,128]{1,0:T(8,128)S(1)}, u32[]{:S(2)}, u32[]{:S(2)}) collective-permute-start(f32[256,128]{1,0:T(8,128)S(1)} %dynamic-slice_bitcast_fusion), channel_id=1, source_target_pairs={{0,3},{1,2},{2,1},{3,0},{4,7},{5,6},{6,5},{7,4},{8,11},{9,10},{10,... | collective-permute-start | bytes 393224 | tf_op jit(solution)/shard_map/ppermute | solution.py:151
  82.0 5.5 %collective-permute-done.23.refs_2_ = f32[64,512]{1,0:T(8,128)S(1)} collective-permute-done((f32[64,512]{1,0:T(8,128)S(1)}, f32[64,512]{1,0:T(8,128)S(1)}, u32[]{:S(2)}, u32[]{:S(2)}) %collective-permute-start.23) | collective-permute-done | bytes 131104 | tf_op jit(solution)/shard_map/ppermute | solution.py:139
  91.8 2.0 %collective-permute-done.34.refs_14_.refs_6_ = f32[128,512]{1,0:T(8,128)S(1)} collective-permute-done((f32[128,512]{1,0:T(8,128)S(1)}, f32[128,512]{1,0:T(8,128)S(1)}, u32[]{:S(2)}, u32[]{:S(2)}) %collective-permute-start.34) | collective-permute-done | bytes 262176 | tf_op jit(solution)/shard_map/ppermute | solution.py:139
  93.9 2.0 %collective-permute-done.35.refs_15_.refs_7_ = f32[128,512]{1,0:T(8,128)S(1)} collective-permute-done((f32[128,512]{1,0:T(8,128)S(1)}, f32[128,512]{1,0:T(8,128)S(1)}, u32[]{:S(2)}, u32[]{:S(2)}) %collective-permute-start.35) | collective-permute-done | bytes 262176 | tf_op jit(solution)/shard_map/ppermute | solution.py:139
  95.8 2.0 %shard_map.42 = (f32[1024,128]{1,0:T(8,128)S(1)}, f32[64,512]{1,0:T(8,128)S(1)}, f32[64,512]{1,0:T(8,128)S(1)}) custom-call(f32[1024,128]{1,0:T(8,128)S(1)} %get-tuple-element.21.x, f32[64,512]{1,0:T(8,128)S(1)} %shard_map.41.mine, f32[64,512]{1,0:T(8,128)S(1)} %collective-permute-done.29.other, f32[128,512]{1,0:T(8,128)S(1)} %get-tuple-element.30.refs_8_.refs_0_, ...), custom_call_target="tpu_custom_call" | custom-call | flops 268435456 | bytes 5767168 | tf_op jit(solution)/shard_map/pallas_call | solution.py:127
  100.4 1.9 %collective-permute-start.38 = (f32[64,512]{1,0:T(8,128)S(1)}, f32[64,512]{1,0:T(8,128)S(1)}, u32[]{:S(2)}, u32[]{:S(2)}) collective-permute-start(f32[64,512]{1,0:T(8,128)S(1)} %add.17.refs_0_), channel_id=1, source_target_pairs={{0,16},{8,24},{16,0},{24,8},{1,17},{9,25},{17,1},{25,9},{2,18},{10... | collective-permute-start | bytes 393224 | tf_op jit(solution)/shard_map/ppermute | solution.py:139
  103.8 3.6 %collective-permute-done.37.refs_1_ = f32[64,512]{1,0:T(8,128)S(1)} collective-permute-done((f32[64,512]{1,0:T(8,128)S(1)}, f32[64,512]{1,0:T(8,128)S(1)}, u32[]{:S(2)}, u32[]{:S(2)}) %collective-permute-start.37) | collective-permute-done | bytes 131104 | tf_op jit(solution)/shard_map/ppermute | solution.py:139
  107.4 5.7 %collective-permute-done.38.refs_2_ = f32[64,512]{1,0:T(8,128)S(1)} collective-permute-done((f32[64,512]{1,0:T(8,128)S(1)}, f32[64,512]{1,0:T(8,128)S(1)}, u32[]{:S(2)}, u32[]{:S(2)}) %collective-permute-start.38) | collective-permute-done | bytes 131104 | tf_op jit(solution)/shard_map/ppermute | solution.py:139
  115.2 1.8 %shard_map.44 = f32[1024,128]{1,0:T(8,128)} custom-call(f32[1024,128]{1,0:T(8,128)S(1)} %get-tuple-element.24.x, f32[64,512]{1,0:T(8,128)S(1)} %shard_map.43.mine, f32[64,512]{1,0:T(8,128)S(1)} %collective-permute-done.44.other, f32[128,512]{1,0:T(8,128)S(1)} %get-tuple-element.28.refs_8_.refs_0_, f32[128,512]{1,0:T(8,128)S(1)} %get-tuple-element.27.refs_9_.refs_1_, ...), custom_call_target="tpu_custom_call" | custom-call | flops 134217728 | bytes 3407872 | tf_op jit(solution)/shard_map/pallas_call | solution.py:127
  (94 shorter events, 37.4 us)
Async XLA Ops:
  1.2 17.5 %collective-permute-start.2 = (f32[128,512]{1,0:T(8,128)S(1)}, f32[128,512]{1,0:T(8,128)S(1)}, u32[]{:S(2)}, u32[]{:S(2)}) collective-permute-start(f32[128,512]{1,0:T(8,128)S(1)} %get-tuple-element.32.refs_0_), channel_id=1, source_target_pairs={{0,2},{2,0},{1,3},{3,1},{4,6},{6,4},{5,7},{7,5},{8,10},{10,8},{9,1... | collective-permute-start | bytes 786440 | tf_op jit(solution)/shard_map/ppermute | solution.py:139
  4.3 16.4 %collective-permute-start.1 = (f32[128,512]{1,0:T(8,128)S(1)}, f32[128,512]{1,0:T(8,128)S(1)}, u32[]{:S(2)}, u32[]{:S(2)}) collective-permute-start(f32[128,512]{1,0:T(8,128)S(1)} %get-tuple-element.31.refs_1_), channel_id=1, source_target_pairs={{0,1},{1,0},{2,3},{3,2},{4,5},{5,4},{6,7},{7,6},{8,9},{9,8},{10,11... | collective-permute-start | bytes 786440 | tf_op jit(solution)/shard_map/ppermute | solution.py:139
  6.4 11.4 %collective-permute-start.11 = (f32[256,128]{1,0:T(8,128)S(1)}, f32[256,128]{1,0:T(8,128)S(1)}, u32[]{:S(2)}, u32[]{:S(2)}) collective-permute-start(f32[256,128]{1,0:T(8,128)S(1)} %dynamic-slice_bitcast_fusion.2), channel_id=1, source_target_pairs={{0,2},{2,0},{1,3},{3,1},{4,6},{6,4},{5,7},{7,5},{8,10},{10,8},{9,1... | collective-permute-start | bytes 393224 | tf_op jit(solution)/shard_map/ppermute | solution.py:139
  6.5 12.1 %collective-permute-start.12 = (f32[256,128]{1,0:T(8,128)S(1)}, f32[256,128]{1,0:T(8,128)S(1)}, u32[]{:S(2)}, u32[]{:S(2)}) collective-permute-start(f32[256,128]{1,0:T(8,128)S(1)} %dynamic-slice_bitcast_fusion.2), channel_id=1, source_target_pairs={{0,3},{1,2},{2,1},{3,0},{4,7},{5,6},{6,5},{7,4},{8,11},{9,10},{10,... | collective-permute-start | bytes 393224 | tf_op jit(solution)/shard_map/ppermute | solution.py:151
  18.6 22.9 %collective-permute-start.13 = (f32[256,384]{1,0:T(8,128)S(1)}, f32[256,384]{1,0:T(8,128)S(1)}, u32[]{:S(2)}, u32[]{:S(2)}) collective-permute-start(f32[256,384]{1,0:T(8,128)S(1)} %pad_maximum_fusion), channel_id=1, source_target_pairs={{0,4},{4,0},{1,5},{5,1},{2,6},{6,2},{3,7},{7,3},{8,12},{12,8},{9,1... | collective-permute-start | bytes 1179656 | tf_op jit(solution)/shard_map/ppermute | solution.py:139
  18.7 11.7 %collective-permute-start.4 = (f32[128,512]{1,0:T(8,128)S(1)}, f32[128,512]{1,0:T(8,128)S(1)}, u32[]{:S(2)}, u32[]{:S(2)}) collective-permute-start(f32[128,512]{1,0:T(8,128)S(1)} %collective-permute-done.2.refs_4_), channel_id=1, source_target_pairs={{0,1},{1,0},{2,3},{3,2},{4,5},{5,4},{6,7},{7,6},{8,9},{9,8},{10,11... | collective-permute-start | bytes 786440 | tf_op jit(solution)/shard_map/ppermute | solution.py:139
  24.6 17.5 %collective-permute-start.17 = (f32[128,512]{1,0:T(8,128)S(1)}, f32[128,512]{1,0:T(8,128)S(1)}, u32[]{:S(2)}, u32[]{:S(2)}) collective-permute-start(f32[128,512]{1,0:T(8,128)S(1)} %get-tuple-element.30.refs_8_.refs_0_), channel_id=1, source_target_pairs={{0,2},{2,0},{1,3},{3,1},{4,6},{6,4},{5,7},{7,5},{8,10},{10,8},{9,1... | collective-permute-start | bytes 786440 | tf_op jit(solution)/shard_map/ppermute | solution.py:139
  24.8 18.4 %collective-permute-start.16 = (f32[128,512]{1,0:T(8,128)S(1)}, f32[128,512]{1,0:T(8,128)S(1)}, u32[]{:S(2)}, u32[]{:S(2)}) collective-permute-start(f32[128,512]{1,0:T(8,128)S(1)} %get-tuple-element.29.refs_9_.refs_1_), channel_id=1, source_target_pairs={{0,1},{1,0},{2,3},{3,2},{4,5},{5,4},{6,7},{7,6},{8,9},{9,8},{10,11... | collective-permute-start | bytes 786440 | tf_op jit(solution)/shard_map/ppermute | solution.py:139
  38.9 12.7 %collective-permute-start.8 = (f32[64,512]{1,0:T(8,128)S(1)}, f32[64,512]{1,0:T(8,128)S(1)}, u32[]{:S(2)}, u32[]{:S(2)}) collective-permute-start(f32[64,512]{1,0:T(8,128)S(1)} %add.14.refs_0_), channel_id=1, source_target_pairs={{0,16},{8,24},{16,0},{24,8},{1,17},{9,25},{17,1},{25,9},{2,18},{10... | collective-permute-start | bytes 393224 | tf_op jit(solution)/shard_map/ppermute | solution.py:139
  41.5 11.3 %collective-permute-start.9 = (f32[64,512]{1,0:T(8,128)S(1)}, f32[64,512]{1,0:T(8,128)S(1)}, u32[]{:S(2)}, u32[]{:S(2)}) collective-permute-start(f32[64,512]{1,0:T(8,128)S(1)} %add.14.refs_0_), channel_id=1, source_target_pairs={{0,24},{8,16},{16,8},{24,0},{1,25},{9,17},{17,9},{25,1},{2,26},{10... | collective-permute-start | bytes 393224 | tf_op jit(solution)/shard_map/ppermute | solution.py:139
  42.1 12.3 %collective-permute-start.15 = (f32[128,512]{1,0:T(8,128)S(1)}, f32[128,512]{1,0:T(8,128)S(1)}, u32[]{:S(2)}, u32[]{:S(2)}) collective-permute-start(f32[128,512]{1,0:T(8,128)S(1)} %get-tuple-element.30.refs_8_.refs_0_), channel_id=1, source_target_pairs={{0,1},{1,0},{2,3},{3,2},{4,5},{5,4},{6,7},{7,6},{8,9},{9,8},{10,11... | collective-permute-start | bytes 786440 | tf_op jit(solution)/shard_map/ppermute | solution.py:139
  43.2 11.2 %collective-permute-start.27 = (f32[256,128]{1,0:T(8,128)S(1)}, f32[256,128]{1,0:T(8,128)S(1)}, u32[]{:S(2)}, u32[]{:S(2)}) collective-permute-start(f32[256,128]{1,0:T(8,128)S(1)} %dynamic-slice_bitcast_fusion.1), channel_id=1, source_target_pairs={{0,3},{1,2},{2,1},{3,0},{4,7},{5,6},{6,5},{7,4},{8,11},{9,10},{10,... | collective-permute-start | bytes 393224 | tf_op jit(solution)/shard_map/ppermute | solution.py:151
  44.4 10.6 %collective-permute-start.18 = (f32[128,512]{1,0:T(8,128)S(1)}, f32[128,512]{1,0:T(8,128)S(1)}, u32[]{:S(2)}, u32[]{:S(2)}) collective-permute-start(f32[128,512]{1,0:T(8,128)S(1)} %get-tuple-element.29.refs_9_.refs_1_), channel_id=1, source_target_pairs={{0,2},{2,0},{1,3},{3,1},{4,6},{6,4},{5,7},{7,5},{8,10},{10,8},{9,1... | collective-permute-start | bytes 786440 | tf_op jit(solution)/shard_map/ppermute | solution.py:139
  54.4 24.7 %collective-permute-start.28 = (f32[256,384]{1,0:T(8,128)S(1)}, f32[256,384]{1,0:T(8,128)S(1)}, u32[]{:S(2)}, u32[]{:S(2)}) collective-permute-start(f32[256,384]{1,0:T(8,128)S(1)} %pad_maximum_fusion.1), channel_id=1, source_target_pairs={{0,4},{4,0},{1,5},{5,1},{2,6},{6,2},{3,7},{7,3},{8,12},{12,8},{9,1... | collective-permute-start | bytes 1179656 | tf_op jit(solution)/shard_map/ppermute | solution.py:139
  61.5 16.2 %collective-permute-start.32 = (f32[128,512]{1,0:T(8,128)S(1)}, f32[128,512]{1,0:T(8,128)S(1)}, u32[]{:S(2)}, u32[]{:S(2)}) collective-permute-start(f32[128,512]{1,0:T(8,128)S(1)} %get-tuple-element.28.refs_8_.refs_0_), channel_id=1, source_target_pairs={{0,2},{2,0},{1,3},{3,1},{4,6},{6,4},{5,7},{7,5},{8,10},{10,8},{9,1... | collective-permute-start | bytes 786440 | tf_op jit(solution)/shard_map/ppermute | solution.py:139
  62.9 15.6 %collective-permute-start.31 = (f32[128,512]{1,0:T(8,128)S(1)}, f32[128,512]{1,0:T(8,128)S(1)}, u32[]{:S(2)}, u32[]{:S(2)}) collective-permute-start(f32[128,512]{1,0:T(8,128)S(1)} %get-tuple-element.27.refs_9_.refs_1_), channel_id=1, source_target_pairs={{0,1},{1,0},{2,3},{3,2},{4,5},{5,4},{6,7},{7,6},{8,9},{9,8},{10,11... | collective-permute-start | bytes 786440 | tf_op jit(solution)/shard_map/ppermute | solution.py:139
  74.8 12.7 %collective-permute-start.23 = (f32[64,512]{1,0:T(8,128)S(1)}, f32[64,512]{1,0:T(8,128)S(1)}, u32[]{:S(2)}, u32[]{:S(2)}) collective-permute-start(f32[64,512]{1,0:T(8,128)S(1)} %add.16.refs_0_), channel_id=1, source_target_pairs={{0,16},{8,24},{16,0},{24,8},{1,17},{9,25},{17,1},{25,9},{2,18},{10... | collective-permute-start | bytes 393224 | tf_op jit(solution)/shard_map/ppermute | solution.py:139
  77.8 10.8 %collective-permute-start.24 = (f32[64,512]{1,0:T(8,128)S(1)}, f32[64,512]{1,0:T(8,128)S(1)}, u32[]{:S(2)}, u32[]{:S(2)}) collective-permute-start(f32[64,512]{1,0:T(8,128)S(1)} %add.16.refs_0_), channel_id=1, source_target_pairs={{0,24},{8,16},{16,8},{24,0},{1,25},{9,17},{17,9},{25,1},{2,26},{10... | collective-permute-start | bytes 393224 | tf_op jit(solution)/shard_map/ppermute | solution.py:139
  78.5 12.5 %collective-permute-start.30 = (f32[128,512]{1,0:T(8,128)S(1)}, f32[128,512]{1,0:T(8,128)S(1)}, u32[]{:S(2)}, u32[]{:S(2)}) collective-permute-start(f32[128,512]{1,0:T(8,128)S(1)} %get-tuple-element.28.refs_8_.refs_0_), channel_id=1, source_target_pairs={{0,1},{1,0},{2,3},{3,2},{4,5},{5,4},{6,7},{7,6},{8,9},{9,8},{10,11... | collective-permute-start | bytes 786440 | tf_op jit(solution)/shard_map/ppermute | solution.py:139
  79.1 11.9 %collective-permute-start.42 = (f32[256,128]{1,0:T(8,128)S(1)}, f32[256,128]{1,0:T(8,128)S(1)}, u32[]{:S(2)}, u32[]{:S(2)}) collective-permute-start(f32[256,128]{1,0:T(8,128)S(1)} %dynamic-slice_bitcast_fusion), channel_id=1, source_target_pairs={{0,3},{1,2},{2,1},{3,0},{4,7},{5,6},{6,5},{7,4},{8,11},{9,10},{10,... | collective-permute-start | bytes 393224 | tf_op jit(solution)/shard_map/ppermute | solution.py:151
  81.0 10.8 %collective-permute-start.33 = (f32[128,512]{1,0:T(8,128)S(1)}, f32[128,512]{1,0:T(8,128)S(1)}, u32[]{:S(2)}, u32[]{:S(2)}) collective-permute-start(f32[128,512]{1,0:T(8,128)S(1)} %get-tuple-element.27.refs_9_.refs_1_), channel_id=1, source_target_pairs={{0,2},{2,0},{1,3},{3,1},{4,6},{6,4},{5,7},{7,5},{8,10},{10,8},{9,1... | collective-permute-start | bytes 786440 | tf_op jit(solution)/shard_map/ppermute | solution.py:139
  91.0 12.7 %collective-permute-start.43 = (f32[256,384]{1,0:T(8,128)S(1)}, f32[256,384]{1,0:T(8,128)S(1)}, u32[]{:S(2)}, u32[]{:S(2)}) collective-permute-start(f32[256,384]{1,0:T(8,128)S(1)} %pad_maximum_fusion.2), channel_id=1, source_target_pairs={{0,4},{4,0},{1,5},{5,1},{2,6},{6,2},{3,7},{7,3},{8,12},{12,8},{9,1... | collective-permute-start | bytes 1179656 | tf_op jit(solution)/shard_map/ppermute | solution.py:139
  100.4 12.8 %collective-permute-start.38 = (f32[64,512]{1,0:T(8,128)S(1)}, f32[64,512]{1,0:T(8,128)S(1)}, u32[]{:S(2)}, u32[]{:S(2)}) collective-permute-start(f32[64,512]{1,0:T(8,128)S(1)} %add.17.refs_0_), channel_id=1, source_target_pairs={{0,16},{8,24},{16,0},{24,8},{1,17},{9,25},{17,1},{25,9},{2,18},{10... | collective-permute-start | bytes 393224 | tf_op jit(solution)/shard_map/ppermute | solution.py:139
  102.3 10.9 %collective-permute-start.39 = (f32[64,512]{1,0:T(8,128)S(1)}, f32[64,512]{1,0:T(8,128)S(1)}, u32[]{:S(2)}, u32[]{:S(2)}) collective-permute-start(f32[64,512]{1,0:T(8,128)S(1)} %add.17.refs_0_), channel_id=1, source_target_pairs={{0,24},{8,16},{16,8},{24,0},{1,25},{9,17},{17,9},{25,1},{2,26},{10... | collective-permute-start | bytes 393224 | tf_op jit(solution)/shard_map/ppermute | solution.py:139
  (25 other events, 189.5 us)

commit v5 on v4

--- a/solution.py
+++ b/solution.py
@@ -77,11 +77,11 @@
         out[at, :] = current[at, :] - dot3(ref[...], coefficients, NT)
 
 
-def middle_kernel(x, mine, other, *refs):
-    v, core = place()
-    old, new, (out, keep, send) = refs[:PIECES], refs[PIECES : 2 * PIECES], refs[2 * PIECES :]
+def turn_kernel(x, mine, other, *refs):
+    v, core = place()
+    old, new, (out, total) = refs[:PIECES], refs[PIECES:-2], refs[-2:]
     update(x, out, old, both_halves(mine, other, core), v)
-    give_out(project(out, new, v), core, keep, send)
+    total[...] = project(out, new, v)
 
 
 def last_kernel(x, mine, other, *refs):
@@ -94,20 +94,17 @@
     total = refs[0][...]
     for i in range(1, n):
         total = total + refs[i][...]
-    factor, exchanged, *mine = refs[n:-1]
-    out = refs[-1]
+    factor, first, across, exchanged, out = refs[n:]
     share = factor.shape[-1]
-    half = factor.shape[-2] // 2
-    mine = [factor[panel, pl.ds(pl.multiple_of(core * half, 8), half), :]] + [a[...] for a in mine]
-    other = [factor[panel, pl.ds(pl.multiple_of((1 - core) * half, 8), half), :]]
-    other += [exchanged[:, i * share : (i + 1) * share] for i in range(3)]
-    sums = [None, None]
-    parts = split_columns(total, v, share)
-    for block in range(4):
-        for i, t in enumerate((mine[block], other[block])):
-            part = dot3(parts[block], t, NT)
-            sums[i] = part if sums[i] is None else sums[i] + part
-    out[...] = jnp.where(core == 0, jnp.concatenate(sums, axis=1), jnp.concatenate(sums[::-1], axis=1))
+    on_x = core == 0
+    own, along_x, along_y, far = split_columns(total, v, share)
+    second = jnp.concatenate([exchanged[:, :share], exchanged[:, share : 2 * share]], axis=0)
+    a, b = across[...], exchanged[:, 2 * share :]
+    across = jnp.concatenate([jnp.where(on_x, a, b), jnp.where(on_x, b, a)], axis=0)
+    sums = dot3(own, factor[panel], NT)
+    sums += dot3(jnp.where(on_x, along_x, along_y), first[...], NT)
+    sums += dot3(jnp.where(on_x, along_y, along_x), second, NT)
+    out[...] = sums + dot3(far, across, NT)
 
 
 def split_columns(total, v, share):
@@ -147,15 +144,21 @@
     return a, b, xa, xb, ya, yb, swap(ya, "x"), swap(xb, "y")
 
 
-def cross(a):
-    return lax.ppermute(a, ("y", "x"), [(i, i ^ 3) for i in range(4)])
+def gather_factor(own):
+    half, core = own.shape[0] // 2, lax.axis_index("core")
+    axes = ("core", "y", "x")
+    n = lax.axis_size(axes)
+    first = lax.ppermute(own, axes, [(i, i ^ (2 if i >= n // 2 else 1)) for i in range(n)])
+    mine = lax.dynamic_slice(own, (core * half, 0), (half, own.shape[1]))
+    across = lax.ppermute(mine, axes, [(i, i ^ 3) for i in range(n)])
+    joined = jnp.concatenate([first[:half], first[half:], across], axis=1)
+    return first, across, swap(joined, "core")
 
 
 def fast(vectors, reflectors, triangles):
     rows, share = vectors.shape
     panels, _, width = reflectors.shape
-    core, sums = lax.axis_index("core"), lax.axis_size("z")
-    half = width // 2
+    sums = lax.axis_size("z")
     part = jax.ShapeDtypeStruct((share // 2, width), F32)
     whole = jax.ShapeDtypeStruct((rows, share), F32)
     work = 2 * rows * width * share
@@ -164,10 +167,7 @@
     sections, factors = {}, {}
     for k in reversed(range(panels)):
         sections[k] = gather(reflectors[k])
-        own = lax.dynamic_slice(triangles[k], (core * half, 0), (half, share))
-        received = swap(own, "x"), swap(own, "y"), cross(own)
-        joined = jnp.concatenate(received, axis=1)
-        factors[k] = (swap(joined, "core"), *received)
+        factors[k] = gather_factor(triangles[k])
         if k == top:
             pieces = list(sections[k])
             pieces[4], reflectors, triangles = lax.optimization_barrier((pieces[4], reflectors, triangles))
@@ -181,16 +181,17 @@
         )[0]
         return mine, swap(mine, "core")
 
-    early, late = sections[top][:-2], sections[top][-2:]
-    total = call(early_kernel, [jax.ShapeDtypeStruct((share, width), F32)], [vectors, *early], work * 3 // 4)[0]
-    keep, send = call(late_kernel, [part, part], [vectors, total, *late], work // 4)
+    total = jax.ShapeDtypeStruct((share, width), F32)
+    ahead = {k: a[:-2] for k, a in sections.items()}
+    sum_so_far = call(early_kernel, [total], [vectors, *ahead[top]], work * 3 // 4)[0]
     current = vectors
-    for k in reversed(range(1, panels)):
+    for k in reversed(range(panels)):
+        keep, send = call(late_kernel, [part, part], [current, sum_so_far, *sections[k][-2:]], work // 4)
         c = reduced(keep, send, k)
-        current, keep, send = call(
-            middle_kernel, [whole, part, part], [current, *c, *sections[k], *sections[k - 1]], 2 * work
-        )
-    c = reduced(keep, send, 0)
+        if k > 0:
+            current, sum_so_far = call(
+                turn_kernel, [whole, total], [current, *c, *sections[k], *ahead[k - 1]], work * 7 // 4
+            )
     return call(last_kernel, [whole], [current, *c, *sections[0]], work)[0]
 
 

time: 117 us -> 108 us (0.923)
  waiting for transfers between devices: 58.9 us -> 49.7 us
  starting transfers between devices: 47.3 us -> 46 us
    ppermute x42 -> x36, waiting for transfers between devices: 57.9 us -> 35.4 us  [swap(): return lax.ppermute(a, axis, [(i, i ^ by) for i in range(n)])]
    ppermute x3 -> x6, waiting for transfers between devices: 0.99 us -> 14.3 us  [the longest x3 10.2 us: gather_factor(): across = lax.ppermute(mine, axes, [(i, i ^ 3) for i in range(n)])]
    ppermute x42 -> x36, starting transfers between devices: 41.3 us -> 38.1 us  [swap(): return lax.ppermute(a, axis, [(i, i ^ by) for i in range(n)])]
    ppermute x3 -> x6, starting transfers between devices: 5.99 us -> 7.93 us  [the longest x3 5.09 us: gather_factor(): across = lax.ppermute(mine, axes, [(i, i ^ 3) for i in range(n)])]
    pallas_call x8 -> x10, Pallas kernels: 9.08 us -> 9.48 us  [call(): pl.pallas_call(kernel, out_shape=outs, in_specs=vmem(len(args)), out_spec...]
  transfers between devices with their start and end apart: 45 -> 42, of which waited for: 21 -> 20; matrix products, arithmetic and copies ran while one was open for 0% -> 1% of each run, Pallas kernels for 6% -> 7%
where the time goes in v5:
time: 108 us
  waiting for transfers between devices  49.7 us (46%)
  starting transfers between devices  46 us (43%)
  Pallas kernels  9.48 us (9%)
  local copies, waits for them, and re-layouts  2.34 us (2%)
    ppermute x36, starting transfers between devices, swap(): return lax.ppermute(a, axis, [(i, i ^ by) for i in range(n)])  38.1 us
    ppermute x36, waiting for transfers between devices, swap(): return lax.ppermute(a, axis, [(i, i ^ by) for i in range(n)])  35.4 us
    ppermute x3, waiting for transfers between devices, gather_factor(): across = lax.ppermute(mine, axes, [(i, i ^ 3) for i in range(n)])  10.2 us
    pallas_call x10, Pallas kernels, call(): pl.pallas_call(kernel, out_shape=outs, in_specs=vmem(len(args)), out_spec...  9.48 us
    ppermute x3, starting transfers between devices, gather_factor(): across = lax.ppermute(mine, axes, [(i, i ^ 3) for i in range(n)])  5.09 us
    ppermute x3, waiting for transfers between devices, gather_factor(): lax.ppermute(own, axes, [(i, i ^ (2 if i >= n // 2 else 1)) for i in rang...  4.13 us
    ppermute x3, starting transfers between devices, gather_factor(): lax.ppermute(own, axes, [(i, i ^ (2 if i >= n // 2 else 1)) for i in rang...  2.85 us
  transfers between devices with their start and end apart: 42, of which 20 were waited for; matrix products, arithmetic and copies ran while one was open for 1% of the time, Pallas kernels for 7%

profile of v5, /device:TPU:0, one launch (start us, length us, event | category | flops | bytes accessed | tf_op | source)
XLA Modules:
  0.0 108.0 jit_solution(1578360508839475336)
XLA Ops:
  1.1 3.1 %collective-permute-start.2 = (f32[128,512]{1,0:T(8,128)S(1)}, f32[128,512]{1,0:T(8,128)S(1)}, u32[]{:S(2)}, u32[]{:S(2)}) collective-permute-start(f32[128,512]{1,0:T(8,128)S(1)} %get-tuple-element.36.refs_0_), channel_id=1, source_target_pairs={{0,2},{2,0},{1,3},{3,1},{4,6},{6,4},{5,7},{7,5},{8,10},{10,8},{9,1... | collective-permute-start | bytes 786440 | tf_op jit(solution)/shard_map/ppermute | solution.py:136
  9.3 2.1 %collective-permute-done.2.refs_4_ = f32[128,512]{1,0:T(8,128)S(1)} collective-permute-done((f32[128,512]{1,0:T(8,128)S(1)}, f32[128,512]{1,0:T(8,128)S(1)}, u32[]{:S(2)}, u32[]{:S(2)}) %collective-permute-start.2) | collective-permute-done | bytes 262176 | tf_op jit(solution)/shard_map/ppermute | solution.py:136
  11.3 2.9 %collective-permute-start.11 = (f32[256,128]{1,0:T(8,128)S(1)}, f32[256,128]{1,0:T(8,128)S(1)}, u32[]{:S(2)}, u32[]{:S(2)}) collective-permute-start(f32[256,128]{1,0:T(8,128)S(1)} %dynamic-slice_bitcast_fusion.2), channel_id=1, source_target_pairs={{0,3},{1,2},{2,1},{3,0},{4,7},{5,6},{6,5},{7,4},{8,11},{9,10},{10,... | collective-permute-start | bytes 393224 | tf_op jit(solution)/shard_map/ppermute | solution.py:153
  14.9 4.1 %collective-permute-done.10.refs_5_ = f32[512,128]{1,0:T(8,128)S(1)} collective-permute-done((f32[512,128]{1,0:T(8,128)S(1)}, f32[512,128]{1,0:T(8,128)S(1)}, u32[]{:S(2)}, u32[]{:S(2)}) %collective-permute-start.10) | collective-permute-done | bytes 262176 | tf_op jit(solution)/shard_map/ppermute | solution.py:151
  19.1 6.8 %collective-permute-done.11.refs_6_ = f32[256,128]{1,0:T(8,128)S(1)} collective-permute-done((f32[256,128]{1,0:T(8,128)S(1)}, f32[256,128]{1,0:T(8,128)S(1)}, u32[]{:S(2)}, u32[]{:S(2)}) %collective-permute-start.11) | collective-permute-done | bytes 131104 | tf_op jit(solution)/shard_map/ppermute | solution.py:153
  29.5 1.6 %collective-permute-start.15 = (f32[128,512]{1,0:T(8,128)S(1)}, f32[128,512]{1,0:T(8,128)S(1)}, u32[]{:S(2)}, u32[]{:S(2)}) collective-permute-start(f32[128,512]{1,0:T(8,128)S(1)} %get-tuple-element.33.refs_9_.refs_1_), channel_id=1, source_target_pairs={{0,1},{1,0},{2,3},{3,2},{4,5},{5,4},{6,7},{7,6},{8,9},{9,8},{10,11... | collective-permute-start | bytes 786440 | tf_op jit(solution)/shard_map/ppermute | solution.py:136
  31.6 1.7 %collective-permute-start.7 = (f32[64,512]{1,0:T(8,128)S(1)}, f32[64,512]{1,0:T(8,128)S(1)}, u32[]{:S(2)}, u32[]{:S(2)}) collective-permute-start(f32[64,512]{1,0:T(8,128)S(1)} %add.14.refs_0_), channel_id=1, source_target_pairs={{0,8},{8,0},{16,24},{24,16},{1,9},{9,1},{17,25},{25,17},{2,10},{10... | collective-permute-start | bytes 393224 | tf_op jit(solution)/shard_map/ppermute | solution.py:136
  33.2 2.6 %collective-permute-start.8 = (f32[64,512]{1,0:T(8,128)S(1)}, f32[64,512]{1,0:T(8,128)S(1)}, u32[]{:S(2)}, u32[]{:S(2)}) collective-permute-start(f32[64,512]{1,0:T(8,128)S(1)} %add.14.refs_0_), channel_id=1, source_target_pairs={{0,16},{8,24},{16,0},{24,8},{1,17},{9,25},{17,1},{25,9},{2,18},{10... | collective-permute-start | bytes 393224 | tf_op jit(solution)/shard_map/ppermute | solution.py:136
  36.6 2.4 %collective-permute-done.7.refs_1_ = f32[64,512]{1,0:T(8,128)S(1)} collective-permute-done((f32[64,512]{1,0:T(8,128)S(1)}, f32[64,512]{1,0:T(8,128)S(1)}, u32[]{:S(2)}, u32[]{:S(2)}) %collective-permute-start.7) | collective-permute-done | bytes 131104 | tf_op jit(solution)/shard_map/ppermute | solution.py:136
  39.0 3.1 %collective-permute-start.9 = (f32[64,512]{1,0:T(8,128)S(1)}, f32[64,512]{1,0:T(8,128)S(1)}, u32[]{:S(2)}, u32[]{:S(2)}) collective-permute-start(f32[64,512]{1,0:T(8,128)S(1)} %add.14.refs_0_), channel_id=1, source_target_pairs={{0,24},{8,16},{16,8},{24,0},{1,25},{9,17},{17,9},{25,1},{2,26},{10... | collective-permute-start | bytes 393224 | tf_op jit(solution)/shard_map/ppermute | solution.py:136
  42.1 1.7 %collective-permute-done.8.refs_2_ = f32[64,512]{1,0:T(8,128)S(1)} collective-permute-done((f32[64,512]{1,0:T(8,128)S(1)}, f32[64,512]{1,0:T(8,128)S(1)}, u32[]{:S(2)}, u32[]{:S(2)}) %collective-permute-start.8) | collective-permute-done | bytes 131104 | tf_op jit(solution)/shard_map/ppermute | solution.py:136
  47.7 3.4 %collective-permute-done.25.refs_6_ = f32[256,128]{1,0:T(8,128)S(1)} collective-permute-done((f32[256,128]{1,0:T(8,128)S(1)}, f32[256,128]{1,0:T(8,128)S(1)}, u32[]{:S(2)}, u32[]{:S(2)}) %collective-permute-start.25) | collective-permute-done | bytes 131104 | tf_op jit(solution)/shard_map/ppermute | solution.py:153
  53.3 2.4 %collective-permute-done.14.refs_10_.refs_2_ = f32[128,512]{1,0:T(8,128)S(1)} collective-permute-done((f32[128,512]{1,0:T(8,128)S(1)}, f32[128,512]{1,0:T(8,128)S(1)}, u32[]{:S(2)}, u32[]{:S(2)}) %collective-permute-start.14) | collective-permute-done | bytes 262176 | tf_op jit(solution)/shard_map/ppermute | solution.py:136
  55.7 2.5 %collective-permute-done.17.refs_13_.refs_5_ = f32[128,512]{1,0:T(8,128)S(1)} collective-permute-done((f32[128,512]{1,0:T(8,128)S(1)}, f32[128,512]{1,0:T(8,128)S(1)}, u32[]{:S(2)}, u32[]{:S(2)}) %collective-permute-start.17) | collective-permute-done | bytes 262176 | tf_op jit(solution)/shard_map/ppermute | solution.py:136
  60.3 1.8 %shard_map.40 = (f32[1024,128]{1,0:T(8,128)S(1)}, f32[128,512]{1,0:T(8,128)S(1)}) custom-call(f32[1024,128]{1,0:T(8,128)S(1)} %copy-done.1, f32[64,512]{1,0:T(8,128)S(1)} %shard_map.39.mine, f32[64,512]{1,0:T(8,128)S(1)} %collective-permute-done.13.other, f32[128,512]{1,0:T(8,128)S(1)} %get-tuple-element.36.refs_0_, ...), custom_call_target="tpu_custom_call" | custom-call | flops 234881024 | bytes 5242880 | tf_op jit(solution)/shard_map/pallas_call | solution.py:124
  66.5 2.3 %collective-permute-start.22 = (f32[64,512]{1,0:T(8,128)S(1)}, f32[64,512]{1,0:T(8,128)S(1)}, u32[]{:S(2)}, u32[]{:S(2)}) collective-permute-start(f32[64,512]{1,0:T(8,128)S(1)} %add.16.refs_0_), channel_id=1, source_target_pairs={{0,16},{8,24},{16,0},{24,8},{1,17},{9,25},{17,1},{25,9},{2,18},{10... | collective-permute-start | bytes 393224 | tf_op jit(solution)/shard_map/ppermute | solution.py:136
  68.9 1.9 %collective-permute-start.23 = (f32[64,512]{1,0:T(8,128)S(1)}, f32[64,512]{1,0:T(8,128)S(1)}, u32[]{:S(2)}, u32[]{:S(2)}) collective-permute-start(f32[64,512]{1,0:T(8,128)S(1)} %add.16.refs_0_), channel_id=1, source_target_pairs={{0,24},{8,16},{16,8},{24,0},{1,25},{9,17},{17,9},{25,1},{2,26},{10... | collective-permute-start | bytes 393224 | tf_op jit(solution)/shard_map/ppermute | solution.py:136
  71.7 2.0 %collective-permute-start.31 = (f32[128,512]{1,0:T(8,128)S(1)}, f32[128,512]{1,0:T(8,128)S(1)}, u32[]{:S(2)}, u32[]{:S(2)}) collective-permute-start(f32[128,512]{1,0:T(8,128)S(1)} %get-tuple-element.31.refs_9_.refs_1_), channel_id=1, source_target_pairs={{0,2},{2,0},{1,3},{3,1},{4,6},{6,4},{5,7},{7,5},{8,10},{10,8},{9,1... | collective-permute-start | bytes 786440 | tf_op jit(solution)/shard_map/ppermute | solution.py:136
  74.4 5.0 %collective-permute-done.22.refs_2_ = f32[64,512]{1,0:T(8,128)S(1)} collective-permute-done((f32[64,512]{1,0:T(8,128)S(1)}, f32[64,512]{1,0:T(8,128)S(1)}, u32[]{:S(2)}, u32[]{:S(2)}) %collective-permute-start.22) | collective-permute-done | bytes 131104 | tf_op jit(solution)/shard_map/ppermute | solution.py:136
  84.1 1.8 %shard_map.43 = (f32[1024,128]{1,0:T(8,128)S(1)}, f32[128,512]{1,0:T(8,128)S(1)}) custom-call(f32[1024,128]{1,0:T(8,128)S(1)} %get-tuple-element.23.x, f32[64,512]{1,0:T(8,128)S(1)} %shard_map.42.mine, f32[64,512]{1,0:T(8,128)S(1)} %collective-permute-done.27.other, f32[128,512]{1,0:T(8,128)S(1)} %get-tuple-element.34.refs_8_.refs_0_, ...), custom_call_target="tpu_custom_call" | custom-call | flops 234881024 | bytes 5242880 | tf_op jit(solution)/shard_map/pallas_call | solution.py:124
  89.2 2.1 %collective-permute-start.35 = (f32[64,512]{1,0:T(8,128)S(1)}, f32[64,512]{1,0:T(8,128)S(1)}, u32[]{:S(2)}, u32[]{:S(2)}) collective-permute-start(f32[64,512]{1,0:T(8,128)S(1)} %add.17.refs_0_), channel_id=1, source_target_pairs={{0,8},{8,0},{16,24},{24,16},{1,9},{9,1},{17,25},{25,17},{2,10},{10... | collective-permute-start | bytes 393224 | tf_op jit(solution)/shard_map/ppermute | solution.py:136
  93.7 3.1 %collective-permute-done.35.refs_1_ = f32[64,512]{1,0:T(8,128)S(1)} collective-permute-done((f32[64,512]{1,0:T(8,128)S(1)}, f32[64,512]{1,0:T(8,128)S(1)}, u32[]{:S(2)}, u32[]{:S(2)}) %collective-permute-start.35) | collective-permute-done | bytes 131104 | tf_op jit(solution)/shard_map/ppermute | solution.py:136
  96.8 7.3 %collective-permute-done.36.refs_2_ = f32[64,512]{1,0:T(8,128)S(1)} collective-permute-done((f32[64,512]{1,0:T(8,128)S(1)}, f32[64,512]{1,0:T(8,128)S(1)}, u32[]{:S(2)}, u32[]{:S(2)}) %collective-permute-start.36) | collective-permute-done | bytes 131104 | tf_op jit(solution)/shard_map/ppermute | solution.py:136
  106.2 1.8 %shard_map.46 = f32[1024,128]{1,0:T(8,128)} custom-call(f32[1024,128]{1,0:T(8,128)S(1)} %get-tuple-element.27.x, f32[64,512]{1,0:T(8,128)S(1)} %shard_map.45.mine, f32[64,512]{1,0:T(8,128)S(1)} %collective-permute-done.41.other, f32[128,512]{1,0:T(8,128)S(1)} %get-tuple-element.32.refs_8_.refs_0_, f32[128,512]{1,0:T(8,128)S(1)} %get-tuple-element.31.refs_9_.refs_1_, ...), custom_call_target="tpu_custom_call" | custom-call | flops 134217728 | bytes 3407872 | tf_op jit(solution)/shard_map/pallas_call | solution.py:124
  (92 shorter events, 38.1 us)
Async XLA Ops:
  1.1 10.2 %collective-permute-start.2 = (f32[128,512]{1,0:T(8,128)S(1)}, f32[128,512]{1,0:T(8,128)S(1)}, u32[]{:S(2)}, u32[]{:S(2)}) collective-permute-start(f32[128,512]{1,0:T(8,128)S(1)} %get-tuple-element.36.refs_0_), channel_id=1, source_target_pairs={{0,2},{2,0},{1,3},{3,1},{4,6},{6,4},{5,7},{7,5},{8,10},{10,8},{9,1... | collective-permute-start | bytes 786440 | tf_op jit(solution)/shard_map/ppermute | solution.py:136
  4.2 10.1 %collective-permute-start.1 = (f32[128,512]{1,0:T(8,128)S(1)}, f32[128,512]{1,0:T(8,128)S(1)}, u32[]{:S(2)}, u32[]{:S(2)}) collective-permute-start(f32[128,512]{1,0:T(8,128)S(1)} %get-tuple-element.35.refs_1_), channel_id=1, source_target_pairs={{0,1},{1,0},{2,3},{3,2},{4,5},{5,4},{6,7},{7,6},{8,9},{9,8},{10,11... | collective-permute-start | bytes 786440 | tf_op jit(solution)/shard_map/ppermute | solution.py:136
  6.7 12.3 %collective-permute-start.10 = (f32[512,128]{1,0:T(8,128)S(1)}, f32[512,128]{1,0:T(8,128)S(1)}, u32[]{:S(2)}, u32[]{:S(2)}) collective-permute-start(f32[512,128]{1,0:T(8,128)S(1)} %get-tuple-element.42), channel_id=1, source_target_pairs={{0,1},{1,0},{2,3},{3,2},{4,6},{5,7},{6,4},{7,5},{8,9},{9,8},{10,11... | collective-permute-start | bytes 786440 | tf_op jit(solution)/shard_map/ppermute | solution.py:151
  7.3 18.8 %collective-permute-start = (f32[128,512]{1,0:T(8,128)S(1)}, f32[128,512]{1,0:T(8,128)S(1)}, u32[]{:S(2)}, u32[]{:S(2)}) collective-permute-start(f32[128,512]{1,0:T(8,128)S(1)} %get-tuple-element.36.refs_0_), channel_id=1, source_target_pairs={{0,1},{1,0},{2,3},{3,2},{4,5},{5,4},{6,7},{7,6},{8,9},{9,8},{10,11... | collective-permute-start | bytes 786440 | tf_op jit(solution)/shard_map/ppermute | solution.py:136
  8.8 17.3 %collective-permute-start.3 = (f32[128,512]{1,0:T(8,128)S(1)}, f32[128,512]{1,0:T(8,128)S(1)}, u32[]{:S(2)}, u32[]{:S(2)}) collective-permute-start(f32[128,512]{1,0:T(8,128)S(1)} %get-tuple-element.35.refs_1_), channel_id=1, source_target_pairs={{0,2},{2,0},{1,3},{3,1},{4,6},{6,4},{5,7},{7,5},{8,10},{10,8},{9,1... | collective-permute-start | bytes 786440 | tf_op jit(solution)/shard_map/ppermute | solution.py:136
  11.3 14.5 %collective-permute-start.11 = (f32[256,128]{1,0:T(8,128)S(1)}, f32[256,128]{1,0:T(8,128)S(1)}, u32[]{:S(2)}, u32[]{:S(2)}) collective-permute-start(f32[256,128]{1,0:T(8,128)S(1)} %dynamic-slice_bitcast_fusion.2), channel_id=1, source_target_pairs={{0,3},{1,2},{2,1},{3,0},{4,7},{5,6},{6,5},{7,4},{8,11},{9,10},{10,... | collective-permute-start | bytes 393224 | tf_op jit(solution)/shard_map/ppermute | solution.py:153
  14.3 14.6 %collective-permute-start.4 = (f32[128,512]{1,0:T(8,128)S(1)}, f32[128,512]{1,0:T(8,128)S(1)}, u32[]{:S(2)}, u32[]{:S(2)}) collective-permute-start(f32[128,512]{1,0:T(8,128)S(1)} %collective-permute-done.2.refs_4_), channel_id=1, source_target_pairs={{0,1},{1,0},{2,3},{3,2},{4,5},{5,4},{6,7},{7,6},{8,9},{9,8},{10,11... | collective-permute-start | bytes 786440 | tf_op jit(solution)/shard_map/ppermute | solution.py:136
  25.9 9.9 %collective-permute-start.12 = (f32[256,384]{1,0:T(8,128)S(1)}, f32[256,384]{1,0:T(8,128)S(1)}, u32[]{:S(2)}, u32[]{:S(2)}) collective-permute-start(f32[256,384]{1,0:T(8,128)S(1)} %pad_maximum_fusion), channel_id=1, source_target_pairs={{0,4},{4,0},{1,5},{5,1},{2,6},{6,2},{3,7},{7,3},{8,12},{12,8},{9,1... | collective-permute-start | bytes 1179656 | tf_op jit(solution)/shard_map/ppermute | solution.py:136
  29.5 23.7 %collective-permute-start.15 = (f32[128,512]{1,0:T(8,128)S(1)}, f32[128,512]{1,0:T(8,128)S(1)}, u32[]{:S(2)}, u32[]{:S(2)}) collective-permute-start(f32[128,512]{1,0:T(8,128)S(1)} %get-tuple-element.33.refs_9_.refs_1_), channel_id=1, source_target_pairs={{0,1},{1,0},{2,3},{3,2},{4,5},{5,4},{6,7},{7,6},{8,9},{9,8},{10,11... | collective-permute-start | bytes 786440 | tf_op jit(solution)/shard_map/ppermute | solution.py:136
  31.0 20.9 %collective-permute-start.16 = (f32[128,512]{1,0:T(8,128)S(1)}, f32[128,512]{1,0:T(8,128)S(1)}, u32[]{:S(2)}, u32[]{:S(2)}) collective-permute-start(f32[128,512]{1,0:T(8,128)S(1)} %get-tuple-element.34.refs_8_.refs_0_), channel_id=1, source_target_pairs={{0,2},{2,0},{1,3},{3,1},{4,6},{6,4},{5,7},{7,5},{8,10},{10,8},{9,1... | collective-permute-start | bytes 786440 | tf_op jit(solution)/shard_map/ppermute | solution.py:136
  33.2 10.6 %collective-permute-start.8 = (f32[64,512]{1,0:T(8,128)S(1)}, f32[64,512]{1,0:T(8,128)S(1)}, u32[]{:S(2)}, u32[]{:S(2)}) collective-permute-start(f32[64,512]{1,0:T(8,128)S(1)} %add.14.refs_0_), channel_id=1, source_target_pairs={{0,16},{8,24},{16,0},{24,8},{1,17},{9,25},{17,1},{25,9},{2,18},{10... | collective-permute-start | bytes 393224 | tf_op jit(solution)/shard_map/ppermute | solution.py:136
  35.9 17.3 %collective-permute-start.24 = (f32[512,128]{1,0:T(8,128)S(1)}, f32[512,128]{1,0:T(8,128)S(1)}, u32[]{:S(2)}, u32[]{:S(2)}) collective-permute-start(f32[512,128]{1,0:T(8,128)S(1)} %get-tuple-element.38), channel_id=1, source_target_pairs={{0,1},{1,0},{2,3},{3,2},{4,6},{5,7},{6,4},{7,5},{8,9},{9,8},{10,11... | collective-permute-start | bytes 786440 | tf_op jit(solution)/shard_map/ppermute | solution.py:151
  45.9 9.8 %collective-permute-start.14 = (f32[128,512]{1,0:T(8,128)S(1)}, f32[128,512]{1,0:T(8,128)S(1)}, u32[]{:S(2)}, u32[]{:S(2)}) collective-permute-start(f32[128,512]{1,0:T(8,128)S(1)} %get-tuple-element.34.refs_8_.refs_0_), channel_id=1, source_target_pairs={{0,1},{1,0},{2,3},{3,2},{4,5},{5,4},{6,7},{7,6},{8,9},{9,8},{10,11... | collective-permute-start | bytes 786440 | tf_op jit(solution)/shard_map/ppermute | solution.py:136
  51.9 10.2 %collective-permute-start.18 = (f32[128,512]{1,0:T(8,128)S(1)}, f32[128,512]{1,0:T(8,128)S(1)}, u32[]{:S(2)}, u32[]{:S(2)}) collective-permute-start(f32[128,512]{1,0:T(8,128)S(1)} %collective-permute-done.16.refs_12_.refs_4_), channel_id=1, source_target_pairs={{0,1},{1,0},{2,3},{3,2},{4,5},{5,4},{6,7},{7,6},{8,9},{9,8},{10,11... | collective-permute-start | bytes 786440 | tf_op jit(solution)/shard_map/ppermute | solution.py:136
  53.1 10.5 %collective-permute-start.19 = (f32[128,512]{1,0:T(8,128)S(1)}, f32[128,512]{1,0:T(8,128)S(1)}, u32[]{:S(2)}, u32[]{:S(2)}) collective-permute-start(f32[128,512]{1,0:T(8,128)S(1)} %collective-permute-done.15.refs_11_.refs_3_), channel_id=1, source_target_pairs={{0,2},{2,0},{1,3},{3,1},{4,6},{6,4},{5,7},{7,5},{8,10},{10,8},{9,1... | collective-permute-start | bytes 786440 | tf_op jit(solution)/shard_map/ppermute | solution.py:136
  55.7 16.0 %collective-permute-start.26 = (f32[256,384]{1,0:T(8,128)S(1)}, f32[256,384]{1,0:T(8,128)S(1)}, u32[]{:S(2)}, u32[]{:S(2)}) collective-permute-start(f32[256,384]{1,0:T(8,128)S(1)} %pad_maximum_fusion.1), channel_id=1, source_target_pairs={{0,4},{4,0},{1,5},{5,1},{2,6},{6,2},{3,7},{7,3},{8,12},{12,8},{9,1... | collective-permute-start | bytes 1179656 | tf_op jit(solution)/shard_map/ppermute | solution.py:136
  58.8 10.1 %collective-permute-start.30 = (f32[128,512]{1,0:T(8,128)S(1)}, f32[128,512]{1,0:T(8,128)S(1)}, u32[]{:S(2)}, u32[]{:S(2)}) collective-permute-start(f32[128,512]{1,0:T(8,128)S(1)} %get-tuple-element.32.refs_8_.refs_0_), channel_id=1, source_target_pairs={{0,2},{2,0},{1,3},{3,1},{4,6},{6,4},{5,7},{7,5},{8,10},{10,8},{9,1... | collective-permute-start | bytes 786440 | tf_op jit(solution)/shard_map/ppermute | solution.py:136
  66.5 12.9 %collective-permute-start.22 = (f32[64,512]{1,0:T(8,128)S(1)}, f32[64,512]{1,0:T(8,128)S(1)}, u32[]{:S(2)}, u32[]{:S(2)}) collective-permute-start(f32[64,512]{1,0:T(8,128)S(1)} %add.16.refs_0_), channel_id=1, source_target_pairs={{0,16},{8,24},{16,0},{24,8},{1,17},{9,25},{17,1},{25,9},{2,18},{10... | collective-permute-start | bytes 393224 | tf_op jit(solution)/shard_map/ppermute | solution.py:136
  68.9 11.7 %collective-permute-start.23 = (f32[64,512]{1,0:T(8,128)S(1)}, f32[64,512]{1,0:T(8,128)S(1)}, u32[]{:S(2)}, u32[]{:S(2)}) collective-permute-start(f32[64,512]{1,0:T(8,128)S(1)} %add.16.refs_0_), channel_id=1, source_target_pairs={{0,24},{8,16},{16,8},{24,0},{1,25},{9,17},{17,9},{25,1},{2,26},{10... | collective-permute-start | bytes 393224 | tf_op jit(solution)/shard_map/ppermute | solution.py:136
  70.8 11.9 %collective-permute-start.28 = (f32[128,512]{1,0:T(8,128)S(1)}, f32[128,512]{1,0:T(8,128)S(1)}, u32[]{:S(2)}, u32[]{:S(2)}) collective-permute-start(f32[128,512]{1,0:T(8,128)S(1)} %get-tuple-element.32.refs_8_.refs_0_), channel_id=1, source_target_pairs={{0,1},{1,0},{2,3},{3,2},{4,5},{5,4},{6,7},{7,6},{8,9},{9,8},{10,11... | collective-permute-start | bytes 786440 | tf_op jit(solution)/shard_map/ppermute | solution.py:136
  71.7 11.6 %collective-permute-start.31 = (f32[128,512]{1,0:T(8,128)S(1)}, f32[128,512]{1,0:T(8,128)S(1)}, u32[]{:S(2)}, u32[]{:S(2)}) collective-permute-start(f32[128,512]{1,0:T(8,128)S(1)} %get-tuple-element.31.refs_9_.refs_1_), channel_id=1, source_target_pairs={{0,2},{2,0},{1,3},{3,1},{4,6},{6,4},{5,7},{7,5},{8,10},{10,8},{9,1... | collective-permute-start | bytes 786440 | tf_op jit(solution)/shard_map/ppermute | solution.py:136
  82.8 10.9 %collective-permute-start.40 = (f32[256,384]{1,0:T(8,128)S(1)}, f32[256,384]{1,0:T(8,128)S(1)}, u32[]{:S(2)}, u32[]{:S(2)}) collective-permute-start(f32[256,384]{1,0:T(8,128)S(1)} %pad_maximum_fusion.2), channel_id=1, source_target_pairs={{0,4},{4,0},{1,5},{5,1},{2,6},{6,2},{3,7},{7,3},{8,12},{12,8},{9,1... | collective-permute-start | bytes 1179656 | tf_op jit(solution)/shard_map/ppermute | solution.py:136
  91.2 12.9 %collective-permute-start.36 = (f32[64,512]{1,0:T(8,128)S(1)}, f32[64,512]{1,0:T(8,128)S(1)}, u32[]{:S(2)}, u32[]{:S(2)}) collective-permute-start(f32[64,512]{1,0:T(8,128)S(1)} %add.17.refs_0_), channel_id=1, source_target_pairs={{0,16},{8,24},{16,0},{24,8},{1,17},{9,25},{17,1},{25,9},{2,18},{10... | collective-permute-start | bytes 393224 | tf_op jit(solution)/shard_map/ppermute | solution.py:136
  92.6 11.5 %collective-permute-start.37 = (f32[64,512]{1,0:T(8,128)S(1)}, f32[64,512]{1,0:T(8,128)S(1)}, u32[]{:S(2)}, u32[]{:S(2)}) collective-permute-start(f32[64,512]{1,0:T(8,128)S(1)} %add.17.refs_0_), channel_id=1, source_target_pairs={{0,24},{8,16},{16,8},{24,0},{1,25},{9,17},{17,9},{25,1},{2,26},{10... | collective-permute-start | bytes 393224 | tf_op jit(solution)/shard_map/ppermute | solution.py:136
  (21 other events, 141.9 us)

commit v6 on v5

--- a/solution.py
+++ b/solution.py
@@ -87,6 +87,22 @@
 def last_kernel(x, mine, other, *refs):
     v, core = place()
     update(x, refs[PIECES], refs[:PIECES], both_halves(mine, other, core), v)
+
+
+def cut_kernel(x, out):
+    half = out.shape[0]
+    out[...] = jnp.where(lax.axis_index("core") == 0, x[:half], x[half:])
+
+
+def join_kernel(first, across, out):
+    half, share = across.shape
+    out[:, :share] = first[:half]
+    out[:, share : 2 * share] = first[half:]
+    out[:, 2 * share :] = across[...]
+
+
+def hold_kernel(x, out):
+    out[...] = x[...]
 
 
 def solve_kernel(panel, n, *refs):
@@ -126,7 +142,7 @@
         out_shape=outs,
         in_specs=vmem(len(args)),
         out_specs=vmem(len(outs)),
-        compiler_params=pltpu.CompilerParams(vmem_limit_bytes=12 * 2**20),
+        compiler_params=pltpu.CompilerParams(vmem_limit_bytes=8 * 2**20),
         cost_estimate=pl.CostEstimate(flops=flops, bytes_accessed=nbytes, transcendentals=0),
     )(*args)
 
@@ -145,13 +161,13 @@
 
 
 def gather_factor(own):
-    half, core = own.shape[0] // 2, lax.axis_index("core")
+    half, share = own.shape[0] // 2, own.shape[1]
     axes = ("core", "y", "x")
     n = lax.axis_size(axes)
     first = lax.ppermute(own, axes, [(i, i ^ (2 if i >= n // 2 else 1)) for i in range(n)])
-    mine = lax.dynamic_slice(own, (core * half, 0), (half, own.shape[1]))
-    across = lax.ppermute(mine, axes, [(i, i ^ 3) for i in range(n)])
-    joined = jnp.concatenate([first[:half], first[half:], across], axis=1)
+    mine = call(cut_kernel, [jax.ShapeDtypeStruct((half, share), F32)], [first], 0)[0]
+    across = lax.ppermute(mine, axes, [(i, i ^ (1 if i >= n // 2 else 2)) for i in range(n)])
+    joined = call(join_kernel, [jax.ShapeDtypeStruct((half, 3 * share), F32)], [first, across], 0)[0]
     return first, across, swap(joined, "core")
 
 
@@ -176,6 +192,7 @@
     def reduced(keep, send, k):
         s = keep + swap(send, "core")
         r = [swap(s, "z", by) for by in range(1, sums)]
+        s = call(hold_kernel, [part], [s], 0)[0]
         mine = call(
             functools.partial(solve_kernel, k, sums), [part], [s, *r, triangles, *factors[k]], width * width * share
         )[0]

time: 108 us -> 107 us (level)
  waiting for transfers between devices: 49.7 us -> 47.2 us
    ppermute x3, waiting for transfers between devices: 10.2 us -> 2.26 us  [gather_factor(): lax.ppermute(mine, axes, [(i, i ^ (1 if i >= n // 2 else 2)) for i in ran...]
    ppermute x36, waiting for transfers between devices: 35.4 us -> 41.9 us  [swap(): return lax.ppermute(a, axis, [(i, i ^ by) for i in range(n)])]
    ppermute x3, starting transfers between devices: 5.09 us -> 3.18 us  [gather_factor(): lax.ppermute(mine, axes, [(i, i ^ (1 if i >= n // 2 else 2)) for i in ran...]
    ppermute x36, starting transfers between devices: 38.1 us -> 39.8 us  [swap(): return lax.ppermute(a, axis, [(i, i ^ by) for i in range(n)])]
    ppermute x3, starting transfers between devices: 2.85 us -> 4.06 us  [gather_factor(): lax.ppermute(own, axes, [(i, i ^ (2 if i >= n // 2 else 1)) for i in rang...]
    slice x5 -> x0, local copies, waits for them, and re-layouts: 1.11 us -> none  [the longest x2 1.05 us: fast(): factors[k] = gather_factor(triangles[k])]
    pallas_call x10 -> x19, Pallas kernels: 9.48 us -> 9.68 us  [call(): pl.pallas_call(kernel, out_shape=outs, in_specs=vmem(len(args)), out_spec...]
  transfers between devices with their start and end apart: 42 -> 42, of which waited for: 20 -> 18; matrix products, arithmetic and copies ran while one was open for 1% -> 1% of each run, Pallas kernels for 7% -> 7%
where the time goes in v6:
time: 107 us
  waiting for transfers between devices  47.2 us (44%)
  starting transfers between devices  47 us (44%)
  Pallas kernels  9.68 us (9%)
  local copies, waits for them, and re-layouts  2.27 us (2%)
    ppermute x36, waiting for transfers between devices, swap(): return lax.ppermute(a, axis, [(i, i ^ by) for i in range(n)])  41.9 us
    ppermute x36, starting transfers between devices, swap(): return lax.ppermute(a, axis, [(i, i ^ by) for i in range(n)])  39.8 us
    pallas_call x19, Pallas kernels, call(): pl.pallas_call(kernel, out_shape=outs, in_specs=vmem(len(args)), out_spec...  9.68 us
    ppermute x3, starting transfers between devices, gather_factor(): lax.ppermute(own, axes, [(i, i ^ (2 if i >= n // 2 else 1)) for i in rang...  4.06 us
    ppermute x3, starting transfers between devices, gather_factor(): lax.ppermute(mine, axes, [(i, i ^ (1 if i >= n // 2 else 2)) for i in ran...  3.18 us
    ppermute x3, waiting for transfers between devices, gather_factor(): lax.ppermute(own, axes, [(i, i ^ (2 if i >= n // 2 else 1)) for i in rang...  3.06 us
    ppermute x3, waiting for transfers between devices, gather_factor(): lax.ppermute(mine, axes, [(i, i ^ (1 if i >= n // 2 else 2)) for i in ran...  2.26 us
  transfers between devices with their start and end apart: 42, of which 18 were waited for; matrix products, arithmetic and copies ran while one was open for 1% of the time, Pallas kernels for 7%

profile of v6, /device:TPU:0, one launch (start us, length us, event | category | flops | bytes accessed | tf_op | source)
XLA Modules:
  0.0 106.6 jit_solution(6383732301752326625)
XLA Ops:
  1.2 3.1 %collective-permute-start.2 = (f32[128,512]{1,0:T(8,128)S(1)}, f32[128,512]{1,0:T(8,128)S(1)}, u32[]{:S(2)}, u32[]{:S(2)}) collective-permute-start(f32[128,512]{1,0:T(8,128)S(1)} %get-tuple-element.36.refs_0_), channel_id=1, source_target_pairs={{0,2},{2,0},{1,3},{3,1},{4,6},{6,4},{5,7},{7,5},{8,10},{10,8},{9,1... | collective-permute-start | bytes 786440 | tf_op jit(solution)/shard_map/ppermute | solution.py:152
  9.3 2.1 %collective-permute-done.2.refs_4_ = f32[128,512]{1,0:T(8,128)S(1)} collective-permute-done((f32[128,512]{1,0:T(8,128)S(1)}, f32[128,512]{1,0:T(8,128)S(1)}, u32[]{:S(2)}, u32[]{:S(2)}) %collective-permute-start.2) | collective-permute-done | bytes 262176 | tf_op jit(solution)/shard_map/ppermute | solution.py:152
  11.4 3.1 %collective-permute-done.10.x.first.refs_5_ = f32[512,128]{1,0:T(8,128)S(1)} collective-permute-done((f32[512,128]{1,0:T(8,128)S(1)}, f32[512,128]{1,0:T(8,128)S(1)}, u32[]{:S(2)}, u32[]{:S(2)}) %collective-permute-start.10) | collective-permute-done | bytes 262176 | tf_op jit(solution)/shard_map/ppermute | solution.py:167
  14.6 5.1 %collective-permute-done.1.refs_3_ = f32[128,512]{1,0:T(8,128)S(1)} collective-permute-done((f32[128,512]{1,0:T(8,128)S(1)}, f32[128,512]{1,0:T(8,128)S(1)}, u32[]{:S(2)}, u32[]{:S(2)}) %collective-permute-start.1) | collective-permute-done | bytes 262176 | tf_op jit(solution)/shard_map/ppermute | solution.py:152
  19.9 2.4 %collective-permute-start.15 = (f32[128,512]{1,0:T(8,128)S(1)}, f32[128,512]{1,0:T(8,128)S(1)}, u32[]{:S(2)}, u32[]{:S(2)}) collective-permute-start(f32[128,512]{1,0:T(8,128)S(1)} %get-tuple-element.33.refs_9_.refs_1_), channel_id=1, source_target_pairs={{0,1},{1,0},{2,3},{3,2},{4,5},{5,4},{6,7},{7,6},{8,9},{9,8},{10,11... | collective-permute-start | bytes 786440 | tf_op jit(solution)/shard_map/ppermute | solution.py:152
  23.4 1.9 %collective-permute-done.refs_2_ = f32[128,512]{1,0:T(8,128)S(1)} collective-permute-done((f32[128,512]{1,0:T(8,128)S(1)}, f32[128,512]{1,0:T(8,128)S(1)}, u32[]{:S(2)}, u32[]{:S(2)}) %collective-permute-start) | collective-permute-done | bytes 262176 | tf_op jit(solution)/shard_map/ppermute | solution.py:152
  27.9 2.0 %collective-permute-start.24 = (f32[512,128]{1,0:T(8,128)S(1)}, f32[512,128]{1,0:T(8,128)S(1)}, u32[]{:S(2)}, u32[]{:S(2)}) collective-permute-start(f32[512,128]{1,0:T(8,128)S(1)} %get-tuple-element.38), channel_id=1, source_target_pairs={{0,1},{1,0},{2,3},{3,2},{4,6},{5,7},{6,4},{7,5},{8,9},{9,8},{10,11... | collective-permute-start | bytes 786440 | tf_op jit(solution)/shard_map/ppermute | solution.py:167
  30.7 3.5 %collective-permute-done.4.refs_0_.refs_6_ = f32[128,512]{1,0:T(8,128)S(1)} collective-permute-done((f32[128,512]{1,0:T(8,128)S(1)}, f32[128,512]{1,0:T(8,128)S(1)}, u32[]{:S(2)}, u32[]{:S(2)}) %collective-permute-start.4) | collective-permute-done | bytes 262176 | tf_op jit(solution)/shard_map/ppermute | solution.py:152
  36.1 1.8 %collective-permute-start.7 = (f32[64,512]{1,0:T(8,128)S(1)}, f32[64,512]{1,0:T(8,128)S(1)}, u32[]{:S(2)}, u32[]{:S(2)}) collective-permute-start(f32[64,512]{1,0:T(8,128)S(1)} %add.9.x), channel_id=1, source_target_pairs={{0,8},{8,0},{16,24},{24,16},{1,9},{9,1},{17,25},{25,17},{2,10},{10... | collective-permute-start | bytes 393224 | tf_op jit(solution)/shard_map/ppermute | solution.py:152
  37.9 2.6 %collective-permute-start.8 = (f32[64,512]{1,0:T(8,128)S(1)}, f32[64,512]{1,0:T(8,128)S(1)}, u32[]{:S(2)}, u32[]{:S(2)}) collective-permute-start(f32[64,512]{1,0:T(8,128)S(1)} %add.9.x), channel_id=1, source_target_pairs={{0,16},{8,24},{16,0},{24,8},{1,17},{9,25},{17,1},{25,9},{2,18},{10... | collective-permute-start | bytes 393224 | tf_op jit(solution)/shard_map/ppermute | solution.py:152
  40.6 1.6 %collective-permute-start.14 = (f32[128,512]{1,0:T(8,128)S(1)}, f32[128,512]{1,0:T(8,128)S(1)}, u32[]{:S(2)}, u32[]{:S(2)}) collective-permute-start(f32[128,512]{1,0:T(8,128)S(1)} %get-tuple-element.34.refs_8_.refs_0_), channel_id=1, source_target_pairs={{0,1},{1,0},{2,3},{3,2},{4,5},{5,4},{6,7},{7,6},{8,9},{9,8},{10,11... | collective-permute-start | bytes 786440 | tf_op jit(solution)/shard_map/ppermute | solution.py:152
  43.7 1.6 %collective-permute-start.18 = (f32[128,512]{1,0:T(8,128)S(1)}, f32[128,512]{1,0:T(8,128)S(1)}, u32[]{:S(2)}, u32[]{:S(2)}) collective-permute-start(f32[128,512]{1,0:T(8,128)S(1)} %collective-permute-done.16.refs_12_.refs_4_), channel_id=1, source_target_pairs={{0,1},{1,0},{2,3},{3,2},{4,5},{5,4},{6,7},{7,6},{8,9},{9,8},{10,11... | collective-permute-start | bytes 786440 | tf_op jit(solution)/shard_map/ppermute | solution.py:152
  45.3 5.4 %collective-permute-done.8.refs_2_ = f32[64,512]{1,0:T(8,128)S(1)} collective-permute-done((f32[64,512]{1,0:T(8,128)S(1)}, f32[64,512]{1,0:T(8,128)S(1)}, u32[]{:S(2)}, u32[]{:S(2)}) %collective-permute-start.8) | collective-permute-done | bytes 131104 | tf_op jit(solution)/shard_map/ppermute | solution.py:152
  53.5 2.3 %collective-permute-done.25.across.refs_6_ = f32[256,128]{1,0:T(8,128)S(1)} collective-permute-done((f32[256,128]{1,0:T(8,128)S(1)}, f32[256,128]{1,0:T(8,128)S(1)}, u32[]{:S(2)}, u32[]{:S(2)}) %collective-permute-start.25) | collective-permute-done | bytes 131104 | tf_op jit(solution)/shard_map/ppermute | solution.py:169
  59.9 1.8 %shard_map.43 = (f32[1024,128]{1,0:T(8,128)S(1)}, f32[128,512]{1,0:T(8,128)S(1)}) custom-call(f32[1024,128]{1,0:T(8,128)S(1)} %copy-done.1, f32[64,512]{1,0:T(8,128)S(1)} %shard_map.42.mine, f32[64,512]{1,0:T(8,128)S(1)} %collective-permute-done.13.other, f32[128,512]{1,0:T(8,128)S(1)} %get-tuple-element.36.refs_0_, ...), custom_call_target="tpu_custom_call" | custom-call | flops 234881024 | bytes 5242880 | tf_op jit(solution)/shard_map/pallas_call | solution.py:140
  64.6 3.2 %collective-permute-start.22 = (f32[64,512]{1,0:T(8,128)S(1)}, f32[64,512]{1,0:T(8,128)S(1)}, u32[]{:S(2)}, u32[]{:S(2)}) collective-permute-start(f32[64,512]{1,0:T(8,128)S(1)} %add.10.x), channel_id=1, source_target_pairs={{0,16},{8,24},{16,0},{24,8},{1,17},{9,25},{17,1},{25,9},{2,18},{10... | collective-permute-start | bytes 393224 | tf_op jit(solution)/shard_map/ppermute | solution.py:152
  67.8 1.8 %collective-permute-start.23 = (f32[64,512]{1,0:T(8,128)S(1)}, f32[64,512]{1,0:T(8,128)S(1)}, u32[]{:S(2)}, u32[]{:S(2)}) collective-permute-start(f32[64,512]{1,0:T(8,128)S(1)} %add.10.x), channel_id=1, source_target_pairs={{0,24},{8,16},{16,8},{24,0},{1,25},{9,17},{17,9},{25,1},{2,26},{10... | collective-permute-start | bytes 393224 | tf_op jit(solution)/shard_map/ppermute | solution.py:152
  71.2 1.6 %collective-permute-start.39 = (f32[256,128]{1,0:T(8,128)S(1)}, f32[256,128]{1,0:T(8,128)S(1)}, u32[]{:S(2)}, u32[]{:S(2)}) collective-permute-start(f32[256,128]{1,0:T(8,128)S(1)} %shard_map.52), channel_id=1, source_target_pairs={{0,2},{1,3},{2,0},{3,1},{4,5},{5,4},{6,7},{7,6},{8,10},{9,11},{10,... | collective-permute-start | bytes 393224 | tf_op jit(solution)/shard_map/ppermute | solution.py:169
  73.3 4.6 %collective-permute-done.22.refs_2_ = f32[64,512]{1,0:T(8,128)S(1)} collective-permute-done((f32[64,512]{1,0:T(8,128)S(1)}, f32[64,512]{1,0:T(8,128)S(1)}, u32[]{:S(2)}, u32[]{:S(2)}) %collective-permute-start.22) | collective-permute-done | bytes 131104 | tf_op jit(solution)/shard_map/ppermute | solution.py:152
  82.4 1.8 %shard_map.49 = (f32[1024,128]{1,0:T(8,128)S(1)}, f32[128,512]{1,0:T(8,128)S(1)}) custom-call(f32[1024,128]{1,0:T(8,128)S(1)} %get-tuple-element.23.x, f32[64,512]{1,0:T(8,128)S(1)} %shard_map.48.mine, f32[64,512]{1,0:T(8,128)S(1)} %collective-permute-done.27.other, f32[128,512]{1,0:T(8,128)S(1)} %get-tuple-element.34.refs_8_.refs_0_, ...), custom_call_target="tpu_custom_call" | custom-call | flops 234881024 | bytes 5242880 | tf_op jit(solution)/shard_map/pallas_call | solution.py:140
  87.4 2.4 %collective-permute-start.35 = (f32[64,512]{1,0:T(8,128)S(1)}, f32[64,512]{1,0:T(8,128)S(1)}, u32[]{:S(2)}, u32[]{:S(2)}) collective-permute-start(f32[64,512]{1,0:T(8,128)S(1)} %add.11.x), channel_id=1, source_target_pairs={{0,8},{8,0},{16,24},{24,16},{1,9},{9,1},{17,25},{25,17},{2,10},{10... | collective-permute-start | bytes 393224 | tf_op jit(solution)/shard_map/ppermute | solution.py:152
  92.6 3.0 %collective-permute-done.35.refs_1_ = f32[64,512]{1,0:T(8,128)S(1)} collective-permute-done((f32[64,512]{1,0:T(8,128)S(1)}, f32[64,512]{1,0:T(8,128)S(1)}, u32[]{:S(2)}, u32[]{:S(2)}) %collective-permute-start.35) | collective-permute-done | bytes 131104 | tf_op jit(solution)/shard_map/ppermute | solution.py:152
  95.6 7.1 %collective-permute-done.36.refs_2_ = f32[64,512]{1,0:T(8,128)S(1)} collective-permute-done((f32[64,512]{1,0:T(8,128)S(1)}, f32[64,512]{1,0:T(8,128)S(1)}, u32[]{:S(2)}, u32[]{:S(2)}) %collective-permute-start.36) | collective-permute-done | bytes 131104 | tf_op jit(solution)/shard_map/ppermute | solution.py:152
  104.8 1.8 %shard_map.55 = f32[1024,128]{1,0:T(8,128)} custom-call(f32[1024,128]{1,0:T(8,128)S(1)} %get-tuple-element.27.x, f32[64,512]{1,0:T(8,128)S(1)} %shard_map.54.mine, f32[64,512]{1,0:T(8,128)S(1)} %collective-permute-done.41.other, f32[128,512]{1,0:T(8,128)S(1)} %get-tuple-element.32.refs_8_.refs_0_, f32[128,512]{1,0:T(8,128)S(1)} %get-tuple-element.31.refs_9_.refs_1_, ...), custom_call_target="tpu_custom_call" | custom-call | flops 134217728 | bytes 3407872 | tf_op jit(solution)/shard_map/pallas_call | solution.py:140
  (92 shorter events, 39.0 us)
Async XLA Ops:
  1.2 10.2 %collective-permute-start.2 = (f32[128,512]{1,0:T(8,128)S(1)}, f32[128,512]{1,0:T(8,128)S(1)}, u32[]{:S(2)}, u32[]{:S(2)}) collective-permute-start(f32[128,512]{1,0:T(8,128)S(1)} %get-tuple-element.36.refs_0_), channel_id=1, source_target_pairs={{0,2},{2,0},{1,3},{3,1},{4,6},{6,4},{5,7},{7,5},{8,10},{10,8},{9,1... | collective-permute-start | bytes 786440 | tf_op jit(solution)/shard_map/ppermute | solution.py:152
  6.8 12.9 %collective-permute-start.1 = (f32[128,512]{1,0:T(8,128)S(1)}, f32[128,512]{1,0:T(8,128)S(1)}, u32[]{:S(2)}, u32[]{:S(2)}) collective-permute-start(f32[128,512]{1,0:T(8,128)S(1)} %get-tuple-element.35.refs_1_), channel_id=1, source_target_pairs={{0,1},{1,0},{2,3},{3,2},{4,5},{5,4},{6,7},{7,6},{8,9},{9,8},{10,11... | collective-permute-start | bytes 786440 | tf_op jit(solution)/shard_map/ppermute | solution.py:152
  7.3 18.0 %collective-permute-start = (f32[128,512]{1,0:T(8,128)S(1)}, f32[128,512]{1,0:T(8,128)S(1)}, u32[]{:S(2)}, u32[]{:S(2)}) collective-permute-start(f32[128,512]{1,0:T(8,128)S(1)} %get-tuple-element.36.refs_0_), channel_id=1, source_target_pairs={{0,1},{1,0},{2,3},{3,2},{4,5},{5,4},{6,7},{7,6},{8,9},{9,8},{10,11... | collective-permute-start | bytes 786440 | tf_op jit(solution)/shard_map/ppermute | solution.py:152
  8.8 18.0 %collective-permute-start.3 = (f32[128,512]{1,0:T(8,128)S(1)}, f32[128,512]{1,0:T(8,128)S(1)}, u32[]{:S(2)}, u32[]{:S(2)}) collective-permute-start(f32[128,512]{1,0:T(8,128)S(1)} %get-tuple-element.35.refs_1_), channel_id=1, source_target_pairs={{0,2},{2,0},{1,3},{3,1},{4,6},{6,4},{5,7},{7,5},{8,10},{10,8},{9,1... | collective-permute-start | bytes 786440 | tf_op jit(solution)/shard_map/ppermute | solution.py:152
  19.9 18.0 %collective-permute-start.15 = (f32[128,512]{1,0:T(8,128)S(1)}, f32[128,512]{1,0:T(8,128)S(1)}, u32[]{:S(2)}, u32[]{:S(2)}) collective-permute-start(f32[128,512]{1,0:T(8,128)S(1)} %get-tuple-element.33.refs_9_.refs_1_), channel_id=1, source_target_pairs={{0,1},{1,0},{2,3},{3,2},{4,5},{5,4},{6,7},{7,6},{8,9},{9,8},{10,11... | collective-permute-start | bytes 786440 | tf_op jit(solution)/shard_map/ppermute | solution.py:152
  22.2 18.2 %collective-permute-start.16 = (f32[128,512]{1,0:T(8,128)S(1)}, f32[128,512]{1,0:T(8,128)S(1)}, u32[]{:S(2)}, u32[]{:S(2)}) collective-permute-start(f32[128,512]{1,0:T(8,128)S(1)} %get-tuple-element.34.refs_8_.refs_0_), channel_id=1, source_target_pairs={{0,2},{2,0},{1,3},{3,1},{4,6},{6,4},{5,7},{7,5},{8,10},{10,8},{9,1... | collective-permute-start | bytes 786440 | tf_op jit(solution)/shard_map/ppermute | solution.py:152
  26.8 15.3 %collective-permute-start.12 = (f32[256,384]{1,0:T(8,128)S(1)}, f32[256,384]{1,0:T(8,128)S(1)}, u32[]{:S(2)}, u32[]{:S(2)}) collective-permute-start(f32[256,384]{1,0:T(8,128)S(1)} %shard_map.41), channel_id=1, source_target_pairs={{0,4},{4,0},{1,5},{5,1},{2,6},{6,2},{3,7},{7,3},{8,12},{12,8},{9,1... | collective-permute-start | bytes 1179656 | tf_op jit(solution)/shard_map/ppermute | solution.py:152
  27.9 12.6 %collective-permute-start.24 = (f32[512,128]{1,0:T(8,128)S(1)}, f32[512,128]{1,0:T(8,128)S(1)}, u32[]{:S(2)}, u32[]{:S(2)}) collective-permute-start(f32[512,128]{1,0:T(8,128)S(1)} %get-tuple-element.38), channel_id=1, source_target_pairs={{0,1},{1,0},{2,3},{3,2},{4,6},{5,7},{6,4},{7,5},{8,9},{9,8},{10,11... | collective-permute-start | bytes 786440 | tf_op jit(solution)/shard_map/ppermute | solution.py:167
  37.9 12.9 %collective-permute-start.8 = (f32[64,512]{1,0:T(8,128)S(1)}, f32[64,512]{1,0:T(8,128)S(1)}, u32[]{:S(2)}, u32[]{:S(2)}) collective-permute-start(f32[64,512]{1,0:T(8,128)S(1)} %add.9.x), channel_id=1, source_target_pairs={{0,16},{8,24},{16,0},{24,8},{1,17},{9,25},{17,1},{25,9},{2,18},{10... | collective-permute-start | bytes 393224 | tf_op jit(solution)/shard_map/ppermute | solution.py:152
  40.5 11.8 %collective-permute-start.9 = (f32[64,512]{1,0:T(8,128)S(1)}, f32[64,512]{1,0:T(8,128)S(1)}, u32[]{:S(2)}, u32[]{:S(2)}) collective-permute-start(f32[64,512]{1,0:T(8,128)S(1)} %add.9.x), channel_id=1, source_target_pairs={{0,24},{8,16},{16,8},{24,0},{1,25},{9,17},{17,9},{25,1},{2,26},{10... | collective-permute-start | bytes 393224 | tf_op jit(solution)/shard_map/ppermute | solution.py:152
  40.6 15.2 %collective-permute-start.14 = (f32[128,512]{1,0:T(8,128)S(1)}, f32[128,512]{1,0:T(8,128)S(1)}, u32[]{:S(2)}, u32[]{:S(2)}) collective-permute-start(f32[128,512]{1,0:T(8,128)S(1)} %get-tuple-element.34.refs_8_.refs_0_), channel_id=1, source_target_pairs={{0,1},{1,0},{2,3},{3,2},{4,5},{5,4},{6,7},{7,6},{8,9},{9,8},{10,11... | collective-permute-start | bytes 786440 | tf_op jit(solution)/shard_map/ppermute | solution.py:152
  42.2 14.2 %collective-permute-start.17 = (f32[128,512]{1,0:T(8,128)S(1)}, f32[128,512]{1,0:T(8,128)S(1)}, u32[]{:S(2)}, u32[]{:S(2)}) collective-permute-start(f32[128,512]{1,0:T(8,128)S(1)} %get-tuple-element.33.refs_9_.refs_1_), channel_id=1, source_target_pairs={{0,2},{2,0},{1,3},{3,1},{4,6},{6,4},{5,7},{7,5},{8,10},{10,8},{9,1... | collective-permute-start | bytes 786440 | tf_op jit(solution)/shard_map/ppermute | solution.py:152
  43.7 14.1 %collective-permute-start.18 = (f32[128,512]{1,0:T(8,128)S(1)}, f32[128,512]{1,0:T(8,128)S(1)}, u32[]{:S(2)}, u32[]{:S(2)}) collective-permute-start(f32[128,512]{1,0:T(8,128)S(1)} %collective-permute-done.16.refs_12_.refs_4_), channel_id=1, source_target_pairs={{0,1},{1,0},{2,3},{3,2},{4,5},{5,4},{6,7},{7,6},{8,9},{9,8},{10,11... | collective-permute-start | bytes 786440 | tf_op jit(solution)/shard_map/ppermute | solution.py:152
  52.3 9.4 %collective-permute-start.19 = (f32[128,512]{1,0:T(8,128)S(1)}, f32[128,512]{1,0:T(8,128)S(1)}, u32[]{:S(2)}, u32[]{:S(2)}) collective-permute-start(f32[128,512]{1,0:T(8,128)S(1)} %collective-permute-done.15.refs_11_.refs_3_), channel_id=1, source_target_pairs={{0,2},{2,0},{1,3},{3,1},{4,6},{6,4},{5,7},{7,5},{8,10},{10,8},{9,1... | collective-permute-start | bytes 786440 | tf_op jit(solution)/shard_map/ppermute | solution.py:152
  55.8 15.4 %collective-permute-start.26 = (f32[256,384]{1,0:T(8,128)S(1)}, f32[256,384]{1,0:T(8,128)S(1)}, u32[]{:S(2)}, u32[]{:S(2)}) collective-permute-start(f32[256,384]{1,0:T(8,128)S(1)} %shard_map.47), channel_id=1, source_target_pairs={{0,4},{4,0},{1,5},{5,1},{2,6},{6,2},{3,7},{7,3},{8,12},{12,8},{9,1... | collective-permute-start | bytes 1179656 | tf_op jit(solution)/shard_map/ppermute | solution.py:152
  57.8 10.0 %collective-permute-start.30 = (f32[128,512]{1,0:T(8,128)S(1)}, f32[128,512]{1,0:T(8,128)S(1)}, u32[]{:S(2)}, u32[]{:S(2)}) collective-permute-start(f32[128,512]{1,0:T(8,128)S(1)} %get-tuple-element.32.refs_8_.refs_0_), channel_id=1, source_target_pairs={{0,2},{2,0},{1,3},{3,1},{4,6},{6,4},{5,7},{7,5},{8,10},{10,8},{9,1... | collective-permute-start | bytes 786440 | tf_op jit(solution)/shard_map/ppermute | solution.py:152
  59.4 10.3 %collective-permute-start.38 = (f32[512,128]{1,0:T(8,128)S(1)}, f32[512,128]{1,0:T(8,128)S(1)}, u32[]{:S(2)}, u32[]{:S(2)}) collective-permute-start(f32[512,128]{1,0:T(8,128)S(1)} %get-tuple-element.37), channel_id=1, source_target_pairs={{0,1},{1,0},{2,3},{3,2},{4,6},{5,7},{6,4},{7,5},{8,9},{9,8},{10,11... | collective-permute-start | bytes 786440 | tf_op jit(solution)/shard_map/ppermute | solution.py:167
  64.6 13.2 %collective-permute-start.22 = (f32[64,512]{1,0:T(8,128)S(1)}, f32[64,512]{1,0:T(8,128)S(1)}, u32[]{:S(2)}, u32[]{:S(2)}) collective-permute-start(f32[64,512]{1,0:T(8,128)S(1)} %add.10.x), channel_id=1, source_target_pairs={{0,16},{8,24},{16,0},{24,8},{1,17},{9,25},{17,1},{25,9},{2,18},{10... | collective-permute-start | bytes 393224 | tf_op jit(solution)/shard_map/ppermute | solution.py:152
  67.8 11.0 %collective-permute-start.23 = (f32[64,512]{1,0:T(8,128)S(1)}, f32[64,512]{1,0:T(8,128)S(1)}, u32[]{:S(2)}, u32[]{:S(2)}) collective-permute-start(f32[64,512]{1,0:T(8,128)S(1)} %add.10.x), channel_id=1, source_target_pairs={{0,24},{8,16},{16,8},{24,0},{1,25},{9,17},{17,9},{25,1},{2,26},{10... | collective-permute-start | bytes 393224 | tf_op jit(solution)/shard_map/ppermute | solution.py:152
  69.6 11.5 %collective-permute-start.28 = (f32[128,512]{1,0:T(8,128)S(1)}, f32[128,512]{1,0:T(8,128)S(1)}, u32[]{:S(2)}, u32[]{:S(2)}) collective-permute-start(f32[128,512]{1,0:T(8,128)S(1)} %get-tuple-element.32.refs_8_.refs_0_), channel_id=1, source_target_pairs={{0,1},{1,0},{2,3},{3,2},{4,5},{5,4},{6,7},{7,6},{8,9},{9,8},{10,11... | collective-permute-start | bytes 786440 | tf_op jit(solution)/shard_map/ppermute | solution.py:152
  71.2 9.8 %collective-permute-start.39 = (f32[256,128]{1,0:T(8,128)S(1)}, f32[256,128]{1,0:T(8,128)S(1)}, u32[]{:S(2)}, u32[]{:S(2)}) collective-permute-start(f32[256,128]{1,0:T(8,128)S(1)} %shard_map.52), channel_id=1, source_target_pairs={{0,2},{1,3},{2,0},{3,1},{4,5},{5,4},{6,7},{7,6},{8,10},{9,11},{10,... | collective-permute-start | bytes 393224 | tf_op jit(solution)/shard_map/ppermute | solution.py:169
  81.1 11.4 %collective-permute-start.40 = (f32[256,384]{1,0:T(8,128)S(1)}, f32[256,384]{1,0:T(8,128)S(1)}, u32[]{:S(2)}, u32[]{:S(2)}) collective-permute-start(f32[256,384]{1,0:T(8,128)S(1)} %shard_map.53), channel_id=1, source_target_pairs={{0,4},{4,0},{1,5},{5,1},{2,6},{6,2},{3,7},{7,3},{8,12},{12,8},{9,1... | collective-permute-start | bytes 1179656 | tf_op jit(solution)/shard_map/ppermute | solution.py:152
  89.8 12.9 %collective-permute-start.36 = (f32[64,512]{1,0:T(8,128)S(1)}, f32[64,512]{1,0:T(8,128)S(1)}, u32[]{:S(2)}, u32[]{:S(2)}) collective-permute-start(f32[64,512]{1,0:T(8,128)S(1)} %add.11.x), channel_id=1, source_target_pairs={{0,16},{8,24},{16,0},{24,8},{1,17},{9,25},{17,1},{25,9},{2,18},{10... | collective-permute-start | bytes 393224 | tf_op jit(solution)/shard_map/ppermute | solution.py:152
  91.1 11.5 %collective-permute-start.37 = (f32[64,512]{1,0:T(8,128)S(1)}, f32[64,512]{1,0:T(8,128)S(1)}, u32[]{:S(2)}, u32[]{:S(2)}) collective-permute-start(f32[64,512]{1,0:T(8,128)S(1)} %add.11.x), channel_id=1, source_target_pairs={{0,24},{8,16},{16,8},{24,0},{1,25},{9,17},{17,9},{25,1},{2,26},{10... | collective-permute-start | bytes 393224 | tf_op jit(solution)/shard_map/ppermute | solution.py:152
  (21 other events, 160.5 us)

commit v7 on v6

--- a/solution.py
+++ b/solution.py
@@ -19,10 +19,27 @@
     return head, (a - head.astype(F32)).astype(BF16)
 
 
-def dot3(a, b, dims):
-    (ah, al), (bh, bl) = split(a), split(b)
-    one = functools.partial(lax.dot_general, dimension_numbers=dims, preferred_element_type=F32)
-    return one(ah, bh) + (one(ah, bl) + one(al, bh))
+def dot(a, b, dims):
+    return lax.dot_general(a, b, dims, preferred_element_type=F32)
+
+
+def stack(pair):
+    return jnp.concatenate(pair, axis=0)
+
+
+def dot_left(a, b, dims):
+    ah, al = split(a)
+    bh, bl = split(b)
+    n = a.shape[0]
+    both = dot(stack((ah, al)), bh, dims)
+    return both[:n] + (both[n:] + dot(ah, bl, dims))
+
+
+def dot_right(a, stacked, dims):
+    ah, al = split(a)
+    n = stacked.shape[0] // 2
+    both = dot(ah, stacked, dims)
+    return both[:, :n] + (both[:, n:] + dot(al, stacked[:n], dims))
 
 
 def place():
@@ -42,7 +59,7 @@
     total = None
     for block, first, ref in blocks_of(refs, skip):
         x = current[window(v, block, first, ref.shape[0]), :]
-        part = dot3(x.T, ref[...], NN)
+        part = dot_left(x.T, ref[...], NN)
         total = part if total is None else total + part
     return total
 
@@ -72,9 +89,10 @@
 
 
 def update(current, out, refs, coefficients, v):
+    stacked = stack(split(coefficients))
     for block, first, ref in blocks_of(refs):
         at = window(v, block, first, ref.shape[0])
-        out[at, :] = current[at, :] - dot3(ref[...], coefficients, NT)
+        out[at, :] = current[at, :] - dot_right(ref[...], stacked, NT)
 
 
 def turn_kernel(x, mine, other, *refs):
@@ -117,10 +135,10 @@
     second = jnp.concatenate([exchanged[:, :share], exchanged[:, share : 2 * share]], axis=0)
     a, b = across[...], exchanged[:, 2 * share :]
     across = jnp.concatenate([jnp.where(on_x, a, b), jnp.where(on_x, b, a)], axis=0)
-    sums = dot3(own, factor[panel], NT)
-    sums += dot3(jnp.where(on_x, along_x, along_y), first[...], NT)
-    sums += dot3(jnp.where(on_x, along_y, along_x), second, NT)
-    out[...] = sums + dot3(far, across, NT)
+    sums = dot_left(own, factor[panel], NT)
+    sums += dot_left(jnp.where(on_x, along_x, along_y), first[...], NT)
+    sums += dot_left(jnp.where(on_x, along_y, along_x), second, NT)
+    out[...] = sums + dot_left(far, across, NT)
 
 
 def split_columns(total, v, share):

time: 107 us -> 107 us (level)
  transfers between devices with their start and end apart: 42 -> 42, of which waited for: 18 -> 19; matrix products, arithmetic and copies ran while one was open for 1% -> 1% of each run, Pallas kernels for 7% -> 7%
where the time goes in v7:
time: 107 us; the launch traced here: 106 us
  waiting for transfers between devices  47.7 us (45%)
  starting transfers between devices  46.9 us (44%)
  Pallas kernels  9.28 us (9%)
  local copies, waits for them, and re-layouts  2.27 us (2%)
    ppermute x36, waiting for transfers between devices, swap(): return lax.ppermute(a, axis, [(i, i ^ by) for i in range(n)])  42.2 us
    ppermute x36, starting transfers between devices, swap(): return lax.ppermute(a, axis, [(i, i ^ by) for i in range(n)])  39.7 us
    pallas_call x19, Pallas kernels, call(): pl.pallas_call(kernel, out_shape=outs, in_specs=vmem(len(args)), out_spec...  9.28 us
    ppermute x3, starting transfers between devices, gather_factor(): lax.ppermute(own, axes, [(i, i ^ (2 if i >= n // 2 else 1)) for i in rang...  4.07 us
    ppermute x3, starting transfers between devices, gather_factor(): lax.ppermute(mine, axes, [(i, i ^ (1 if i >= n // 2 else 2)) for i in ran...  3.18 us
    ppermute x3, waiting for transfers between devices, gather_factor(): lax.ppermute(own, axes, [(i, i ^ (2 if i >= n // 2 else 1)) for i in rang...  3.06 us
    ppermute x3, waiting for transfers between devices, gather_factor(): lax.ppermute(mine, axes, [(i, i ^ (1 if i >= n // 2 else 2)) for i in ran...  2.45 us
  transfers between devices with their start and end apart: 42, of which 19 were waited for; matrix products, arithmetic and copies ran while one was open for 1% of the time, Pallas kernels for 7%

profile of v7, /device:TPU:0, one launch (start us, length us, event | category | flops | bytes accessed | tf_op | source)
XLA Modules:
  0.0 106.5 jit_solution(3462410734060494634)
XLA Ops:
  1.2 3.1 %collective-permute-start.2 = (f32[128,512]{1,0:T(8,128)S(1)}, f32[128,512]{1,0:T(8,128)S(1)}, u32[]{:S(2)}, u32[]{:S(2)}) collective-permute-start(f32[128,512]{1,0:T(8,128)S(1)} %get-tuple-element.36.refs_0_), channel_id=1, source_target_pairs={{0,2},{2,0},{1,3},{3,1},{4,6},{6,4},{5,7},{7,5},{8,10},{10,8},{9,1... | collective-permute-start | bytes 786440 | tf_op jit(solution)/shard_map/ppermute | solution.py:170
  9.3 2.1 %collective-permute-done.2.refs_4_ = f32[128,512]{1,0:T(8,128)S(1)} collective-permute-done((f32[128,512]{1,0:T(8,128)S(1)}, f32[128,512]{1,0:T(8,128)S(1)}, u32[]{:S(2)}, u32[]{:S(2)}) %collective-permute-start.2) | collective-permute-done | bytes 262176 | tf_op jit(solution)/shard_map/ppermute | solution.py:170
  11.4 3.1 %collective-permute-done.10.x.first.refs_5_ = f32[512,128]{1,0:T(8,128)S(1)} collective-permute-done((f32[512,128]{1,0:T(8,128)S(1)}, f32[512,128]{1,0:T(8,128)S(1)}, u32[]{:S(2)}, u32[]{:S(2)}) %collective-permute-start.10) | collective-permute-done | bytes 262176 | tf_op jit(solution)/shard_map/ppermute | solution.py:185
  14.6 5.1 %collective-permute-done.1.refs_3_ = f32[128,512]{1,0:T(8,128)S(1)} collective-permute-done((f32[128,512]{1,0:T(8,128)S(1)}, f32[128,512]{1,0:T(8,128)S(1)}, u32[]{:S(2)}, u32[]{:S(2)}) %collective-permute-start.1) | collective-permute-done | bytes 262176 | tf_op jit(solution)/shard_map/ppermute | solution.py:170
  19.9 2.4 %collective-permute-start.15 = (f32[128,512]{1,0:T(8,128)S(1)}, f32[128,512]{1,0:T(8,128)S(1)}, u32[]{:S(2)}, u32[]{:S(2)}) collective-permute-start(f32[128,512]{1,0:T(8,128)S(1)} %get-tuple-element.33.refs_9_.refs_1_), channel_id=1, source_target_pairs={{0,1},{1,0},{2,3},{3,2},{4,5},{5,4},{6,7},{7,6},{8,9},{9,8},{10,11... | collective-permute-start | bytes 786440 | tf_op jit(solution)/shard_map/ppermute | solution.py:170
  23.4 1.9 %collective-permute-done.refs_2_ = f32[128,512]{1,0:T(8,128)S(1)} collective-permute-done((f32[128,512]{1,0:T(8,128)S(1)}, f32[128,512]{1,0:T(8,128)S(1)}, u32[]{:S(2)}, u32[]{:S(2)}) %collective-permute-start) | collective-permute-done | bytes 262176 | tf_op jit(solution)/shard_map/ppermute | solution.py:170
  27.9 2.0 %collective-permute-start.24 = (f32[512,128]{1,0:T(8,128)S(1)}, f32[512,128]{1,0:T(8,128)S(1)}, u32[]{:S(2)}, u32[]{:S(2)}) collective-permute-start(f32[512,128]{1,0:T(8,128)S(1)} %get-tuple-element.38), channel_id=1, source_target_pairs={{0,1},{1,0},{2,3},{3,2},{4,6},{5,7},{6,4},{7,5},{8,9},{9,8},{10,11... | collective-permute-start | bytes 786440 | tf_op jit(solution)/shard_map/ppermute | solution.py:185
  30.7 3.5 %collective-permute-done.4.refs_0_.refs_6_ = f32[128,512]{1,0:T(8,128)S(1)} collective-permute-done((f32[128,512]{1,0:T(8,128)S(1)}, f32[128,512]{1,0:T(8,128)S(1)}, u32[]{:S(2)}, u32[]{:S(2)}) %collective-permute-start.4) | collective-permute-done | bytes 262176 | tf_op jit(solution)/shard_map/ppermute | solution.py:170
  36.1 1.8 %collective-permute-start.7 = (f32[64,512]{1,0:T(8,128)S(1)}, f32[64,512]{1,0:T(8,128)S(1)}, u32[]{:S(2)}, u32[]{:S(2)}) collective-permute-start(f32[64,512]{1,0:T(8,128)S(1)} %add.9.x), channel_id=1, source_target_pairs={{0,8},{8,0},{16,24},{24,16},{1,9},{9,1},{17,25},{25,17},{2,10},{10... | collective-permute-start | bytes 393224 | tf_op jit(solution)/shard_map/ppermute | solution.py:170
  37.9 2.6 %collective-permute-start.8 = (f32[64,512]{1,0:T(8,128)S(1)}, f32[64,512]{1,0:T(8,128)S(1)}, u32[]{:S(2)}, u32[]{:S(2)}) collective-permute-start(f32[64,512]{1,0:T(8,128)S(1)} %add.9.x), channel_id=1, source_target_pairs={{0,16},{8,24},{16,0},{24,8},{1,17},{9,25},{17,1},{25,9},{2,18},{10... | collective-permute-start | bytes 393224 | tf_op jit(solution)/shard_map/ppermute | solution.py:170
  40.5 1.6 %collective-permute-start.14 = (f32[128,512]{1,0:T(8,128)S(1)}, f32[128,512]{1,0:T(8,128)S(1)}, u32[]{:S(2)}, u32[]{:S(2)}) collective-permute-start(f32[128,512]{1,0:T(8,128)S(1)} %get-tuple-element.34.refs_8_.refs_0_), channel_id=1, source_target_pairs={{0,1},{1,0},{2,3},{3,2},{4,5},{5,4},{6,7},{7,6},{8,9},{9,8},{10,11... | collective-permute-start | bytes 786440 | tf_op jit(solution)/shard_map/ppermute | solution.py:170
  43.7 1.6 %collective-permute-start.18 = (f32[128,512]{1,0:T(8,128)S(1)}, f32[128,512]{1,0:T(8,128)S(1)}, u32[]{:S(2)}, u32[]{:S(2)}) collective-permute-start(f32[128,512]{1,0:T(8,128)S(1)} %collective-permute-done.16.refs_12_.refs_4_), channel_id=1, source_target_pairs={{0,1},{1,0},{2,3},{3,2},{4,5},{5,4},{6,7},{7,6},{8,9},{9,8},{10,11... | collective-permute-start | bytes 786440 | tf_op jit(solution)/shard_map/ppermute | solution.py:170
  45.3 5.5 %collective-permute-done.8.refs_2_ = f32[64,512]{1,0:T(8,128)S(1)} collective-permute-done((f32[64,512]{1,0:T(8,128)S(1)}, f32[64,512]{1,0:T(8,128)S(1)}, u32[]{:S(2)}, u32[]{:S(2)}) %collective-permute-start.8) | collective-permute-done | bytes 131104 | tf_op jit(solution)/shard_map/ppermute | solution.py:170
  53.3 2.4 %collective-permute-done.25.across.refs_6_ = f32[256,128]{1,0:T(8,128)S(1)} collective-permute-done((f32[256,128]{1,0:T(8,128)S(1)}, f32[256,128]{1,0:T(8,128)S(1)}, u32[]{:S(2)}, u32[]{:S(2)}) %collective-permute-start.25) | collective-permute-done | bytes 131104 | tf_op jit(solution)/shard_map/ppermute | solution.py:187
  59.9 1.9 %shard_map.43 = (f32[1024,128]{1,0:T(8,128)S(1)}, f32[128,512]{1,0:T(8,128)S(1)}) custom-call(f32[1024,128]{1,0:T(8,128)S(1)} %copy-done.1, f32[64,512]{1,0:T(8,128)S(1)} %shard_map.42.mine, f32[64,512]{1,0:T(8,128)S(1)} %collective-permute-done.13.other, f32[128,512]{1,0:T(8,128)S(1)} %get-tuple-element.36.refs_0_, ...), custom_call_target="tpu_custom_call" | custom-call | flops 234881024 | bytes 5242880 | tf_op jit(solution)/shard_map/pallas_call | solution.py:158
  64.6 3.2 %collective-permute-start.22 = (f32[64,512]{1,0:T(8,128)S(1)}, f32[64,512]{1,0:T(8,128)S(1)}, u32[]{:S(2)}, u32[]{:S(2)}) collective-permute-start(f32[64,512]{1,0:T(8,128)S(1)} %add.10.x), channel_id=1, source_target_pairs={{0,16},{8,24},{16,0},{24,8},{1,17},{9,25},{17,1},{25,9},{2,18},{10... | collective-permute-start | bytes 393224 | tf_op jit(solution)/shard_map/ppermute | solution.py:170
  67.9 1.8 %collective-permute-start.23 = (f32[64,512]{1,0:T(8,128)S(1)}, f32[64,512]{1,0:T(8,128)S(1)}, u32[]{:S(2)}, u32[]{:S(2)}) collective-permute-start(f32[64,512]{1,0:T(8,128)S(1)} %add.10.x), channel_id=1, source_target_pairs={{0,24},{8,16},{16,8},{24,0},{1,25},{9,17},{17,9},{25,1},{2,26},{10... | collective-permute-start | bytes 393224 | tf_op jit(solution)/shard_map/ppermute | solution.py:170
  71.2 1.6 %collective-permute-start.39 = (f32[256,128]{1,0:T(8,128)S(1)}, f32[256,128]{1,0:T(8,128)S(1)}, u32[]{:S(2)}, u32[]{:S(2)}) collective-permute-start(f32[256,128]{1,0:T(8,128)S(1)} %shard_map.52), channel_id=1, source_target_pairs={{0,2},{1,3},{2,0},{3,1},{4,5},{5,4},{6,7},{7,6},{8,10},{9,11},{10,... | collective-permute-start | bytes 393224 | tf_op jit(solution)/shard_map/ppermute | solution.py:187
  73.3 4.6 %collective-permute-done.22.refs_2_ = f32[64,512]{1,0:T(8,128)S(1)} collective-permute-done((f32[64,512]{1,0:T(8,128)S(1)}, f32[64,512]{1,0:T(8,128)S(1)}, u32[]{:S(2)}, u32[]{:S(2)}) %collective-permute-start.22) | collective-permute-done | bytes 131104 | tf_op jit(solution)/shard_map/ppermute | solution.py:170
  82.2 1.9 %shard_map.49 = (f32[1024,128]{1,0:T(8,128)S(1)}, f32[128,512]{1,0:T(8,128)S(1)}) custom-call(f32[1024,128]{1,0:T(8,128)S(1)} %get-tuple-element.23.x, f32[64,512]{1,0:T(8,128)S(1)} %shard_map.48.mine, f32[64,512]{1,0:T(8,128)S(1)} %collective-permute-done.27.other, f32[128,512]{1,0:T(8,128)S(1)} %get-tuple-element.34.refs_8_.refs_0_, ...), custom_call_target="tpu_custom_call" | custom-call | flops 234881024 | bytes 5242880 | tf_op jit(solution)/shard_map/pallas_call | solution.py:158
  87.4 2.4 %collective-permute-start.35 = (f32[64,512]{1,0:T(8,128)S(1)}, f32[64,512]{1,0:T(8,128)S(1)}, u32[]{:S(2)}, u32[]{:S(2)}) collective-permute-start(f32[64,512]{1,0:T(8,128)S(1)} %add.11.x), channel_id=1, source_target_pairs={{0,8},{8,0},{16,24},{24,16},{1,9},{9,1},{17,25},{25,17},{2,10},{10... | collective-permute-start | bytes 393224 | tf_op jit(solution)/shard_map/ppermute | solution.py:170
  92.5 3.1 %collective-permute-done.35.refs_1_ = f32[64,512]{1,0:T(8,128)S(1)} collective-permute-done((f32[64,512]{1,0:T(8,128)S(1)}, f32[64,512]{1,0:T(8,128)S(1)}, u32[]{:S(2)}, u32[]{:S(2)}) %collective-permute-start.35) | collective-permute-done | bytes 131104 | tf_op jit(solution)/shard_map/ppermute | solution.py:170
  95.6 7.1 %collective-permute-done.36.refs_2_ = f32[64,512]{1,0:T(8,128)S(1)} collective-permute-done((f32[64,512]{1,0:T(8,128)S(1)}, f32[64,512]{1,0:T(8,128)S(1)}, u32[]{:S(2)}, u32[]{:S(2)}) %collective-permute-start.36) | collective-permute-done | bytes 131104 | tf_op jit(solution)/shard_map/ppermute | solution.py:170
  104.6 1.9 %shard_map.55 = f32[1024,128]{1,0:T(8,128)} custom-call(f32[1024,128]{1,0:T(8,128)S(1)} %get-tuple-element.27.x, f32[64,512]{1,0:T(8,128)S(1)} %shard_map.54.mine, f32[64,512]{1,0:T(8,128)S(1)} %collective-permute-done.41.other, f32[128,512]{1,0:T(8,128)S(1)} %get-tuple-element.32.refs_8_.refs_0_, f32[128,512]{1,0:T(8,128)S(1)} %get-tuple-element.31.refs_9_.refs_1_, ...), custom_call_target="tpu_custom_call" | custom-call | flops 134217728 | bytes 3407872 | tf_op jit(solution)/shard_map/pallas_call | solution.py:158
  (92 shorter events, 38.3 us)
Async XLA Ops:
  1.2 10.2 %collective-permute-start.2 = (f32[128,512]{1,0:T(8,128)S(1)}, f32[128,512]{1,0:T(8,128)S(1)}, u32[]{:S(2)}, u32[]{:S(2)}) collective-permute-start(f32[128,512]{1,0:T(8,128)S(1)} %get-tuple-element.36.refs_0_), channel_id=1, source_target_pairs={{0,2},{2,0},{1,3},{3,1},{4,6},{6,4},{5,7},{7,5},{8,10},{10,8},{9,1... | collective-permute-start | bytes 786440 | tf_op jit(solution)/shard_map/ppermute | solution.py:170
  6.8 12.9 %collective-permute-start.1 = (f32[128,512]{1,0:T(8,128)S(1)}, f32[128,512]{1,0:T(8,128)S(1)}, u32[]{:S(2)}, u32[]{:S(2)}) collective-permute-start(f32[128,512]{1,0:T(8,128)S(1)} %get-tuple-element.35.refs_1_), channel_id=1, source_target_pairs={{0,1},{1,0},{2,3},{3,2},{4,5},{5,4},{6,7},{7,6},{8,9},{9,8},{10,11... | collective-permute-start | bytes 786440 | tf_op jit(solution)/shard_map/ppermute | solution.py:170
  7.3 18.0 %collective-permute-start = (f32[128,512]{1,0:T(8,128)S(1)}, f32[128,512]{1,0:T(8,128)S(1)}, u32[]{:S(2)}, u32[]{:S(2)}) collective-permute-start(f32[128,512]{1,0:T(8,128)S(1)} %get-tuple-element.36.refs_0_), channel_id=1, source_target_pairs={{0,1},{1,0},{2,3},{3,2},{4,5},{5,4},{6,7},{7,6},{8,9},{9,8},{10,11... | collective-permute-start | bytes 786440 | tf_op jit(solution)/shard_map/ppermute | solution.py:170
  8.8 18.0 %collective-permute-start.3 = (f32[128,512]{1,0:T(8,128)S(1)}, f32[128,512]{1,0:T(8,128)S(1)}, u32[]{:S(2)}, u32[]{:S(2)}) collective-permute-start(f32[128,512]{1,0:T(8,128)S(1)} %get-tuple-element.35.refs_1_), channel_id=1, source_target_pairs={{0,2},{2,0},{1,3},{3,1},{4,6},{6,4},{5,7},{7,5},{8,10},{10,8},{9,1... | collective-permute-start | bytes 786440 | tf_op jit(solution)/shard_map/ppermute | solution.py:170
  19.9 18.0 %collective-permute-start.15 = (f32[128,512]{1,0:T(8,128)S(1)}, f32[128,512]{1,0:T(8,128)S(1)}, u32[]{:S(2)}, u32[]{:S(2)}) collective-permute-start(f32[128,512]{1,0:T(8,128)S(1)} %get-tuple-element.33.refs_9_.refs_1_), channel_id=1, source_target_pairs={{0,1},{1,0},{2,3},{3,2},{4,5},{5,4},{6,7},{7,6},{8,9},{9,8},{10,11... | collective-permute-start | bytes 786440 | tf_op jit(solution)/shard_map/ppermute | solution.py:170
  22.2 18.2 %collective-permute-start.16 = (f32[128,512]{1,0:T(8,128)S(1)}, f32[128,512]{1,0:T(8,128)S(1)}, u32[]{:S(2)}, u32[]{:S(2)}) collective-permute-start(f32[128,512]{1,0:T(8,128)S(1)} %get-tuple-element.34.refs_8_.refs_0_), channel_id=1, source_target_pairs={{0,2},{2,0},{1,3},{3,1},{4,6},{6,4},{5,7},{7,5},{8,10},{10,8},{9,1... | collective-permute-start | bytes 786440 | tf_op jit(solution)/shard_map/ppermute | solution.py:170
  26.8 15.3 %collective-permute-start.12 = (f32[256,384]{1,0:T(8,128)S(1)}, f32[256,384]{1,0:T(8,128)S(1)}, u32[]{:S(2)}, u32[]{:S(2)}) collective-permute-start(f32[256,384]{1,0:T(8,128)S(1)} %shard_map.41), channel_id=1, source_target_pairs={{0,4},{4,0},{1,5},{5,1},{2,6},{6,2},{3,7},{7,3},{8,12},{12,8},{9,1... | collective-permute-start | bytes 1179656 | tf_op jit(solution)/shard_map/ppermute | solution.py:170
  27.9 12.6 %collective-permute-start.24 = (f32[512,128]{1,0:T(8,128)S(1)}, f32[512,128]{1,0:T(8,128)S(1)}, u32[]{:S(2)}, u32[]{:S(2)}) collective-permute-start(f32[512,128]{1,0:T(8,128)S(1)} %get-tuple-element.38), channel_id=1, source_target_pairs={{0,1},{1,0},{2,3},{3,2},{4,6},{5,7},{6,4},{7,5},{8,9},{9,8},{10,11... | collective-permute-start | bytes 786440 | tf_op jit(solution)/shard_map/ppermute | solution.py:185
  37.9 12.9 %collective-permute-start.8 = (f32[64,512]{1,0:T(8,128)S(1)}, f32[64,512]{1,0:T(8,128)S(1)}, u32[]{:S(2)}, u32[]{:S(2)}) collective-permute-start(f32[64,512]{1,0:T(8,128)S(1)} %add.9.x), channel_id=1, source_target_pairs={{0,16},{8,24},{16,0},{24,8},{1,17},{9,25},{17,1},{25,9},{2,18},{10... | collective-permute-start | bytes 393224 | tf_op jit(solution)/shard_map/ppermute | solution.py:170
  40.5 11.8 %collective-permute-start.9 = (f32[64,512]{1,0:T(8,128)S(1)}, f32[64,512]{1,0:T(8,128)S(1)}, u32[]{:S(2)}, u32[]{:S(2)}) collective-permute-start(f32[64,512]{1,0:T(8,128)S(1)} %add.9.x), channel_id=1, source_target_pairs={{0,24},{8,16},{16,8},{24,0},{1,25},{9,17},{17,9},{25,1},{2,26},{10... | collective-permute-start | bytes 393224 | tf_op jit(solution)/shard_map/ppermute | solution.py:170
  40.5 15.2 %collective-permute-start.14 = (f32[128,512]{1,0:T(8,128)S(1)}, f32[128,512]{1,0:T(8,128)S(1)}, u32[]{:S(2)}, u32[]{:S(2)}) collective-permute-start(f32[128,512]{1,0:T(8,128)S(1)} %get-tuple-element.34.refs_8_.refs_0_), channel_id=1, source_target_pairs={{0,1},{1,0},{2,3},{3,2},{4,5},{5,4},{6,7},{7,6},{8,9},{9,8},{10,11... | collective-permute-start | bytes 786440 | tf_op jit(solution)/shard_map/ppermute | solution.py:170
  42.2 14.2 %collective-permute-start.17 = (f32[128,512]{1,0:T(8,128)S(1)}, f32[128,512]{1,0:T(8,128)S(1)}, u32[]{:S(2)}, u32[]{:S(2)}) collective-permute-start(f32[128,512]{1,0:T(8,128)S(1)} %get-tuple-element.33.refs_9_.refs_1_), channel_id=1, source_target_pairs={{0,2},{2,0},{1,3},{3,1},{4,6},{6,4},{5,7},{7,5},{8,10},{10,8},{9,1... | collective-permute-start | bytes 786440 | tf_op jit(solution)/shard_map/ppermute | solution.py:170
  43.7 14.1 %collective-permute-start.18 = (f32[128,512]{1,0:T(8,128)S(1)}, f32[128,512]{1,0:T(8,128)S(1)}, u32[]{:S(2)}, u32[]{:S(2)}) collective-permute-start(f32[128,512]{1,0:T(8,128)S(1)} %collective-permute-done.16.refs_12_.refs_4_), channel_id=1, source_target_pairs={{0,1},{1,0},{2,3},{3,2},{4,5},{5,4},{6,7},{7,6},{8,9},{9,8},{10,11... | collective-permute-start | bytes 786440 | tf_op jit(solution)/shard_map/ppermute | solution.py:170
  52.3 9.5 %collective-permute-start.19 = (f32[128,512]{1,0:T(8,128)S(1)}, f32[128,512]{1,0:T(8,128)S(1)}, u32[]{:S(2)}, u32[]{:S(2)}) collective-permute-start(f32[128,512]{1,0:T(8,128)S(1)} %collective-permute-done.15.refs_11_.refs_3_), channel_id=1, source_target_pairs={{0,2},{2,0},{1,3},{3,1},{4,6},{6,4},{5,7},{7,5},{8,10},{10,8},{9,1... | collective-permute-start | bytes 786440 | tf_op jit(solution)/shard_map/ppermute | solution.py:170
  55.8 15.4 %collective-permute-start.26 = (f32[256,384]{1,0:T(8,128)S(1)}, f32[256,384]{1,0:T(8,128)S(1)}, u32[]{:S(2)}, u32[]{:S(2)}) collective-permute-start(f32[256,384]{1,0:T(8,128)S(1)} %shard_map.47), channel_id=1, source_target_pairs={{0,4},{4,0},{1,5},{5,1},{2,6},{6,2},{3,7},{7,3},{8,12},{12,8},{9,1... | collective-permute-start | bytes 1179656 | tf_op jit(solution)/shard_map/ppermute | solution.py:170
  57.8 10.0 %collective-permute-start.30 = (f32[128,512]{1,0:T(8,128)S(1)}, f32[128,512]{1,0:T(8,128)S(1)}, u32[]{:S(2)}, u32[]{:S(2)}) collective-permute-start(f32[128,512]{1,0:T(8,128)S(1)} %get-tuple-element.32.refs_8_.refs_0_), channel_id=1, source_target_pairs={{0,2},{2,0},{1,3},{3,1},{4,6},{6,4},{5,7},{7,5},{8,10},{10,8},{9,1... | collective-permute-start | bytes 786440 | tf_op jit(solution)/shard_map/ppermute | solution.py:170
  59.3 10.3 %collective-permute-start.38 = (f32[512,128]{1,0:T(8,128)S(1)}, f32[512,128]{1,0:T(8,128)S(1)}, u32[]{:S(2)}, u32[]{:S(2)}) collective-permute-start(f32[512,128]{1,0:T(8,128)S(1)} %get-tuple-element.37), channel_id=1, source_target_pairs={{0,1},{1,0},{2,3},{3,2},{4,6},{5,7},{6,4},{7,5},{8,9},{9,8},{10,11... | collective-permute-start | bytes 786440 | tf_op jit(solution)/shard_map/ppermute | solution.py:185
  64.6 13.2 %collective-permute-start.22 = (f32[64,512]{1,0:T(8,128)S(1)}, f32[64,512]{1,0:T(8,128)S(1)}, u32[]{:S(2)}, u32[]{:S(2)}) collective-permute-start(f32[64,512]{1,0:T(8,128)S(1)} %add.10.x), channel_id=1, source_target_pairs={{0,16},{8,24},{16,0},{24,8},{1,17},{9,25},{17,1},{25,9},{2,18},{10... | collective-permute-start | bytes 393224 | tf_op jit(solution)/shard_map/ppermute | solution.py:170
  67.9 10.9 %collective-permute-start.23 = (f32[64,512]{1,0:T(8,128)S(1)}, f32[64,512]{1,0:T(8,128)S(1)}, u32[]{:S(2)}, u32[]{:S(2)}) collective-permute-start(f32[64,512]{1,0:T(8,128)S(1)} %add.10.x), channel_id=1, source_target_pairs={{0,24},{8,16},{16,8},{24,0},{1,25},{9,17},{17,9},{25,1},{2,26},{10... | collective-permute-start | bytes 393224 | tf_op jit(solution)/shard_map/ppermute | solution.py:170
  69.6 11.3 %collective-permute-start.28 = (f32[128,512]{1,0:T(8,128)S(1)}, f32[128,512]{1,0:T(8,128)S(1)}, u32[]{:S(2)}, u32[]{:S(2)}) collective-permute-start(f32[128,512]{1,0:T(8,128)S(1)} %get-tuple-element.32.refs_8_.refs_0_), channel_id=1, source_target_pairs={{0,1},{1,0},{2,3},{3,2},{4,5},{5,4},{6,7},{7,6},{8,9},{9,8},{10,11... | collective-permute-start | bytes 786440 | tf_op jit(solution)/shard_map/ppermute | solution.py:170
  71.2 9.6 %collective-permute-start.39 = (f32[256,128]{1,0:T(8,128)S(1)}, f32[256,128]{1,0:T(8,128)S(1)}, u32[]{:S(2)}, u32[]{:S(2)}) collective-permute-start(f32[256,128]{1,0:T(8,128)S(1)} %shard_map.52), channel_id=1, source_target_pairs={{0,2},{1,3},{2,0},{3,1},{4,5},{5,4},{6,7},{7,6},{8,10},{9,11},{10,... | collective-permute-start | bytes 393224 | tf_op jit(solution)/shard_map/ppermute | solution.py:187
  80.9 11.6 %collective-permute-start.40 = (f32[256,384]{1,0:T(8,128)S(1)}, f32[256,384]{1,0:T(8,128)S(1)}, u32[]{:S(2)}, u32[]{:S(2)}) collective-permute-start(f32[256,384]{1,0:T(8,128)S(1)} %shard_map.53), channel_id=1, source_target_pairs={{0,4},{4,0},{1,5},{5,1},{2,6},{6,2},{3,7},{7,3},{8,12},{12,8},{9,1... | collective-permute-start | bytes 1179656 | tf_op jit(solution)/shard_map/ppermute | solution.py:170
  89.9 12.9 %collective-permute-start.36 = (f32[64,512]{1,0:T(8,128)S(1)}, f32[64,512]{1,0:T(8,128)S(1)}, u32[]{:S(2)}, u32[]{:S(2)}) collective-permute-start(f32[64,512]{1,0:T(8,128)S(1)} %add.11.x), channel_id=1, source_target_pairs={{0,16},{8,24},{16,0},{24,8},{1,17},{9,25},{17,1},{25,9},{2,18},{10... | collective-permute-start | bytes 393224 | tf_op jit(solution)/shard_map/ppermute | solution.py:170
  91.1 11.7 %collective-permute-start.37 = (f32[64,512]{1,0:T(8,128)S(1)}, f32[64,512]{1,0:T(8,128)S(1)}, u32[]{:S(2)}, u32[]{:S(2)}) collective-permute-start(f32[64,512]{1,0:T(8,128)S(1)} %add.11.x), channel_id=1, source_target_pairs={{0,24},{8,16},{16,8},{24,0},{1,25},{9,17},{17,9},{25,1},{2,26},{10... | collective-permute-start | bytes 393224 | tf_op jit(solution)/shard_map/ppermute | solution.py:170
  (21 other events, 160.2 us)

commit v8 on v7

--- a/solution.py
+++ b/solution.py
@@ -35,11 +35,11 @@
     return both[:n] + (both[n:] + dot(ah, bl, dims))
 
 
-def dot_right(a, stacked, dims):
+def dot_right(a, b):
     ah, al = split(a)
-    n = stacked.shape[0] // 2
-    both = dot(ah, stacked, dims)
-    return both[:, :n] + (both[:, n:] + dot(al, stacked[:n], dims))
+    n = b.shape[1] // 2
+    both = dot(ah, b, NN)
+    return both[:, :n] + (both[:, n:] + dot(al, b[:, :n], NN))
 
 
 def place():
@@ -56,12 +56,11 @@
 
 
 def project(current, refs, v, skip=0):
-    total = None
+    x, r = [], []
     for block, first, ref in blocks_of(refs, skip):
-        x = current[window(v, block, first, ref.shape[0]), :]
-        part = dot_left(x.T, ref[...], NN)
-        total = part if total is None else total + part
-    return total
+        x.append(current[window(v, block, first, ref.shape[0]), :].T)
+        r.append(ref[...])
+    return dot_left(jnp.concatenate(x, axis=1), jnp.concatenate(r, axis=0), NN)
 
 
 def give_out(total, core, keep, send):
@@ -82,29 +81,40 @@
     give_out(total[...] + project(x, refs, v, PIECES - len(refs)), core, keep, send)
 
 
-def both_halves(mine, other, core):
+def coefficients(mine, other, core):
     a, b = mine[...], other[...]
     first = core == 0
-    return jnp.concatenate([jnp.where(first, a, b), jnp.where(first, b, a)], axis=0)
-
-
-def update(current, out, refs, coefficients, v):
-    stacked = stack(split(coefficients))
-    for block, first, ref in blocks_of(refs):
+    rows = jnp.concatenate([jnp.where(first, a, b), jnp.where(first, b, a)], axis=0)
+    return jnp.concatenate(split(rows.T), axis=1)
+
+
+def update(current, out, refs, c, v, after=None):
+    for i, (block, first, ref) in enumerate(blocks_of(refs)):
         at = window(v, block, first, ref.shape[0])
-        out[at, :] = current[at, :] - dot_right(ref[...], stacked, NT)
+        out[at, :] = current[at, :] - dot_right(ref[...], c)
+        if after is not None:
+            after(i, at)
 
 
 def turn_kernel(x, mine, other, *refs):
     v, core = place()
     old, new, (out, total) = refs[:PIECES], refs[PIECES:-2], refs[-2:]
-    update(x, out, old, both_halves(mine, other, core), v)
+    update(x, out, old, coefficients(mine, other, core), v)
     total[...] = project(out, new, v)
 
 
 def last_kernel(x, mine, other, *refs):
     v, core = place()
-    update(x, refs[PIECES], refs[:PIECES], both_halves(mine, other, core), v)
+    refs, (out, made, sems) = refs[:PIECES], refs[PIECES:]
+    copies = []
+
+    def leave(i, at):
+        copies.append(pltpu.make_async_copy(made.at[at, :], out.at[at, :], sems.at[i]))
+        copies[-1].start()
+
+    update(x, made, refs, coefficients(mine, other, core), v, leave)
+    for copy in copies:
+        copy.wait()
 
 
 def cut_kernel(x, out):
@@ -153,13 +163,14 @@
     return [pl.BlockSpec(memory_space=pltpu.VMEM)] * n
 
 
-def call(kernel, outs, args, flops):
+def call(kernel, outs, args, flops, out_space=pltpu.VMEM, scratch=()):
     nbytes = sum(4 * a.size for a in args) + sum(4 * o.size for o in outs)
     return pl.pallas_call(
         kernel,
         out_shape=outs,
         in_specs=vmem(len(args)),
-        out_specs=vmem(len(outs)),
+        out_specs=[pl.BlockSpec(memory_space=out_space)] * len(outs),
+        scratch_shapes=list(scratch),
         compiler_params=pltpu.CompilerParams(vmem_limit_bytes=8 * 2**20),
         cost_estimate=pl.CostEstimate(flops=flops, bytes_accessed=nbytes, transcendentals=0),
     )(*args)
@@ -170,9 +181,12 @@
     return lax.ppermute(a, axis, [(i, i ^ by) for i in range(n)])
 
 
-def gather(block):
+def gather(block, first):
     half = block.shape[0] // 2
-    a, b = block[:half], block[half:]
+    a = block[:half]
+    if first:
+        a, block = lax.optimization_barrier((a, block))
+    b = block[half:]
     ya, xb = swap(a, "y"), swap(b, "x")
     xa, yb = swap(a, "x"), swap(b, "y")
     return a, b, xa, xb, ya, yb, swap(ya, "x"), swap(xb, "y")
@@ -200,7 +214,7 @@
 
     sections, factors = {}, {}
     for k in reversed(range(panels)):
-        sections[k] = gather(reflectors[k])
+        sections[k] = gather(reflectors[k], k == top)
         factors[k] = gather_factor(triangles[k])
         if k == top:
             pieces = list(sections[k])
@@ -227,7 +241,8 @@
             current, sum_so_far = call(
                 turn_kernel, [whole, total], [current, *c, *sections[k], *ahead[k - 1]], work * 7 // 4
             )
-    return call(last_kernel, [whole], [current, *c, *sections[0]], work)[0]
+    scratch = [pltpu.VMEM(whole.shape, F32), pltpu.SemaphoreType.DMA((PIECES,))]
+    return call(last_kernel, [whole], [current, *c, *sections[0]], work, pl.ANY, scratch)[0]
 
 
 def general(vectors, reflectors, triangles):

time: 107 us -> 106 us (level)
  Pallas kernels: 9.28 us -> 7.28 us
    pallas_call x19, Pallas kernels: 9.28 us -> 7.28 us  [call(): pl.pallas_call(kernel, out_shape=outs, in_specs=vmem(len(args)), out_spec...]
    squeeze x0 -> x1, local copies, waits for them, and re-layouts: none -> 1.23 us  [fast(): sections[k] = gather(reflectors[k], k == top)]
  transfers between devices with their start and end apart: 42 -> 42, of which waited for: 19 -> 20; matrix products, arithmetic and copies ran while one was open for 1% -> 0% of each run, Pallas kernels for 7% -> 5%
where the time goes in v8:
time: 106 us; the launch traced here: 105 us
  waiting for transfers between devices  47.5 us (45%)
  starting transfers between devices  47.4 us (45%)
  Pallas kernels  7.28 us (7%)
  local copies, waits for them, and re-layouts  2.35 us (2%)
    ppermute x36, waiting for transfers between devices, swap(): return lax.ppermute(a, axis, [(i, i ^ by) for i in range(n)])  43 us
    ppermute x36, starting transfers between devices, swap(): return lax.ppermute(a, axis, [(i, i ^ by) for i in range(n)])  40.5 us
    pallas_call x19, Pallas kernels, call(): pl.pallas_call(kernel, out_shape=outs, in_specs=vmem(len(args)), out_spec...  7.28 us
    ppermute x3, starting transfers between devices, gather_factor(): lax.ppermute(own, axes, [(i, i ^ (2 if i >= n // 2 else 1)) for i in rang...  3.79 us
    ppermute x3, starting transfers between devices, gather_factor(): lax.ppermute(mine, axes, [(i, i ^ (1 if i >= n // 2 else 2)) for i in ran...  3.18 us
    ppermute x3, waiting for transfers between devices, gather_factor(): lax.ppermute(mine, axes, [(i, i ^ (1 if i >= n // 2 else 2)) for i in ran...  2.45 us
  transfers between devices with their start and end apart: 42, of which 20 were waited for; matrix products, arithmetic and copies ran while one was open for 0% of the time, Pallas kernels for 5%

profile of v8, /device:TPU:0, one launch (start us, length us, event | category | flops | bytes accessed | tf_op | source)
XLA Modules:
  0.0 105.0 jit_solution(653687510262298951)
XLA Ops:
  2.2 3.1 %collective-permute-start.2 = (f32[128,512]{1,0:T(8,128)S(1)}, f32[128,512]{1,0:T(8,128)S(1)}, u32[]{:S(2)}, u32[]{:S(2)}) collective-permute-start(f32[128,512]{1,0:T(8,128)S(1)} %slice_bitcast_fusion.8.refs_0_), channel_id=1, source_target_pairs={{0,2},{2,0},{1,3},{3,1},{4,6},{6,4},{5,7},{7,5},{8,10},{10,8},{9,1... | collective-permute-start | bytes 786440 | tf_op jit(solution)/shard_map/ppermute | solution.py:181
  5.3 1.6 %collective-permute-start.10 = (f32[512,128]{1,0:T(8,128)S(1)}, f32[512,128]{1,0:T(8,128)S(1)}, u32[]{:S(2)}, u32[]{:S(2)}) collective-permute-start(f32[512,128]{1,0:T(8,128)S(1)} %slice_bitcast_fusion.7), channel_id=1, source_target_pairs={{0,1},{1,0},{2,3},{3,2},{4,6},{5,7},{6,4},{7,5},{8,9},{9,8},{10,11... | collective-permute-start | bytes 786440 | tf_op jit(solution)/shard_map/ppermute | solution.py:199
  7.5 1.9 %collective-permute-start = (f32[128,512]{1,0:T(8,128)S(1)}, f32[128,512]{1,0:T(8,128)S(1)}, u32[]{:S(2)}, u32[]{:S(2)}) collective-permute-start(f32[128,512]{1,0:T(8,128)S(1)} %slice_bitcast_fusion.8.refs_0_), channel_id=1, source_target_pairs={{0,1},{1,0},{2,3},{3,2},{4,5},{5,4},{6,7},{7,6},{8,9},{9,8},{10,11... | collective-permute-start | bytes 786440 | tf_op jit(solution)/shard_map/ppermute | solution.py:181
  9.5 3.0 %collective-permute-done.2.refs_4_ = f32[128,512]{1,0:T(8,128)S(1)} collective-permute-done((f32[128,512]{1,0:T(8,128)S(1)}, f32[128,512]{1,0:T(8,128)S(1)}, u32[]{:S(2)}, u32[]{:S(2)}) %collective-permute-start.2) | collective-permute-done | bytes 262176 | tf_op jit(solution)/shard_map/ppermute | solution.py:181
  12.4 2.1 %collective-permute-done.10.x.first.refs_5_ = f32[512,128]{1,0:T(8,128)S(1)} collective-permute-done((f32[512,128]{1,0:T(8,128)S(1)}, f32[512,128]{1,0:T(8,128)S(1)}, u32[]{:S(2)}, u32[]{:S(2)}) %collective-permute-start.10) | collective-permute-done | bytes 262176 | tf_op jit(solution)/shard_map/ppermute | solution.py:199
  14.7 4.2 %collective-permute-done.1.refs_3_ = f32[128,512]{1,0:T(8,128)S(1)} collective-permute-done((f32[128,512]{1,0:T(8,128)S(1)}, f32[128,512]{1,0:T(8,128)S(1)}, u32[]{:S(2)}, u32[]{:S(2)}) %collective-permute-start.1) | collective-permute-done | bytes 262176 | tf_op jit(solution)/shard_map/ppermute | solution.py:181
  19.9 2.3 %collective-permute-start.15 = (f32[128,512]{1,0:T(8,128)S(1)}, f32[128,512]{1,0:T(8,128)S(1)}, u32[]{:S(2)}, u32[]{:S(2)}) collective-permute-start(f32[128,512]{1,0:T(8,128)S(1)} %get-tuple-element.37.refs_9_.refs_1_), channel_id=1, source_target_pairs={{0,1},{1,0},{2,3},{3,2},{4,5},{5,4},{6,7},{7,6},{8,9},{9,8},{10,11... | collective-permute-start | bytes 786440 | tf_op jit(solution)/shard_map/ppermute | solution.py:181
  24.6 3.4 %collective-permute-done.5.refs_1_.refs_7_ = f32[128,512]{1,0:T(8,128)S(1)} collective-permute-done((f32[128,512]{1,0:T(8,128)S(1)}, f32[128,512]{1,0:T(8,128)S(1)}, u32[]{:S(2)}, u32[]{:S(2)}) %collective-permute-start.5) | collective-permute-done | bytes 262176 | tf_op jit(solution)/shard_map/ppermute | solution.py:181
  28.0 1.7 %collective-permute-start.24 = (f32[512,128]{1,0:T(8,128)S(1)}, f32[512,128]{1,0:T(8,128)S(1)}, u32[]{:S(2)}, u32[]{:S(2)}) collective-permute-start(f32[512,128]{1,0:T(8,128)S(1)} %get-tuple-element.40), channel_id=1, source_target_pairs={{0,1},{1,0},{2,3},{3,2},{4,6},{5,7},{6,4},{7,5},{8,9},{9,8},{10,11... | collective-permute-start | bytes 786440 | tf_op jit(solution)/shard_map/ppermute | solution.py:199
  30.3 4.0 %collective-permute-done.4.refs_0_.refs_6_ = f32[128,512]{1,0:T(8,128)S(1)} collective-permute-done((f32[128,512]{1,0:T(8,128)S(1)}, f32[128,512]{1,0:T(8,128)S(1)}, u32[]{:S(2)}, u32[]{:S(2)}) %collective-permute-start.4) | collective-permute-done | bytes 262176 | tf_op jit(solution)/shard_map/ppermute | solution.py:181
  36.1 1.8 %collective-permute-start.7 = (f32[64,512]{1,0:T(8,128)S(1)}, f32[64,512]{1,0:T(8,128)S(1)}, u32[]{:S(2)}, u32[]{:S(2)}) collective-permute-start(f32[64,512]{1,0:T(8,128)S(1)} %add.9.x), channel_id=1, source_target_pairs={{0,8},{8,0},{16,24},{24,16},{1,9},{9,1},{17,25},{25,17},{2,10},{10... | collective-permute-start | bytes 393224 | tf_op jit(solution)/shard_map/ppermute | solution.py:181
  37.9 2.6 %collective-permute-start.8 = (f32[64,512]{1,0:T(8,128)S(1)}, f32[64,512]{1,0:T(8,128)S(1)}, u32[]{:S(2)}, u32[]{:S(2)}) collective-permute-start(f32[64,512]{1,0:T(8,128)S(1)} %add.9.x), channel_id=1, source_target_pairs={{0,16},{8,24},{16,0},{24,8},{1,17},{9,25},{17,1},{25,9},{2,18},{10... | collective-permute-start | bytes 393224 | tf_op jit(solution)/shard_map/ppermute | solution.py:181
  40.5 1.7 %collective-permute-start.14 = (f32[128,512]{1,0:T(8,128)S(1)}, f32[128,512]{1,0:T(8,128)S(1)}, u32[]{:S(2)}, u32[]{:S(2)}) collective-permute-start(f32[128,512]{1,0:T(8,128)S(1)} %get-tuple-element.38.refs_8_.refs_0_), channel_id=1, source_target_pairs={{0,1},{1,0},{2,3},{3,2},{4,5},{5,4},{6,7},{7,6},{8,9},{9,8},{10,11... | collective-permute-start | bytes 786440 | tf_op jit(solution)/shard_map/ppermute | solution.py:181
  43.8 1.6 %collective-permute-start.18 = (f32[128,512]{1,0:T(8,128)S(1)}, f32[128,512]{1,0:T(8,128)S(1)}, u32[]{:S(2)}, u32[]{:S(2)}) collective-permute-start(f32[128,512]{1,0:T(8,128)S(1)} %collective-permute-done.16.refs_12_.refs_4_), channel_id=1, source_target_pairs={{0,1},{1,0},{2,3},{3,2},{4,5},{5,4},{6,7},{7,6},{8,9},{9,8},{10,11... | collective-permute-start | bytes 786440 | tf_op jit(solution)/shard_map/ppermute | solution.py:181
  45.3 5.5 %collective-permute-done.8.refs_2_ = f32[64,512]{1,0:T(8,128)S(1)} collective-permute-done((f32[64,512]{1,0:T(8,128)S(1)}, f32[64,512]{1,0:T(8,128)S(1)}, u32[]{:S(2)}, u32[]{:S(2)}) %collective-permute-start.8) | collective-permute-done | bytes 131104 | tf_op jit(solution)/shard_map/ppermute | solution.py:181
  53.3 2.4 %collective-permute-done.25.across.refs_6_ = f32[256,128]{1,0:T(8,128)S(1)} collective-permute-done((f32[256,128]{1,0:T(8,128)S(1)}, f32[256,128]{1,0:T(8,128)S(1)}, u32[]{:S(2)}, u32[]{:S(2)}) %collective-permute-start.25) | collective-permute-done | bytes 131104 | tf_op jit(solution)/shard_map/ppermute | solution.py:201
  64.7 2.6 %collective-permute-start.22 = (f32[64,512]{1,0:T(8,128)S(1)}, f32[64,512]{1,0:T(8,128)S(1)}, u32[]{:S(2)}, u32[]{:S(2)}) collective-permute-start(f32[64,512]{1,0:T(8,128)S(1)} %add.10.x), channel_id=1, source_target_pairs={{0,16},{8,24},{16,0},{24,8},{1,17},{9,25},{17,1},{25,9},{2,18},{10... | collective-permute-start | bytes 393224 | tf_op jit(solution)/shard_map/ppermute | solution.py:181
  67.3 2.4 %collective-permute-start.23 = (f32[64,512]{1,0:T(8,128)S(1)}, f32[64,512]{1,0:T(8,128)S(1)}, u32[]{:S(2)}, u32[]{:S(2)}) collective-permute-start(f32[64,512]{1,0:T(8,128)S(1)} %add.10.x), channel_id=1, source_target_pairs={{0,24},{8,16},{16,8},{24,0},{1,25},{9,17},{17,9},{25,1},{2,26},{10... | collective-permute-start | bytes 393224 | tf_op jit(solution)/shard_map/ppermute | solution.py:181
  71.2 1.6 %collective-permute-start.39 = (f32[256,128]{1,0:T(8,128)S(1)}, f32[256,128]{1,0:T(8,128)S(1)}, u32[]{:S(2)}, u32[]{:S(2)}) collective-permute-start(f32[256,128]{1,0:T(8,128)S(1)} %shard_map.52), channel_id=1, source_target_pairs={{0,2},{1,3},{2,0},{3,1},{4,5},{5,4},{6,7},{7,6},{8,10},{9,11},{10,... | collective-permute-start | bytes 393224 | tf_op jit(solution)/shard_map/ppermute | solution.py:201
  73.3 4.2 %collective-permute-done.22.refs_2_ = f32[64,512]{1,0:T(8,128)S(1)} collective-permute-done((f32[64,512]{1,0:T(8,128)S(1)}, f32[64,512]{1,0:T(8,128)S(1)}, u32[]{:S(2)}, u32[]{:S(2)}) %collective-permute-start.22) | collective-permute-done | bytes 131104 | tf_op jit(solution)/shard_map/ppermute | solution.py:181
  84.1 1.6 %collective-permute-done.33.refs_1_.refs_7_ = f32[128,512]{1,0:T(8,128)S(1)} collective-permute-done((f32[128,512]{1,0:T(8,128)S(1)}, f32[128,512]{1,0:T(8,128)S(1)}, u32[]{:S(2)}, u32[]{:S(2)}) %collective-permute-start.33) | collective-permute-done | bytes 262176 | tf_op jit(solution)/shard_map/ppermute | solution.py:181
  89.0 2.0 %collective-permute-start.36 = (f32[64,512]{1,0:T(8,128)S(1)}, f32[64,512]{1,0:T(8,128)S(1)}, u32[]{:S(2)}, u32[]{:S(2)}) collective-permute-start(f32[64,512]{1,0:T(8,128)S(1)} %add.11.x), channel_id=1, source_target_pairs={{0,16},{8,24},{16,0},{24,8},{1,17},{9,25},{17,1},{25,9},{2,18},{10... | collective-permute-start | bytes 393224 | tf_op jit(solution)/shard_map/ppermute | solution.py:181
  92.3 3.2 %collective-permute-done.35.refs_1_ = f32[64,512]{1,0:T(8,128)S(1)} collective-permute-done((f32[64,512]{1,0:T(8,128)S(1)}, f32[64,512]{1,0:T(8,128)S(1)}, u32[]{:S(2)}, u32[]{:S(2)}) %collective-permute-start.35) | collective-permute-done | bytes 131104 | tf_op jit(solution)/shard_map/ppermute | solution.py:181
  96.7 4.9 %collective-permute-done.37.refs_3_ = f32[64,512]{1,0:T(8,128)S(1)} collective-permute-done((f32[64,512]{1,0:T(8,128)S(1)}, f32[64,512]{1,0:T(8,128)S(1)}, u32[]{:S(2)}, u32[]{:S(2)}) %collective-permute-start.37) | collective-permute-done | bytes 131104 | tf_op jit(solution)/shard_map/ppermute | solution.py:181
  (94 shorter events, 39.4 us)
Async XLA Ops:
  2.2 10.2 %collective-permute-start.2 = (f32[128,512]{1,0:T(8,128)S(1)}, f32[128,512]{1,0:T(8,128)S(1)}, u32[]{:S(2)}, u32[]{:S(2)}) collective-permute-start(f32[128,512]{1,0:T(8,128)S(1)} %slice_bitcast_fusion.8.refs_0_), channel_id=1, source_target_pairs={{0,2},{2,0},{1,3},{3,1},{4,6},{6,4},{5,7},{7,5},{8,10},{10,8},{9,1... | collective-permute-start | bytes 786440 | tf_op jit(solution)/shard_map/ppermute | solution.py:181
  6.9 12.0 %collective-permute-start.1 = (f32[128,512]{1,0:T(8,128)S(1)}, f32[128,512]{1,0:T(8,128)S(1)}, u32[]{:S(2)}, u32[]{:S(2)}) collective-permute-start(f32[128,512]{1,0:T(8,128)S(1)} %slice.55.refs_1_), channel_id=1, source_target_pairs={{0,1},{1,0},{2,3},{3,2},{4,5},{5,4},{6,7},{7,6},{8,9},{9,8},{10,11... | collective-permute-start | bytes 786440 | tf_op jit(solution)/shard_map/ppermute | solution.py:181
  7.5 15.4 %collective-permute-start.3 = (f32[128,512]{1,0:T(8,128)S(1)}, f32[128,512]{1,0:T(8,128)S(1)}, u32[]{:S(2)}, u32[]{:S(2)}) collective-permute-start(f32[128,512]{1,0:T(8,128)S(1)} %slice.55.refs_1_), channel_id=1, source_target_pairs={{0,2},{2,0},{1,3},{3,1},{4,6},{6,4},{5,7},{7,5},{8,10},{10,8},{9,1... | collective-permute-start | bytes 786440 | tf_op jit(solution)/shard_map/ppermute | solution.py:181
  7.5 16.9 %collective-permute-start = (f32[128,512]{1,0:T(8,128)S(1)}, f32[128,512]{1,0:T(8,128)S(1)}, u32[]{:S(2)}, u32[]{:S(2)}) collective-permute-start(f32[128,512]{1,0:T(8,128)S(1)} %slice_bitcast_fusion.8.refs_0_), channel_id=1, source_target_pairs={{0,1},{1,0},{2,3},{3,2},{4,5},{5,4},{6,7},{7,6},{8,9},{9,8},{10,11... | collective-permute-start | bytes 786440 | tf_op jit(solution)/shard_map/ppermute | solution.py:181
  19.9 18.1 %collective-permute-start.15 = (f32[128,512]{1,0:T(8,128)S(1)}, f32[128,512]{1,0:T(8,128)S(1)}, u32[]{:S(2)}, u32[]{:S(2)}) collective-permute-start(f32[128,512]{1,0:T(8,128)S(1)} %get-tuple-element.37.refs_9_.refs_1_), channel_id=1, source_target_pairs={{0,1},{1,0},{2,3},{3,2},{4,5},{5,4},{6,7},{7,6},{8,9},{9,8},{10,11... | collective-permute-start | bytes 786440 | tf_op jit(solution)/shard_map/ppermute | solution.py:181
  22.2 18.3 %collective-permute-start.16 = (f32[128,512]{1,0:T(8,128)S(1)}, f32[128,512]{1,0:T(8,128)S(1)}, u32[]{:S(2)}, u32[]{:S(2)}) collective-permute-start(f32[128,512]{1,0:T(8,128)S(1)} %get-tuple-element.38.refs_8_.refs_0_), channel_id=1, source_target_pairs={{0,2},{2,0},{1,3},{3,1},{4,6},{6,4},{5,7},{7,5},{8,10},{10,8},{9,1... | collective-permute-start | bytes 786440 | tf_op jit(solution)/shard_map/ppermute | solution.py:181
  22.9 11.4 %collective-permute-start.4 = (f32[128,512]{1,0:T(8,128)S(1)}, f32[128,512]{1,0:T(8,128)S(1)}, u32[]{:S(2)}, u32[]{:S(2)}) collective-permute-start(f32[128,512]{1,0:T(8,128)S(1)} %collective-permute-done.2.refs_4_), channel_id=1, source_target_pairs={{0,1},{1,0},{2,3},{3,2},{4,5},{5,4},{6,7},{7,6},{8,9},{9,8},{10,11... | collective-permute-start | bytes 786440 | tf_op jit(solution)/shard_map/ppermute | solution.py:181
  24.5 17.8 %collective-permute-start.12 = (f32[256,384]{1,0:T(8,128)S(1)}, f32[256,384]{1,0:T(8,128)S(1)}, u32[]{:S(2)}, u32[]{:S(2)}) collective-permute-start(f32[256,384]{1,0:T(8,128)S(1)} %shard_map.41), channel_id=1, source_target_pairs={{0,4},{4,0},{1,5},{5,1},{2,6},{6,2},{3,7},{7,3},{8,12},{12,8},{9,1... | collective-permute-start | bytes 1179656 | tf_op jit(solution)/shard_map/ppermute | solution.py:181
  28.0 12.5 %collective-permute-start.24 = (f32[512,128]{1,0:T(8,128)S(1)}, f32[512,128]{1,0:T(8,128)S(1)}, u32[]{:S(2)}, u32[]{:S(2)}) collective-permute-start(f32[512,128]{1,0:T(8,128)S(1)} %get-tuple-element.40), channel_id=1, source_target_pairs={{0,1},{1,0},{2,3},{3,2},{4,6},{5,7},{6,4},{7,5},{8,9},{9,8},{10,11... | collective-permute-start | bytes 786440 | tf_op jit(solution)/shard_map/ppermute | solution.py:199
  37.9 12.9 %collective-permute-start.8 = (f32[64,512]{1,0:T(8,128)S(1)}, f32[64,512]{1,0:T(8,128)S(1)}, u32[]{:S(2)}, u32[]{:S(2)}) collective-permute-start(f32[64,512]{1,0:T(8,128)S(1)} %add.9.x), channel_id=1, source_target_pairs={{0,16},{8,24},{16,0},{24,8},{1,17},{9,25},{17,1},{25,9},{2,18},{10... | collective-permute-start | bytes 393224 | tf_op jit(solution)/shard_map/ppermute | solution.py:181
  40.5 11.8 %collective-permute-start.9 = (f32[64,512]{1,0:T(8,128)S(1)}, f32[64,512]{1,0:T(8,128)S(1)}, u32[]{:S(2)}, u32[]{:S(2)}) collective-permute-start(f32[64,512]{1,0:T(8,128)S(1)} %add.9.x), channel_id=1, source_target_pairs={{0,24},{8,16},{16,8},{24,0},{1,25},{9,17},{17,9},{25,1},{2,26},{10... | collective-permute-start | bytes 393224 | tf_op jit(solution)/shard_map/ppermute | solution.py:181
  40.5 15.3 %collective-permute-start.14 = (f32[128,512]{1,0:T(8,128)S(1)}, f32[128,512]{1,0:T(8,128)S(1)}, u32[]{:S(2)}, u32[]{:S(2)}) collective-permute-start(f32[128,512]{1,0:T(8,128)S(1)} %get-tuple-element.38.refs_8_.refs_0_), channel_id=1, source_target_pairs={{0,1},{1,0},{2,3},{3,2},{4,5},{5,4},{6,7},{7,6},{8,9},{9,8},{10,11... | collective-permute-start | bytes 786440 | tf_op jit(solution)/shard_map/ppermute | solution.py:181
  42.2 14.2 %collective-permute-start.17 = (f32[128,512]{1,0:T(8,128)S(1)}, f32[128,512]{1,0:T(8,128)S(1)}, u32[]{:S(2)}, u32[]{:S(2)}) collective-permute-start(f32[128,512]{1,0:T(8,128)S(1)} %get-tuple-element.37.refs_9_.refs_1_), channel_id=1, source_target_pairs={{0,2},{2,0},{1,3},{3,1},{4,6},{6,4},{5,7},{7,5},{8,10},{10,8},{9,1... | collective-permute-start | bytes 786440 | tf_op jit(solution)/shard_map/ppermute | solution.py:181
  43.8 14.1 %collective-permute-start.18 = (f32[128,512]{1,0:T(8,128)S(1)}, f32[128,512]{1,0:T(8,128)S(1)}, u32[]{:S(2)}, u32[]{:S(2)}) collective-permute-start(f32[128,512]{1,0:T(8,128)S(1)} %collective-permute-done.16.refs_12_.refs_4_), channel_id=1, source_target_pairs={{0,1},{1,0},{2,3},{3,2},{4,5},{5,4},{6,7},{7,6},{8,9},{9,8},{10,11... | collective-permute-start | bytes 786440 | tf_op jit(solution)/shard_map/ppermute | solution.py:181
  55.8 15.4 %collective-permute-start.26 = (f32[256,384]{1,0:T(8,128)S(1)}, f32[256,384]{1,0:T(8,128)S(1)}, u32[]{:S(2)}, u32[]{:S(2)}) collective-permute-start(f32[256,384]{1,0:T(8,128)S(1)} %shard_map.47), channel_id=1, source_target_pairs={{0,4},{4,0},{1,5},{5,1},{2,6},{6,2},{3,7},{7,3},{8,12},{12,8},{9,1... | collective-permute-start | bytes 1179656 | tf_op jit(solution)/shard_map/ppermute | solution.py:181
  57.9 9.4 %collective-permute-start.30 = (f32[128,512]{1,0:T(8,128)S(1)}, f32[128,512]{1,0:T(8,128)S(1)}, u32[]{:S(2)}, u32[]{:S(2)}) collective-permute-start(f32[128,512]{1,0:T(8,128)S(1)} %get-tuple-element.36.refs_8_.refs_0_), channel_id=1, source_target_pairs={{0,2},{2,0},{1,3},{3,1},{4,6},{6,4},{5,7},{7,5},{8,10},{10,8},{9,1... | collective-permute-start | bytes 786440 | tf_op jit(solution)/shard_map/ppermute | solution.py:181
  59.4 10.3 %collective-permute-start.38 = (f32[512,128]{1,0:T(8,128)S(1)}, f32[512,128]{1,0:T(8,128)S(1)}, u32[]{:S(2)}, u32[]{:S(2)}) collective-permute-start(f32[512,128]{1,0:T(8,128)S(1)} %get-tuple-element.39), channel_id=1, source_target_pairs={{0,1},{1,0},{2,3},{3,2},{4,6},{5,7},{6,4},{7,5},{8,9},{9,8},{10,11... | collective-permute-start | bytes 786440 | tf_op jit(solution)/shard_map/ppermute | solution.py:199
  63.1 9.7 %collective-permute-start.21 = (f32[64,512]{1,0:T(8,128)S(1)}, f32[64,512]{1,0:T(8,128)S(1)}, u32[]{:S(2)}, u32[]{:S(2)}) collective-permute-start(f32[64,512]{1,0:T(8,128)S(1)} %add.10.x), channel_id=1, source_target_pairs={{0,8},{8,0},{16,24},{24,16},{1,9},{9,1},{17,25},{25,17},{2,10},{10... | collective-permute-start | bytes 393224 | tf_op jit(solution)/shard_map/ppermute | solution.py:181
  64.7 12.8 %collective-permute-start.22 = (f32[64,512]{1,0:T(8,128)S(1)}, f32[64,512]{1,0:T(8,128)S(1)}, u32[]{:S(2)}, u32[]{:S(2)}) collective-permute-start(f32[64,512]{1,0:T(8,128)S(1)} %add.10.x), channel_id=1, source_target_pairs={{0,16},{8,24},{16,0},{24,8},{1,17},{9,25},{17,1},{25,9},{2,18},{10... | collective-permute-start | bytes 393224 | tf_op jit(solution)/shard_map/ppermute | solution.py:181
  67.3 11.5 %collective-permute-start.23 = (f32[64,512]{1,0:T(8,128)S(1)}, f32[64,512]{1,0:T(8,128)S(1)}, u32[]{:S(2)}, u32[]{:S(2)}) collective-permute-start(f32[64,512]{1,0:T(8,128)S(1)} %add.10.x), channel_id=1, source_target_pairs={{0,24},{8,16},{16,8},{24,0},{1,25},{9,17},{17,9},{25,1},{2,26},{10... | collective-permute-start | bytes 393224 | tf_op jit(solution)/shard_map/ppermute | solution.py:181
  69.7 11.2 %collective-permute-start.28 = (f32[128,512]{1,0:T(8,128)S(1)}, f32[128,512]{1,0:T(8,128)S(1)}, u32[]{:S(2)}, u32[]{:S(2)}) collective-permute-start(f32[128,512]{1,0:T(8,128)S(1)} %get-tuple-element.36.refs_8_.refs_0_), channel_id=1, source_target_pairs={{0,1},{1,0},{2,3},{3,2},{4,5},{5,4},{6,7},{7,6},{8,9},{9,8},{10,11... | collective-permute-start | bytes 786440 | tf_op jit(solution)/shard_map/ppermute | solution.py:181
  71.2 9.6 %collective-permute-start.39 = (f32[256,128]{1,0:T(8,128)S(1)}, f32[256,128]{1,0:T(8,128)S(1)}, u32[]{:S(2)}, u32[]{:S(2)}) collective-permute-start(f32[256,128]{1,0:T(8,128)S(1)} %shard_map.52), channel_id=1, source_target_pairs={{0,2},{1,3},{2,0},{3,1},{4,5},{5,4},{6,7},{7,6},{8,10},{9,11},{10,... | collective-permute-start | bytes 393224 | tf_op jit(solution)/shard_map/ppermute | solution.py:201
  80.9 11.4 %collective-permute-start.40 = (f32[256,384]{1,0:T(8,128)S(1)}, f32[256,384]{1,0:T(8,128)S(1)}, u32[]{:S(2)}, u32[]{:S(2)}) collective-permute-start(f32[256,384]{1,0:T(8,128)S(1)} %shard_map.53), channel_id=1, source_target_pairs={{0,4},{4,0},{1,5},{5,1},{2,6},{6,2},{3,7},{7,3},{8,12},{12,8},{9,1... | collective-permute-start | bytes 1179656 | tf_op jit(solution)/shard_map/ppermute | solution.py:181
  90.9 10.6 %collective-permute-start.37 = (f32[64,512]{1,0:T(8,128)S(1)}, f32[64,512]{1,0:T(8,128)S(1)}, u32[]{:S(2)}, u32[]{:S(2)}) collective-permute-start(f32[64,512]{1,0:T(8,128)S(1)} %add.11.x), channel_id=1, source_target_pairs={{0,24},{8,16},{16,8},{24,0},{1,25},{9,17},{17,9},{25,1},{2,26},{10... | collective-permute-start | bytes 393224 | tf_op jit(solution)/shard_map/ppermute | solution.py:181
  (21 other events, 145.0 us)

commit v9 on v8

--- a/solution.py
+++ b/solution.py
@@ -181,12 +181,9 @@
     return lax.ppermute(a, axis, [(i, i ^ by) for i in range(n)])
 
 
-def gather(block, first):
+def gather(block):
     half = block.shape[0] // 2
-    a = block[:half]
-    if first:
-        a, block = lax.optimization_barrier((a, block))
-    b = block[half:]
+    a, b = block[:half], block[half:]
     ya, xb = swap(a, "y"), swap(b, "x")
     xa, yb = swap(a, "x"), swap(b, "y")
     return a, b, xa, xb, ya, yb, swap(ya, "x"), swap(xb, "y")
@@ -214,7 +211,7 @@
 
     sections, factors = {}, {}
     for k in reversed(range(panels)):
-        sections[k] = gather(reflectors[k], k == top)
+        sections[k] = gather(reflectors[k])
         factors[k] = gather_factor(triangles[k])
         if k == top:
             pieces = list(sections[k])

time: 106 us -> 106 us (level)
    squeeze x1 -> x0, local copies, waits for them, and re-layouts: 1.23 us -> none  [fast(): sections[k] = gather(reflectors[k], k == top)]
  transfers between devices with their start and end apart: 42 -> 42, of which waited for: 20 -> 21; matrix products, arithmetic and copies ran while one was open for 0% -> 1% of each run, Pallas kernels for 5% -> 5%
where the time goes in v9:
time: 106 us; the launch traced here: 105 us
  waiting for transfers between devices  47.7 us (45%)
  starting transfers between devices  47.2 us (45%)
  Pallas kernels  7.28 us (7%)
  local copies, waits for them, and re-layouts  2.27 us (2%)
    ppermute x36, waiting for transfers between devices, swap(): return lax.ppermute(a, axis, [(i, i ^ by) for i in range(n)])  42.2 us
    ppermute x36, starting transfers between devices, swap(): return lax.ppermute(a, axis, [(i, i ^ by) for i in range(n)])  39.9 us
    pallas_call x19, Pallas kernels, call(): pl.pallas_call(kernel, out_shape=outs, in_specs=vmem(len(args)), out_spec...  7.28 us
    ppermute x3, starting transfers between devices, gather_factor(): lax.ppermute(own, axes, [(i, i ^ (2 if i >= n // 2 else 1)) for i in rang...  4.07 us
    ppermute x3, starting transfers between devices, gather_factor(): lax.ppermute(mine, axes, [(i, i ^ (1 if i >= n // 2 else 2)) for i in ran...  3.18 us
    ppermute x3, waiting for transfers between devices, gather_factor(): lax.ppermute(own, axes, [(i, i ^ (2 if i >= n // 2 else 1)) for i in rang...  3.06 us
    ppermute x3, waiting for transfers between devices, gather_factor(): lax.ppermute(mine, axes, [(i, i ^ (1 if i >= n // 2 else 2)) for i in ran...  2.45 us
  transfers between devices with their start and end apart: 42, of which 21 were waited for; matrix products, arithmetic and copies ran while one was open for 1% of the time, Pallas kernels for 5%

profile of v9, /device:TPU:0, one launch (start us, length us, event | category | flops | bytes accessed | tf_op | source)
XLA Modules:
  0.0 104.8 jit_solution(2728813068381036252)
XLA Ops:
  1.2 3.1 %collective-permute-start.2 = (f32[128,512]{1,0:T(8,128)S(1)}, f32[128,512]{1,0:T(8,128)S(1)}, u32[]{:S(2)}, u32[]{:S(2)}) collective-permute-start(f32[128,512]{1,0:T(8,128)S(1)} %get-tuple-element.36.refs_0_), channel_id=1, source_target_pairs={{0,2},{2,0},{1,3},{3,1},{4,6},{6,4},{5,7},{7,5},{8,10},{10,8},{9,1... | collective-permute-start | bytes 786440 | tf_op jit(solution)/shard_map/ppermute | solution.py:181
  9.3 2.1 %collective-permute-done.2.refs_4_ = f32[128,512]{1,0:T(8,128)S(1)} collective-permute-done((f32[128,512]{1,0:T(8,128)S(1)}, f32[128,512]{1,0:T(8,128)S(1)}, u32[]{:S(2)}, u32[]{:S(2)}) %collective-permute-start.2) | collective-permute-done | bytes 262176 | tf_op jit(solution)/shard_map/ppermute | solution.py:181
  11.4 3.1 %collective-permute-done.10.x.first.refs_5_ = f32[512,128]{1,0:T(8,128)S(1)} collective-permute-done((f32[512,128]{1,0:T(8,128)S(1)}, f32[512,128]{1,0:T(8,128)S(1)}, u32[]{:S(2)}, u32[]{:S(2)}) %collective-permute-start.10) | collective-permute-done | bytes 262176 | tf_op jit(solution)/shard_map/ppermute | solution.py:196
  14.6 5.1 %collective-permute-done.1.refs_3_ = f32[128,512]{1,0:T(8,128)S(1)} collective-permute-done((f32[128,512]{1,0:T(8,128)S(1)}, f32[128,512]{1,0:T(8,128)S(1)}, u32[]{:S(2)}, u32[]{:S(2)}) %collective-permute-start.1) | collective-permute-done | bytes 262176 | tf_op jit(solution)/shard_map/ppermute | solution.py:181
  19.9 2.4 %collective-permute-start.15 = (f32[128,512]{1,0:T(8,128)S(1)}, f32[128,512]{1,0:T(8,128)S(1)}, u32[]{:S(2)}, u32[]{:S(2)}) collective-permute-start(f32[128,512]{1,0:T(8,128)S(1)} %get-tuple-element.33.refs_9_.refs_1_), channel_id=1, source_target_pairs={{0,1},{1,0},{2,3},{3,2},{4,5},{5,4},{6,7},{7,6},{8,9},{9,8},{10,11... | collective-permute-start | bytes 786440 | tf_op jit(solution)/shard_map/ppermute | solution.py:181
  23.4 1.9 %collective-permute-done.refs_2_ = f32[128,512]{1,0:T(8,128)S(1)} collective-permute-done((f32[128,512]{1,0:T(8,128)S(1)}, f32[128,512]{1,0:T(8,128)S(1)}, u32[]{:S(2)}, u32[]{:S(2)}) %collective-permute-start) | collective-permute-done | bytes 262176 | tf_op jit(solution)/shard_map/ppermute | solution.py:181
  25.3 1.6 %collective-permute-start.4 = (f32[128,512]{1,0:T(8,128)S(1)}, f32[128,512]{1,0:T(8,128)S(1)}, u32[]{:S(2)}, u32[]{:S(2)}) collective-permute-start(f32[128,512]{1,0:T(8,128)S(1)} %collective-permute-done.2.refs_4_), channel_id=1, source_target_pairs={{0,1},{1,0},{2,3},{3,2},{4,5},{5,4},{6,7},{7,6},{8,9},{9,8},{10,11... | collective-permute-start | bytes 786440 | tf_op jit(solution)/shard_map/ppermute | solution.py:181
  27.9 2.0 %collective-permute-start.24 = (f32[512,128]{1,0:T(8,128)S(1)}, f32[512,128]{1,0:T(8,128)S(1)}, u32[]{:S(2)}, u32[]{:S(2)}) collective-permute-start(f32[512,128]{1,0:T(8,128)S(1)} %get-tuple-element.38), channel_id=1, source_target_pairs={{0,1},{1,0},{2,3},{3,2},{4,6},{5,7},{6,4},{7,5},{8,9},{9,8},{10,11... | collective-permute-start | bytes 786440 | tf_op jit(solution)/shard_map/ppermute | solution.py:196
  30.5 3.7 %collective-permute-done.4.refs_0_.refs_6_ = f32[128,512]{1,0:T(8,128)S(1)} collective-permute-done((f32[128,512]{1,0:T(8,128)S(1)}, f32[128,512]{1,0:T(8,128)S(1)}, u32[]{:S(2)}, u32[]{:S(2)}) %collective-permute-start.4) | collective-permute-done | bytes 262176 | tf_op jit(solution)/shard_map/ppermute | solution.py:181
  36.0 1.8 %collective-permute-start.7 = (f32[64,512]{1,0:T(8,128)S(1)}, f32[64,512]{1,0:T(8,128)S(1)}, u32[]{:S(2)}, u32[]{:S(2)}) collective-permute-start(f32[64,512]{1,0:T(8,128)S(1)} %add.9.x), channel_id=1, source_target_pairs={{0,8},{8,0},{16,24},{24,16},{1,9},{9,1},{17,25},{25,17},{2,10},{10... | collective-permute-start | bytes 393224 | tf_op jit(solution)/shard_map/ppermute | solution.py:181
  37.8 2.6 %collective-permute-start.8 = (f32[64,512]{1,0:T(8,128)S(1)}, f32[64,512]{1,0:T(8,128)S(1)}, u32[]{:S(2)}, u32[]{:S(2)}) collective-permute-start(f32[64,512]{1,0:T(8,128)S(1)} %add.9.x), channel_id=1, source_target_pairs={{0,16},{8,24},{16,0},{24,8},{1,17},{9,25},{17,1},{25,9},{2,18},{10... | collective-permute-start | bytes 393224 | tf_op jit(solution)/shard_map/ppermute | solution.py:181
  40.4 1.6 %collective-permute-start.14 = (f32[128,512]{1,0:T(8,128)S(1)}, f32[128,512]{1,0:T(8,128)S(1)}, u32[]{:S(2)}, u32[]{:S(2)}) collective-permute-start(f32[128,512]{1,0:T(8,128)S(1)} %get-tuple-element.34.refs_8_.refs_0_), channel_id=1, source_target_pairs={{0,1},{1,0},{2,3},{3,2},{4,5},{5,4},{6,7},{7,6},{8,9},{9,8},{10,11... | collective-permute-start | bytes 786440 | tf_op jit(solution)/shard_map/ppermute | solution.py:181
  43.6 1.6 %collective-permute-start.18 = (f32[128,512]{1,0:T(8,128)S(1)}, f32[128,512]{1,0:T(8,128)S(1)}, u32[]{:S(2)}, u32[]{:S(2)}) collective-permute-start(f32[128,512]{1,0:T(8,128)S(1)} %collective-permute-done.16.refs_12_.refs_4_), channel_id=1, source_target_pairs={{0,1},{1,0},{2,3},{3,2},{4,5},{5,4},{6,7},{7,6},{8,9},{9,8},{10,11... | collective-permute-start | bytes 786440 | tf_op jit(solution)/shard_map/ppermute | solution.py:181
  45.2 5.5 %collective-permute-done.8.refs_2_ = f32[64,512]{1,0:T(8,128)S(1)} collective-permute-done((f32[64,512]{1,0:T(8,128)S(1)}, f32[64,512]{1,0:T(8,128)S(1)}, u32[]{:S(2)}, u32[]{:S(2)}) %collective-permute-start.8) | collective-permute-done | bytes 131104 | tf_op jit(solution)/shard_map/ppermute | solution.py:181
  53.2 2.4 %collective-permute-done.25.across.refs_6_ = f32[256,128]{1,0:T(8,128)S(1)} collective-permute-done((f32[256,128]{1,0:T(8,128)S(1)}, f32[256,128]{1,0:T(8,128)S(1)}, u32[]{:S(2)}, u32[]{:S(2)}) %collective-permute-start.25) | collective-permute-done | bytes 131104 | tf_op jit(solution)/shard_map/ppermute | solution.py:198
  64.5 2.6 %collective-permute-start.22 = (f32[64,512]{1,0:T(8,128)S(1)}, f32[64,512]{1,0:T(8,128)S(1)}, u32[]{:S(2)}, u32[]{:S(2)}) collective-permute-start(f32[64,512]{1,0:T(8,128)S(1)} %add.10.x), channel_id=1, source_target_pairs={{0,16},{8,24},{16,0},{24,8},{1,17},{9,25},{17,1},{25,9},{2,18},{10... | collective-permute-start | bytes 393224 | tf_op jit(solution)/shard_map/ppermute | solution.py:181
  67.1 2.4 %collective-permute-start.23 = (f32[64,512]{1,0:T(8,128)S(1)}, f32[64,512]{1,0:T(8,128)S(1)}, u32[]{:S(2)}, u32[]{:S(2)}) collective-permute-start(f32[64,512]{1,0:T(8,128)S(1)} %add.10.x), channel_id=1, source_target_pairs={{0,24},{8,16},{16,8},{24,0},{1,25},{9,17},{17,9},{25,1},{2,26},{10... | collective-permute-start | bytes 393224 | tf_op jit(solution)/shard_map/ppermute | solution.py:181
  71.1 1.6 %collective-permute-start.39 = (f32[256,128]{1,0:T(8,128)S(1)}, f32[256,128]{1,0:T(8,128)S(1)}, u32[]{:S(2)}, u32[]{:S(2)}) collective-permute-start(f32[256,128]{1,0:T(8,128)S(1)} %shard_map.52), channel_id=1, source_target_pairs={{0,2},{1,3},{2,0},{3,1},{4,5},{5,4},{6,7},{7,6},{8,10},{9,11},{10,... | collective-permute-start | bytes 393224 | tf_op jit(solution)/shard_map/ppermute | solution.py:198
  73.2 4.2 %collective-permute-done.22.refs_2_ = f32[64,512]{1,0:T(8,128)S(1)} collective-permute-done((f32[64,512]{1,0:T(8,128)S(1)}, f32[64,512]{1,0:T(8,128)S(1)}, u32[]{:S(2)}, u32[]{:S(2)}) %collective-permute-start.22) | collective-permute-done | bytes 131104 | tf_op jit(solution)/shard_map/ppermute | solution.py:181
  83.9 1.6 %collective-permute-done.33.refs_1_.refs_7_ = f32[128,512]{1,0:T(8,128)S(1)} collective-permute-done((f32[128,512]{1,0:T(8,128)S(1)}, f32[128,512]{1,0:T(8,128)S(1)}, u32[]{:S(2)}, u32[]{:S(2)}) %collective-permute-start.33) | collective-permute-done | bytes 262176 | tf_op jit(solution)/shard_map/ppermute | solution.py:181
  87.2 1.6 %collective-permute-start.35 = (f32[64,512]{1,0:T(8,128)S(1)}, f32[64,512]{1,0:T(8,128)S(1)}, u32[]{:S(2)}, u32[]{:S(2)}) collective-permute-start(f32[64,512]{1,0:T(8,128)S(1)} %add.11.x), channel_id=1, source_target_pairs={{0,8},{8,0},{16,24},{24,16},{1,9},{9,1},{17,25},{25,17},{2,10},{10... | collective-permute-start | bytes 393224 | tf_op jit(solution)/shard_map/ppermute | solution.py:181
  88.8 2.0 %collective-permute-start.36 = (f32[64,512]{1,0:T(8,128)S(1)}, f32[64,512]{1,0:T(8,128)S(1)}, u32[]{:S(2)}, u32[]{:S(2)}) collective-permute-start(f32[64,512]{1,0:T(8,128)S(1)} %add.11.x), channel_id=1, source_target_pairs={{0,16},{8,24},{16,0},{24,8},{1,17},{9,25},{17,1},{25,9},{2,18},{10... | collective-permute-start | bytes 393224 | tf_op jit(solution)/shard_map/ppermute | solution.py:181
  92.2 3.2 %collective-permute-done.35.refs_1_ = f32[64,512]{1,0:T(8,128)S(1)} collective-permute-done((f32[64,512]{1,0:T(8,128)S(1)}, f32[64,512]{1,0:T(8,128)S(1)}, u32[]{:S(2)}, u32[]{:S(2)}) %collective-permute-start.35) | collective-permute-done | bytes 131104 | tf_op jit(solution)/shard_map/ppermute | solution.py:181
  96.5 4.9 %collective-permute-done.37.refs_3_ = f32[64,512]{1,0:T(8,128)S(1)} collective-permute-done((f32[64,512]{1,0:T(8,128)S(1)}, f32[64,512]{1,0:T(8,128)S(1)}, u32[]{:S(2)}, u32[]{:S(2)}) %collective-permute-start.37) | collective-permute-done | bytes 131104 | tf_op jit(solution)/shard_map/ppermute | solution.py:181
  (92 shorter events, 40.2 us)
Async XLA Ops:
  1.2 10.2 %collective-permute-start.2 = (f32[128,512]{1,0:T(8,128)S(1)}, f32[128,512]{1,0:T(8,128)S(1)}, u32[]{:S(2)}, u32[]{:S(2)}) collective-permute-start(f32[128,512]{1,0:T(8,128)S(1)} %get-tuple-element.36.refs_0_), channel_id=1, source_target_pairs={{0,2},{2,0},{1,3},{3,1},{4,6},{6,4},{5,7},{7,5},{8,10},{10,8},{9,1... | collective-permute-start | bytes 786440 | tf_op jit(solution)/shard_map/ppermute | solution.py:181
  5.2 9.2 %collective-permute-start.10 = (f32[512,128]{1,0:T(8,128)S(1)}, f32[512,128]{1,0:T(8,128)S(1)}, u32[]{:S(2)}, u32[]{:S(2)}) collective-permute-start(f32[512,128]{1,0:T(8,128)S(1)} %slice_bitcast_fusion.6), channel_id=1, source_target_pairs={{0,1},{1,0},{2,3},{3,2},{4,6},{5,7},{6,4},{7,5},{8,9},{9,8},{10,11... | collective-permute-start | bytes 786440 | tf_op jit(solution)/shard_map/ppermute | solution.py:196
  6.8 12.9 %collective-permute-start.1 = (f32[128,512]{1,0:T(8,128)S(1)}, f32[128,512]{1,0:T(8,128)S(1)}, u32[]{:S(2)}, u32[]{:S(2)}) collective-permute-start(f32[128,512]{1,0:T(8,128)S(1)} %get-tuple-element.35.refs_1_), channel_id=1, source_target_pairs={{0,1},{1,0},{2,3},{3,2},{4,5},{5,4},{6,7},{7,6},{8,9},{9,8},{10,11... | collective-permute-start | bytes 786440 | tf_op jit(solution)/shard_map/ppermute | solution.py:181
  7.3 18.0 %collective-permute-start = (f32[128,512]{1,0:T(8,128)S(1)}, f32[128,512]{1,0:T(8,128)S(1)}, u32[]{:S(2)}, u32[]{:S(2)}) collective-permute-start(f32[128,512]{1,0:T(8,128)S(1)} %get-tuple-element.36.refs_0_), channel_id=1, source_target_pairs={{0,1},{1,0},{2,3},{3,2},{4,5},{5,4},{6,7},{7,6},{8,9},{9,8},{10,11... | collective-permute-start | bytes 786440 | tf_op jit(solution)/shard_map/ppermute | solution.py:181
  8.8 18.0 %collective-permute-start.3 = (f32[128,512]{1,0:T(8,128)S(1)}, f32[128,512]{1,0:T(8,128)S(1)}, u32[]{:S(2)}, u32[]{:S(2)}) collective-permute-start(f32[128,512]{1,0:T(8,128)S(1)} %get-tuple-element.35.refs_1_), channel_id=1, source_target_pairs={{0,2},{2,0},{1,3},{3,1},{4,6},{6,4},{5,7},{7,5},{8,10},{10,8},{9,1... | collective-permute-start | bytes 786440 | tf_op jit(solution)/shard_map/ppermute | solution.py:181
  19.9 17.9 %collective-permute-start.15 = (f32[128,512]{1,0:T(8,128)S(1)}, f32[128,512]{1,0:T(8,128)S(1)}, u32[]{:S(2)}, u32[]{:S(2)}) collective-permute-start(f32[128,512]{1,0:T(8,128)S(1)} %get-tuple-element.33.refs_9_.refs_1_), channel_id=1, source_target_pairs={{0,1},{1,0},{2,3},{3,2},{4,5},{5,4},{6,7},{7,6},{8,9},{9,8},{10,11... | collective-permute-start | bytes 786440 | tf_op jit(solution)/shard_map/ppermute | solution.py:181
  22.2 18.1 %collective-permute-start.16 = (f32[128,512]{1,0:T(8,128)S(1)}, f32[128,512]{1,0:T(8,128)S(1)}, u32[]{:S(2)}, u32[]{:S(2)}) collective-permute-start(f32[128,512]{1,0:T(8,128)S(1)} %get-tuple-element.34.refs_8_.refs_0_), channel_id=1, source_target_pairs={{0,2},{2,0},{1,3},{3,1},{4,6},{6,4},{5,7},{7,5},{8,10},{10,8},{9,1... | collective-permute-start | bytes 786440 | tf_op jit(solution)/shard_map/ppermute | solution.py:181
  26.8 15.2 %collective-permute-start.12 = (f32[256,384]{1,0:T(8,128)S(1)}, f32[256,384]{1,0:T(8,128)S(1)}, u32[]{:S(2)}, u32[]{:S(2)}) collective-permute-start(f32[256,384]{1,0:T(8,128)S(1)} %shard_map.41), channel_id=1, source_target_pairs={{0,4},{4,0},{1,5},{5,1},{2,6},{6,2},{3,7},{7,3},{8,12},{12,8},{9,1... | collective-permute-start | bytes 1179656 | tf_op jit(solution)/shard_map/ppermute | solution.py:181
  27.9 12.5 %collective-permute-start.24 = (f32[512,128]{1,0:T(8,128)S(1)}, f32[512,128]{1,0:T(8,128)S(1)}, u32[]{:S(2)}, u32[]{:S(2)}) collective-permute-start(f32[512,128]{1,0:T(8,128)S(1)} %get-tuple-element.38), channel_id=1, source_target_pairs={{0,1},{1,0},{2,3},{3,2},{4,6},{5,7},{6,4},{7,5},{8,9},{9,8},{10,11... | collective-permute-start | bytes 786440 | tf_op jit(solution)/shard_map/ppermute | solution.py:196
  37.8 12.9 %collective-permute-start.8 = (f32[64,512]{1,0:T(8,128)S(1)}, f32[64,512]{1,0:T(8,128)S(1)}, u32[]{:S(2)}, u32[]{:S(2)}) collective-permute-start(f32[64,512]{1,0:T(8,128)S(1)} %add.9.x), channel_id=1, source_target_pairs={{0,16},{8,24},{16,0},{24,8},{1,17},{9,25},{17,1},{25,9},{2,18},{10... | collective-permute-start | bytes 393224 | tf_op jit(solution)/shard_map/ppermute | solution.py:181
  40.4 11.8 %collective-permute-start.9 = (f32[64,512]{1,0:T(8,128)S(1)}, f32[64,512]{1,0:T(8,128)S(1)}, u32[]{:S(2)}, u32[]{:S(2)}) collective-permute-start(f32[64,512]{1,0:T(8,128)S(1)} %add.9.x), channel_id=1, source_target_pairs={{0,24},{8,16},{16,8},{24,0},{1,25},{9,17},{17,9},{25,1},{2,26},{10... | collective-permute-start | bytes 393224 | tf_op jit(solution)/shard_map/ppermute | solution.py:181
  40.4 15.2 %collective-permute-start.14 = (f32[128,512]{1,0:T(8,128)S(1)}, f32[128,512]{1,0:T(8,128)S(1)}, u32[]{:S(2)}, u32[]{:S(2)}) collective-permute-start(f32[128,512]{1,0:T(8,128)S(1)} %get-tuple-element.34.refs_8_.refs_0_), channel_id=1, source_target_pairs={{0,1},{1,0},{2,3},{3,2},{4,5},{5,4},{6,7},{7,6},{8,9},{9,8},{10,11... | collective-permute-start | bytes 786440 | tf_op jit(solution)/shard_map/ppermute | solution.py:181
  42.1 14.2 %collective-permute-start.17 = (f32[128,512]{1,0:T(8,128)S(1)}, f32[128,512]{1,0:T(8,128)S(1)}, u32[]{:S(2)}, u32[]{:S(2)}) collective-permute-start(f32[128,512]{1,0:T(8,128)S(1)} %get-tuple-element.33.refs_9_.refs_1_), channel_id=1, source_target_pairs={{0,2},{2,0},{1,3},{3,1},{4,6},{6,4},{5,7},{7,5},{8,10},{10,8},{9,1... | collective-permute-start | bytes 786440 | tf_op jit(solution)/shard_map/ppermute | solution.py:181
  43.6 14.1 %collective-permute-start.18 = (f32[128,512]{1,0:T(8,128)S(1)}, f32[128,512]{1,0:T(8,128)S(1)}, u32[]{:S(2)}, u32[]{:S(2)}) collective-permute-start(f32[128,512]{1,0:T(8,128)S(1)} %collective-permute-done.16.refs_12_.refs_4_), channel_id=1, source_target_pairs={{0,1},{1,0},{2,3},{3,2},{4,5},{5,4},{6,7},{7,6},{8,9},{9,8},{10,11... | collective-permute-start | bytes 786440 | tf_op jit(solution)/shard_map/ppermute | solution.py:181
  55.7 15.4 %collective-permute-start.26 = (f32[256,384]{1,0:T(8,128)S(1)}, f32[256,384]{1,0:T(8,128)S(1)}, u32[]{:S(2)}, u32[]{:S(2)}) collective-permute-start(f32[256,384]{1,0:T(8,128)S(1)} %shard_map.47), channel_id=1, source_target_pairs={{0,4},{4,0},{1,5},{5,1},{2,6},{6,2},{3,7},{7,3},{8,12},{12,8},{9,1... | collective-permute-start | bytes 1179656 | tf_op jit(solution)/shard_map/ppermute | solution.py:181
  57.7 9.4 %collective-permute-start.30 = (f32[128,512]{1,0:T(8,128)S(1)}, f32[128,512]{1,0:T(8,128)S(1)}, u32[]{:S(2)}, u32[]{:S(2)}) collective-permute-start(f32[128,512]{1,0:T(8,128)S(1)} %get-tuple-element.32.refs_8_.refs_0_), channel_id=1, source_target_pairs={{0,2},{2,0},{1,3},{3,1},{4,6},{6,4},{5,7},{7,5},{8,10},{10,8},{9,1... | collective-permute-start | bytes 786440 | tf_op jit(solution)/shard_map/ppermute | solution.py:181
  59.3 10.3 %collective-permute-start.38 = (f32[512,128]{1,0:T(8,128)S(1)}, f32[512,128]{1,0:T(8,128)S(1)}, u32[]{:S(2)}, u32[]{:S(2)}) collective-permute-start(f32[512,128]{1,0:T(8,128)S(1)} %get-tuple-element.37), channel_id=1, source_target_pairs={{0,1},{1,0},{2,3},{3,2},{4,6},{5,7},{6,4},{7,5},{8,9},{9,8},{10,11... | collective-permute-start | bytes 786440 | tf_op jit(solution)/shard_map/ppermute | solution.py:196
  62.9 9.7 %collective-permute-start.21 = (f32[64,512]{1,0:T(8,128)S(1)}, f32[64,512]{1,0:T(8,128)S(1)}, u32[]{:S(2)}, u32[]{:S(2)}) collective-permute-start(f32[64,512]{1,0:T(8,128)S(1)} %add.10.x), channel_id=1, source_target_pairs={{0,8},{8,0},{16,24},{24,16},{1,9},{9,1},{17,25},{25,17},{2,10},{10... | collective-permute-start | bytes 393224 | tf_op jit(solution)/shard_map/ppermute | solution.py:181
  64.5 12.8 %collective-permute-start.22 = (f32[64,512]{1,0:T(8,128)S(1)}, f32[64,512]{1,0:T(8,128)S(1)}, u32[]{:S(2)}, u32[]{:S(2)}) collective-permute-start(f32[64,512]{1,0:T(8,128)S(1)} %add.10.x), channel_id=1, source_target_pairs={{0,16},{8,24},{16,0},{24,8},{1,17},{9,25},{17,1},{25,9},{2,18},{10... | collective-permute-start | bytes 393224 | tf_op jit(solution)/shard_map/ppermute | solution.py:181
  67.1 11.5 %collective-permute-start.23 = (f32[64,512]{1,0:T(8,128)S(1)}, f32[64,512]{1,0:T(8,128)S(1)}, u32[]{:S(2)}, u32[]{:S(2)}) collective-permute-start(f32[64,512]{1,0:T(8,128)S(1)} %add.10.x), channel_id=1, source_target_pairs={{0,24},{8,16},{16,8},{24,0},{1,25},{9,17},{17,9},{25,1},{2,26},{10... | collective-permute-start | bytes 393224 | tf_op jit(solution)/shard_map/ppermute | solution.py:181
  69.5 11.2 %collective-permute-start.28 = (f32[128,512]{1,0:T(8,128)S(1)}, f32[128,512]{1,0:T(8,128)S(1)}, u32[]{:S(2)}, u32[]{:S(2)}) collective-permute-start(f32[128,512]{1,0:T(8,128)S(1)} %get-tuple-element.32.refs_8_.refs_0_), channel_id=1, source_target_pairs={{0,1},{1,0},{2,3},{3,2},{4,5},{5,4},{6,7},{7,6},{8,9},{9,8},{10,11... | collective-permute-start | bytes 786440 | tf_op jit(solution)/shard_map/ppermute | solution.py:181
  71.1 9.6 %collective-permute-start.39 = (f32[256,128]{1,0:T(8,128)S(1)}, f32[256,128]{1,0:T(8,128)S(1)}, u32[]{:S(2)}, u32[]{:S(2)}) collective-permute-start(f32[256,128]{1,0:T(8,128)S(1)} %shard_map.52), channel_id=1, source_target_pairs={{0,2},{1,3},{2,0},{3,1},{4,5},{5,4},{6,7},{7,6},{8,10},{9,11},{10,... | collective-permute-start | bytes 393224 | tf_op jit(solution)/shard_map/ppermute | solution.py:198
  80.8 11.4 %collective-permute-start.40 = (f32[256,384]{1,0:T(8,128)S(1)}, f32[256,384]{1,0:T(8,128)S(1)}, u32[]{:S(2)}, u32[]{:S(2)}) collective-permute-start(f32[256,384]{1,0:T(8,128)S(1)} %shard_map.53), channel_id=1, source_target_pairs={{0,4},{4,0},{1,5},{5,1},{2,6},{6,2},{3,7},{7,3},{8,12},{12,8},{9,1... | collective-permute-start | bytes 1179656 | tf_op jit(solution)/shard_map/ppermute | solution.py:181
  90.8 10.6 %collective-permute-start.37 = (f32[64,512]{1,0:T(8,128)S(1)}, f32[64,512]{1,0:T(8,128)S(1)}, u32[]{:S(2)}, u32[]{:S(2)}) collective-permute-start(f32[64,512]{1,0:T(8,128)S(1)} %add.11.x), channel_id=1, source_target_pairs={{0,24},{8,16},{16,8},{24,0},{1,25},{9,17},{17,9},{25,1},{2,26},{10... | collective-permute-start | bytes 393224 | tf_op jit(solution)/shard_map/ppermute | solution.py:181
  (21 other events, 158.8 us)

commit v10 on v9

--- a/solution.py
+++ b/solution.py
@@ -129,8 +129,47 @@
     out[:, 2 * share :] = across[...]
 
 
+def pick_kernel(panel, x, mine, part):
+    rows, half = mine.shape[0], part.shape[0]
+    first = lax.axis_index("z") * rows
+    mine[...] = x[panel, pl.ds(pl.multiple_of(first, 8), rows), :]
+    part[...] = x[panel, pl.ds(pl.multiple_of(first + lax.axis_index("core") * half, 8), half), :]
+
+
+def pack_kernel(first, across, out):
+    rows = first.shape[0]
+    out[:rows] = first[...]
+    out[rows:] = across[...]
+
+
+def spread_kernel(*refs):
+    refs, out = refs[:-1], refs[-1]
+    n, z = len(refs), lax.axis_index("z")
+    rows = refs[0].shape[0] * 2 // 3
+    for by, ref in enumerate(refs):
+        at = (z ^ by) * rows
+        out[pl.ds(pl.multiple_of(at, 8), rows), :] = ref[:rows]
+        out[pl.ds(pl.multiple_of(n * rows + (z ^ by) * (rows // 2), 8), rows // 2), :] = ref[rows:]
+
+
 def hold_kernel(x, out):
     out[...] = x[...]
+
+
+def joined_blocks(first, across, exchanged, share, on_x, n):
+    second = jnp.concatenate([exchanged[:, :share], exchanged[:, share : 2 * share]], axis=0)
+    a, b = across[...], exchanged[:, 2 * share :]
+    return first[...], second, jnp.concatenate([jnp.where(on_x, a, b), jnp.where(on_x, b, a)], axis=0)
+
+
+def spread_blocks(mine, other, share, on_x, n):
+    rows = mine.shape[0] * 2 // 3
+    half = rows // (2 * n)
+    across = []
+    for at in range(rows, mine.shape[0], half):
+        a, b = mine[at : at + half], other[at : at + half]
+        across += [jnp.where(on_x, a, b), jnp.where(on_x, b, a)]
+    return mine[:rows], other[:rows], jnp.concatenate(across, axis=0)
 
 
 def solve_kernel(panel, n, *refs):
@@ -138,15 +177,13 @@
     total = refs[0][...]
     for i in range(1, n):
         total = total + refs[i][...]
-    factor, first, across, exchanged, out = refs[n:]
+    factor, *blocks, out = refs[n:]
     share = factor.shape[-1]
     on_x = core == 0
     own, along_x, along_y, far = split_columns(total, v, share)
-    second = jnp.concatenate([exchanged[:, :share], exchanged[:, share : 2 * share]], axis=0)
-    a, b = across[...], exchanged[:, 2 * share :]
-    across = jnp.concatenate([jnp.where(on_x, a, b), jnp.where(on_x, b, a)], axis=0)
+    first, second, across = (spread_blocks if len(blocks) == 2 else joined_blocks)(*blocks, share, on_x, n)
     sums = dot_left(own, factor[panel], NT)
-    sums += dot_left(jnp.where(on_x, along_x, along_y), first[...], NT)
+    sums += dot_left(jnp.where(on_x, along_x, along_y), first, NT)
     sums += dot_left(jnp.where(on_x, along_y, along_x), second, NT)
     out[...] = sums + dot_left(far, across, NT)
 
@@ -200,6 +237,20 @@
     return first, across, swap(joined, "core")
 
 
+def spread_factor(triangles, k):
+    _, rows, share = triangles.shape
+    axes, planes = ("core", "y", "x"), lax.axis_size("z")
+    n, rows = lax.axis_size(axes), rows // planes
+    shapes = [jax.ShapeDtypeStruct((r, share), F32) for r in (rows, rows // 2, rows * 3 // 2, rows * 3 // 2 * planes)]
+    mine, part = call(functools.partial(pick_kernel, k), shapes[:2], [triangles], 0)
+    first = lax.ppermute(mine, axes, [(i, i ^ (2 if i >= n // 2 else 1)) for i in range(n)])
+    across = lax.ppermute(part, axes, [(i, i ^ 3) for i in range(n)])
+    packed = call(pack_kernel, shapes[2:3], [first, across], 0)[0]
+    others = [swap(packed, "z", by) for by in range(1, planes)]
+    joined = call(spread_kernel, shapes[3:], [packed, *others], 0)[0]
+    return joined, swap(joined, "core")
+
+
 def fast(vectors, reflectors, triangles):
     rows, share = vectors.shape
     panels, _, width = reflectors.shape
@@ -212,10 +263,10 @@
     sections, factors = {}, {}
     for k in reversed(range(panels)):
         sections[k] = gather(reflectors[k])
-        factors[k] = gather_factor(triangles[k])
+        factors[k] = spread_factor(triangles, k) if k == top else gather_factor(triangles[k])
         if k == top:
             pieces = list(sections[k])
-            pieces[4], reflectors, triangles = lax.optimization_barrier((pieces[4], reflectors, triangles))
+            pieces[0], reflectors = lax.optimization_barrier((pieces[0], reflectors))
             sections[k] = tuple(pieces)
 
     def reduced(keep, send, k):

time: 106 us -> 111 us (1.047); the launches traced: 105 us -> 111 us
  waiting for transfers between devices: 47.7 us -> 54.2 us
    ppermute x0 -> x2, waiting for transfers between devices: none -> 5.86 us  [the longest x1 5.85 us: spread_factor(): across = lax.ppermute(part, axes, [(i, i ^ 3) for i in range(n)])]
    ppermute x0 -> x2, starting transfers between devices: none -> 3.05 us  [the longest x1 2.91 us: spread_factor(): across = lax.ppermute(part, axes, [(i, i ^ 3) for i in range(n)])]
    ppermute x3 -> x2, waiting for transfers between devices: 3.06 us -> 0.18 us  [gather_factor(): lax.ppermute(own, axes, [(i, i ^ (2 if i >= n // 2 else 1)) for i in rang...]
    ppermute x36 -> x39, waiting for transfers between devices: 42.2 us -> 44.6 us  [swap(): return lax.ppermute(a, axis, [(i, i ^ by) for i in range(n)])]
    ppermute x3 -> x2, starting transfers between devices: 3.18 us -> 1.08 us  [gather_factor(): lax.ppermute(mine, axes, [(i, i ^ (1 if i >= n // 2 else 2)) for i in ran...]
    ppermute x3 -> x2, waiting for transfers between devices: 2.45 us -> 3.6 us  [gather_factor(): lax.ppermute(mine, axes, [(i, i ^ (1 if i >= n // 2 else 2)) for i in ran...]
    slice x2, local copies, waits for them, and re-layouts: 1.25 us -> 2.39 us  [gather(): a, b = (block[:half], block[half:])]
    ppermute x3 -> x2, starting transfers between devices: 4.07 us -> 3.27 us  [gather_factor(): lax.ppermute(own, axes, [(i, i ^ (2 if i >= n // 2 else 1)) for i in rang...]
  transfers between devices with their start and end apart: 42 -> 45, of which waited for: 21 -> 22; matrix products, arithmetic and copies ran while one was open for 1% -> 1% of each run, Pallas kernels for 5% -> 5%
where the time goes in v10:
time: 111 us
  waiting for transfers between devices  54.2 us (49%)
  starting transfers between devices  46.7 us (42%)
  Pallas kernels  7.29 us (7%)
  local copies, waits for them, and re-layouts  2.43 us (2%)
    ppermute x39, waiting for transfers between devices, swap(): return lax.ppermute(a, axis, [(i, i ^ by) for i in range(n)])  44.6 us
    ppermute x39, starting transfers between devices, swap(): return lax.ppermute(a, axis, [(i, i ^ by) for i in range(n)])  39.3 us
    pallas_call x20, Pallas kernels, call(): pl.pallas_call(kernel, out_shape=outs, in_specs=vmem(len(args)), out_spec...  7.29 us
    ppermute x1, waiting for transfers between devices, spread_factor(): across = lax.ppermute(part, axes, [(i, i ^ 3) for i in range(n)])  5.85 us
    ppermute x2, waiting for transfers between devices, gather_factor(): lax.ppermute(mine, axes, [(i, i ^ (1 if i >= n // 2 else 2)) for i in ran...  3.6 us
    ppermute x2, starting transfers between devices, gather_factor(): lax.ppermute(own, axes, [(i, i ^ (2 if i >= n // 2 else 1)) for i in rang...  3.27 us
    ppermute x1, starting transfers between devices, spread_factor(): across = lax.ppermute(part, axes, [(i, i ^ 3) for i in range(n)])  2.91 us
    slice x2, local copies, waits for them, and re-layouts, gather(): a, b = (block[:half], block[half:])  2.39 us
  transfers between devices with their start and end apart: 45, of which 22 were waited for; matrix products, arithmetic and copies ran while one was open for 1% of the time, Pallas kernels for 5%

profile of v10, /device:TPU:0, one launch (start us, length us, event | category | flops | bytes accessed | tf_op | source)
XLA Modules:
  0.0 110.9 jit_solution(11766319106015852009)
XLA Ops:
  1.1 3.0 %collective-permute-start.1 = (f32[128,512]{1,0:T(8,128)S(1)}, f32[128,512]{1,0:T(8,128)S(1)}, u32[]{:S(2)}, u32[]{:S(2)}) collective-permute-start(f32[128,512]{1,0:T(8,128)S(1)} %get-tuple-element.37.refs_1_), channel_id=1, source_target_pairs={{0,1},{1,0},{2,3},{3,2},{4,5},{5,4},{6,7},{7,6},{8,9},{9,8},{10,11... | collective-permute-start | bytes 786440 | tf_op jit(solution)/shard_map/ppermute | solution.py:218
  4.3 2.9 %collective-permute-start.11 = (f32[64,128]{1,0:T(8,128)S(1)}, f32[64,128]{1,0:T(8,128)S(1)}, u32[]{:S(2)}, u32[]{:S(2)}) collective-permute-start(f32[64,128]{1,0:T(8,128)S(1)} %get-tuple-element.23), channel_id=1, source_target_pairs={{0,3},{1,2},{2,1},{3,0},{4,7},{5,6},{6,5},{7,4},{8,11},{9,10},{10,... | collective-permute-start | bytes 98312 | tf_op jit(solution)/shard_map/ppermute | solution.py:247
  7.2 5.9 %collective-permute-done.11.across = f32[64,128]{1,0:T(8,128)S(1)} collective-permute-done((f32[64,128]{1,0:T(8,128)S(1)}, f32[64,128]{1,0:T(8,128)S(1)}, u32[]{:S(2)}, u32[]{:S(2)}) %collective-permute-start.11) | collective-permute-done | bytes 32800 | tf_op jit(solution)/shard_map/ppermute | solution.py:247
  13.1 1.6 %collective-permute-start.12 = (f32[192,128]{1,0:T(8,128)S(1)}, f32[192,128]{1,0:T(8,128)S(1)}, u32[]{:S(2)}, u32[]{:S(2)}) collective-permute-start(f32[192,128]{1,0:T(8,128)S(1)} %shard_map.41.refs_0_), channel_id=1, source_target_pairs={{0,8},{8,0},{16,24},{24,16},{1,9},{9,1},{17,25},{25,17},{2,10},{10... | collective-permute-start | bytes 294920 | tf_op jit(solution)/shard_map/ppermute | solution.py:218
  14.7 2.6 %collective-permute-start.13 = (f32[192,128]{1,0:T(8,128)S(1)}, f32[192,128]{1,0:T(8,128)S(1)}, u32[]{:S(2)}, u32[]{:S(2)}) collective-permute-start(f32[192,128]{1,0:T(8,128)S(1)} %shard_map.41.refs_0_), channel_id=1, source_target_pairs={{0,16},{8,24},{16,0},{24,8},{1,17},{9,25},{17,1},{25,9},{2,18},{10... | collective-permute-start | bytes 294920 | tf_op jit(solution)/shard_map/ppermute | solution.py:218
  17.8 1.5 %collective-permute-start.3 = (f32[128,512]{1,0:T(8,128)S(1)}, f32[128,512]{1,0:T(8,128)S(1)}, u32[]{:S(2)}, u32[]{:S(2)}) collective-permute-start(f32[128,512]{1,0:T(8,128)S(1)} %get-tuple-element.37.refs_1_), channel_id=1, source_target_pairs={{0,2},{2,0},{1,3},{3,1},{4,6},{6,4},{5,7},{7,5},{8,10},{10,8},{9,1... | collective-permute-start | bytes 786440 | tf_op jit(solution)/shard_map/ppermute | solution.py:218
  24.7 3.4 %collective-permute-done.14.refs_3_ = f32[192,128]{1,0:T(8,128)S(1)} collective-permute-done((f32[192,128]{1,0:T(8,128)S(1)}, f32[192,128]{1,0:T(8,128)S(1)}, u32[]{:S(2)}, u32[]{:S(2)}) %collective-permute-start.14) | collective-permute-done | bytes 98336 | tf_op jit(solution)/shard_map/ppermute | solution.py:218
  30.2 1.9 %collective-permute-done.3.refs_5_ = f32[128,512]{1,0:T(8,128)S(1)} collective-permute-done((f32[128,512]{1,0:T(8,128)S(1)}, f32[128,512]{1,0:T(8,128)S(1)}, u32[]{:S(2)}, u32[]{:S(2)}) %collective-permute-start.3) | collective-permute-done | bytes 262176 | tf_op jit(solution)/shard_map/ppermute | solution.py:218
  33.7 3.8 %collective-permute-done.5.refs_1_.refs_7_ = f32[128,512]{1,0:T(8,128)S(1)} collective-permute-done((f32[128,512]{1,0:T(8,128)S(1)}, f32[128,512]{1,0:T(8,128)S(1)}, u32[]{:S(2)}, u32[]{:S(2)}) %collective-permute-start.5) | collective-permute-done | bytes 262176 | tf_op jit(solution)/shard_map/ppermute | solution.py:218
  37.5 1.8 %collective-permute-start.27 = (f32[512,128]{1,0:T(8,128)S(1)}, f32[512,128]{1,0:T(8,128)S(1)}, u32[]{:S(2)}, u32[]{:S(2)}) collective-permute-start(f32[512,128]{1,0:T(8,128)S(1)} %get-tuple-element.40), channel_id=1, source_target_pairs={{0,1},{1,0},{2,3},{3,2},{4,6},{5,7},{6,4},{7,5},{8,9},{9,8},{10,11... | collective-permute-start | bytes 786440 | tf_op jit(solution)/shard_map/ppermute | solution.py:233
  43.8 3.3 %collective-permute-start.9 = (f32[64,512]{1,0:T(8,128)S(1)}, f32[64,512]{1,0:T(8,128)S(1)}, u32[]{:S(2)}, u32[]{:S(2)}) collective-permute-start(f32[64,512]{1,0:T(8,128)S(1)} %add.9.x), channel_id=1, source_target_pairs={{0,24},{8,16},{16,8},{24,0},{1,25},{9,17},{17,9},{25,1},{2,26},{10... | collective-permute-start | bytes 393224 | tf_op jit(solution)/shard_map/ppermute | solution.py:218
  51.3 4.7 %collective-permute-done.8.refs_2_ = f32[64,512]{1,0:T(8,128)S(1)} collective-permute-done((f32[64,512]{1,0:T(8,128)S(1)}, f32[64,512]{1,0:T(8,128)S(1)}, u32[]{:S(2)}, u32[]{:S(2)}) %collective-permute-start.8) | collective-permute-done | bytes 131104 | tf_op jit(solution)/shard_map/ppermute | solution.py:218
  56.5 1.5 %collective-permute-start.22 = (f32[128,512]{1,0:T(8,128)S(1)}, f32[128,512]{1,0:T(8,128)S(1)}, u32[]{:S(2)}, u32[]{:S(2)}) collective-permute-start(f32[128,512]{1,0:T(8,128)S(1)} %collective-permute-done.18.refs_11_.refs_3_), channel_id=1, source_target_pairs={{0,2},{2,0},{1,3},{3,1},{4,6},{6,4},{5,7},{7,5},{8,10},{10,8},{9,1... | collective-permute-start | bytes 786440 | tf_op jit(solution)/shard_map/ppermute | solution.py:218
  58.5 3.6 %collective-permute-done.28.across.refs_6_ = f32[256,128]{1,0:T(8,128)S(1)} collective-permute-done((f32[256,128]{1,0:T(8,128)S(1)}, f32[256,128]{1,0:T(8,128)S(1)}, u32[]{:S(2)}, u32[]{:S(2)}) %collective-permute-start.28) | collective-permute-done | bytes 131104 | tf_op jit(solution)/shard_map/ppermute | solution.py:235
  68.5 2.5 %collective-permute-done.32.refs_11_.refs_3_ = f32[128,512]{1,0:T(8,128)S(1)} collective-permute-done((f32[128,512]{1,0:T(8,128)S(1)}, f32[128,512]{1,0:T(8,128)S(1)}, u32[]{:S(2)}, u32[]{:S(2)}) %collective-permute-start.32) | collective-permute-done | bytes 262176 | tf_op jit(solution)/shard_map/ppermute | solution.py:218
  75.2 1.5 %collective-permute-start.34 = (f32[128,512]{1,0:T(8,128)S(1)}, f32[128,512]{1,0:T(8,128)S(1)}, u32[]{:S(2)}, u32[]{:S(2)}) collective-permute-start(f32[128,512]{1,0:T(8,128)S(1)} %get-tuple-element.33.refs_9_.refs_1_), channel_id=1, source_target_pairs={{0,2},{2,0},{1,3},{3,1},{4,6},{6,4},{5,7},{7,5},{8,10},{10,8},{9,1... | collective-permute-start | bytes 786440 | tf_op jit(solution)/shard_map/ppermute | solution.py:218
  76.8 5.2 %collective-permute-done.25.refs_2_ = f32[64,512]{1,0:T(8,128)S(1)} collective-permute-done((f32[64,512]{1,0:T(8,128)S(1)}, f32[64,512]{1,0:T(8,128)S(1)}, u32[]{:S(2)}, u32[]{:S(2)}) %collective-permute-start.25) | collective-permute-done | bytes 131104 | tf_op jit(solution)/shard_map/ppermute | solution.py:218
  82.0 2.1 %collective-permute-start.35 = (f32[128,512]{1,0:T(8,128)S(1)}, f32[128,512]{1,0:T(8,128)S(1)}, u32[]{:S(2)}, u32[]{:S(2)}) collective-permute-start(f32[128,512]{1,0:T(8,128)S(1)} %collective-permute-done.33.refs_12_.refs_4_), channel_id=1, source_target_pairs={{0,1},{1,0},{2,3},{3,2},{4,5},{5,4},{6,7},{7,6},{8,9},{9,8},{10,11... | collective-permute-start | bytes 786440 | tf_op jit(solution)/shard_map/ppermute | solution.py:218
  87.8 2.3 %collective-permute-done.35.refs_0_.refs_6_ = f32[128,512]{1,0:T(8,128)S(1)} collective-permute-done((f32[128,512]{1,0:T(8,128)S(1)}, f32[128,512]{1,0:T(8,128)S(1)}, u32[]{:S(2)}, u32[]{:S(2)}) %collective-permute-start.35) | collective-permute-done | bytes 262176 | tf_op jit(solution)/shard_map/ppermute | solution.py:218
  92.7 2.6 %collective-permute-start.38 = (f32[64,512]{1,0:T(8,128)S(1)}, f32[64,512]{1,0:T(8,128)S(1)}, u32[]{:S(2)}, u32[]{:S(2)}) collective-permute-start(f32[64,512]{1,0:T(8,128)S(1)} %add.11.x), channel_id=1, source_target_pairs={{0,8},{8,0},{16,24},{24,16},{1,9},{9,1},{17,25},{25,17},{2,10},{10... | collective-permute-start | bytes 393224 | tf_op jit(solution)/shard_map/ppermute | solution.py:218
  95.3 2.4 %collective-permute-start.40 = (f32[64,512]{1,0:T(8,128)S(1)}, f32[64,512]{1,0:T(8,128)S(1)}, u32[]{:S(2)}, u32[]{:S(2)}) collective-permute-start(f32[64,512]{1,0:T(8,128)S(1)} %add.11.x), channel_id=1, source_target_pairs={{0,24},{8,16},{16,8},{24,0},{1,25},{9,17},{17,9},{25,1},{2,26},{10... | collective-permute-start | bytes 393224 | tf_op jit(solution)/shard_map/ppermute | solution.py:218
  97.8 1.8 %collective-permute-done.38.refs_1_ = f32[64,512]{1,0:T(8,128)S(1)} collective-permute-done((f32[64,512]{1,0:T(8,128)S(1)}, f32[64,512]{1,0:T(8,128)S(1)}, u32[]{:S(2)}, u32[]{:S(2)}) %collective-permute-start.38) | collective-permute-done | bytes 131104 | tf_op jit(solution)/shard_map/ppermute | solution.py:218
  99.6 8.0 %collective-permute-done.39.refs_2_ = f32[64,512]{1,0:T(8,128)S(1)} collective-permute-done((f32[64,512]{1,0:T(8,128)S(1)}, f32[64,512]{1,0:T(8,128)S(1)}, u32[]{:S(2)}, u32[]{:S(2)}) %collective-permute-start.39) | collective-permute-done | bytes 131104 | tf_op jit(solution)/shard_map/ppermute | solution.py:218
  109.4 1.5 %shard_map.56 = f32[1024,128]{1,0:T(8,128)} custom-call(f32[1024,128]{1,0:T(8,128)S(1)} %get-tuple-element.29.x, f32[64,512]{1,0:T(8,128)S(1)} %shard_map.55.mine, f32[64,512]{1,0:T(8,128)S(1)} %collective-permute-done.44.other, f32[128,512]{1,0:T(8,128)S(1)} %get-tuple-element.34.refs_8_.refs_0_, f32[128,512]{1,0:T(8,128)S(1)} %get-tuple-element.33.refs_9_.refs_1_, ...), custom_call_target="tpu_custom_call" | custom-call | flops 134217728 | bytes 3407872 | tf_op jit(solution)/shard_map/pallas_call | solution.py:205
  (96 shorter events, 39.2 us)
Async XLA Ops:
  1.1 21.7 %collective-permute-start.1 = (f32[128,512]{1,0:T(8,128)S(1)}, f32[128,512]{1,0:T(8,128)S(1)}, u32[]{:S(2)}, u32[]{:S(2)}) collective-permute-start(f32[128,512]{1,0:T(8,128)S(1)} %get-tuple-element.37.refs_1_), channel_id=1, source_target_pairs={{0,1},{1,0},{2,3},{3,2},{4,5},{5,4},{6,7},{7,6},{8,9},{9,8},{10,11... | collective-permute-start | bytes 786440 | tf_op jit(solution)/shard_map/ppermute | solution.py:218
  17.3 12.3 %collective-permute-start.2 = (f32[128,512]{1,0:T(8,128)S(1)}, f32[128,512]{1,0:T(8,128)S(1)}, u32[]{:S(2)}, u32[]{:S(2)}) collective-permute-start(f32[128,512]{1,0:T(8,128)S(1)} %get-tuple-element.19.refs_0_), channel_id=1, source_target_pairs={{0,2},{2,0},{1,3},{3,1},{4,6},{6,4},{5,7},{7,5},{8,10},{10,8},{9,1... | collective-permute-start | bytes 786440 | tf_op jit(solution)/shard_map/ppermute | solution.py:218
  17.8 14.3 %collective-permute-start.3 = (f32[128,512]{1,0:T(8,128)S(1)}, f32[128,512]{1,0:T(8,128)S(1)}, u32[]{:S(2)}, u32[]{:S(2)}) collective-permute-start(f32[128,512]{1,0:T(8,128)S(1)} %get-tuple-element.37.refs_1_), channel_id=1, source_target_pairs={{0,2},{2,0},{1,3},{3,1},{4,6},{6,4},{5,7},{7,5},{8,10},{10,8},{9,1... | collective-permute-start | bytes 786440 | tf_op jit(solution)/shard_map/ppermute | solution.py:218
  19.4 12.8 %collective-permute-start = (f32[128,512]{1,0:T(8,128)S(1)}, f32[128,512]{1,0:T(8,128)S(1)}, u32[]{:S(2)}, u32[]{:S(2)}) collective-permute-start(f32[128,512]{1,0:T(8,128)S(1)} %get-tuple-element.19.refs_0_), channel_id=1, source_target_pairs={{0,1},{1,0},{2,3},{3,2},{4,5},{5,4},{6,7},{7,6},{8,9},{9,8},{10,11... | collective-permute-start | bytes 786440 | tf_op jit(solution)/shard_map/ppermute | solution.py:218
  22.9 14.6 %collective-permute-start.5 = (f32[128,512]{1,0:T(8,128)S(1)}, f32[128,512]{1,0:T(8,128)S(1)}, u32[]{:S(2)}, u32[]{:S(2)}) collective-permute-start(f32[128,512]{1,0:T(8,128)S(1)} %collective-permute-done.1.refs_3_), channel_id=1, source_target_pairs={{0,2},{2,0},{1,3},{3,1},{4,6},{6,4},{5,7},{7,5},{8,10},{10,8},{9,1... | collective-permute-start | bytes 786440 | tf_op jit(solution)/shard_map/ppermute | solution.py:218
  28.1 15.1 %collective-permute-start.18 = (f32[128,512]{1,0:T(8,128)S(1)}, f32[128,512]{1,0:T(8,128)S(1)}, u32[]{:S(2)}, u32[]{:S(2)}) collective-permute-start(f32[128,512]{1,0:T(8,128)S(1)} %get-tuple-element.35.refs_9_.refs_1_), channel_id=1, source_target_pairs={{0,1},{1,0},{2,3},{3,2},{4,5},{5,4},{6,7},{7,6},{8,9},{9,8},{10,11... | collective-permute-start | bytes 786440 | tf_op jit(solution)/shard_map/ppermute | solution.py:218
  29.6 14.2 %collective-permute-start.19 = (f32[128,512]{1,0:T(8,128)S(1)}, f32[128,512]{1,0:T(8,128)S(1)}, u32[]{:S(2)}, u32[]{:S(2)}) collective-permute-start(f32[128,512]{1,0:T(8,128)S(1)} %get-tuple-element.36.refs_8_.refs_0_), channel_id=1, source_target_pairs={{0,2},{2,0},{1,3},{3,1},{4,6},{6,4},{5,7},{7,5},{8,10},{10,8},{9,1... | collective-permute-start | bytes 786440 | tf_op jit(solution)/shard_map/ppermute | solution.py:218
  32.1 16.5 %collective-permute-start.15 = (f32[768,128]{1,0:T(8,128)S(1)}, f32[768,128]{1,0:T(8,128)S(1)}, u32[]{:S(2)}, u32[]{:S(2)}) collective-permute-start(f32[768,128]{1,0:T(8,128)S(1)} %shard_map.42.refs_5_), channel_id=1, source_target_pairs={{0,4},{4,0},{1,5},{5,1},{2,6},{6,2},{3,7},{7,3},{8,12},{12,8},{9,1... | collective-permute-start | bytes 1179656 | tf_op jit(solution)/shard_map/ppermute | solution.py:218
  43.1 12.8 %collective-permute-start.8 = (f32[64,512]{1,0:T(8,128)S(1)}, f32[64,512]{1,0:T(8,128)S(1)}, u32[]{:S(2)}, u32[]{:S(2)}) collective-permute-start(f32[64,512]{1,0:T(8,128)S(1)} %add.9.x), channel_id=1, source_target_pairs={{0,16},{8,24},{16,0},{24,8},{1,17},{9,25},{17,1},{25,9},{2,18},{10... | collective-permute-start | bytes 393224 | tf_op jit(solution)/shard_map/ppermute | solution.py:218
  43.8 12.7 %collective-permute-start.9 = (f32[64,512]{1,0:T(8,128)S(1)}, f32[64,512]{1,0:T(8,128)S(1)}, u32[]{:S(2)}, u32[]{:S(2)}) collective-permute-start(f32[64,512]{1,0:T(8,128)S(1)} %add.9.x), channel_id=1, source_target_pairs={{0,24},{8,16},{16,8},{24,0},{1,25},{9,17},{17,9},{25,1},{2,26},{10... | collective-permute-start | bytes 393224 | tf_op jit(solution)/shard_map/ppermute | solution.py:218
  47.1 15.0 %collective-permute-start.17 = (f32[128,512]{1,0:T(8,128)S(1)}, f32[128,512]{1,0:T(8,128)S(1)}, u32[]{:S(2)}, u32[]{:S(2)}) collective-permute-start(f32[128,512]{1,0:T(8,128)S(1)} %get-tuple-element.36.refs_8_.refs_0_), channel_id=1, source_target_pairs={{0,1},{1,0},{2,3},{3,2},{4,5},{5,4},{6,7},{7,6},{8,9},{9,8},{10,11... | collective-permute-start | bytes 786440 | tf_op jit(solution)/shard_map/ppermute | solution.py:218
  48.6 14.1 %collective-permute-start.20 = (f32[128,512]{1,0:T(8,128)S(1)}, f32[128,512]{1,0:T(8,128)S(1)}, u32[]{:S(2)}, u32[]{:S(2)}) collective-permute-start(f32[128,512]{1,0:T(8,128)S(1)} %get-tuple-element.35.refs_9_.refs_1_), channel_id=1, source_target_pairs={{0,2},{2,0},{1,3},{3,1},{4,6},{6,4},{5,7},{7,5},{8,10},{10,8},{9,1... | collective-permute-start | bytes 786440 | tf_op jit(solution)/shard_map/ppermute | solution.py:218
  49.8 13.5 %collective-permute-start.21 = (f32[128,512]{1,0:T(8,128)S(1)}, f32[128,512]{1,0:T(8,128)S(1)}, u32[]{:S(2)}, u32[]{:S(2)}) collective-permute-start(f32[128,512]{1,0:T(8,128)S(1)} %collective-permute-done.19.refs_12_.refs_4_), channel_id=1, source_target_pairs={{0,1},{1,0},{2,3},{3,2},{4,5},{5,4},{6,7},{7,6},{8,9},{9,8},{10,11... | collective-permute-start | bytes 786440 | tf_op jit(solution)/shard_map/ppermute | solution.py:218
  56.5 10.1 %collective-permute-start.22 = (f32[128,512]{1,0:T(8,128)S(1)}, f32[128,512]{1,0:T(8,128)S(1)}, u32[]{:S(2)}, u32[]{:S(2)}) collective-permute-start(f32[128,512]{1,0:T(8,128)S(1)} %collective-permute-done.18.refs_11_.refs_3_), channel_id=1, source_target_pairs={{0,2},{2,0},{1,3},{3,1},{4,6},{6,4},{5,7},{7,5},{8,10},{10,8},{9,1... | collective-permute-start | bytes 786440 | tf_op jit(solution)/shard_map/ppermute | solution.py:218
  62.2 12.5 %collective-permute-start.29 = (f32[256,384]{1,0:T(8,128)S(1)}, f32[256,384]{1,0:T(8,128)S(1)}, u32[]{:S(2)}, u32[]{:S(2)}) collective-permute-start(f32[256,384]{1,0:T(8,128)S(1)} %shard_map.48), channel_id=1, source_target_pairs={{0,4},{4,0},{1,5},{5,1},{2,6},{6,2},{3,7},{7,3},{8,12},{12,8},{9,1... | collective-permute-start | bytes 1179656 | tf_op jit(solution)/shard_map/ppermute | solution.py:218
  63.8 10.1 %collective-permute-start.41 = (f32[512,128]{1,0:T(8,128)S(1)}, f32[512,128]{1,0:T(8,128)S(1)}, u32[]{:S(2)}, u32[]{:S(2)}) collective-permute-start(f32[512,128]{1,0:T(8,128)S(1)} %get-tuple-element.39), channel_id=1, source_target_pairs={{0,1},{1,0},{2,3},{3,2},{4,6},{5,7},{6,4},{7,5},{8,9},{9,8},{10,11... | collective-permute-start | bytes 786440 | tf_op jit(solution)/shard_map/ppermute | solution.py:233
  71.0 10.9 %collective-permute-start.25 = (f32[64,512]{1,0:T(8,128)S(1)}, f32[64,512]{1,0:T(8,128)S(1)}, u32[]{:S(2)}, u32[]{:S(2)}) collective-permute-start(f32[64,512]{1,0:T(8,128)S(1)} %add.10.x), channel_id=1, source_target_pairs={{0,16},{8,24},{16,0},{24,8},{1,17},{9,25},{17,1},{25,9},{2,18},{10... | collective-permute-start | bytes 393224 | tf_op jit(solution)/shard_map/ppermute | solution.py:218
  72.4 11.6 %collective-permute-start.26 = (f32[64,512]{1,0:T(8,128)S(1)}, f32[64,512]{1,0:T(8,128)S(1)}, u32[]{:S(2)}, u32[]{:S(2)}) collective-permute-start(f32[64,512]{1,0:T(8,128)S(1)} %add.10.x), channel_id=1, source_target_pairs={{0,24},{8,16},{16,8},{24,0},{1,25},{9,17},{17,9},{25,1},{2,26},{10... | collective-permute-start | bytes 393224 | tf_op jit(solution)/shard_map/ppermute | solution.py:218
  73.8 11.3 %collective-permute-start.31 = (f32[128,512]{1,0:T(8,128)S(1)}, f32[128,512]{1,0:T(8,128)S(1)}, u32[]{:S(2)}, u32[]{:S(2)}) collective-permute-start(f32[128,512]{1,0:T(8,128)S(1)} %get-tuple-element.34.refs_8_.refs_0_), channel_id=1, source_target_pairs={{0,1},{1,0},{2,3},{3,2},{4,5},{5,4},{6,7},{7,6},{8,9},{9,8},{10,11... | collective-permute-start | bytes 786440 | tf_op jit(solution)/shard_map/ppermute | solution.py:218
  74.7 10.4 %collective-permute-start.42 = (f32[256,128]{1,0:T(8,128)S(1)}, f32[256,128]{1,0:T(8,128)S(1)}, u32[]{:S(2)}, u32[]{:S(2)}) collective-permute-start(f32[256,128]{1,0:T(8,128)S(1)} %shard_map.53), channel_id=1, source_target_pairs={{0,2},{1,3},{2,0},{3,1},{4,5},{5,4},{6,7},{7,6},{8,10},{9,11},{10,... | collective-permute-start | bytes 393224 | tf_op jit(solution)/shard_map/ppermute | solution.py:235
  75.2 10.5 %collective-permute-start.34 = (f32[128,512]{1,0:T(8,128)S(1)}, f32[128,512]{1,0:T(8,128)S(1)}, u32[]{:S(2)}, u32[]{:S(2)}) collective-permute-start(f32[128,512]{1,0:T(8,128)S(1)} %get-tuple-element.33.refs_9_.refs_1_), channel_id=1, source_target_pairs={{0,2},{2,0},{1,3},{3,1},{4,6},{6,4},{5,7},{7,5},{8,10},{10,8},{9,1... | collective-permute-start | bytes 786440 | tf_op jit(solution)/shard_map/ppermute | solution.py:218
  85.2 12.6 %collective-permute-start.43 = (f32[256,384]{1,0:T(8,128)S(1)}, f32[256,384]{1,0:T(8,128)S(1)}, u32[]{:S(2)}, u32[]{:S(2)}) collective-permute-start(f32[256,384]{1,0:T(8,128)S(1)} %shard_map.54), channel_id=1, source_target_pairs={{0,4},{4,0},{1,5},{5,1},{2,6},{6,2},{3,7},{7,3},{8,12},{12,8},{9,1... | collective-permute-start | bytes 1179656 | tf_op jit(solution)/shard_map/ppermute | solution.py:218
  95.3 12.2 %collective-permute-start.39 = (f32[64,512]{1,0:T(8,128)S(1)}, f32[64,512]{1,0:T(8,128)S(1)}, u32[]{:S(2)}, u32[]{:S(2)}) collective-permute-start(f32[64,512]{1,0:T(8,128)S(1)} %add.11.x), channel_id=1, source_target_pairs={{0,16},{8,24},{16,0},{24,8},{1,17},{9,25},{17,1},{25,9},{2,18},{10... | collective-permute-start | bytes 393224 | tf_op jit(solution)/shard_map/ppermute | solution.py:218
  95.3 12.2 %collective-permute-start.40 = (f32[64,512]{1,0:T(8,128)S(1)}, f32[64,512]{1,0:T(8,128)S(1)}, u32[]{:S(2)}, u32[]{:S(2)}) collective-permute-start(f32[64,512]{1,0:T(8,128)S(1)} %add.11.x), channel_id=1, source_target_pairs={{0,24},{8,16},{16,8},{24,0},{1,25},{9,17},{17,9},{25,1},{2,26},{10... | collective-permute-start | bytes 393224 | tf_op jit(solution)/shard_map/ppermute | solution.py:218
  (23 other events, 149.9 us)

commit v11 on v10

--- a/solution.py
+++ b/solution.py
@@ -152,6 +152,30 @@
         out[pl.ds(pl.multiple_of(n * rows + (z ^ by) * (rows // 2), 8), rows // 2), :] = ref[rows:]
 
 
+def two_steps(planes, k, top):
+    return planes == 4 and k == top
+
+
+def summed(refs):
+    if len(refs) != 6:
+        return sum((ref[...] for ref in refs[1:]), refs[0][...])
+    own, near, *far, pair, across = refs
+    half = pair.shape[0]
+    lower = (own[half:] + near[half:]) + (far[0][...] + far[1][...])
+    return jnp.concatenate([pair[...] + across[...], lower], axis=0)
+
+
+def meet_kernel(keep, received, out, low):
+    total = keep[...] + received[...]
+    out[...] = total
+    low[...] = total[low.shape[0] :]
+
+
+def pair_kernel(own, near, out):
+    half = out.shape[0]
+    out[...] = own[:half] + near[:half]
+
+
 def hold_kernel(x, out):
     out[...] = x[...]
 
@@ -172,12 +196,10 @@
     return mine[:rows], other[:rows], jnp.concatenate(across, axis=0)
 
 
-def solve_kernel(panel, n, *refs):
+def solve_kernel(panel, n, count, *refs):
     v, core = place()
-    total = refs[0][...]
-    for i in range(1, n):
-        total = total + refs[i][...]
-    factor, *blocks, out = refs[n:]
+    total = summed(refs[:count])
+    factor, *blocks, out = refs[count:]
     share = factor.shape[-1]
     on_x = core == 0
     own, along_x, along_y, far = split_columns(total, v, share)
@@ -270,11 +292,22 @@
             sections[k] = tuple(pieces)
 
     def reduced(keep, send, k):
-        s = keep + swap(send, "core")
-        r = [swap(s, "z", by) for by in range(1, sums)]
+        received = swap(send, "core")
+        if two_steps(sums, k, top):
+            piece = jax.ShapeDtypeStruct((share // 4, width), F32)
+            s, low = call(meet_kernel, [part, piece], [keep, received], 0)
+            r = [swap(s, "z", 1), swap(low, "z", 2), swap(low, "z", 3)]
+            pair = call(pair_kernel, [piece], [s, r[0]], 0)[0]
+            r += [pair, swap(pair, "z", 2)]
+        else:
+            s = keep + received
+            r = [swap(s, "z", by) for by in range(1, sums)]
         s = call(hold_kernel, [part], [s], 0)[0]
         mine = call(
-            functools.partial(solve_kernel, k, sums), [part], [s, *r, triangles, *factors[k]], width * width * share
+            functools.partial(solve_kernel, k, sums, 1 + len(r)),
+            [part],
+            [s, *r, triangles, *factors[k]],
+            width * width * share,
         )[0]
         return mine, swap(mine, "core")
 

time: 111 us -> 110 us (level)
  waiting for transfers between devices: 54.2 us -> 52.8 us
    ppermute x2, waiting for transfers between devices: 3.6 us -> 0.01 us  [gather_factor(): lax.ppermute(mine, axes, [(i, i ^ (1 if i >= n // 2 else 2)) for i in ran...]
    ppermute x39 -> x40, waiting for transfers between devices: 44.6 us -> 46.5 us  [swap(): return lax.ppermute(a, axis, [(i, i ^ by) for i in range(n)])]
    ppermute x39 -> x40, starting transfers between devices: 39.3 us -> 40.8 us  [swap(): return lax.ppermute(a, axis, [(i, i ^ by) for i in range(n)])]
    pallas_call x20 -> x22, Pallas kernels: 7.29 us -> 7.31 us  [call(): pl.pallas_call(kernel, out_shape=outs, in_specs=vmem(len(args)), out_spec...]
  transfers between devices with their start and end apart: 45 -> 46, of which waited for: 22 -> 21; matrix products, arithmetic and copies ran while one was open for 1% -> 1% of each run, Pallas kernels for 5% -> 5%
where the time goes in v11:
time: 110 us
  waiting for transfers between devices  52.8 us (48%)
  starting transfers between devices  47.3 us (43%)
  Pallas kernels  7.31 us (7%)
  local copies, waits for them, and re-layouts  2.43 us (2%)
    ppermute x40, waiting for transfers between devices, swap(): return lax.ppermute(a, axis, [(i, i ^ by) for i in range(n)])  46.5 us
    ppermute x40, starting transfers between devices, swap(): return lax.ppermute(a, axis, [(i, i ^ by) for i in range(n)])  40.8 us
    pallas_call x22, Pallas kernels, call(): pl.pallas_call(kernel, out_shape=outs, in_specs=vmem(len(args)), out_spec...  7.31 us
    ppermute x1, waiting for transfers between devices, spread_factor(): across = lax.ppermute(part, axes, [(i, i ^ 3) for i in range(n)])  5.85 us
    ppermute x1, starting transfers between devices, spread_factor(): across = lax.ppermute(part, axes, [(i, i ^ 3) for i in range(n)])  2.91 us
    slice x2, local copies, waits for them, and re-layouts, gather(): a, b = (block[:half], block[half:])  2.39 us
    ppermute x2, starting transfers between devices, gather_factor(): lax.ppermute(own, axes, [(i, i ^ (2 if i >= n // 2 else 1)) for i in rang...  2.32 us
  transfers between devices with their start and end apart: 46, of which 21 were waited for; matrix products, arithmetic and copies ran while one was open for 1% of the time, Pallas kernels for 5%

profile of v11, /device:TPU:0, one launch (start us, length us, event | category | flops | bytes accessed | tf_op | source)
XLA Modules:
  0.0 110.2 jit_solution(2899266935350990369)
XLA Ops:
  1.1 3.0 %collective-permute-start.1 = (f32[128,512]{1,0:T(8,128)S(1)}, f32[128,512]{1,0:T(8,128)S(1)}, u32[]{:S(2)}, u32[]{:S(2)}) collective-permute-start(f32[128,512]{1,0:T(8,128)S(1)} %get-tuple-element.41.refs_1_), channel_id=1, source_target_pairs={{0,1},{1,0},{2,3},{3,2},{4,5},{5,4},{6,7},{7,6},{8,9},{9,8},{10,11... | collective-permute-start | bytes 786440 | tf_op jit(solution)/shard_map/ppermute | solution.py:240
  4.3 2.9 %collective-permute-start.12 = (f32[64,128]{1,0:T(8,128)S(1)}, f32[64,128]{1,0:T(8,128)S(1)}, u32[]{:S(2)}, u32[]{:S(2)}) collective-permute-start(f32[64,128]{1,0:T(8,128)S(1)} %get-tuple-element.27), channel_id=1, source_target_pairs={{0,3},{1,2},{2,1},{3,0},{4,7},{5,6},{6,5},{7,4},{8,11},{9,10},{10,... | collective-permute-start | bytes 98312 | tf_op jit(solution)/shard_map/ppermute | solution.py:269
  7.2 5.9 %collective-permute-done.12.across = f32[64,128]{1,0:T(8,128)S(1)} collective-permute-done((f32[64,128]{1,0:T(8,128)S(1)}, f32[64,128]{1,0:T(8,128)S(1)}, u32[]{:S(2)}, u32[]{:S(2)}) %collective-permute-start.12) | collective-permute-done | bytes 32800 | tf_op jit(solution)/shard_map/ppermute | solution.py:269
  13.1 1.6 %collective-permute-start.13 = (f32[192,128]{1,0:T(8,128)S(1)}, f32[192,128]{1,0:T(8,128)S(1)}, u32[]{:S(2)}, u32[]{:S(2)}) collective-permute-start(f32[192,128]{1,0:T(8,128)S(1)} %shard_map.43.refs_0_), channel_id=1, source_target_pairs={{0,8},{8,0},{16,24},{24,16},{1,9},{9,1},{17,25},{25,17},{2,10},{10... | collective-permute-start | bytes 294920 | tf_op jit(solution)/shard_map/ppermute | solution.py:240
  14.7 2.6 %collective-permute-start.14 = (f32[192,128]{1,0:T(8,128)S(1)}, f32[192,128]{1,0:T(8,128)S(1)}, u32[]{:S(2)}, u32[]{:S(2)}) collective-permute-start(f32[192,128]{1,0:T(8,128)S(1)} %shard_map.43.refs_0_), channel_id=1, source_target_pairs={{0,16},{8,24},{16,0},{24,8},{1,17},{9,25},{17,1},{25,9},{2,18},{10... | collective-permute-start | bytes 294920 | tf_op jit(solution)/shard_map/ppermute | solution.py:240
  17.8 1.5 %collective-permute-start.3 = (f32[128,512]{1,0:T(8,128)S(1)}, f32[128,512]{1,0:T(8,128)S(1)}, u32[]{:S(2)}, u32[]{:S(2)}) collective-permute-start(f32[128,512]{1,0:T(8,128)S(1)} %get-tuple-element.41.refs_1_), channel_id=1, source_target_pairs={{0,2},{2,0},{1,3},{3,1},{4,6},{6,4},{5,7},{7,5},{8,10},{10,8},{9,1... | collective-permute-start | bytes 786440 | tf_op jit(solution)/shard_map/ppermute | solution.py:240
  24.7 3.4 %collective-permute-done.15.refs_3_ = f32[192,128]{1,0:T(8,128)S(1)} collective-permute-done((f32[192,128]{1,0:T(8,128)S(1)}, f32[192,128]{1,0:T(8,128)S(1)}, u32[]{:S(2)}, u32[]{:S(2)}) %collective-permute-start.15) | collective-permute-done | bytes 98336 | tf_op jit(solution)/shard_map/ppermute | solution.py:240
  30.2 1.9 %collective-permute-done.3.refs_5_ = f32[128,512]{1,0:T(8,128)S(1)} collective-permute-done((f32[128,512]{1,0:T(8,128)S(1)}, f32[128,512]{1,0:T(8,128)S(1)}, u32[]{:S(2)}, u32[]{:S(2)}) %collective-permute-start.3) | collective-permute-done | bytes 262176 | tf_op jit(solution)/shard_map/ppermute | solution.py:240
  33.7 3.8 %collective-permute-done.5.refs_1_.refs_7_ = f32[128,512]{1,0:T(8,128)S(1)} collective-permute-done((f32[128,512]{1,0:T(8,128)S(1)}, f32[128,512]{1,0:T(8,128)S(1)}, u32[]{:S(2)}, u32[]{:S(2)}) %collective-permute-start.5) | collective-permute-done | bytes 262176 | tf_op jit(solution)/shard_map/ppermute | solution.py:240
  37.5 1.8 %collective-permute-start.28 = (f32[512,128]{1,0:T(8,128)S(1)}, f32[512,128]{1,0:T(8,128)S(1)}, u32[]{:S(2)}, u32[]{:S(2)}) collective-permute-start(f32[512,128]{1,0:T(8,128)S(1)} %get-tuple-element.44), channel_id=1, source_target_pairs={{0,1},{1,0},{2,3},{3,2},{4,6},{5,7},{6,4},{7,5},{8,9},{9,8},{10,11... | collective-permute-start | bytes 786440 | tf_op jit(solution)/shard_map/ppermute | solution.py:255
  43.8 3.3 %collective-permute-start.9 = (f32[32,512]{1,0:T(8,128)S(1)}, f32[32,512]{1,0:T(8,128)S(1)}, u32[]{:S(2)}, u32[]{:S(2)}) collective-permute-start(f32[32,512]{1,0:T(8,128)S(1)} %get-tuple-element.25), channel_id=1, source_target_pairs={{0,24},{8,16},{16,8},{24,0},{1,25},{9,17},{17,9},{25,1},{2,26},{10... | collective-permute-start | bytes 196616 | tf_op jit(solution)/shard_map/ppermute | solution.py:240
  49.1 2.3 %collective-permute-done.8.refs_2_ = f32[32,512]{1,0:T(8,128)S(1)} collective-permute-done((f32[32,512]{1,0:T(8,128)S(1)}, f32[32,512]{1,0:T(8,128)S(1)}, u32[]{:S(2)}, u32[]{:S(2)}) %collective-permute-start.8) | collective-permute-done | bytes 65568 | tf_op jit(solution)/shard_map/ppermute | solution.py:240
  54.0 4.8 %collective-permute-done.10.refs_5_ = f32[32,512]{1,0:T(8,128)S(1)} collective-permute-done((f32[32,512]{1,0:T(8,128)S(1)}, f32[32,512]{1,0:T(8,128)S(1)}, u32[]{:S(2)}, u32[]{:S(2)}) %collective-permute-start.10) | collective-permute-done | bytes 65568 | tf_op jit(solution)/shard_map/ppermute | solution.py:240
  61.6 1.6 %collective-permute-start.33 = (f32[128,512]{1,0:T(8,128)S(1)}, f32[128,512]{1,0:T(8,128)S(1)}, u32[]{:S(2)}, u32[]{:S(2)}) collective-permute-start(f32[128,512]{1,0:T(8,128)S(1)} %get-tuple-element.37.refs_9_.refs_1_), channel_id=1, source_target_pairs={{0,1},{1,0},{2,3},{3,2},{4,5},{5,4},{6,7},{7,6},{8,9},{9,8},{10,11... | collective-permute-start | bytes 786440 | tf_op jit(solution)/shard_map/ppermute | solution.py:240
  67.6 2.7 %collective-permute-done.33.refs_11_.refs_3_ = f32[128,512]{1,0:T(8,128)S(1)} collective-permute-done((f32[128,512]{1,0:T(8,128)S(1)}, f32[128,512]{1,0:T(8,128)S(1)}, u32[]{:S(2)}, u32[]{:S(2)}) %collective-permute-start.33) | collective-permute-done | bytes 262176 | tf_op jit(solution)/shard_map/ppermute | solution.py:240
  70.3 2.0 %collective-permute-done.34.refs_12_.refs_4_ = f32[128,512]{1,0:T(8,128)S(1)} collective-permute-done((f32[128,512]{1,0:T(8,128)S(1)}, f32[128,512]{1,0:T(8,128)S(1)}, u32[]{:S(2)}, u32[]{:S(2)}) %collective-permute-start.34) | collective-permute-done | bytes 262176 | tf_op jit(solution)/shard_map/ppermute | solution.py:240
  75.2 1.5 %collective-permute-start.35 = (f32[128,512]{1,0:T(8,128)S(1)}, f32[128,512]{1,0:T(8,128)S(1)}, u32[]{:S(2)}, u32[]{:S(2)}) collective-permute-start(f32[128,512]{1,0:T(8,128)S(1)} %get-tuple-element.37.refs_9_.refs_1_), channel_id=1, source_target_pairs={{0,2},{2,0},{1,3},{3,1},{4,6},{6,4},{5,7},{7,5},{8,10},{10,8},{9,1... | collective-permute-start | bytes 786440 | tf_op jit(solution)/shard_map/ppermute | solution.py:240
  76.8 4.4 %collective-permute-done.26.refs_2_ = f32[64,512]{1,0:T(8,128)S(1)} collective-permute-done((f32[64,512]{1,0:T(8,128)S(1)}, f32[64,512]{1,0:T(8,128)S(1)}, u32[]{:S(2)}, u32[]{:S(2)}) %collective-permute-start.26) | collective-permute-done | bytes 131104 | tf_op jit(solution)/shard_map/ppermute | solution.py:240
  87.3 2.0 %collective-permute-done.36.refs_0_.refs_6_ = f32[128,512]{1,0:T(8,128)S(1)} collective-permute-done((f32[128,512]{1,0:T(8,128)S(1)}, f32[128,512]{1,0:T(8,128)S(1)}, u32[]{:S(2)}, u32[]{:S(2)}) %collective-permute-start.36) | collective-permute-done | bytes 262176 | tf_op jit(solution)/shard_map/ppermute | solution.py:240
  89.3 1.6 %collective-permute-done.37.refs_1_.refs_7_ = f32[128,512]{1,0:T(8,128)S(1)} collective-permute-done((f32[128,512]{1,0:T(8,128)S(1)}, f32[128,512]{1,0:T(8,128)S(1)}, u32[]{:S(2)}, u32[]{:S(2)}) %collective-permute-start.37) | collective-permute-done | bytes 262176 | tf_op jit(solution)/shard_map/ppermute | solution.py:240
  92.7 1.8 %collective-permute-start.39 = (f32[64,512]{1,0:T(8,128)S(1)}, f32[64,512]{1,0:T(8,128)S(1)}, u32[]{:S(2)}, u32[]{:S(2)}) collective-permute-start(f32[64,512]{1,0:T(8,128)S(1)} %add.7.x), channel_id=1, source_target_pairs={{0,8},{8,0},{16,24},{24,16},{1,9},{9,1},{17,25},{25,17},{2,10},{10... | collective-permute-start | bytes 393224 | tf_op jit(solution)/shard_map/ppermute | solution.py:240
  94.5 2.6 %collective-permute-start.41 = (f32[64,512]{1,0:T(8,128)S(1)}, f32[64,512]{1,0:T(8,128)S(1)}, u32[]{:S(2)}, u32[]{:S(2)}) collective-permute-start(f32[64,512]{1,0:T(8,128)S(1)} %add.7.x), channel_id=1, source_target_pairs={{0,24},{8,16},{16,8},{24,0},{1,25},{9,17},{17,9},{25,1},{2,26},{10... | collective-permute-start | bytes 393224 | tf_op jit(solution)/shard_map/ppermute | solution.py:240
  97.2 1.6 %collective-permute-done.39.refs_1_ = f32[64,512]{1,0:T(8,128)S(1)} collective-permute-done((f32[64,512]{1,0:T(8,128)S(1)}, f32[64,512]{1,0:T(8,128)S(1)}, u32[]{:S(2)}, u32[]{:S(2)}) %collective-permute-start.39) | collective-permute-done | bytes 131104 | tf_op jit(solution)/shard_map/ppermute | solution.py:240
  98.8 8.0 %collective-permute-done.40.refs_2_ = f32[64,512]{1,0:T(8,128)S(1)} collective-permute-done((f32[64,512]{1,0:T(8,128)S(1)}, f32[64,512]{1,0:T(8,128)S(1)}, u32[]{:S(2)}, u32[]{:S(2)}) %collective-permute-start.40) | collective-permute-done | bytes 131104 | tf_op jit(solution)/shard_map/ppermute | solution.py:240
  (99 shorter events, 41.1 us)
Async XLA Ops:
  1.1 21.7 %collective-permute-start.1 = (f32[128,512]{1,0:T(8,128)S(1)}, f32[128,512]{1,0:T(8,128)S(1)}, u32[]{:S(2)}, u32[]{:S(2)}) collective-permute-start(f32[128,512]{1,0:T(8,128)S(1)} %get-tuple-element.41.refs_1_), channel_id=1, source_target_pairs={{0,1},{1,0},{2,3},{3,2},{4,5},{5,4},{6,7},{7,6},{8,9},{9,8},{10,11... | collective-permute-start | bytes 786440 | tf_op jit(solution)/shard_map/ppermute | solution.py:240
  17.3 12.3 %collective-permute-start.2 = (f32[128,512]{1,0:T(8,128)S(1)}, f32[128,512]{1,0:T(8,128)S(1)}, u32[]{:S(2)}, u32[]{:S(2)}) collective-permute-start(f32[128,512]{1,0:T(8,128)S(1)} %get-tuple-element.21.refs_0_), channel_id=1, source_target_pairs={{0,2},{2,0},{1,3},{3,1},{4,6},{6,4},{5,7},{7,5},{8,10},{10,8},{9,1... | collective-permute-start | bytes 786440 | tf_op jit(solution)/shard_map/ppermute | solution.py:240
  17.8 14.3 %collective-permute-start.3 = (f32[128,512]{1,0:T(8,128)S(1)}, f32[128,512]{1,0:T(8,128)S(1)}, u32[]{:S(2)}, u32[]{:S(2)}) collective-permute-start(f32[128,512]{1,0:T(8,128)S(1)} %get-tuple-element.41.refs_1_), channel_id=1, source_target_pairs={{0,2},{2,0},{1,3},{3,1},{4,6},{6,4},{5,7},{7,5},{8,10},{10,8},{9,1... | collective-permute-start | bytes 786440 | tf_op jit(solution)/shard_map/ppermute | solution.py:240
  19.4 12.8 %collective-permute-start = (f32[128,512]{1,0:T(8,128)S(1)}, f32[128,512]{1,0:T(8,128)S(1)}, u32[]{:S(2)}, u32[]{:S(2)}) collective-permute-start(f32[128,512]{1,0:T(8,128)S(1)} %get-tuple-element.21.refs_0_), channel_id=1, source_target_pairs={{0,1},{1,0},{2,3},{3,2},{4,5},{5,4},{6,7},{7,6},{8,9},{9,8},{10,11... | collective-permute-start | bytes 786440 | tf_op jit(solution)/shard_map/ppermute | solution.py:240
  22.9 14.6 %collective-permute-start.5 = (f32[128,512]{1,0:T(8,128)S(1)}, f32[128,512]{1,0:T(8,128)S(1)}, u32[]{:S(2)}, u32[]{:S(2)}) collective-permute-start(f32[128,512]{1,0:T(8,128)S(1)} %collective-permute-done.1.refs_3_), channel_id=1, source_target_pairs={{0,2},{2,0},{1,3},{3,1},{4,6},{6,4},{5,7},{7,5},{8,10},{10,8},{9,1... | collective-permute-start | bytes 786440 | tf_op jit(solution)/shard_map/ppermute | solution.py:240
  28.1 15.1 %collective-permute-start.19 = (f32[128,512]{1,0:T(8,128)S(1)}, f32[128,512]{1,0:T(8,128)S(1)}, u32[]{:S(2)}, u32[]{:S(2)}) collective-permute-start(f32[128,512]{1,0:T(8,128)S(1)} %get-tuple-element.39.refs_9_.refs_1_), channel_id=1, source_target_pairs={{0,1},{1,0},{2,3},{3,2},{4,5},{5,4},{6,7},{7,6},{8,9},{9,8},{10,11... | collective-permute-start | bytes 786440 | tf_op jit(solution)/shard_map/ppermute | solution.py:240
  29.6 14.2 %collective-permute-start.20 = (f32[128,512]{1,0:T(8,128)S(1)}, f32[128,512]{1,0:T(8,128)S(1)}, u32[]{:S(2)}, u32[]{:S(2)}) collective-permute-start(f32[128,512]{1,0:T(8,128)S(1)} %get-tuple-element.40.refs_8_.refs_0_), channel_id=1, source_target_pairs={{0,2},{2,0},{1,3},{3,1},{4,6},{6,4},{5,7},{7,5},{8,10},{10,8},{9,1... | collective-permute-start | bytes 786440 | tf_op jit(solution)/shard_map/ppermute | solution.py:240
  32.1 16.5 %collective-permute-start.16 = (f32[768,128]{1,0:T(8,128)S(1)}, f32[768,128]{1,0:T(8,128)S(1)}, u32[]{:S(2)}, u32[]{:S(2)}) collective-permute-start(f32[768,128]{1,0:T(8,128)S(1)} %shard_map.44.refs_7_), channel_id=1, source_target_pairs={{0,4},{4,0},{1,5},{5,1},{2,6},{6,2},{3,7},{7,3},{8,12},{12,8},{9,1... | collective-permute-start | bytes 1179656 | tf_op jit(solution)/shard_map/ppermute | solution.py:240
  37.5 9.6 %collective-permute-start.28 = (f32[512,128]{1,0:T(8,128)S(1)}, f32[512,128]{1,0:T(8,128)S(1)}, u32[]{:S(2)}, u32[]{:S(2)}) collective-permute-start(f32[512,128]{1,0:T(8,128)S(1)} %get-tuple-element.44), channel_id=1, source_target_pairs={{0,1},{1,0},{2,3},{3,2},{4,6},{5,7},{6,4},{7,5},{8,9},{9,8},{10,11... | collective-permute-start | bytes 786440 | tf_op jit(solution)/shard_map/ppermute | solution.py:255
  42.6 10.3 %collective-permute-start.7 = (f32[64,512]{1,0:T(8,128)S(1)}, f32[64,512]{1,0:T(8,128)S(1)}, u32[]{:S(2)}, u32[]{:S(2)}) collective-permute-start(f32[64,512]{1,0:T(8,128)S(1)} %get-tuple-element.24.x.own), channel_id=1, source_target_pairs={{0,8},{8,0},{16,24},{24,16},{1,9},{9,1},{17,25},{25,17},{2,10},{10... | collective-permute-start | bytes 393224 | tf_op jit(solution)/shard_map/ppermute | solution.py:240
  43.8 9.7 %collective-permute-start.9 = (f32[32,512]{1,0:T(8,128)S(1)}, f32[32,512]{1,0:T(8,128)S(1)}, u32[]{:S(2)}, u32[]{:S(2)}) collective-permute-start(f32[32,512]{1,0:T(8,128)S(1)} %get-tuple-element.25), channel_id=1, source_target_pairs={{0,24},{8,16},{16,8},{24,0},{1,25},{9,17},{17,9},{25,1},{2,26},{10... | collective-permute-start | bytes 196616 | tf_op jit(solution)/shard_map/ppermute | solution.py:240
  47.1 14.4 %collective-permute-start.18 = (f32[128,512]{1,0:T(8,128)S(1)}, f32[128,512]{1,0:T(8,128)S(1)}, u32[]{:S(2)}, u32[]{:S(2)}) collective-permute-start(f32[128,512]{1,0:T(8,128)S(1)} %get-tuple-element.40.refs_8_.refs_0_), channel_id=1, source_target_pairs={{0,1},{1,0},{2,3},{3,2},{4,5},{5,4},{6,7},{7,6},{8,9},{9,8},{10,11... | collective-permute-start | bytes 786440 | tf_op jit(solution)/shard_map/ppermute | solution.py:240
  48.6 13.0 %collective-permute-start.21 = (f32[128,512]{1,0:T(8,128)S(1)}, f32[128,512]{1,0:T(8,128)S(1)}, u32[]{:S(2)}, u32[]{:S(2)}) collective-permute-start(f32[128,512]{1,0:T(8,128)S(1)} %get-tuple-element.39.refs_9_.refs_1_), channel_id=1, source_target_pairs={{0,2},{2,0},{1,3},{3,1},{4,6},{6,4},{5,7},{7,5},{8,10},{10,8},{9,1... | collective-permute-start | bytes 786440 | tf_op jit(solution)/shard_map/ppermute | solution.py:240
  51.4 11.8 %collective-permute-start.22 = (f32[128,512]{1,0:T(8,128)S(1)}, f32[128,512]{1,0:T(8,128)S(1)}, u32[]{:S(2)}, u32[]{:S(2)}) collective-permute-start(f32[128,512]{1,0:T(8,128)S(1)} %collective-permute-done.20.refs_12_.refs_4_), channel_id=1, source_target_pairs={{0,1},{1,0},{2,3},{3,2},{4,5},{5,4},{6,7},{7,6},{8,9},{9,8},{10,11... | collective-permute-start | bytes 786440 | tf_op jit(solution)/shard_map/ppermute | solution.py:240
  61.5 13.1 %collective-permute-start.30 = (f32[256,384]{1,0:T(8,128)S(1)}, f32[256,384]{1,0:T(8,128)S(1)}, u32[]{:S(2)}, u32[]{:S(2)}) collective-permute-start(f32[256,384]{1,0:T(8,128)S(1)} %shard_map.50), channel_id=1, source_target_pairs={{0,4},{4,0},{1,5},{5,1},{2,6},{6,2},{3,7},{7,3},{8,12},{12,8},{9,1... | collective-permute-start | bytes 1179656 | tf_op jit(solution)/shard_map/ppermute | solution.py:240
  63.7 9.4 %collective-permute-start.42 = (f32[512,128]{1,0:T(8,128)S(1)}, f32[512,128]{1,0:T(8,128)S(1)}, u32[]{:S(2)}, u32[]{:S(2)}) collective-permute-start(f32[512,128]{1,0:T(8,128)S(1)} %get-tuple-element.43), channel_id=1, source_target_pairs={{0,1},{1,0},{2,3},{3,2},{4,6},{5,7},{6,4},{7,5},{8,9},{9,8},{10,11... | collective-permute-start | bytes 786440 | tf_op jit(solution)/shard_map/ppermute | solution.py:255
  70.3 10.9 %collective-permute-start.26 = (f32[64,512]{1,0:T(8,128)S(1)}, f32[64,512]{1,0:T(8,128)S(1)}, u32[]{:S(2)}, u32[]{:S(2)}) collective-permute-start(f32[64,512]{1,0:T(8,128)S(1)} %add.6.x), channel_id=1, source_target_pairs={{0,16},{8,24},{16,0},{24,8},{1,17},{9,25},{17,1},{25,9},{2,18},{10... | collective-permute-start | bytes 393224 | tf_op jit(solution)/shard_map/ppermute | solution.py:240
  72.4 10.0 %collective-permute-start.27 = (f32[64,512]{1,0:T(8,128)S(1)}, f32[64,512]{1,0:T(8,128)S(1)}, u32[]{:S(2)}, u32[]{:S(2)}) collective-permute-start(f32[64,512]{1,0:T(8,128)S(1)} %add.6.x), channel_id=1, source_target_pairs={{0,24},{8,16},{16,8},{24,0},{1,25},{9,17},{17,9},{25,1},{2,26},{10... | collective-permute-start | bytes 393224 | tf_op jit(solution)/shard_map/ppermute | solution.py:240
  73.1 11.3 %collective-permute-start.32 = (f32[128,512]{1,0:T(8,128)S(1)}, f32[128,512]{1,0:T(8,128)S(1)}, u32[]{:S(2)}, u32[]{:S(2)}) collective-permute-start(f32[128,512]{1,0:T(8,128)S(1)} %get-tuple-element.38.refs_8_.refs_0_), channel_id=1, source_target_pairs={{0,1},{1,0},{2,3},{3,2},{4,5},{5,4},{6,7},{7,6},{8,9},{9,8},{10,11... | collective-permute-start | bytes 786440 | tf_op jit(solution)/shard_map/ppermute | solution.py:240
  74.7 9.6 %collective-permute-start.43 = (f32[256,128]{1,0:T(8,128)S(1)}, f32[256,128]{1,0:T(8,128)S(1)}, u32[]{:S(2)}, u32[]{:S(2)}) collective-permute-start(f32[256,128]{1,0:T(8,128)S(1)} %shard_map.55), channel_id=1, source_target_pairs={{0,2},{1,3},{2,0},{3,1},{4,5},{5,4},{6,7},{7,6},{8,10},{9,11},{10,... | collective-permute-start | bytes 393224 | tf_op jit(solution)/shard_map/ppermute | solution.py:257
  75.2 10.8 %collective-permute-start.35 = (f32[128,512]{1,0:T(8,128)S(1)}, f32[128,512]{1,0:T(8,128)S(1)}, u32[]{:S(2)}, u32[]{:S(2)}) collective-permute-start(f32[128,512]{1,0:T(8,128)S(1)} %get-tuple-element.37.refs_9_.refs_1_), channel_id=1, source_target_pairs={{0,2},{2,0},{1,3},{3,1},{4,6},{6,4},{5,7},{7,5},{8,10},{10,8},{9,1... | collective-permute-start | bytes 786440 | tf_op jit(solution)/shard_map/ppermute | solution.py:240
  84.4 12.8 %collective-permute-start.44 = (f32[256,384]{1,0:T(8,128)S(1)}, f32[256,384]{1,0:T(8,128)S(1)}, u32[]{:S(2)}, u32[]{:S(2)}) collective-permute-start(f32[256,384]{1,0:T(8,128)S(1)} %shard_map.56), channel_id=1, source_target_pairs={{0,4},{4,0},{1,5},{5,1},{2,6},{6,2},{3,7},{7,3},{8,12},{12,8},{9,1... | collective-permute-start | bytes 1179656 | tf_op jit(solution)/shard_map/ppermute | solution.py:240
  94.5 12.2 %collective-permute-start.40 = (f32[64,512]{1,0:T(8,128)S(1)}, f32[64,512]{1,0:T(8,128)S(1)}, u32[]{:S(2)}, u32[]{:S(2)}) collective-permute-start(f32[64,512]{1,0:T(8,128)S(1)} %add.7.x), channel_id=1, source_target_pairs={{0,16},{8,24},{16,0},{24,8},{1,17},{9,25},{17,1},{25,9},{2,18},{10... | collective-permute-start | bytes 393224 | tf_op jit(solution)/shard_map/ppermute | solution.py:240
  94.5 12.2 %collective-permute-start.41 = (f32[64,512]{1,0:T(8,128)S(1)}, f32[64,512]{1,0:T(8,128)S(1)}, u32[]{:S(2)}, u32[]{:S(2)}) collective-permute-start(f32[64,512]{1,0:T(8,128)S(1)} %add.7.x), channel_id=1, source_target_pairs={{0,24},{8,16},{16,8},{24,0},{1,25},{9,17},{17,9},{25,1},{2,26},{10... | collective-permute-start | bytes 393224 | tf_op jit(solution)/shard_map/ppermute | solution.py:240
  (24 other events, 159.0 us)

commit v12 on v11

--- a/solution.py
+++ b/solution.py
@@ -152,8 +152,8 @@
         out[pl.ds(pl.multiple_of(n * rows + (z ^ by) * (rows // 2), 8), rows // 2), :] = ref[rows:]
 
 
-def two_steps(planes, k, top):
-    return planes == 4 and k == top
+def two_steps(planes, k):
+    return planes == 4 and k == 0
 
 
 def summed(refs):
@@ -293,7 +293,7 @@
 
     def reduced(keep, send, k):
         received = swap(send, "core")
-        if two_steps(sums, k, top):
+        if two_steps(sums, k):
             piece = jax.ShapeDtypeStruct((share // 4, width), F32)
             s, low = call(meet_kernel, [part, piece], [keep, received], 0)
             r = [swap(s, "z", 1), swap(low, "z", 2), swap(low, "z", 3)]

time: 110 us -> 111 us (level)
    ppermute x40, waiting for transfers between devices: 46.5 us -> 42.9 us  [swap(): return lax.ppermute(a, axis, [(i, i ^ by) for i in range(n)])]
    ppermute x2, waiting for transfers between devices: 0.01 us -> 3.6 us  [gather_factor(): lax.ppermute(mine, axes, [(i, i ^ (1 if i >= n // 2 else 2)) for i in ran...]
  transfers between devices with their start and end apart: 46 -> 46, of which waited for: 21 -> 23; matrix products, arithmetic and copies ran while one was open for 1% -> 1% of each run, Pallas kernels for 5% -> 5%
where the time goes in v12:
time: 111 us; the launch traced here: 110 us
  waiting for transfers between devices  52.5 us (47%)
  starting transfers between devices  47.8 us (43%)
  Pallas kernels  7.31 us (7%)
  local copies, waits for them, and re-layouts  2.43 us (2%)
    ppermute x40, waiting for transfers between devices, swap(): return lax.ppermute(a, axis, [(i, i ^ by) for i in range(n)])  42.9 us
    ppermute x40, starting transfers between devices, swap(): return lax.ppermute(a, axis, [(i, i ^ by) for i in range(n)])  40.4 us
    pallas_call x22, Pallas kernels, call(): pl.pallas_call(kernel, out_shape=outs, in_specs=vmem(len(args)), out_spec...  7.31 us
    ppermute x1, waiting for transfers between devices, spread_factor(): across = lax.ppermute(part, axes, [(i, i ^ 3) for i in range(n)])  5.85 us
    ppermute x2, waiting for transfers between devices, gather_factor(): lax.ppermute(mine, axes, [(i, i ^ (1 if i >= n // 2 else 2)) for i in ran...  3.6 us
    ppermute x2, starting transfers between devices, gather_factor(): lax.ppermute(own, axes, [(i, i ^ (2 if i >= n // 2 else 1)) for i in rang...  3.27 us
    ppermute x1, starting transfers between devices, spread_factor(): across = lax.ppermute(part, axes, [(i, i ^ 3) for i in range(n)])  2.91 us
    slice x2, local copies, waits for them, and re-layouts, gather(): a, b = (block[:half], block[half:])  2.39 us
  transfers between devices with their start and end apart: 46, of which 23 were waited for; matrix products, arithmetic and copies ran while one was open for 1% of the time, Pallas kernels for 5%

profile of v12, /device:TPU:0, one launch (start us, length us, event | category | flops | bytes accessed | tf_op | source)
XLA Modules:
  0.0 110.4 jit_solution(14195276266711049061)
XLA Ops:
  1.1 3.0 %collective-permute-start.1 = (f32[128,512]{1,0:T(8,128)S(1)}, f32[128,512]{1,0:T(8,128)S(1)}, u32[]{:S(2)}, u32[]{:S(2)}) collective-permute-start(f32[128,512]{1,0:T(8,128)S(1)} %get-tuple-element.41.refs_1_), channel_id=1, source_target_pairs={{0,1},{1,0},{2,3},{3,2},{4,5},{5,4},{6,7},{7,6},{8,9},{9,8},{10,11... | collective-permute-start | bytes 786440 | tf_op jit(solution)/shard_map/ppermute | solution.py:240
  4.3 2.9 %collective-permute-start.11 = (f32[64,128]{1,0:T(8,128)S(1)}, f32[64,128]{1,0:T(8,128)S(1)}, u32[]{:S(2)}, u32[]{:S(2)}) collective-permute-start(f32[64,128]{1,0:T(8,128)S(1)} %get-tuple-element.25), channel_id=1, source_target_pairs={{0,3},{1,2},{2,1},{3,0},{4,7},{5,6},{6,5},{7,4},{8,11},{9,10},{10,... | collective-permute-start | bytes 98312 | tf_op jit(solution)/shard_map/ppermute | solution.py:269
  7.2 5.9 %collective-permute-done.11.across = f32[64,128]{1,0:T(8,128)S(1)} collective-permute-done((f32[64,128]{1,0:T(8,128)S(1)}, f32[64,128]{1,0:T(8,128)S(1)}, u32[]{:S(2)}, u32[]{:S(2)}) %collective-permute-start.11) | collective-permute-done | bytes 32800 | tf_op jit(solution)/shard_map/ppermute | solution.py:269
  13.1 1.6 %collective-permute-start.12 = (f32[192,128]{1,0:T(8,128)S(1)}, f32[192,128]{1,0:T(8,128)S(1)}, u32[]{:S(2)}, u32[]{:S(2)}) collective-permute-start(f32[192,128]{1,0:T(8,128)S(1)} %shard_map.41.refs_0_), channel_id=1, source_target_pairs={{0,8},{8,0},{16,24},{24,16},{1,9},{9,1},{17,25},{25,17},{2,10},{10... | collective-permute-start | bytes 294920 | tf_op jit(solution)/shard_map/ppermute | solution.py:240
  14.7 2.6 %collective-permute-start.13 = (f32[192,128]{1,0:T(8,128)S(1)}, f32[192,128]{1,0:T(8,128)S(1)}, u32[]{:S(2)}, u32[]{:S(2)}) collective-permute-start(f32[192,128]{1,0:T(8,128)S(1)} %shard_map.41.refs_0_), channel_id=1, source_target_pairs={{0,16},{8,24},{16,0},{24,8},{1,17},{9,25},{17,1},{25,9},{2,18},{10... | collective-permute-start | bytes 294920 | tf_op jit(solution)/shard_map/ppermute | solution.py:240
  17.8 1.5 %collective-permute-start.3 = (f32[128,512]{1,0:T(8,128)S(1)}, f32[128,512]{1,0:T(8,128)S(1)}, u32[]{:S(2)}, u32[]{:S(2)}) collective-permute-start(f32[128,512]{1,0:T(8,128)S(1)} %get-tuple-element.41.refs_1_), channel_id=1, source_target_pairs={{0,2},{2,0},{1,3},{3,1},{4,6},{6,4},{5,7},{7,5},{8,10},{10,8},{9,1... | collective-permute-start | bytes 786440 | tf_op jit(solution)/shard_map/ppermute | solution.py:240
  24.7 3.4 %collective-permute-done.14.refs_3_ = f32[192,128]{1,0:T(8,128)S(1)} collective-permute-done((f32[192,128]{1,0:T(8,128)S(1)}, f32[192,128]{1,0:T(8,128)S(1)}, u32[]{:S(2)}, u32[]{:S(2)}) %collective-permute-start.14) | collective-permute-done | bytes 98336 | tf_op jit(solution)/shard_map/ppermute | solution.py:240
  30.2 1.9 %collective-permute-done.3.refs_5_ = f32[128,512]{1,0:T(8,128)S(1)} collective-permute-done((f32[128,512]{1,0:T(8,128)S(1)}, f32[128,512]{1,0:T(8,128)S(1)}, u32[]{:S(2)}, u32[]{:S(2)}) %collective-permute-start.3) | collective-permute-done | bytes 262176 | tf_op jit(solution)/shard_map/ppermute | solution.py:240
  33.7 3.8 %collective-permute-done.5.refs_1_.refs_7_ = f32[128,512]{1,0:T(8,128)S(1)} collective-permute-done((f32[128,512]{1,0:T(8,128)S(1)}, f32[128,512]{1,0:T(8,128)S(1)}, u32[]{:S(2)}, u32[]{:S(2)}) %collective-permute-start.5) | collective-permute-done | bytes 262176 | tf_op jit(solution)/shard_map/ppermute | solution.py:240
  37.5 1.8 %collective-permute-start.27 = (f32[512,128]{1,0:T(8,128)S(1)}, f32[512,128]{1,0:T(8,128)S(1)}, u32[]{:S(2)}, u32[]{:S(2)}) collective-permute-start(f32[512,128]{1,0:T(8,128)S(1)} %get-tuple-element.44), channel_id=1, source_target_pairs={{0,1},{1,0},{2,3},{3,2},{4,6},{5,7},{6,4},{7,5},{8,9},{9,8},{10,11... | collective-permute-start | bytes 786440 | tf_op jit(solution)/shard_map/ppermute | solution.py:255
  43.8 3.3 %collective-permute-start.9 = (f32[64,512]{1,0:T(8,128)S(1)}, f32[64,512]{1,0:T(8,128)S(1)}, u32[]{:S(2)}, u32[]{:S(2)}) collective-permute-start(f32[64,512]{1,0:T(8,128)S(1)} %add.6.x), channel_id=1, source_target_pairs={{0,24},{8,16},{16,8},{24,0},{1,25},{9,17},{17,9},{25,1},{2,26},{10... | collective-permute-start | bytes 393224 | tf_op jit(solution)/shard_map/ppermute | solution.py:240
  51.3 4.7 %collective-permute-done.8.refs_2_ = f32[64,512]{1,0:T(8,128)S(1)} collective-permute-done((f32[64,512]{1,0:T(8,128)S(1)}, f32[64,512]{1,0:T(8,128)S(1)}, u32[]{:S(2)}, u32[]{:S(2)}) %collective-permute-start.8) | collective-permute-done | bytes 131104 | tf_op jit(solution)/shard_map/ppermute | solution.py:240
  56.5 1.5 %collective-permute-start.22 = (f32[128,512]{1,0:T(8,128)S(1)}, f32[128,512]{1,0:T(8,128)S(1)}, u32[]{:S(2)}, u32[]{:S(2)}) collective-permute-start(f32[128,512]{1,0:T(8,128)S(1)} %collective-permute-done.18.refs_11_.refs_3_), channel_id=1, source_target_pairs={{0,2},{2,0},{1,3},{3,1},{4,6},{6,4},{5,7},{7,5},{8,10},{10,8},{9,1... | collective-permute-start | bytes 786440 | tf_op jit(solution)/shard_map/ppermute | solution.py:240
  58.5 3.6 %collective-permute-done.28.across.refs_6_ = f32[256,128]{1,0:T(8,128)S(1)} collective-permute-done((f32[256,128]{1,0:T(8,128)S(1)}, f32[256,128]{1,0:T(8,128)S(1)}, u32[]{:S(2)}, u32[]{:S(2)}) %collective-permute-start.28) | collective-permute-done | bytes 131104 | tf_op jit(solution)/shard_map/ppermute | solution.py:257
  68.5 2.5 %collective-permute-done.32.refs_11_.refs_3_ = f32[128,512]{1,0:T(8,128)S(1)} collective-permute-done((f32[128,512]{1,0:T(8,128)S(1)}, f32[128,512]{1,0:T(8,128)S(1)}, u32[]{:S(2)}, u32[]{:S(2)}) %collective-permute-start.32) | collective-permute-done | bytes 262176 | tf_op jit(solution)/shard_map/ppermute | solution.py:240
  75.2 1.5 %collective-permute-start.34 = (f32[128,512]{1,0:T(8,128)S(1)}, f32[128,512]{1,0:T(8,128)S(1)}, u32[]{:S(2)}, u32[]{:S(2)}) collective-permute-start(f32[128,512]{1,0:T(8,128)S(1)} %get-tuple-element.37.refs_9_.refs_1_), channel_id=1, source_target_pairs={{0,2},{2,0},{1,3},{3,1},{4,6},{6,4},{5,7},{7,5},{8,10},{10,8},{9,1... | collective-permute-start | bytes 786440 | tf_op jit(solution)/shard_map/ppermute | solution.py:240
  76.8 5.2 %collective-permute-done.25.refs_2_ = f32[64,512]{1,0:T(8,128)S(1)} collective-permute-done((f32[64,512]{1,0:T(8,128)S(1)}, f32[64,512]{1,0:T(8,128)S(1)}, u32[]{:S(2)}, u32[]{:S(2)}) %collective-permute-start.25) | collective-permute-done | bytes 131104 | tf_op jit(solution)/shard_map/ppermute | solution.py:240
  82.0 2.1 %collective-permute-start.35 = (f32[128,512]{1,0:T(8,128)S(1)}, f32[128,512]{1,0:T(8,128)S(1)}, u32[]{:S(2)}, u32[]{:S(2)}) collective-permute-start(f32[128,512]{1,0:T(8,128)S(1)} %collective-permute-done.33.refs_12_.refs_4_), channel_id=1, source_target_pairs={{0,1},{1,0},{2,3},{3,2},{4,5},{5,4},{6,7},{7,6},{8,9},{9,8},{10,11... | collective-permute-start | bytes 786440 | tf_op jit(solution)/shard_map/ppermute | solution.py:240
  87.8 2.3 %collective-permute-done.35.refs_0_.refs_6_ = f32[128,512]{1,0:T(8,128)S(1)} collective-permute-done((f32[128,512]{1,0:T(8,128)S(1)}, f32[128,512]{1,0:T(8,128)S(1)}, u32[]{:S(2)}, u32[]{:S(2)}) %collective-permute-start.35) | collective-permute-done | bytes 262176 | tf_op jit(solution)/shard_map/ppermute | solution.py:240
  92.7 2.6 %collective-permute-start.38 = (f32[64,512]{1,0:T(8,128)S(1)}, f32[64,512]{1,0:T(8,128)S(1)}, u32[]{:S(2)}, u32[]{:S(2)}) collective-permute-start(f32[64,512]{1,0:T(8,128)S(1)} %get-tuple-element.35.x.own), channel_id=1, source_target_pairs={{0,8},{8,0},{16,24},{24,16},{1,9},{9,1},{17,25},{25,17},{2,10},{10... | collective-permute-start | bytes 393224 | tf_op jit(solution)/shard_map/ppermute | solution.py:240
  95.3 2.4 %collective-permute-start.40 = (f32[32,512]{1,0:T(8,128)S(1)}, f32[32,512]{1,0:T(8,128)S(1)}, u32[]{:S(2)}, u32[]{:S(2)}) collective-permute-start(f32[32,512]{1,0:T(8,128)S(1)} %get-tuple-element.36), channel_id=1, source_target_pairs={{0,24},{8,16},{16,8},{24,0},{1,25},{9,17},{17,9},{25,1},{2,26},{10... | collective-permute-start | bytes 196616 | tf_op jit(solution)/shard_map/ppermute | solution.py:240
  97.7 1.8 %collective-permute-done.38.near.refs_1_ = f32[64,512]{1,0:T(8,128)S(1)} collective-permute-done((f32[64,512]{1,0:T(8,128)S(1)}, f32[64,512]{1,0:T(8,128)S(1)}, u32[]{:S(2)}, u32[]{:S(2)}) %collective-permute-start.38) | collective-permute-done | bytes 131104 | tf_op jit(solution)/shard_map/ppermute | solution.py:240
  100.7 3.3 %collective-permute-done.39.refs_2_ = f32[32,512]{1,0:T(8,128)S(1)} collective-permute-done((f32[32,512]{1,0:T(8,128)S(1)}, f32[32,512]{1,0:T(8,128)S(1)}, u32[]{:S(2)}, u32[]{:S(2)}) %collective-permute-start.39) | collective-permute-done | bytes 65568 | tf_op jit(solution)/shard_map/ppermute | solution.py:240
  104.0 3.0 %collective-permute-done.41.refs_5_ = f32[32,512]{1,0:T(8,128)S(1)} collective-permute-done((f32[32,512]{1,0:T(8,128)S(1)}, f32[32,512]{1,0:T(8,128)S(1)}, u32[]{:S(2)}, u32[]{:S(2)}) %collective-permute-start.41) | collective-permute-done | bytes 65568 | tf_op jit(solution)/shard_map/ppermute | solution.py:240
  (99 shorter events, 41.8 us)
Async XLA Ops:
  1.1 21.7 %collective-permute-start.1 = (f32[128,512]{1,0:T(8,128)S(1)}, f32[128,512]{1,0:T(8,128)S(1)}, u32[]{:S(2)}, u32[]{:S(2)}) collective-permute-start(f32[128,512]{1,0:T(8,128)S(1)} %get-tuple-element.41.refs_1_), channel_id=1, source_target_pairs={{0,1},{1,0},{2,3},{3,2},{4,5},{5,4},{6,7},{7,6},{8,9},{9,8},{10,11... | collective-permute-start | bytes 786440 | tf_op jit(solution)/shard_map/ppermute | solution.py:240
  17.3 12.3 %collective-permute-start.2 = (f32[128,512]{1,0:T(8,128)S(1)}, f32[128,512]{1,0:T(8,128)S(1)}, u32[]{:S(2)}, u32[]{:S(2)}) collective-permute-start(f32[128,512]{1,0:T(8,128)S(1)} %get-tuple-element.21.refs_0_), channel_id=1, source_target_pairs={{0,2},{2,0},{1,3},{3,1},{4,6},{6,4},{5,7},{7,5},{8,10},{10,8},{9,1... | collective-permute-start | bytes 786440 | tf_op jit(solution)/shard_map/ppermute | solution.py:240
  17.8 14.3 %collective-permute-start.3 = (f32[128,512]{1,0:T(8,128)S(1)}, f32[128,512]{1,0:T(8,128)S(1)}, u32[]{:S(2)}, u32[]{:S(2)}) collective-permute-start(f32[128,512]{1,0:T(8,128)S(1)} %get-tuple-element.41.refs_1_), channel_id=1, source_target_pairs={{0,2},{2,0},{1,3},{3,1},{4,6},{6,4},{5,7},{7,5},{8,10},{10,8},{9,1... | collective-permute-start | bytes 786440 | tf_op jit(solution)/shard_map/ppermute | solution.py:240
  19.4 12.8 %collective-permute-start = (f32[128,512]{1,0:T(8,128)S(1)}, f32[128,512]{1,0:T(8,128)S(1)}, u32[]{:S(2)}, u32[]{:S(2)}) collective-permute-start(f32[128,512]{1,0:T(8,128)S(1)} %get-tuple-element.21.refs_0_), channel_id=1, source_target_pairs={{0,1},{1,0},{2,3},{3,2},{4,5},{5,4},{6,7},{7,6},{8,9},{9,8},{10,11... | collective-permute-start | bytes 786440 | tf_op jit(solution)/shard_map/ppermute | solution.py:240
  22.9 14.6 %collective-permute-start.5 = (f32[128,512]{1,0:T(8,128)S(1)}, f32[128,512]{1,0:T(8,128)S(1)}, u32[]{:S(2)}, u32[]{:S(2)}) collective-permute-start(f32[128,512]{1,0:T(8,128)S(1)} %collective-permute-done.1.refs_3_), channel_id=1, source_target_pairs={{0,2},{2,0},{1,3},{3,1},{4,6},{6,4},{5,7},{7,5},{8,10},{10,8},{9,1... | collective-permute-start | bytes 786440 | tf_op jit(solution)/shard_map/ppermute | solution.py:240
  28.1 15.1 %collective-permute-start.18 = (f32[128,512]{1,0:T(8,128)S(1)}, f32[128,512]{1,0:T(8,128)S(1)}, u32[]{:S(2)}, u32[]{:S(2)}) collective-permute-start(f32[128,512]{1,0:T(8,128)S(1)} %get-tuple-element.39.refs_9_.refs_1_), channel_id=1, source_target_pairs={{0,1},{1,0},{2,3},{3,2},{4,5},{5,4},{6,7},{7,6},{8,9},{9,8},{10,11... | collective-permute-start | bytes 786440 | tf_op jit(solution)/shard_map/ppermute | solution.py:240
  29.6 14.2 %collective-permute-start.19 = (f32[128,512]{1,0:T(8,128)S(1)}, f32[128,512]{1,0:T(8,128)S(1)}, u32[]{:S(2)}, u32[]{:S(2)}) collective-permute-start(f32[128,512]{1,0:T(8,128)S(1)} %get-tuple-element.40.refs_8_.refs_0_), channel_id=1, source_target_pairs={{0,2},{2,0},{1,3},{3,1},{4,6},{6,4},{5,7},{7,5},{8,10},{10,8},{9,1... | collective-permute-start | bytes 786440 | tf_op jit(solution)/shard_map/ppermute | solution.py:240
  32.1 16.5 %collective-permute-start.15 = (f32[768,128]{1,0:T(8,128)S(1)}, f32[768,128]{1,0:T(8,128)S(1)}, u32[]{:S(2)}, u32[]{:S(2)}) collective-permute-start(f32[768,128]{1,0:T(8,128)S(1)} %shard_map.42.refs_5_), channel_id=1, source_target_pairs={{0,4},{4,0},{1,5},{5,1},{2,6},{6,2},{3,7},{7,3},{8,12},{12,8},{9,1... | collective-permute-start | bytes 1179656 | tf_op jit(solution)/shard_map/ppermute | solution.py:240
  37.5 9.6 %collective-permute-start.27 = (f32[512,128]{1,0:T(8,128)S(1)}, f32[512,128]{1,0:T(8,128)S(1)}, u32[]{:S(2)}, u32[]{:S(2)}) collective-permute-start(f32[512,128]{1,0:T(8,128)S(1)} %get-tuple-element.44), channel_id=1, source_target_pairs={{0,1},{1,0},{2,3},{3,2},{4,6},{5,7},{6,4},{7,5},{8,9},{9,8},{10,11... | collective-permute-start | bytes 786440 | tf_op jit(solution)/shard_map/ppermute | solution.py:255
  43.1 12.8 %collective-permute-start.8 = (f32[64,512]{1,0:T(8,128)S(1)}, f32[64,512]{1,0:T(8,128)S(1)}, u32[]{:S(2)}, u32[]{:S(2)}) collective-permute-start(f32[64,512]{1,0:T(8,128)S(1)} %add.6.x), channel_id=1, source_target_pairs={{0,16},{8,24},{16,0},{24,8},{1,17},{9,25},{17,1},{25,9},{2,18},{10... | collective-permute-start | bytes 393224 | tf_op jit(solution)/shard_map/ppermute | solution.py:240
  43.8 12.7 %collective-permute-start.9 = (f32[64,512]{1,0:T(8,128)S(1)}, f32[64,512]{1,0:T(8,128)S(1)}, u32[]{:S(2)}, u32[]{:S(2)}) collective-permute-start(f32[64,512]{1,0:T(8,128)S(1)} %add.6.x), channel_id=1, source_target_pairs={{0,24},{8,16},{16,8},{24,0},{1,25},{9,17},{17,9},{25,1},{2,26},{10... | collective-permute-start | bytes 393224 | tf_op jit(solution)/shard_map/ppermute | solution.py:240
  47.1 15.0 %collective-permute-start.17 = (f32[128,512]{1,0:T(8,128)S(1)}, f32[128,512]{1,0:T(8,128)S(1)}, u32[]{:S(2)}, u32[]{:S(2)}) collective-permute-start(f32[128,512]{1,0:T(8,128)S(1)} %get-tuple-element.40.refs_8_.refs_0_), channel_id=1, source_target_pairs={{0,1},{1,0},{2,3},{3,2},{4,5},{5,4},{6,7},{7,6},{8,9},{9,8},{10,11... | collective-permute-start | bytes 786440 | tf_op jit(solution)/shard_map/ppermute | solution.py:240
  48.6 14.1 %collective-permute-start.20 = (f32[128,512]{1,0:T(8,128)S(1)}, f32[128,512]{1,0:T(8,128)S(1)}, u32[]{:S(2)}, u32[]{:S(2)}) collective-permute-start(f32[128,512]{1,0:T(8,128)S(1)} %get-tuple-element.39.refs_9_.refs_1_), channel_id=1, source_target_pairs={{0,2},{2,0},{1,3},{3,1},{4,6},{6,4},{5,7},{7,5},{8,10},{10,8},{9,1... | collective-permute-start | bytes 786440 | tf_op jit(solution)/shard_map/ppermute | solution.py:240
  49.8 13.5 %collective-permute-start.21 = (f32[128,512]{1,0:T(8,128)S(1)}, f32[128,512]{1,0:T(8,128)S(1)}, u32[]{:S(2)}, u32[]{:S(2)}) collective-permute-start(f32[128,512]{1,0:T(8,128)S(1)} %collective-permute-done.19.refs_12_.refs_4_), channel_id=1, source_target_pairs={{0,1},{1,0},{2,3},{3,2},{4,5},{5,4},{6,7},{7,6},{8,9},{9,8},{10,11... | collective-permute-start | bytes 786440 | tf_op jit(solution)/shard_map/ppermute | solution.py:240
  56.5 10.1 %collective-permute-start.22 = (f32[128,512]{1,0:T(8,128)S(1)}, f32[128,512]{1,0:T(8,128)S(1)}, u32[]{:S(2)}, u32[]{:S(2)}) collective-permute-start(f32[128,512]{1,0:T(8,128)S(1)} %collective-permute-done.18.refs_11_.refs_3_), channel_id=1, source_target_pairs={{0,2},{2,0},{1,3},{3,1},{4,6},{6,4},{5,7},{7,5},{8,10},{10,8},{9,1... | collective-permute-start | bytes 786440 | tf_op jit(solution)/shard_map/ppermute | solution.py:240
  62.2 12.5 %collective-permute-start.29 = (f32[256,384]{1,0:T(8,128)S(1)}, f32[256,384]{1,0:T(8,128)S(1)}, u32[]{:S(2)}, u32[]{:S(2)}) collective-permute-start(f32[256,384]{1,0:T(8,128)S(1)} %shard_map.48), channel_id=1, source_target_pairs={{0,4},{4,0},{1,5},{5,1},{2,6},{6,2},{3,7},{7,3},{8,12},{12,8},{9,1... | collective-permute-start | bytes 1179656 | tf_op jit(solution)/shard_map/ppermute | solution.py:240
  63.3 9.2 %collective-permute-start.33 = (f32[128,512]{1,0:T(8,128)S(1)}, f32[128,512]{1,0:T(8,128)S(1)}, u32[]{:S(2)}, u32[]{:S(2)}) collective-permute-start(f32[128,512]{1,0:T(8,128)S(1)} %get-tuple-element.38.refs_8_.refs_0_), channel_id=1, source_target_pairs={{0,2},{2,0},{1,3},{3,1},{4,6},{6,4},{5,7},{7,5},{8,10},{10,8},{9,1... | collective-permute-start | bytes 786440 | tf_op jit(solution)/shard_map/ppermute | solution.py:240
  63.8 10.1 %collective-permute-start.42 = (f32[512,128]{1,0:T(8,128)S(1)}, f32[512,128]{1,0:T(8,128)S(1)}, u32[]{:S(2)}, u32[]{:S(2)}) collective-permute-start(f32[512,128]{1,0:T(8,128)S(1)} %get-tuple-element.43), channel_id=1, source_target_pairs={{0,1},{1,0},{2,3},{3,2},{4,6},{5,7},{6,4},{7,5},{8,9},{9,8},{10,11... | collective-permute-start | bytes 786440 | tf_op jit(solution)/shard_map/ppermute | solution.py:255
  71.0 10.9 %collective-permute-start.25 = (f32[64,512]{1,0:T(8,128)S(1)}, f32[64,512]{1,0:T(8,128)S(1)}, u32[]{:S(2)}, u32[]{:S(2)}) collective-permute-start(f32[64,512]{1,0:T(8,128)S(1)} %add.7.x), channel_id=1, source_target_pairs={{0,16},{8,24},{16,0},{24,8},{1,17},{9,25},{17,1},{25,9},{2,18},{10... | collective-permute-start | bytes 393224 | tf_op jit(solution)/shard_map/ppermute | solution.py:240
  72.4 11.6 %collective-permute-start.26 = (f32[64,512]{1,0:T(8,128)S(1)}, f32[64,512]{1,0:T(8,128)S(1)}, u32[]{:S(2)}, u32[]{:S(2)}) collective-permute-start(f32[64,512]{1,0:T(8,128)S(1)} %add.7.x), channel_id=1, source_target_pairs={{0,24},{8,16},{16,8},{24,0},{1,25},{9,17},{17,9},{25,1},{2,26},{10... | collective-permute-start | bytes 393224 | tf_op jit(solution)/shard_map/ppermute | solution.py:240
  73.8 11.3 %collective-permute-start.31 = (f32[128,512]{1,0:T(8,128)S(1)}, f32[128,512]{1,0:T(8,128)S(1)}, u32[]{:S(2)}, u32[]{:S(2)}) collective-permute-start(f32[128,512]{1,0:T(8,128)S(1)} %get-tuple-element.38.refs_8_.refs_0_), channel_id=1, source_target_pairs={{0,1},{1,0},{2,3},{3,2},{4,5},{5,4},{6,7},{7,6},{8,9},{9,8},{10,11... | collective-permute-start | bytes 786440 | tf_op jit(solution)/shard_map/ppermute | solution.py:240
  74.7 10.4 %collective-permute-start.43 = (f32[256,128]{1,0:T(8,128)S(1)}, f32[256,128]{1,0:T(8,128)S(1)}, u32[]{:S(2)}, u32[]{:S(2)}) collective-permute-start(f32[256,128]{1,0:T(8,128)S(1)} %shard_map.55), channel_id=1, source_target_pairs={{0,2},{1,3},{2,0},{3,1},{4,5},{5,4},{6,7},{7,6},{8,10},{9,11},{10,... | collective-permute-start | bytes 393224 | tf_op jit(solution)/shard_map/ppermute | solution.py:257
  75.2 10.5 %collective-permute-start.34 = (f32[128,512]{1,0:T(8,128)S(1)}, f32[128,512]{1,0:T(8,128)S(1)}, u32[]{:S(2)}, u32[]{:S(2)}) collective-permute-start(f32[128,512]{1,0:T(8,128)S(1)} %get-tuple-element.37.refs_9_.refs_1_), channel_id=1, source_target_pairs={{0,2},{2,0},{1,3},{3,1},{4,6},{6,4},{5,7},{7,5},{8,10},{10,8},{9,1... | collective-permute-start | bytes 786440 | tf_op jit(solution)/shard_map/ppermute | solution.py:240
  85.2 15.6 %collective-permute-start.44 = (f32[256,384]{1,0:T(8,128)S(1)}, f32[256,384]{1,0:T(8,128)S(1)}, u32[]{:S(2)}, u32[]{:S(2)}) collective-permute-start(f32[256,384]{1,0:T(8,128)S(1)} %shard_map.56), channel_id=1, source_target_pairs={{0,4},{4,0},{1,5},{5,1},{2,6},{6,2},{3,7},{7,3},{8,12},{12,8},{9,1... | collective-permute-start | bytes 1179656 | tf_op jit(solution)/shard_map/ppermute | solution.py:240
  (24 other events, 156.0 us)
